TPU v7x, 32 devices: a whole 2x2x4 slice. The times are simulated.
32 devices in a mesh: table: 16 (over z, y, x), narrow: 2 (over core).
Axes of the slice: x: 2, y: 2, z: 4, core: 2. Of those that a mesh axis runs over, the one named last changes fastest.
Arguments:
- table_rows: bfloat16 [16384, 256], P('table'), may hold values from -3 to 3
- accum: float32 [16384], P('table'), may hold values from 1 to 100
- factor_down: bfloat16 [2048, 256], P('narrow'), may hold values from -0.125 to 0.125
- factor_up: bfloat16 [2048, 256], P('narrow'), may hold values from -0.375 to 0.375
- cross_bias: float32 [2048], replicated, may hold values from -3 to 3
- out_weight: bfloat16 [2048], replicated, may hold values from -0.125 to 0.125
- target: float32 [4096], P(('table', 'narrow')), may hold values from 0 to 1
- bag_rows: int32 [512, 512], P(('table', 'narrow')), may hold values from -1 to 1023, as said below
- slot_target: int32 [512, 128], P(('table', 'narrow')), may hold values from -1 to 1023, as said below
Outputs:
- logits: float32 [4096], P(('table', 'narrow'))
- down_grad: float32 [2048, 256], P('narrow')
- up_grad: float32 [2048, 256], P('narrow')
- new_rows: bfloat16 [16384, 256], P('table')
- new_accum: float32 [16384], P(('table', 'narrow'))
Inputs may be any that keep to these rules, and one draw needn't show every extreme that they name: `slot_target`: for each source device (its 16 rows): every bag 0 .. 1023 is named by exactly one slot and the other slots hold -1; in every draw each source device has one window all of whose 128 slots are used. `bag_rows`: A used slot holds 1 to 4 rows of the window first and -1 after them; an unused slot holds -1 only; each source device has a slot with 4 lookups.
All inputs are finite; a program needn't handle non-finite values.
Results may differ from a plain program's by a relative error of at most 0.0077.
Values may be sent and summed in bfloat16 or wider, within the bound.
No kernel may reach another device: no remote copies, remote signals or barrier semaphores. Data moves between devices by JAX's collectives and lax.ppermute only.
A program may use at most 64 MiB of HBM per device.

v0:
```python
import math

import jax
import jax.numpy as jnp
from jax import lax
from jax.sharding import PartitionSpec as P

FEAT = 8
HOT = 4


LEARN_RATE = 0.2
LOSS_SCALE = 32.0
ADA_EPS = 1e-06


def transposed_dot(left, right):
    return lax.dot_general(
        left, right, (((0,), (0,)), ((), ())), preferred_element_type=jnp.float32
    )


def rows_dot(left, right):
    return lax.dot_general(
        left, right, (((1,), (1,)), ((), ())), preferred_element_type=jnp.float32
    )


def local(
    table_rows, accum, factor_down, factor_up, cross_bias, out_weight, target, bag_rows, slot_target
):
    tables = lax.axis_size("table")
    narrows = lax.axis_size("narrow")
    row_dev, emb_width = table_rows.shape
    pools_per = slot_target.shape[1]
    samples = target.shape[0]
    bag_count = samples * FEAT
    slot_count = tables * pools_per
    asked = lax.all_to_all(bag_rows, "table", split_axis=0, concat_axis=0, tiled=True)
    lookup_ids = asked.reshape(slot_count, HOT)
    positions = lax.broadcasted_iota(jnp.int32, (1, row_dev), 1)
    counts = jnp.zeros((slot_count, row_dev), jnp.bfloat16)
    for lookup in range(HOT):
        counts = counts + (lookup_ids[:, lookup : lookup + 1] == positions).astype(jnp.bfloat16)
    pool_sums = jnp.dot(counts, table_rows, preferred_element_type=jnp.float32)
    pool_out = pool_sums.astype(jnp.bfloat16).reshape(tables, pools_per, emb_width)
    arrived = lax.all_to_all(pool_out, "table", split_axis=0, concat_axis=0, tiled=True).reshape(
        slot_count, emb_width
    )
    bag_index = lax.broadcasted_iota(jnp.int32, (bag_count, 1), 0)
    placing = (slot_target.reshape(1, slot_count) == bag_index).astype(jnp.bfloat16)
    pooled_feats = (
        jnp.dot(placing, arrived, preferred_element_type=jnp.float32)
        .astype(jnp.bfloat16)
        .reshape(samples, FEAT * emb_width)
    )
    down_full, up_full = (
        lax.all_gather(factor_down, "narrow", axis=0, tiled=True),
        lax.all_gather(factor_up, "narrow", axis=0, tiled=True),
    )
    hidden = jnp.dot(pooled_feats, down_full, preferred_element_type=jnp.float32).astype(
        jnp.bfloat16
    )
    cross_out = rows_dot(hidden, up_full)
    feats_f = pooled_feats.astype(jnp.float32)
    shifted = cross_out + cross_bias
    mixed_out = feats_f * shifted + feats_f
    weight_f = out_weight.astype(jnp.float32)
    logits = jnp.sum(mixed_out * weight_f, axis=1)
    dlogit = LOSS_SCALE * (jax.nn.sigmoid(logits) - target)
    dmixed = dlogit[:, None] * weight_f
    dcross = (dmixed * feats_f).astype(jnp.bfloat16)
    dhidden = jnp.dot(dcross, up_full, preferred_element_type=jnp.float32).astype(jnp.bfloat16)
    back_term = rows_dot(dhidden, down_full)
    dpooled = (dmixed * (shifted + 1.0) + back_term).astype(jnp.bfloat16)
    narrow_sum = lax.psum_scatter(
        jnp.concatenate(
            [transposed_dot(pooled_feats, dhidden), transposed_dot(dcross, hidden)], axis=1
        ).astype(jnp.bfloat16),
        "narrow",
        scatter_dimension=0,
        tiled=True,
    ).astype(jnp.float32)
    grand_total = lax.psum(narrow_sum, "table")
    batch_all = samples * tables * narrows
    grand_total = grand_total * (1.0 / math.sqrt(batch_all))
    rank_size = factor_down.shape[1]
    down_grad = grand_total[:, :rank_size]
    up_grad = grand_total[:, rank_size:]
    bag_grads = dpooled.reshape(bag_count, emb_width)
    slot_grads = (
        transposed_dot(placing, bag_grads)
        .astype(jnp.bfloat16)
        .reshape(tables, pools_per, emb_width)
    )
    returned = lax.all_to_all(slot_grads, "table", split_axis=0, concat_axis=0, tiled=True).reshape(
        slot_count, emb_width
    )
    local_grad = transposed_dot(counts, returned)
    narrow_index = lax.axis_index("narrow")
    share_size = row_dev // narrows
    row_grad = lax.psum(local_grad.astype(jnp.bfloat16), "narrow").astype(jnp.float32)
    accum_all = accum + jnp.mean(row_grad * row_grad, axis=1)
    new_rows = (
        table_rows.astype(jnp.float32)
        - LEARN_RATE * row_grad * lax.rsqrt(accum_all + ADA_EPS)[:, None]
    ).astype(jnp.bfloat16)
    new_accum = lax.dynamic_slice_in_dim(accum_all, narrow_index * share_size, share_size, 0)
    return (logits, down_grad, up_grad, new_rows, new_accum)


def solution(mesh):
    in_specs = (
        P("table", None),
        P("table"),
        P("narrow", None),
        P("narrow", None),
        P(),
        P(),
        P(("table", "narrow")),
        P(("table", "narrow"), None),
        P(("table", "narrow"), None),
    )
    out_specs = (
        P(("table", "narrow")),
        P("narrow", None),
        P("narrow", None),
        P("table", None),
        P(("table", "narrow")),
    )
    return jax.shard_map(local, mesh=mesh, in_specs=in_specs, out_specs=out_specs, check_vma=False)
```

profile of v0, /device:TPU:0, one launch (start us, length us, event | category | flops | bytes accessed | tf_op | source)
XLA Modules:
  0.0 247.3 jit_solution(3443778541291321474)
XLA Ops:
  7.2 0.8 all_to_all.12
  8.0 15.5 %all_to_all.19 = s32[16,1,512]{2,1,0:T(1,128)S(1)} all-to-all(s32[16,1,512]{2,1,0:T(1,128)S(1)} %all_to_all.12), channel_id=1, replica_groups=mesh['table'=16,'narrow'=2] {'table'}, dimensions={0} | all-to-all | bytes 65536 | tf_op jit(solution)/shard_map/all_to_all | solution.py:39
  23.5 0.1 reduce
  23.5 1.1 reshape.40
  24.6 0.0 copy-start.2
  24.6 2.0 slice_reduce_fusion.3
  26.6 0.0 copy-done.2
  26.6 6.1 %fusion.15 = bf16[2048,256]{1,0:T(8,128)(2,1)} fusion(bf16[1024,256]{1,0:T(8,128)(2,1)S(1)} %copy-done.2, s32[2048]{0:T(1024)S(1)} %get-tuple-element.21, s32[2048]{0:T(1024)S(1)} %get-tuple-element.22, s32[2048]{0:T(1024)S(1)} %get-tuple-element.23, s32[2048]{0:T(1024)S(1)} %get-tuple-element.20), kind=kOutput, calls=%fused_computation.18 | convolution fusion | flops 1107820544 | bytes 1605632 | tf_op jit(solution)/shard_map/dot_general | solution.py:45
  32.7 3.8 %all-to-all-start.1 = ((bf16[16,128,256]{2,1,0:T(8,128)(2,1)}), bf16[16,128,256]{2,1,0:T(8,128)(2,1)S(1)}, u32[]{:S(2)}, u32[]{:S(2)}) async-start(bf16[16,128,256]{2,1,0:T(8,128)(2,1)} %bitcast.1), calls=%async_computation.1 | async-start | bytes 2097152 | tf_op jit(solution)/shard_map/all_to_all | solution.py:47
  36.5 0.0 all-gather.3.cloned.1.call-start
  36.5 0.7 all-gather.3.cloned.1.call-update
  37.2 0.0 all-gather.5.cloned.1.call-start
  37.3 0.7 all-gather.5.cloned.1.call-update
  38.0 0.0 copy-done.4
  38.0 21.7 %all-to-all-done.1 = bf16[16,128,256]{2,1,0:T(8,128)(2,1)S(1)} async-done(((bf16[16,128,256]{2,1,0:T(8,128)(2,1)}), bf16[16,128,256]{2,1,0:T(8,128)(2,1)S(1)}, u32[]{:S(2)}, u32[]{:S(2)}) %all-to-all-start.1) | async-done | bytes 1048608 | tf_op jit(solution)/shard_map/all_to_all | solution.py:47
  59.8 1.5 fusion.23
  61.2 0.0 copy-start.3
  61.2 0.2 reshape.43
  61.5 0.0 copy-start.8
  61.5 0.0 all-gather.3.cloned.1.call-done
  61.5 1.5 convolution_convert_fusion.3
  63.1 0.0 all-gather.5.cloned.1.call-done
  63.1 2.0 fusion.29
  65.1 0.0 copy-start.6
  65.1 0.4 convolution_convert_fusion.2
  65.5 0.5 fusion.19
  66.0 0.2 reshape.44
  66.3 3.3 %fusion.18 = bf16[2048,256]{1,0:T(8,128)(2,1)} fusion(bf16[1024,256]{1,0:T(8,128)(2,1)S(1)} %reshape.44, s32[2048]{0:T(1024)S(1)} %bitcast.22), kind=kOutput, calls=%fused_computation.19 | convolution fusion | flops 1076363264 | bytes 1581056 | tf_op jit(solution)/shard_map/dot_general | solution.py:18
  69.6 5.8 %all-to-all-start.2 = ((bf16[16,128,256]{2,1,0:T(8,128)(2,1)}), bf16[16,128,256]{2,1,0:T(8,128)(2,1)S(1)}, u32[]{:S(2)}, u32[]{:S(2)}) async-start(bf16[16,128,256]{2,1,0:T(8,128)(2,1)} %bitcast.3), calls=%async_computation.3 | async-start | bytes 2097152 | tf_op jit(solution)/shard_map/all_to_all | solution.py:96
  75.4 0.2 all-reduce.3.cloned.1.call-start
  75.6 0.5 convolution_convert_fusion
  76.2 23.0 %all-to-all-done.2 = bf16[16,128,256]{2,1,0:T(8,128)(2,1)S(1)} async-done(((bf16[16,128,256]{2,1,0:T(8,128)(2,1)}), bf16[16,128,256]{2,1,0:T(8,128)(2,1)S(1)}, u32[]{:S(2)}, u32[]{:S(2)}) %all-to-all-start.2) | async-done | bytes 1048608 | tf_op jit(solution)/shard_map/all_to_all | solution.py:96
  99.1 5.5 %fusion.20 = bf16[1024,256]{1,0:T(8,128)(2,1)} fusion(bf16[2048,256]{1,0:T(8,128)(2,1)S(1)} %bitcast.20, s32[2048]{0:T(1024)S(1)} %get-tuple-element.21, s32[2048]{0:T(1024)S(1)} %get-tuple-element.22, s32[2048]{0:T(1024)S(1)} %get-tuple-element.23, s32[2048]{0:T(1024)S(1)} %get-tuple-element.20), kind=kOutput, calls=%fused_computation.31 | convolution fusion | flops 1107558400 | bytes 1605632 | tf_op jit(solution)/shard_map/dot_general | solution.py:18
  104.6 0.0 all-reduce.3.cloned.1.call-update
  104.6 0.0 reduce-scatter.2.cloned.1.call-start
  104.7 0.5 convolution_convert_fusion.1
  105.2 1.5 pad_maximum_fusion
  106.7 0.0 reduce-scatter.2.cloned.1.call-update
  106.7 17.0 %all-reduce.3.cloned.1.call-done = bf16[1024,256]{1,0:T(8,128)(2,1)} async-done(((bf16[1024,256]{1,0:T(8,128)(2,1)}), bf16[1024,256]{1,0:T(8,128)(2,1)}) %all-reduce.3.cloned.1.call-update) | async-done | bytes 524304 | tf_op jit(solution)/shard_map/psum | solution.py:102
  123.7 1.3 fusion.24
  125.0 0.7 dynamic_slice.3
  125.7 2.1 fusion.26
  127.8 8.9 %reduce-scatter.2.cloned.1.call-done = bf16[1024,512]{0,1:T(8,128)(2,1)} async-done(((bf16[2048,512]{0,1:T(8,128)(2,1)}), bf16[1024,512]{0,1:T(8,128)(2,1)}) %reduce-scatter.2.cloned.1.call-update) | async-done | bytes 1048592 | tf_op jit(solution)/shard_map/reduce_scatter | solution.py:76
  136.7 100.9 %all-reduce.4 = f32[1024,512]{0,1:T(8,128)S(1)} all-reduce(bf16[1024,512]{0,1:T(8,128)(2,1)} %reduce-scatter.2.cloned.1.call-done), channel_id=1, replica_groups=mesh['table'=16,'narrow'=2] {'table'}, use_global_device_ids=true, to_apply=%region_2.0 | all-reduce | flops 524288 | bytes 3145728 | tf_op jit(solution)/shard_map/psum | solution.py:84
  237.7 0.2 broadcast_multiply_fusion
  237.9 0.2 fusion.33
  238.2 1.3 copy.19
  239.5 1.3 copy.18
  (15 shorter events, 0.0 us)
Async XLA Ops:
  24.6 2.0 copy-start.2
  32.7 5.3 %copy-start.4 = (bf16[2048]{0:T(1024)(128)(2,1)S(1)}, bf16[2048]{0:T(1024)(128)(2,1)}, u32[]{:S(2)}) copy-start(bf16[2048]{0:T(1024)(128)(2,1)} %param.14) | copy-start | bytes 12292
  32.7 27.1 %copy-start.7 = (s32[16,128]{1,0:T(8,128)S(1)}, s32[16,128]{1,0:T(8,128)}, u32[]{:S(2)}) copy-start(s32[16,128]{1,0:T(8,128)} %param.17) | copy-start | bytes 24580
  32.7 27.1 %all-to-all-start.1 = ((bf16[16,128,256]{2,1,0:T(8,128)(2,1)}), bf16[16,128,256]{2,1,0:T(8,128)(2,1)S(1)}, u32[]{:S(2)}, u32[]{:S(2)}) async-start(bf16[16,128,256]{2,1,0:T(8,128)(2,1)} %bitcast.1), calls=%async_computation.1 | async-start | bytes 2097152 | tf_op jit(solution)/shard_map/all_to_all | solution.py:47
  36.5 25.0 %all-gather.3.cloned.1.call-start = ((), (), s32[]{:S(2)}) async-start(), calls=%async_computation.4 | async-start | bytes 1572864 | tf_op jit(solution)/shard_map/all_gather | solution.py:58
  37.2 25.9 %all-gather.5.cloned.1.call-start = ((), (), s32[]{:S(2)}) async-start(), calls=%async_computation.5 | async-start | bytes 1572864 | tf_op jit(solution)/shard_map/all_gather | solution.py:59
  61.2 1.9 copy-start.3
  61.5 3.6 %copy-start.8 = (f32[128]{0:T(128)S(1)}, f32[128]{0:T(128)}, u32[]{:S(2)}) copy-start(f32[128]{0:T(128)} %param.15) | copy-start | bytes 1540
  63.1 2.4 copy-start
  63.1 2.0 copy-start.1
  65.1 0.9 copy-start.6
  69.6 29.5 %all-to-all-start.2 = ((bf16[16,128,256]{2,1,0:T(8,128)(2,1)}), bf16[16,128,256]{2,1,0:T(8,128)(2,1)S(1)}, u32[]{:S(2)}, u32[]{:S(2)}) async-start(bf16[16,128,256]{2,1,0:T(8,128)(2,1)} %bitcast.3), calls=%async_computation.3 | async-start | bytes 2097152 | tf_op jit(solution)/shard_map/all_to_all | solution.py:96
  75.4 48.3 %all-reduce.3.cloned.1.call-start = ((), (), s32[]{:S(2)}) async-start(), calls=%async_computation.7 | async-start | bytes 1048576 | tf_op jit(solution)/shard_map/psum | solution.py:102
  104.6 32.1 %reduce-scatter.2.cloned.1.call-start = ((), (), s32[]{:S(2)}) async-start(), calls=%async_computation.6 | async-start | bytes 3145728 | tf_op jit(solution)/shard_map/reduce_scatter | solution.py:76
  106.7 18.3 %copy-start.5 = (f32[1024]{0:T(1024)S(1)}, f32[1024]{0:T(1024)}, u32[]{:S(2)}) copy-start(f32[1024]{0:T(1024)} %param.10) | copy-start | bytes 12292
Sparse Core Ops, SparseCore 0:
  38.9 10.2 all-gather.2
  50.7 10.1 all-gather.4
  104.8 18.9 all-reduce.2
  125.9 10.7 reduce-scatter.1
where the time goes:
time: 248 us; the launch traced here: 247 us
  blocking collectives  116 us (47%)
  waiting for transfers between devices  72.1 us (29%)
  matrix products  21.7 us (9%)
  between operations  14 us (6%)
  starting transfers between devices  9.95 us (4%)
  local copies, waits for them, and re-layouts  7.88 us (3%)
  other arithmetic  5.22 us (2%)
    psum x1, blocking collectives, local(): grand_total = lax.psum(narrow_sum, 'table')  101 us
    all_to_all x1, waiting for transfers between devices, local(): lax.all_to_all(slot_grads, 'table', split_axis=0, concat_axis=0, tiled=True)  23 us
    all_to_all x1, waiting for transfers between devices, local(): lax.all_to_all(pool_out, 'table', split_axis=0, concat_axis=0, tiled=True)  21.7 us
    psum x1, waiting for transfers between devices, local(): lax.psum(local_grad.astype(jnp.bfloat16), 'narrow').astype(jnp.float32)  17 us
    all_to_all x1, blocking collectives, local(): lax.all_to_all(bag_rows, 'table', split_axis=0, concat_axis=0, tiled=True)  15.5 us
    dot_general x4, matrix products, transposed_dot(): lax.dot_general(left, right, (((0,), (0,)), ((), ())), preferred_element_...  9.82 us
    reduce_scatter x1, waiting for transfers between devices, local(): lax.psum_scatter(jnp.concatenate([transposed_dot(pooled_feats, dhidden),...  8.95 us
    dot_general x1, matrix products, local(): pool_sums = jnp.dot(counts, table_rows, preferred_element_type=jnp.float32)  6.07 us
  transfers between devices with their start and end apart: 6, of which 4 were waited for; matrix products, arithmetic and copies ran while one was open for 4% of the time, Pallas kernels for 0%

commit v1 on v0

--- a/solution.py
+++ b/solution.py
@@ -24,6 +24,65 @@
     return lax.dot_general(
         left, right, (((1,), (1,)), ((), ())), preferred_element_type=jnp.float32
     )
+
+
+def group_levels(size):
+    levels = []
+    stride = 1
+    while size % 4 == 0:
+        levels.append((stride, 4))
+        stride, size = stride * 4, size // 4
+    if size > 1:
+        levels.append((stride, size))
+    return levels
+
+
+def partner_index(index, stride, group, step):
+    place = (index // stride) % group
+    if group & (group - 1) == 0:
+        other = place ^ step
+    else:
+        other = (place + step) % group
+    return index + (other - place) * stride
+
+
+def sent_from(axis, stride, group, step):
+    size = lax.axis_size(axis)
+    return [(partner_index(i, stride, group, step), i) for i in range(size)]
+
+
+def scatter_sum(blocks, axis, levels):
+    index = lax.axis_index(axis)
+    for stride, group in levels:
+        rows = blocks.shape[0] // group
+        place = (index // stride) % group
+        total = lax.dynamic_slice_in_dim(blocks, place * rows, rows, 0).astype(jnp.float32)
+        for step in range(1, group):
+            pairs = sent_from(axis, stride, group, step)
+            if group & (group - 1) == 0:
+                goal = place ^ step
+            else:
+                goal = (place + group - step) % group
+            outgoing = lax.dynamic_slice_in_dim(blocks, goal * rows, rows, 0)
+            total = total + lax.ppermute(outgoing, axis, pairs).astype(jnp.float32)
+        blocks = total.astype(jnp.bfloat16)
+    return blocks
+
+
+def gather_blocks(block, axis, levels):
+    index = lax.axis_index(axis)
+    for stride, group in reversed(levels):
+        rows = block.shape[0]
+        place = (index // stride) % group
+        whole = jnp.zeros((group * rows,) + block.shape[1:], block.dtype)
+        whole = lax.dynamic_update_slice_in_dim(whole, block, place * rows, 0)
+        for step in range(1, group):
+            origin = partner_index(index, stride, group, step)
+            came = lax.ppermute(block, axis, sent_from(axis, stride, group, step))
+            spot = (origin // stride) % group
+            whole = lax.dynamic_update_slice_in_dim(whole, came, spot * rows, 0)
+        block = whole
+    return block
 
 
 def local(
@@ -54,10 +113,10 @@
         .astype(jnp.bfloat16)
         .reshape(samples, FEAT * emb_width)
     )
-    down_full, up_full = (
-        lax.all_gather(factor_down, "narrow", axis=0, tiled=True),
-        lax.all_gather(factor_up, "narrow", axis=0, tiled=True),
-    )
+    narrow_levels = group_levels(narrows)
+    table_levels = group_levels(tables)
+    down_full = gather_blocks(factor_down, "narrow", narrow_levels)
+    up_full = gather_blocks(factor_up, "narrow", narrow_levels)
     hidden = jnp.dot(pooled_feats, down_full, preferred_element_type=jnp.float32).astype(
         jnp.bfloat16
     )
@@ -73,15 +132,12 @@
     dhidden = jnp.dot(dcross, up_full, preferred_element_type=jnp.float32).astype(jnp.bfloat16)
     back_term = rows_dot(dhidden, down_full)
     dpooled = (dmixed * (shifted + 1.0) + back_term).astype(jnp.bfloat16)
-    narrow_sum = lax.psum_scatter(
-        jnp.concatenate(
-            [transposed_dot(pooled_feats, dhidden), transposed_dot(dcross, hidden)], axis=1
-        ).astype(jnp.bfloat16),
-        "narrow",
-        scatter_dimension=0,
-        tiled=True,
-    ).astype(jnp.float32)
-    grand_total = lax.psum(narrow_sum, "table")
+    grad_terms = jnp.concatenate(
+        [transposed_dot(pooled_feats, dhidden), transposed_dot(dcross, hidden)], axis=1
+    ).astype(jnp.bfloat16)
+    narrow_sum = scatter_sum(grad_terms, "narrow", narrow_levels)
+    table_sum = scatter_sum(narrow_sum, "table", table_levels)
+    grand_total = gather_blocks(table_sum, "table", table_levels).astype(jnp.float32)
     batch_all = samples * tables * narrows
     grand_total = grand_total * (1.0 / math.sqrt(batch_all))
     rank_size = factor_down.shape[1]
@@ -99,7 +155,13 @@
     local_grad = transposed_dot(counts, returned)
     narrow_index = lax.axis_index("narrow")
     share_size = row_dev // narrows
-    row_grad = lax.psum(local_grad.astype(jnp.bfloat16), "narrow").astype(jnp.float32)
+    sent_grad = local_grad.astype(jnp.bfloat16)
+    if narrows == 2:
+        other_grad = lax.ppermute(sent_grad, "narrow", sent_from("narrow", 1, 2, 1))
+        row_grad = sent_grad.astype(jnp.float32) + other_grad.astype(jnp.float32)
+    else:
+        share = scatter_sum(sent_grad, "narrow", narrow_levels)
+        row_grad = gather_blocks(share, "narrow", narrow_levels).astype(jnp.float32)
     accum_all = accum + jnp.mean(row_grad * row_grad, axis=1)
     new_rows = (
         table_rows.astype(jnp.float32)

time: 248 us -> 155 us (0.62)
  blocking collectives: 116 us -> 15.5 us
  starting transfers between devices: 9.95 us -> 30.4 us
  between operations: 14 us -> 1.17 us
  waiting for transfers between devices: 72.1 us -> 62.5 us
  local copies, waits for them, and re-layouts: 7.88 us -> 16.5 us
    psum x1 -> x0, blocking collectives: 101 us -> none  [local(): grand_total = lax.psum(narrow_sum, 'table')]
    ppermute x0 -> x16, waiting for transfers between devices: none -> 44.3 us  [the longest x7 26 us: scatter_sum(): total = total + lax.ppermute(outgoing, axis, pairs).astype(jnp.float32)]
    all_to_all x1, waiting for transfers between devices: 23 us -> 0.01 us  [local(): lax.all_to_all(slot_grads, 'table', split_axis=0, concat_axis=0, tiled=True)]
    ppermute x0 -> x16, starting transfers between devices: none -> 20.7 us  [the longest x7 11.6 us: scatter_sum(): total = total + lax.ppermute(outgoing, axis, pairs).astype(jnp.float32)]
    psum x1 -> x0, waiting for transfers between devices: 17 us -> none  [local(): lax.psum(local_grad.astype(jnp.bfloat16), 'narrow').astype(jnp.float32)]
    reduce_scatter x1 -> x0, waiting for transfers between devices: 8.95 us -> none  [local(): lax.psum_scatter(jnp.concatenate([transposed_dot(pooled_feats, dhidden),...]
    dynamic_update_slice x0 -> x12, local copies, waits for them, and re-layouts: none -> 4.47 us  [the longest x8 2.27 us: gather_blocks(): whole = lax.dynamic_update_slice_in_dim(whole, came, spot * rows, 0)]
    all_to_all x1, waiting for transfers between devices: 21.7 us -> 18.1 us  [local(): lax.all_to_all(pool_out, 'table', split_axis=0, concat_axis=0, tiled=True)]
  transfers between devices with their start and end apart: 6 -> 18, of which waited for: 4 -> 10; matrix products, arithmetic and copies ran while one was open for 4% -> 10% of each run, Pallas kernels for 0% -> 0%
where the time goes in v1:
time: 155 us; the launch traced here: 153 us
  waiting for transfers between devices  62.5 us (40%)
  starting transfers between devices  30.4 us (20%)
  matrix products  23.5 us (15%)
  local copies, waits for them, and re-layouts  16.5 us (11%)
  blocking collectives  15.5 us (10%)
  other arithmetic  3.91 us (3%)
    ppermute x7, waiting for transfers between devices, scatter_sum(): total = total + lax.ppermute(outgoing, axis, pairs).astype(jnp.float32)  26 us
    ppermute x8, waiting for transfers between devices, gather_blocks(): came = lax.ppermute(block, axis, sent_from(axis, stride, group, step))  18.2 us
    all_to_all x1, waiting for transfers between devices, local(): lax.all_to_all(pool_out, 'table', split_axis=0, concat_axis=0, tiled=True)  18.1 us
    all_to_all x1, blocking collectives, local(): lax.all_to_all(bag_rows, 'table', split_axis=0, concat_axis=0, tiled=True)  15.5 us
    ppermute x7, starting transfers between devices, scatter_sum(): total = total + lax.ppermute(outgoing, axis, pairs).astype(jnp.float32)  11.6 us
    dot_general x4, matrix products, transposed_dot(): lax.dot_general(left, right, (((0,), (0,)), ((), ())), preferred_element_...  10.6 us
    ppermute x8, starting transfers between devices, gather_blocks(): came = lax.ppermute(block, axis, sent_from(axis, stride, group, step))  9 us
    dot_general x1, matrix products, local(): pool_sums = jnp.dot(counts, table_rows, preferred_element_type=jnp.float32)  6.06 us
  transfers between devices with their start and end apart: 18, of which 10 were waited for; matrix products, arithmetic and copies ran while one was open for 10% of the time, Pallas kernels for 0%

profile of v1, /device:TPU:0, one launch (start us, length us, event | category | flops | bytes accessed | tf_op | source)
XLA Modules:
  0.0 153.5 jit_solution(16227634414283813144)
XLA Ops:
  0.6 0.8 all_to_all.12
  1.4 15.5 %all_to_all.19 = s32[16,1,512]{2,1,0:T(1,128)S(1)} all-to-all(s32[16,1,512]{2,1,0:T(1,128)S(1)} %all_to_all.12), channel_id=1, replica_groups=mesh['table'=16,'narrow'=2] {'table'}, dimensions={0} | all-to-all | bytes 65536 | tf_op jit(solution)/shard_map/all_to_all | solution.py:98
  17.0 1.1 reshape.40
  18.1 2.0 %slice_reduce_fusion.3 = (s32[2048]{0:T(1024)S(1)}, s32[2048]{0:T(1024)S(1)}, s32[2048]{0:T(1024)S(1)}, s32[2048]{0:T(1024)S(1)}) fusion(s32[2048,4]{1,0:T(8,128)S(1)} %reshape.40), kind=kLoop, calls=%fused_computation.46 | loop fusion | bytes 65536 | tf_op jit(solution)/shard_map/slice | solution.py:103
  20.1 6.1 %fusion.15 = bf16[2048,256]{1,0:T(8,128)(2,1)} fusion(bf16[1024,256]{1,0:T(8,128)(2,1)S(1)} %copy-done.2, s32[2048]{0:T(1024)S(1)} %get-tuple-element.21, s32[2048]{0:T(1024)S(1)} %get-tuple-element.22, s32[2048]{0:T(1024)S(1)} %get-tuple-element.23, s32[2048]{0:T(1024)S(1)} %get-tuple-element.20), kind=kOutput, calls=%fused_computation.18 | convolution fusion | flops 1107820544 | bytes 1605632 | tf_op jit(solution)/shard_map/dot_general | solution.py:104
  26.2 3.8 %all-to-all-start.1 = ((bf16[16,128,256]{2,1,0:T(8,128)(2,1)}), bf16[16,128,256]{2,1,0:T(8,128)(2,1)S(1)}, u32[]{:S(2)}, u32[]{:S(2)}) async-start(bf16[16,128,256]{2,1,0:T(8,128)(2,1)} %bitcast.1), calls=%async_computation.1 | async-start | bytes 2097152 | tf_op jit(solution)/shard_map/all_to_all | solution.py:106
  30.0 0.5 collective-permute-start
  30.6 1.1 constant_dynamic-update-slice_fusion.9
  31.8 1.1 constant_dynamic-update-slice_fusion.11
  32.9 1.1 constant_dynamic-update-slice_fusion.8
  34.0 1.1 constant_dynamic-update-slice_fusion.10
  35.1 18.1 %all-to-all-done.1 = bf16[16,128,256]{2,1,0:T(8,128)(2,1)S(1)} async-done(((bf16[16,128,256]{2,1,0:T(8,128)(2,1)}), bf16[16,128,256]{2,1,0:T(8,128)(2,1)S(1)}, u32[]{:S(2)}, u32[]{:S(2)}) %all-to-all-start.1) | async-done | bytes 1048608 | tf_op jit(solution)/shard_map/all_to_all | solution.py:106
  53.2 2.3 %fusion.22 = bf16[1024,256]{1,0:T(8,128)(2,1)} fusion(bf16[2048,256]{1,0:T(8,128)(2,1)S(1)} %bitcast.19, s32[2048]{0:T(1024)S(1)} %bitcast.20), kind=kOutput, calls=%fused_computation.33 | convolution fusion | flops 1076101120 | bytes 1581056 | tf_op jit(solution)/shard_map/dot_general | solution.py:112
  55.5 1.3 reshape.43
  56.8 0.3 convolution_convert_fusion.3
  57.1 1.5 fusion.27
  58.6 0.4 convolution_convert_fusion.2
  59.0 0.5 convolution_convert_fusion
  59.5 0.5 convolution_convert_fusion.1
  60.0 1.1 fusion.28
  61.1 0.5 copy-done.1
  61.6 2.5 %fusion.25 = bf16[128,2048]{1,0:T(8,128)(2,1)} fusion(f32[128,2048]{1,0:T(8,128)} %get-tuple-element.35, f32[128]{0:T(128)S(1)} %fusion.32, f32[2048]{0:T(1024)S(1)} %convert_element_type.106, bf16[128,256]{1,0:T(8,128)(2,1)S(1)} %convolution_convert_fusion.2, bf16[2048,256]{1,0:T(8,128)(2,1)S(1)} %copy-done.1), kind=kOutput, calls=%fused_computation.38 | convolution fusion | flops 135528448 | bytes 2695680 | tf_op jit(solution)/shard_map/dot_general | solution.py:24
  64.1 2.1 %reshape.44 = bf16[1024,256]{1,0:T(8,128)(2,1)} reshape(bf16[128,2048]{1,0:T(8,128)(2,1)} %fusion.25) | data formatting | bytes 1048576 | tf_op jit(solution)/shard_map/reshape | solution.py:146
  66.2 1.7 %add_convert_fusion = bf16[1024,512]{0,1:T(8,128)(2,1)S(1)} fusion(bf16[1024,512]{0,1:T(8,128)(2,1)} %collective-permute-done.2, s32[]{:T(128)S(6)} %select_n.161, bf16[2048,256]{0,1:T(8,128)(2,1)S(1)} %convolution_convert_fusion.1, bf16[2048,256]{0,1:T(8,128)(2,1)S(1)} %convolution_convert_fusion), kind=kLoop, calls=%fused_computation.28 | loop fusion | flops 3670016 | bytes 4194308 | tf_op jit(solution)/shard_map/convert_element_type | solution.py:68
  68.0 0.6 collective-permute-start.3
  68.6 2.0 %collective-permute-start.4 = (bf16[256,512]{0,1:T(8,128)(2,1)S(1)}, bf16[256,512]{0,1:T(8,128)(2,1)S(1)}, u32[]{:S(2)}, u32[]{:S(2)}) collective-permute-start(bf16[256,512]{0,1:T(8,128)(2,1)S(1)} %get-tuple-element.30), channel_id=1, source_target_pairs={{4,0},{6,2},{0,4},{2,6},{12,8},{14,10},{8,12},{10,14},{20,16},{22,... | collective-permute-start | bytes 786440 | tf_op jit(solution)/shard_map/ppermute | solution.py:67
  70.6 1.0 collective-permute-start.5
  71.6 3.3 %fusion.18 = bf16[2048,256]{1,0:T(8,128)(2,1)} fusion(bf16[1024,256]{1,0:T(8,128)(2,1)S(1)} %copy-done.4, s32[2048]{0:T(1024)S(1)} %bitcast.21), kind=kOutput, calls=%fused_computation.19 | convolution fusion | flops 1076363264 | bytes 1581056 | tf_op jit(solution)/shard_map/dot_general | solution.py:18
  74.9 5.9 %all-to-all-start.2 = ((bf16[16,128,256]{2,1,0:T(8,128)(2,1)}), bf16[16,128,256]{2,1,0:T(8,128)(2,1)}, u32[]{:S(2)}, u32[]{:S(2)}) async-start(bf16[16,128,256]{2,1,0:T(8,128)(2,1)} %bitcast.3), calls=%async_computation.2 | async-start | bytes 2097152 | tf_op jit(solution)/shard_map/all_to_all | solution.py:152
  80.9 2.3 %collective-permute-done.4 = bf16[256,512]{0,1:T(8,128)(2,1)S(1)} collective-permute-done((bf16[256,512]{0,1:T(8,128)(2,1)S(1)}, bf16[256,512]{0,1:T(8,128)(2,1)S(1)}, u32[]{:S(2)}, u32[]{:S(2)}) %collective-permute-start.4) | collective-permute-done | bytes 262176 | tf_op jit(solution)/shard_map/ppermute | solution.py:67
  83.2 0.3 collective-permute-done.5
  83.9 3.0 %collective-permute-start.6 = (bf16[64,512]{0,1:T(8,128)(2,1)S(1)}, bf16[64,512]{0,1:T(8,128)(2,1)S(1)}, u32[]{:S(2)}, u32[]{:S(2)}) collective-permute-start(bf16[64,512]{0,1:T(8,128)(2,1)S(1)} %get-tuple-element.31), channel_id=1, source_target_pairs={{8,0},{10,2},{12,4},{14,6},{0,8},{2,10},{4,12},{6,14},{24,16},{26,... | collective-permute-start | bytes 196616 | tf_op jit(solution)/shard_map/ppermute | solution.py:67
  86.9 3.6 %collective-permute-start.7 = (bf16[64,512]{0,1:T(8,128)(2,1)S(1)}, bf16[64,512]{0,1:T(8,128)(2,1)S(1)}, u32[]{:S(2)}, u32[]{:S(2)}) collective-permute-start(bf16[64,512]{0,1:T(8,128)(2,1)S(1)} %get-tuple-element.33), channel_id=1, source_target_pairs={{16,0},{18,2},{20,4},{22,6},{24,8},{26,10},{28,12},{30,14},{0,16},... | collective-permute-start | bytes 196616 | tf_op jit(solution)/shard_map/ppermute | solution.py:67
  90.5 1.4 collective-permute-start.8
  91.9 9.8 %collective-permute-done.6 = bf16[64,512]{0,1:T(8,128)(2,1)S(1)} collective-permute-done((bf16[64,512]{0,1:T(8,128)(2,1)S(1)}, bf16[64,512]{0,1:T(8,128)(2,1)S(1)}, u32[]{:S(2)}, u32[]{:S(2)}) %collective-permute-start.6) | collective-permute-done | bytes 65568 | tf_op jit(solution)/shard_map/ppermute | solution.py:67
  101.7 13.6 %collective-permute-done.7 = bf16[64,512]{0,1:T(8,128)(2,1)S(1)} collective-permute-done((bf16[64,512]{0,1:T(8,128)(2,1)S(1)}, bf16[64,512]{0,1:T(8,128)(2,1)S(1)}, u32[]{:S(2)}, u32[]{:S(2)}) %collective-permute-start.7) | collective-permute-done | bytes 65568 | tf_op jit(solution)/shard_map/ppermute | solution.py:67
  115.5 2.4 %collective-permute-start.9 = (bf16[64,512]{0,1:T(8,128)(2,1)S(1)}, bf16[64,512]{0,1:T(8,128)(2,1)S(1)}, u32[]{:S(2)}, u32[]{:S(2)}) collective-permute-start(bf16[64,512]{0,1:T(8,128)(2,1)S(1)} %add_convert_fusion.2), channel_id=1, source_target_pairs={{8,0},{10,2},{12,4},{14,6},{0,8},{2,10},{4,12},{6,14},{24,16},{26,... | collective-permute-start | bytes 196616 | tf_op jit(solution)/shard_map/ppermute | solution.py:81
  118.0 2.4 %collective-permute-start.11 = (bf16[64,512]{0,1:T(8,128)(2,1)S(1)}, bf16[64,512]{0,1:T(8,128)(2,1)S(1)}, u32[]{:S(2)}, u32[]{:S(2)}) collective-permute-start(bf16[64,512]{0,1:T(8,128)(2,1)S(1)} %add_convert_fusion.2), channel_id=1, source_target_pairs={{24,0},{26,2},{28,4},{30,6},{16,8},{18,10},{20,12},{22,14},{8,16},... | collective-permute-start | bytes 196616 | tf_op jit(solution)/shard_map/ppermute | solution.py:81
  120.4 1.5 collective-permute-done.9
  121.9 7.3 %collective-permute-done.10 = bf16[64,512]{0,1:T(8,128)(2,1)S(1)} collective-permute-done((bf16[64,512]{0,1:T(8,128)(2,1)S(1)}, bf16[64,512]{0,1:T(8,128)(2,1)S(1)}, u32[]{:S(2)}, u32[]{:S(2)}) %collective-permute-start.10) | collective-permute-done | bytes 65568 | tf_op jit(solution)/shard_map/ppermute | solution.py:81
  129.5 1.5 collective-permute-start.12
  131.0 2.0 %collective-permute-start.13 = (bf16[256,512]{1,0:T(8,128)(2,1)S(1)}, bf16[256,512]{1,0:T(8,128)(2,1)S(1)}, u32[]{:S(2)}, u32[]{:S(2)}) collective-permute-start(bf16[256,512]{1,0:T(8,128)(2,1)S(1)} %constant_dynamic-update-slice_fusion.4), channel_id=1, source_target_pairs={{4,0},{6,2},{0,4},{2,6},{12,8},{14,10},{8,12},{10,14},{20,16},{22,... | collective-permute-start | bytes 786440 | tf_op jit(solution)/shard_map/ppermute | solution.py:81
  133.5 5.3 %collective-permute-done.12 = bf16[256,512]{1,0:T(8,128)(2,1)S(1)} collective-permute-done((bf16[256,512]{1,0:T(8,128)(2,1)S(1)}, bf16[256,512]{1,0:T(8,128)(2,1)S(1)}, u32[]{:S(2)}, u32[]{:S(2)}) %collective-permute-start.12) | collective-permute-done | bytes 262176 | tf_op jit(solution)/shard_map/ppermute | solution.py:81
  138.9 4.1 %collective-permute-done.13 = bf16[256,512]{1,0:T(8,128)(2,1)S(1)} collective-permute-done((bf16[256,512]{1,0:T(8,128)(2,1)S(1)}, bf16[256,512]{1,0:T(8,128)(2,1)S(1)}, u32[]{:S(2)}, u32[]{:S(2)}) %collective-permute-start.13) | collective-permute-done | bytes 262176 | tf_op jit(solution)/shard_map/ppermute | solution.py:81
  143.1 6.2 %fusion.19 = bf16[1024,256]{0,1:T(8,128)(2,1)S(1)} fusion(bf16[2048,256]{1,0:T(8,128)(2,1)} %bitcast.4, s32[2048]{0:T(1024)S(1)} %get-tuple-element.21, s32[2048]{0:T(1024)S(1)} %get-tuple-element.22, s32[2048]{0:T(1024)S(1)} %get-tuple-element.23, s32[2048]{0:T(1024)S(1)} %get-tuple-element.20), kind=kOutput, calls=%fused_computation.32 | convolution fusion | flops 1107558400 | bytes 1605632 | tf_op jit(solution)/shard_map/dot_general | solution.py:18
  149.7 1.5 fusion.33
  151.8 1.0 copy.31
  152.8 0.6 dynamic_slice.43
  (63 shorter events, 2.9 us)
Async XLA Ops:
  18.1 2.0 %copy-start.2 = (bf16[1024,256]{1,0:T(8,128)(2,1)S(1)}, bf16[1024,256]{1,0:T(8,128)(2,1)}, u32[]{:S(2)}) copy-start(bf16[1024,256]{1,0:T(8,128)(2,1)} %param.9) | copy-start | bytes 1572868
  26.2 4.4 %copy-start.6 = (bf16[2048]{0:T(1024)(128)(2,1)S(1)}, bf16[2048]{0:T(1024)(128)(2,1)}, u32[]{:S(2)}) copy-start(bf16[2048]{0:T(1024)(128)(2,1)} %param.14) | copy-start | bytes 12292
  26.2 27.1 %all-to-all-start.1 = ((bf16[16,128,256]{2,1,0:T(8,128)(2,1)}), bf16[16,128,256]{2,1,0:T(8,128)(2,1)S(1)}, u32[]{:S(2)}, u32[]{:S(2)}) async-start(bf16[16,128,256]{2,1,0:T(8,128)(2,1)} %bitcast.1), calls=%async_computation.1 | async-start | bytes 2097152 | tf_op jit(solution)/shard_map/all_to_all | solution.py:106
  29.9 2.9 %collective-permute-start.1 = (bf16[1024,256]{1,0:T(8,128)(2,1)}, bf16[1024,256]{1,0:T(8,128)(2,1)}, u32[]{:S(2)}, u32[]{:S(2)}) collective-permute-start(bf16[1024,256]{1,0:T(8,128)(2,1)} %param.12), channel_id=1, source_target_pairs={{1,0},{0,1},{3,2},{2,3},{5,4},{4,5},{7,6},{6,7},{9,8},{8,9},{11,10... | collective-permute-start | bytes 1572872 | tf_op jit(solution)/shard_map/ppermute | solution.py:81
  30.0 3.9 %collective-permute-start = (bf16[1024,256]{1,0:T(8,128)(2,1)}, bf16[1024,256]{1,0:T(8,128)(2,1)}, u32[]{:S(2)}, u32[]{:S(2)}) collective-permute-start(bf16[1024,256]{1,0:T(8,128)(2,1)} %param.11), channel_id=1, source_target_pairs={{1,0},{0,1},{3,2},{2,3},{5,4},{4,5},{7,6},{6,7},{9,8},{8,9},{11,10... | collective-permute-start | bytes 1572872 | tf_op jit(solution)/shard_map/ppermute | solution.py:81
  31.7 21.5 %copy-start.9 = (s32[16,128]{1,0:T(8,128)S(1)}, s32[16,128]{1,0:T(8,128)}, u32[]{:S(2)}) copy-start(s32[16,128]{1,0:T(8,128)} %param.17) | copy-start | bytes 24580
  35.1 21.7 %copy-start = (bf16[2048,256]{1,0:T(8,128)(2,1)}, bf16[2048,256]{1,0:T(8,128)(2,1)S(1)}, u32[]{:S(2)}) copy-start(bf16[2048,256]{1,0:T(8,128)(2,1)S(1)} %constant_dynamic-update-slice_fusion.10) | copy-start | bytes 3145732
  55.5 1.6 %copy-start.5 = (f32[2048]{0:T(1024)S(1)}, f32[2048]{0:T(1024)}, u32[]{:S(2)}) copy-start(f32[2048]{0:T(1024)} %param.13) | copy-start | bytes 24580
  56.8 1.8 %copy-start.10 = (f32[128]{0:T(128)S(1)}, f32[128]{0:T(128)}, u32[]{:S(2)}) copy-start(f32[128]{0:T(128)} %param.15) | copy-start | bytes 1540
  58.6 1.4 copy-start.8
  60.0 1.6 %copy-start.1 = (bf16[2048,256]{1,0:T(8,128)(2,1)S(1)}, bf16[2048,256]{1,0:T(8,128)(2,1)}, u32[]{:S(2)}) copy-start(bf16[2048,256]{1,0:T(8,128)(2,1)} %copy-done) | copy-start | bytes 3145732
  61.1 5.1 %collective-permute-start.2 = (bf16[1024,512]{0,1:T(8,128)(2,1)}, bf16[1024,512]{0,1:T(8,128)(2,1)}, u32[]{:S(2)}, u32[]{:S(2)}) collective-permute-start(bf16[1024,512]{0,1:T(8,128)(2,1)} %fusion.28), channel_id=1, source_target_pairs={{1,0},{0,1},{3,2},{2,3},{5,4},{4,5},{7,6},{6,7},{9,8},{8,9},{11,10... | collective-permute-start | bytes 3145736 | tf_op jit(solution)/shard_map/ppermute | solution.py:67
  66.2 5.4 %copy-start.4 = (bf16[1024,256]{1,0:T(8,128)(2,1)S(1)}, bf16[1024,256]{1,0:T(8,128)(2,1)}, u32[]{:S(2)}) copy-start(bf16[1024,256]{1,0:T(8,128)(2,1)} %reshape.44) | copy-start | bytes 1572868
  68.0 12.9 %collective-permute-start.3 = (bf16[256,512]{0,1:T(8,128)(2,1)S(1)}, bf16[256,512]{0,1:T(8,128)(2,1)S(1)}, u32[]{:S(2)}, u32[]{:S(2)}) collective-permute-start(bf16[256,512]{0,1:T(8,128)(2,1)S(1)} %get-tuple-element.28), channel_id=1, source_target_pairs={{2,0},{0,2},{6,4},{4,6},{10,8},{8,10},{14,12},{12,14},{18,16},{16,... | collective-permute-start | bytes 786440 | tf_op jit(solution)/shard_map/ppermute | solution.py:67
  68.6 14.6 %collective-permute-start.4 = (bf16[256,512]{0,1:T(8,128)(2,1)S(1)}, bf16[256,512]{0,1:T(8,128)(2,1)S(1)}, u32[]{:S(2)}, u32[]{:S(2)}) collective-permute-start(bf16[256,512]{0,1:T(8,128)(2,1)S(1)} %get-tuple-element.30), channel_id=1, source_target_pairs={{4,0},{6,2},{0,4},{2,6},{12,8},{14,10},{8,12},{10,14},{20,16},{22,... | collective-permute-start | bytes 786440 | tf_op jit(solution)/shard_map/ppermute | solution.py:67
  70.6 12.9 %collective-permute-start.5 = (bf16[256,512]{0,1:T(8,128)(2,1)S(1)}, bf16[256,512]{0,1:T(8,128)(2,1)S(1)}, u32[]{:S(2)}, u32[]{:S(2)}) collective-permute-start(bf16[256,512]{0,1:T(8,128)(2,1)S(1)} %get-tuple-element.29), channel_id=1, source_target_pairs={{6,0},{4,2},{2,4},{0,6},{14,8},{12,10},{10,12},{8,14},{22,16},{20,... | collective-permute-start | bytes 786440 | tf_op jit(solution)/shard_map/ppermute | solution.py:67
  74.9 68.2 %all-to-all-start.2 = ((bf16[16,128,256]{2,1,0:T(8,128)(2,1)}), bf16[16,128,256]{2,1,0:T(8,128)(2,1)}, u32[]{:S(2)}, u32[]{:S(2)}) async-start(bf16[16,128,256]{2,1,0:T(8,128)(2,1)} %bitcast.3), calls=%async_computation.2 | async-start | bytes 2097152 | tf_op jit(solution)/shard_map/all_to_all | solution.py:152
  80.9 52.2 %copy-start.3 = (bf16[1024,256]{1,0:T(8,128)(2,1)S(1)}, bf16[1024,256]{1,0:T(8,128)(2,1)}, u32[]{:S(2)}) copy-start(bf16[1024,256]{1,0:T(8,128)(2,1)} %param.9) | copy-start | bytes 1572868
  83.9 17.8 %collective-permute-start.6 = (bf16[64,512]{0,1:T(8,128)(2,1)S(1)}, bf16[64,512]{0,1:T(8,128)(2,1)S(1)}, u32[]{:S(2)}, u32[]{:S(2)}) collective-permute-start(bf16[64,512]{0,1:T(8,128)(2,1)S(1)} %get-tuple-element.31), channel_id=1, source_target_pairs={{8,0},{10,2},{12,4},{14,6},{0,8},{2,10},{4,12},{6,14},{24,16},{26,... | collective-permute-start | bytes 196616 | tf_op jit(solution)/shard_map/ppermute | solution.py:67
  86.9 28.4 %collective-permute-start.7 = (bf16[64,512]{0,1:T(8,128)(2,1)S(1)}, bf16[64,512]{0,1:T(8,128)(2,1)S(1)}, u32[]{:S(2)}, u32[]{:S(2)}) collective-permute-start(bf16[64,512]{0,1:T(8,128)(2,1)S(1)} %get-tuple-element.33), channel_id=1, source_target_pairs={{16,0},{18,2},{20,4},{22,6},{24,8},{26,10},{28,12},{30,14},{0,16},... | collective-permute-start | bytes 196616 | tf_op jit(solution)/shard_map/ppermute | solution.py:67
  90.5 24.7 %collective-permute-start.8 = (bf16[64,512]{0,1:T(8,128)(2,1)S(1)}, bf16[64,512]{0,1:T(8,128)(2,1)S(1)}, u32[]{:S(2)}, u32[]{:S(2)}) collective-permute-start(bf16[64,512]{0,1:T(8,128)(2,1)S(1)} %get-tuple-element.32), channel_id=1, source_target_pairs={{24,0},{26,2},{28,4},{30,6},{16,8},{18,10},{20,12},{22,14},{8,16},... | collective-permute-start | bytes 196616 | tf_op jit(solution)/shard_map/ppermute | solution.py:67
  115.5 6.3 %collective-permute-start.9 = (bf16[64,512]{0,1:T(8,128)(2,1)S(1)}, bf16[64,512]{0,1:T(8,128)(2,1)S(1)}, u32[]{:S(2)}, u32[]{:S(2)}) collective-permute-start(bf16[64,512]{0,1:T(8,128)(2,1)S(1)} %add_convert_fusion.2), channel_id=1, source_target_pairs={{8,0},{10,2},{12,4},{14,6},{0,8},{2,10},{4,12},{6,14},{24,16},{26,... | collective-permute-start | bytes 196616 | tf_op jit(solution)/shard_map/ppermute | solution.py:81
  117.9 11.4 %collective-permute-start.10 = (bf16[64,512]{0,1:T(8,128)(2,1)S(1)}, bf16[64,512]{0,1:T(8,128)(2,1)S(1)}, u32[]{:S(2)}, u32[]{:S(2)}) collective-permute-start(bf16[64,512]{0,1:T(8,128)(2,1)S(1)} %add_convert_fusion.2), channel_id=1, source_target_pairs={{16,0},{18,2},{20,4},{22,6},{24,8},{26,10},{28,12},{30,14},{0,16},... | collective-permute-start | bytes 196616 | tf_op jit(solution)/shard_map/ppermute | solution.py:81
  118.0 11.4 %collective-permute-start.11 = (bf16[64,512]{0,1:T(8,128)(2,1)S(1)}, bf16[64,512]{0,1:T(8,128)(2,1)S(1)}, u32[]{:S(2)}, u32[]{:S(2)}) collective-permute-start(bf16[64,512]{0,1:T(8,128)(2,1)S(1)} %add_convert_fusion.2), channel_id=1, source_target_pairs={{24,0},{26,2},{28,4},{30,6},{16,8},{18,10},{20,12},{22,14},{8,16},... | collective-permute-start | bytes 196616 | tf_op jit(solution)/shard_map/ppermute | solution.py:81
  129.5 9.3 %collective-permute-start.12 = (bf16[256,512]{1,0:T(8,128)(2,1)S(1)}, bf16[256,512]{1,0:T(8,128)(2,1)S(1)}, u32[]{:S(2)}, u32[]{:S(2)}) collective-permute-start(bf16[256,512]{1,0:T(8,128)(2,1)S(1)} %constant_dynamic-update-slice_fusion.4), channel_id=1, source_target_pairs={{2,0},{0,2},{6,4},{4,6},{10,8},{8,10},{14,12},{12,14},{18,16},{16,... | collective-permute-start | bytes 786440 | tf_op jit(solution)/shard_map/ppermute | solution.py:81
  131.0 12.0 %collective-permute-start.13 = (bf16[256,512]{1,0:T(8,128)(2,1)S(1)}, bf16[256,512]{1,0:T(8,128)(2,1)S(1)}, u32[]{:S(2)}, u32[]{:S(2)}) collective-permute-start(bf16[256,512]{1,0:T(8,128)(2,1)S(1)} %constant_dynamic-update-slice_fusion.4), channel_id=1, source_target_pairs={{4,0},{6,2},{0,4},{2,6},{12,8},{14,10},{8,12},{10,14},{20,16},{22,... | collective-permute-start | bytes 786440 | tf_op jit(solution)/shard_map/ppermute | solution.py:81
  133.3 9.7 %collective-permute-start.14 = (bf16[256,512]{1,0:T(8,128)(2,1)S(1)}, bf16[256,512]{1,0:T(8,128)(2,1)S(1)}, u32[]{:S(2)}, u32[]{:S(2)}) collective-permute-start(bf16[256,512]{1,0:T(8,128)(2,1)S(1)} %constant_dynamic-update-slice_fusion.4), channel_id=1, source_target_pairs={{6,0},{4,2},{2,4},{0,6},{14,8},{12,10},{10,12},{8,14},{22,16},{20,... | collective-permute-start | bytes 786440 | tf_op jit(solution)/shard_map/ppermute | solution.py:81
  149.3 2.0 %collective-permute-start.15 = (bf16[1024,256]{0,1:T(8,128)(2,1)S(1)}, bf16[1024,256]{0,1:T(8,128)(2,1)S(1)}, u32[]{:S(2)}, u32[]{:S(2)}) collective-permute-start(bf16[1024,256]{0,1:T(8,128)(2,1)S(1)} %fusion.19), channel_id=1, source_target_pairs={{1,0},{0,1},{3,2},{2,3},{5,4},{4,5},{7,6},{6,7},{9,8},{8,9},{11,10... | collective-permute-start | bytes 1572872 | tf_op jit(solution)/shard_map/ppermute | solution.py:160
  149.7 1.8 %copy-start.7 = (f32[1024]{0:T(1024)S(1)}, f32[1024]{0:T(1024)}, u32[]{:S(2)}) copy-start(f32[1024]{0:T(1024)} %param.10) | copy-start | bytes 12292

commit v2 on v1

v2 whole, which is shorter than its diff:
```python
import math

import jax
import jax.numpy as jnp
from jax import lax
from jax.experimental import pallas as pl
from jax.experimental.pallas import tpu as pltpu
from jax.sharding import PartitionSpec as P

FEAT = 8
HOT = 4


LEARN_RATE = 0.2
LOSS_SCALE = 32.0
ADA_EPS = 1e-06


SLOTS = 128
VMEM_BYTES = 48 * 1024 * 1024


def matmul(left, right):
    return jnp.dot(left, right, preferred_element_type=jnp.float32)


def transposed_dot(left, right):
    return lax.dot_general(
        left, right, (((0,), (0,)), ((), ())), preferred_element_type=jnp.float32
    )


def rows_dot(left, right):
    return lax.dot_general(
        left, right, (((1,), (1,)), ((), ())), preferred_element_type=jnp.float32
    )


def kernel_call(kernel, out_shape, cost, scratch=()):
    flops, moved = cost
    return pl.pallas_call(
        kernel,
        out_shape=out_shape,
        scratch_shapes=scratch,
        compiler_params=pltpu.CompilerParams(vmem_limit_bytes=VMEM_BYTES),
        cost_estimate=pl.CostEstimate(flops=flops, bytes_accessed=moved, transcendentals=0),
    )


def split_ids(ids):
    shifted = ids + 1
    high = lax.shift_right_logical(shifted, 5).astype(jnp.float32).astype(jnp.bfloat16)
    low = (shifted & 31).astype(jnp.float32).astype(jnp.bfloat16)
    return high, low


def lookup_choice():
    shape = (HOT * SLOTS, HOT * SLOTS)
    row = lax.broadcasted_iota(jnp.int32, shape, 0)
    column = lax.broadcasted_iota(jnp.int32, shape, 1)
    wanted = (row & (SLOTS - 1)) * HOT + lax.shift_right_logical(row, 7)
    return jnp.where(wanted == column, 1.0, 0.0).astype(jnp.bfloat16)


def pool_kernel(ids_ref, rows_ref, out_ref):
    blocks = ids_ref.shape[0]
    high, low = split_ids(ids_ref[...])
    choice = lookup_choice()
    columns = (rows_dot(choice, high) * 32.0 + rows_dot(choice, low) - 1.0).astype(jnp.int32)
    rows = rows_ref[...]
    position = lax.broadcasted_iota(jnp.int32, (SLOTS, rows.shape[0]), 1)
    for block in range(blocks):
        counts = jnp.zeros((SLOTS, rows.shape[0]), jnp.float32)
        for lookup in range(HOT):
            column = columns[lookup * SLOTS : (lookup + 1) * SLOTS, block : block + 1]
            counts = counts + jnp.where(column == position, 1.0, 0.0)
        sums = matmul(counts.astype(jnp.bfloat16), rows)
        out_ref[block * SLOTS : (block + 1) * SLOTS, :] = sums.astype(jnp.bfloat16)


def pool_lookups(ids, rows):
    blocks = ids.shape[0]
    flops = 2 * blocks * SLOTS * rows.size
    return kernel_call(
        pool_kernel,
        jax.ShapeDtypeStruct((blocks * SLOTS, rows.shape[1]), jnp.bfloat16),
        (flops, 2 * rows.size + 2 * blocks * SLOTS * rows.shape[1]),
    )(ids, rows)


def counts_kernel(ids_ref, out_ref):
    blocks = ids_ref.shape[0]
    row_dev = out_ref.shape[0]
    high, low = split_ids(ids_ref[...])
    choice = lookup_choice()
    lines = (rows_dot(high, choice) * 32.0 + rows_dot(low, choice) - 1.0).astype(jnp.int32)
    position = lax.broadcasted_iota(jnp.int32, (row_dev, SLOTS), 0)
    for block in range(blocks):
        counts = jnp.zeros((row_dev, SLOTS), jnp.float32)
        for lookup in range(HOT):
            line = lines[block : block + 1, lookup * SLOTS : (lookup + 1) * SLOTS]
            counts = counts + jnp.where(line == position, 1.0, 0.0)
        out_ref[:, block * SLOTS : (block + 1) * SLOTS] = counts.astype(jnp.bfloat16)


def lookup_counts(ids, row_dev):
    slot_count = ids.size // HOT
    return kernel_call(
        counts_kernel,
        jax.ShapeDtypeStruct((row_dev, slot_count), jnp.bfloat16),
        (8 * row_dev * slot_count, 2 * row_dev * slot_count),
    )(ids)


def diagonal(size):
    row = lax.broadcasted_iota(jnp.int32, (size, size), 0)
    return row == lax.broadcasted_iota(jnp.int32, (size, size), 1)


def as_column(line):
    return jnp.sum(jnp.where(diagonal(line.shape[1]), line, 0.0), axis=1, keepdims=True)


def as_line(column):
    return jnp.sum(jnp.where(diagonal(column.shape[0]), column, 0.0), axis=0, keepdims=True)


def dense_kernel(
    place_ref,
    unplace_ref,
    arrived_ref,
    down_ref,
    up_ref,
    bias_ref,
    weight_ref,
    target_ref,
    logits_ref,
    slot_ref,
    terms_ref,
):
    samples = target_ref.shape[1]
    width, rank = down_ref.shape
    emb = width // FEAT
    arrived = arrived_ref[...]
    features = [slice(f * emb, (f + 1) * emb) for f in range(FEAT)]
    pooled = [
        matmul(place_ref[f * samples : (f + 1) * samples, :], arrived).astype(jnp.bfloat16)
        for f in range(FEAT)
    ]
    hidden = jnp.zeros((samples, rank), jnp.float32)
    for f, part in enumerate(features):
        hidden = hidden + matmul(pooled[f], down_ref[part, :])
    hidden = hidden.astype(jnp.bfloat16)
    shifted = []
    summed = jnp.zeros((samples, emb), jnp.float32)
    for f, part in enumerate(features):
        shifted.append(rows_dot(hidden, up_ref[part, :]) + bias_ref[:, part])
        feats = pooled[f].astype(jnp.float32)
        summed = summed + (feats * shifted[f] + feats) * weight_ref[:, part].astype(jnp.float32)
    logits = jnp.sum(summed, axis=1, keepdims=True)
    logits_ref[...] = as_line(logits)
    dlogit = LOSS_SCALE * (jax.nn.sigmoid(logits) - as_column(target_ref[...]))
    dcross = []
    dhidden = jnp.zeros((samples, rank), jnp.float32)
    for f, part in enumerate(features):
        dmixed = dlogit * weight_ref[:, part].astype(jnp.float32)
        dcross.append((dmixed * pooled[f].astype(jnp.float32)).astype(jnp.bfloat16))
        dhidden = dhidden + matmul(dcross[f], up_ref[part, :])
    dhidden = dhidden.astype(jnp.bfloat16)
    dpooled = []
    for f, part in enumerate(features):
        dmixed = dlogit * weight_ref[:, part].astype(jnp.float32)
        back_term = rows_dot(dhidden, down_ref[part, :])
        dpooled.append((dmixed * (shifted[f] + 1.0) + back_term).astype(jnp.bfloat16))
        terms_ref[part, :rank] = transposed_dot(pooled[f], dhidden).astype(jnp.bfloat16)
        terms_ref[part, rank:] = transposed_dot(dcross[f], hidden).astype(jnp.bfloat16)
    bag_grads = jnp.concatenate(dpooled, axis=0)
    for start in range(0, slot_ref.shape[0], 256):
        picked = matmul(unplace_ref[start : start + 256, :], bag_grads)
        slot_ref[start : start + 256, :] = picked.astype(jnp.bfloat16)


def dense_step(place, unplace, arrived, down_full, up_full, bias, weight, target):
    samples = target.shape[0]
    slot_count, emb = arrived.shape
    width, rank = down_full.shape
    flops = 4 * slot_count * samples * width + 12 * samples * width * rank
    moved = 4 * place.size + 4 * arrived.size + 8 * down_full.size
    logits, slot_grads, terms = kernel_call(
        dense_kernel,
        (
            jax.ShapeDtypeStruct((1, samples), jnp.float32),
            jax.ShapeDtypeStruct((slot_count, emb), jnp.bfloat16),
            jax.ShapeDtypeStruct((width, 2 * rank), jnp.bfloat16),
        ),
        (flops, moved),
    )(
        place,
        unplace,
        arrived,
        down_full,
        up_full,
        bias.reshape(1, width),
        weight.reshape(1, width),
        target.reshape(1, samples),
    )
    return logits.reshape(samples), slot_grads, terms


def update_kernel(share_ref, rows_ref, mine_ref, other_ref, accum_ref, rows_out_ref, accum_out_ref):
    chunks = accum_ref.shape[0]
    per_share = accum_out_ref.shape[0]
    for chunk in range(chunks):
        part = slice(chunk * SLOTS, (chunk + 1) * SLOTS)
        row_grad = mine_ref[part, :].astype(jnp.float32) + other_ref[part, :].astype(jnp.float32)
        squares = jnp.mean(row_grad * row_grad, axis=1, keepdims=True)
        accum = as_column(accum_ref[chunk : chunk + 1, :]) + squares
        step = LEARN_RATE * row_grad * lax.rsqrt(accum + ADA_EPS)
        rows_out_ref[part, :] = (rows_ref[part, :].astype(jnp.float32) - step).astype(jnp.bfloat16)

        @pl.when(share_ref[0] == chunk // per_share)
        def _():
            accum_out_ref[chunk % per_share : chunk % per_share + 1, :] = as_line(accum)


def update_rows(share, rows, mine, other, accum, narrows):
    row_dev, emb = rows.shape
    chunks = row_dev // SLOTS
    vmem = pl.BlockSpec(memory_space=pltpu.VMEM)
    new_rows, new_accum = pl.pallas_call(
        update_kernel,
        in_specs=[pl.BlockSpec(memory_space=pltpu.SMEM), vmem, vmem, vmem, vmem],
        out_shape=(
            jax.ShapeDtypeStruct((row_dev, emb), jnp.bfloat16),
            jax.ShapeDtypeStruct((chunks // narrows, SLOTS), jnp.float32),
        ),
        compiler_params=pltpu.CompilerParams(vmem_limit_bytes=VMEM_BYTES),
        cost_estimate=pl.CostEstimate(
            flops=8 * rows.size, bytes_accessed=8 * rows.size, transcendentals=row_dev
        ),
    )(share.reshape(1), rows, mine, other, accum.reshape(chunks, SLOTS))
    return new_rows, new_accum.reshape(row_dev // narrows)


def group_levels(size):
    levels = []
    stride = 1
    while size % 4 == 0:
        levels.append((stride, 4))
        stride, size = stride * 4, size // 4
    if size > 1:
        levels.append((stride, size))
    return levels


def partner_index(index, stride, group, step):
    place = (index // stride) % group
    if group & (group - 1) == 0:
        other = place ^ step
    else:
        other = (place + step) % group
    return index + (other - place) * stride


def sent_from(axis, stride, group, step):
    size = lax.axis_size(axis)
    return [(partner_index(i, stride, group, step), i) for i in range(size)]


def scatter_sum(blocks, axis, levels):
    index = lax.axis_index(axis)
    for stride, group in levels:
        rows = blocks.shape[0] // group
        place = (index // stride) % group
        total = lax.dynamic_slice_in_dim(blocks, place * rows, rows, 0).astype(jnp.float32)
        for step in range(1, group):
            pairs = sent_from(axis, stride, group, step)
            if group & (group - 1) == 0:
                goal = place ^ step
            else:
                goal = (place + group - step) % group
            outgoing = lax.dynamic_slice_in_dim(blocks, goal * rows, rows, 0)
            total = total + lax.ppermute(outgoing, axis, pairs).astype(jnp.float32)
        blocks = total.astype(jnp.bfloat16)
    return blocks


def gather_blocks(block, axis, levels):
    index = lax.axis_index(axis)
    for stride, group in reversed(levels):
        rows = block.shape[0]
        place = (index // stride) % group
        whole = jnp.zeros((group * rows,) + block.shape[1:], block.dtype)
        whole = lax.dynamic_update_slice_in_dim(whole, block, place * rows, 0)
        for step in range(1, group):
            origin = partner_index(index, stride, group, step)
            came = lax.ppermute(block, axis, sent_from(axis, stride, group, step))
            spot = (origin // stride) % group
            whole = lax.dynamic_update_slice_in_dim(whole, came, spot * rows, 0)
        block = whole
    return block


def local(
    table_rows, accum, factor_down, factor_up, cross_bias, out_weight, target, bag_rows, slot_target
):
    tables = lax.axis_size("table")
    narrows = lax.axis_size("narrow")
    row_dev, emb_width = table_rows.shape
    pools_per = slot_target.shape[1]
    samples = target.shape[0]
    bag_count = samples * FEAT
    slot_count = tables * pools_per
    narrow_levels = group_levels(narrows)
    table_levels = group_levels(tables)
    down_full = gather_blocks(factor_down, "narrow", narrow_levels)
    up_full = gather_blocks(factor_up, "narrow", narrow_levels)
    asked = lax.all_to_all(bag_rows, "table", split_axis=0, concat_axis=0, tiled=True)
    lookup_ids = asked.reshape(slot_count // SLOTS, SLOTS * HOT)
    pool_out = pool_lookups(lookup_ids, table_rows).reshape(tables, pools_per, emb_width)
    arrived = lax.all_to_all(pool_out, "table", split_axis=0, concat_axis=0, tiled=True).reshape(
        slot_count, emb_width
    )
    order = jnp.arange(bag_count, dtype=jnp.int32)
    order = (order % samples) * FEAT + order // samples
    goals = slot_target.reshape(1, slot_count)
    place = (goals == order[:, None]).astype(jnp.bfloat16)
    unplace = (goals.reshape(slot_count, 1) == order[None, :]).astype(jnp.bfloat16)
    logits, slot_grads, grad_terms = dense_step(
        place, unplace, arrived, down_full, up_full, cross_bias, out_weight, target
    )
    narrow_sum = scatter_sum(grad_terms, "narrow", narrow_levels)
    returned = lax.all_to_all(
        slot_grads.reshape(tables, pools_per, emb_width),
        "table",
        split_axis=0,
        concat_axis=0,
        tiled=True,
    ).reshape(slot_count, emb_width)
    table_sum = scatter_sum(narrow_sum, "table", table_levels)
    sent_grad = matmul(lookup_counts(lookup_ids, row_dev), returned).astype(jnp.bfloat16)
    table_sum, sent_grad = lax.optimization_barrier((table_sum, sent_grad))
    grand_total = gather_blocks(table_sum, "table", table_levels).astype(jnp.float32)
    batch_all = samples * tables * narrows
    grand_total = grand_total * (1.0 / math.sqrt(batch_all))
    rank_size = factor_down.shape[1]
    down_grad = grand_total[:, :rank_size]
    up_grad = grand_total[:, rank_size:]
    if narrows == 2:
        mine = sent_grad
        other = lax.ppermute(sent_grad, "narrow", sent_from("narrow", 1, 2, 1))
    else:
        share = scatter_sum(sent_grad, "narrow", narrow_levels)
        mine = gather_blocks(share, "narrow", narrow_levels)
        other = jnp.zeros_like(mine)
    new_rows, new_accum = update_rows(
        lax.axis_index("narrow"), table_rows, mine, other, accum, narrows
    )
    return (logits, down_grad, up_grad, new_rows, new_accum)


def solution(mesh):
    in_specs = (
        P("table", None),
        P("table"),
        P("narrow", None),
        P("narrow", None),
        P(),
        P(),
        P(("table", "narrow")),
        P(("table", "narrow"), None),
        P(("table", "narrow"), None),
    )
    out_specs = (
        P(("table", "narrow")),
        P("narrow", None),
        P("narrow", None),
        P("table", None),
        P(("table", "narrow")),
    )
    return jax.shard_map(local, mesh=mesh, in_specs=in_specs, out_specs=out_specs, check_vma=False)
```

time: 155 us -> 139 us (0.90)
  Pallas kernels: 0 us -> 25 us
  matrix products: 23.5 us -> 3.73 us
  waiting for transfers between devices: 62.5 us -> 47.9 us
  local copies, waits for them, and re-layouts: 16.5 us -> 11.8 us
  starting transfers between devices: 30.4 us -> 26.6 us
  other arithmetic: 3.91 us -> 7.13 us
    pallas_call x0 -> x4, Pallas kernels: none -> 25 us  [the longest x1 9.16 us: lookup_counts(): kernel_call(counts_kernel, jax.ShapeDtypeStruct((row_dev, slot_count), jn...]
    dot_general x10 -> x1, matrix products: 23.5 us -> 3.73 us  [matmul(): return jnp.dot(left, right, preferred_element_type=jnp.float32)]
    all_to_all x1, waiting for transfers between devices: 18.1 us -> 12.9 us  [local(): lax.all_to_all(pool_out, 'table', split_axis=0, concat_axis=0, tiled=True)]
    convert_element_type x2, other arithmetic: 0.28 us -> 5.15 us  [the longest x1 2.7 us: local(): place = (goals == order[:, None]).astype(jnp.bfloat16)]
    ppermute x8, waiting for transfers between devices: 18.2 us -> 13.5 us  [gather_blocks(): came = lax.ppermute(block, axis, sent_from(axis, stride, group, step))]
    ppermute x7, waiting for transfers between devices: 26 us -> 21.5 us  [scatter_sum(): total = total + lax.ppermute(outgoing, axis, pairs).astype(jnp.float32)]
    reshape x3 -> x1, local copies, waits for them, and re-layouts: 4.44 us -> 0.01 us  [dense_step(): weight.reshape(1, width)]
    ppermute x7, starting transfers between devices: 11.6 us -> 8.27 us  [scatter_sum(): total = total + lax.ppermute(outgoing, axis, pairs).astype(jnp.float32)]
  transfers between devices with their start and end apart: 18 -> 18, of which waited for: 10 -> 8; matrix products, arithmetic and copies ran while one was open for 10% -> 10% of each run, Pallas kernels for 0% -> 7%
where the time goes in v2:
time: 139 us
  waiting for transfers between devices  47.9 us (34%)
  starting transfers between devices  26.6 us (19%)
  Pallas kernels  25 us (18%)
  blocking collectives  15.5 us (11%)
  local copies, waits for them, and re-layouts  11.8 us (8%)
  other arithmetic  7.13 us (5%)
  matrix products  3.73 us (3%)
    ppermute x7, waiting for transfers between devices, scatter_sum(): total = total + lax.ppermute(outgoing, axis, pairs).astype(jnp.float32)  21.5 us
    all_to_all x1, blocking collectives, local(): lax.all_to_all(bag_rows, 'table', split_axis=0, concat_axis=0, tiled=True)  15.5 us
    ppermute x8, waiting for transfers between devices, gather_blocks(): came = lax.ppermute(block, axis, sent_from(axis, stride, group, step))  13.5 us
    all_to_all x1, waiting for transfers between devices, local(): lax.all_to_all(pool_out, 'table', split_axis=0, concat_axis=0, tiled=True)  12.9 us
    pallas_call x1, Pallas kernels, lookup_counts(): kernel_call(counts_kernel, jax.ShapeDtypeStruct((row_dev, slot_count), jn...  9.16 us
    ppermute x8, starting transfers between devices, gather_blocks(): came = lax.ppermute(block, axis, sent_from(axis, stride, group, step))  8.57 us
    ppermute x7, starting transfers between devices, scatter_sum(): total = total + lax.ppermute(outgoing, axis, pairs).astype(jnp.float32)  8.27 us
    pallas_call x1, Pallas kernels, dense_step(): kernel_call(dense_kernel, (jax.ShapeDtypeStruct((1, samples), jnp.float32...  8.24 us
  transfers between devices with their start and end apart: 18, of which 8 were waited for; matrix products, arithmetic and copies ran while one was open for 10% of the time, Pallas kernels for 7%

profile of v2, /device:TPU:0, one launch (start us, length us, event | category | flops | bytes accessed | tf_op | source)
XLA Modules:
  0.0 138.7 jit_solution(13190482543382668428)
XLA Ops:
  0.6 0.8 all_to_all.13
  1.4 15.5 %all_to_all.21 = s32[16,1,512]{2,1,0:T(1,128)S(1)} all-to-all(s32[16,1,512]{2,1,0:T(1,128)S(1)} %all_to_all.13), channel_id=1, replica_groups=mesh['table'=16,'narrow'=2] {'table'}, dimensions={0} | all-to-all | bytes 65536 | tf_op jit(solution)/shard_map/all_to_all | solution.py:318
  16.9 1.0 copy-done.2
  18.0 5.7 %shard_map.128 = bf16[2048,256]{1,0:T(8,128)(2,1)} custom-call(s32[16,512]{1,0:T(8,128)S(1)} %bitcast.20, bf16[1024,256]{1,0:T(8,128)(2,1)S(1)} %copy-done.2), custom_call_target="tpu_custom_call" | custom-call | flops 1073741824 | bytes 1572864 | tf_op jit(solution)/shard_map/pallas_call | solution.py:84
  23.7 3.7 %all-to-all-start.1 = ((bf16[16,128,256]{2,1,0:T(8,128)(2,1)}), bf16[16,128,256]{2,1,0:T(8,128)(2,1)S(1)}, u32[]{:S(2)}, u32[]{:S(2)}) async-start(bf16[16,128,256]{2,1,0:T(8,128)(2,1)} %bitcast.1), calls=%async_computation.1 | async-start | bytes 2097152 | tf_op jit(solution)/shard_map/all_to_all | solution.py:321
  27.4 0.1 collective-permute-start.1
  27.5 0.5 collective-permute-start
  28.0 0.1 broadcast.127.clone.1
  28.1 1.1 constant_dynamic-update-slice_fusion.9
  29.2 0.1 broadcast.127.clone
  29.2 1.1 constant_dynamic-update-slice_fusion.11
  30.3 2.4 %compare_convert_fusion.unplace_ref = bf16[2048,1024]{1,0:T(8,128)(2,1)} fusion(s32[1024]{0:T(1024)S(1)} %fusion.7, s32[2048]{0:T(1024)S(1)} %bitcast.25), kind=kLoop, calls=%fused_computation | loop fusion | flops 4194304 | bytes 4206592 | tf_op jit(solution)/shard_map/convert_element_type | solution.py:328
  32.8 2.7 %compare_convert_fusion.1.place_ref = bf16[1024,2048]{1,0:T(8,128)(2,1)} fusion(s32[2048]{0:T(1024)S(1)} %bitcast.26, s32[1024]{0:T(1024)S(1)} %fusion.7), kind=kLoop, calls=%fused_computation.1 | loop fusion | flops 4194304 | bytes 4206592 | tf_op jit(solution)/shard_map/convert_element_type | solution.py:327
  35.5 1.1 constant_dynamic-update-slice_fusion.8.up_ref
  36.6 1.1 constant_dynamic-update-slice_fusion.10.down_ref
  37.7 12.9 %all-to-all-done.1 = bf16[16,128,256]{2,1,0:T(8,128)(2,1)S(1)} async-done(((bf16[16,128,256]{2,1,0:T(8,128)(2,1)}), bf16[16,128,256]{2,1,0:T(8,128)(2,1)S(1)}, u32[]{:S(2)}, u32[]{:S(2)}) %all-to-all-start.1) | async-done | bytes 1048608 | tf_op jit(solution)/shard_map/all_to_all | solution.py:321
  50.6 8.2 %shard_map.129 = (f32[1,128]{1,0:T(1,128)}, bf16[2048,256]{1,0:T(8,128)(2,1)S(1)}, bf16[2048,512]{1,0:T(8,128)(2,1)}) custom-call(bf16[1024,2048]{1,0:T(8,128)(2,1)} %compare_convert_fusion.1.place_ref, bf16[2048,1024]{1,0:T(8,128)(2,1)} %compare_convert_fusion.unplace_ref, bf16[2048,256]{1,0:T(8,128)(2,1)S(1)} %bitcast.18, ...), custom_call_target="tpu_custom_call" | custom-call | flops 2952790016 | bytes 14680064 | tf_op jit(solution)/shard_map/pallas_call | solution.py:189
  58.9 1.7 %constant_dynamic-slice_fusion.6 = bf16[1024,512]{1,0:T(8,128)(2,1)S(1)} fusion(bf16[2048,512]{1,0:T(8,128)(2,1)} %get-tuple-element.13, s32[]{:T(128)S(6)} %select_n.194), kind=kLoop, calls=%fused_computation.31 | loop fusion | bytes 2097156 | tf_op jit(solution)/shard_map/dynamic_slice | solution.py:282
  60.6 0.1 collective-permute-start.2
  60.7 6.0 %all-to-all-start.2 = ((bf16[16,128,256]{2,1,0:T(8,128)(2,1)}), bf16[16,128,256]{2,1,0:T(8,128)(2,1)}, u32[]{:S(2)}, u32[]{:S(2)}) async-start(bf16[16,128,256]{2,1,0:T(8,128)(2,1)} %bitcast.19), calls=%async_computation.2 | async-start | bytes 2097152 | tf_op jit(solution)/shard_map/all_to_all | solution.py:333
  66.8 1.5 %add_convert_fusion = bf16[1024,512]{1,0:T(8,128)(2,1)S(1)} fusion(bf16[1024,512]{1,0:T(8,128)(2,1)} %collective-permute-done.2, bf16[2048,512]{1,0:T(8,128)(2,1)S(1)} %copy-done.7, s32[]{:T(128)S(6)} %select_n.191), kind=kLoop, calls=%fused_computation.3 | loop fusion | flops 2097152 | bytes 3145732 | tf_op jit(solution)/shard_map/convert_element_type | solution.py:284
  68.3 0.1 constant_dynamic-slice_fusion.5
  68.4 1.7 %collective-permute-start.3 = (bf16[256,512]{1,0:T(8,128)(2,1)S(1)}, bf16[256,512]{1,0:T(8,128)(2,1)S(1)}, u32[]{:S(2)}, u32[]{:S(2)}) collective-permute-start(bf16[256,512]{1,0:T(8,128)(2,1)S(1)} %get-tuple-element.21), channel_id=1, source_target_pairs={{2,0},{0,2},{6,4},{4,6},{10,8},{8,10},{14,12},{12,14},{18,16},{16,... | collective-permute-start | bytes 786440 | tf_op jit(solution)/shard_map/ppermute | solution.py:283
  70.1 1.5 %collective-permute-start.4 = (bf16[256,512]{1,0:T(8,128)(2,1)S(1)}, bf16[256,512]{1,0:T(8,128)(2,1)S(1)}, u32[]{:S(2)}, u32[]{:S(2)}) collective-permute-start(bf16[256,512]{1,0:T(8,128)(2,1)S(1)} %get-tuple-element.23), channel_id=1, source_target_pairs={{4,0},{6,2},{0,4},{2,6},{12,8},{14,10},{8,12},{10,14},{20,16},{22,... | collective-permute-start | bytes 786440 | tf_op jit(solution)/shard_map/ppermute | solution.py:283
  71.6 0.4 collective-permute-start.5
  72.0 8.3 %collective-permute-done.3 = bf16[256,512]{1,0:T(8,128)(2,1)S(1)} collective-permute-done((bf16[256,512]{1,0:T(8,128)(2,1)S(1)}, bf16[256,512]{1,0:T(8,128)(2,1)S(1)}, u32[]{:S(2)}, u32[]{:S(2)}) %collective-permute-start.3) | collective-permute-done | bytes 262176 | tf_op jit(solution)/shard_map/ppermute | solution.py:283
  80.3 8.2 %collective-permute-done.4 = bf16[256,512]{1,0:T(8,128)(2,1)S(1)} collective-permute-done((bf16[256,512]{1,0:T(8,128)(2,1)S(1)}, bf16[256,512]{1,0:T(8,128)(2,1)S(1)}, u32[]{:S(2)}, u32[]{:S(2)}) %collective-permute-start.4) | collective-permute-done | bytes 262176 | tf_op jit(solution)/shard_map/ppermute | solution.py:283
  88.5 5.0 %collective-permute-done.5 = bf16[256,512]{1,0:T(8,128)(2,1)S(1)} collective-permute-done((bf16[256,512]{1,0:T(8,128)(2,1)S(1)}, bf16[256,512]{1,0:T(8,128)(2,1)S(1)}, u32[]{:S(2)}, u32[]{:S(2)}) %collective-permute-start.5) | collective-permute-done | bytes 262176 | tf_op jit(solution)/shard_map/ppermute | solution.py:283
  93.5 0.1 add_convert_fusion.1
  93.6 0.1 collective-permute-start.6
  93.7 3.2 %collective-permute-start.7 = (bf16[64,512]{1,0:T(8,128)(2,1)S(1)}, bf16[64,512]{1,0:T(8,128)(2,1)S(1)}, u32[]{:S(2)}, u32[]{:S(2)}) collective-permute-start(bf16[64,512]{1,0:T(8,128)(2,1)S(1)} %get-tuple-element.26), channel_id=1, source_target_pairs={{16,0},{18,2},{20,4},{22,6},{24,8},{26,10},{28,12},{30,14},{0,16},... | collective-permute-start | bytes 196616 | tf_op jit(solution)/shard_map/ppermute | solution.py:283
  96.9 1.4 collective-permute-start.8
  98.3 9.2 %shard_map.130 = bf16[1024,2048]{1,0:T(8,128)(2,1)S(1)} custom-call(s32[16,512]{1,0:T(8,128)S(1)} %bitcast.21), custom_call_target="tpu_custom_call" | custom-call | flops 16777216 | bytes 4194304 | tf_op jit(solution)/shard_map/pallas_call | solution.py:108
  107.5 2.0 %copy-done = bf16[1024,2048]{1,0:T(8,128)(2,1)} copy-done((bf16[1024,2048]{1,0:T(8,128)(2,1)}, bf16[1024,2048]{1,0:T(8,128)(2,1)S(1)}, u32[]{:S(2)}) %copy-start) | copy-done | bytes 4194328
  109.5 3.7 %fusion.mine_ref = bf16[1024,256]{1,0:T(8,128)(2,1)S(1)} fusion(bf16[1024,2048]{1,0:T(8,128)(2,1)} %copy-done, bf16[2048,256]{1,0:T(8,128)(2,1)} %bitcast.7), kind=kOutput, calls=%fused_computation.5 | convolution fusion | flops 1074003968 | bytes 5767168 | tf_op jit(solution)/shard_map/dot_general | solution.py:24
  113.2 0.6 collective-permute-start.9
  113.9 2.4 %collective-permute-start.10 = (bf16[64,512]{1,0:T(8,128)(2,1)S(1)}, bf16[64,512]{1,0:T(8,128)(2,1)S(1)}, u32[]{:S(2)}, u32[]{:S(2)}) collective-permute-start(bf16[64,512]{1,0:T(8,128)(2,1)S(1)} %add_convert_fusion.2), channel_id=1, source_target_pairs={{16,0},{18,2},{20,4},{22,6},{24,8},{26,10},{28,12},{30,14},{0,16},... | collective-permute-start | bytes 196616 | tf_op jit(solution)/shard_map/ppermute | solution.py:297
  116.3 1.4 collective-permute-start.11
  117.8 1.6 %collective-permute-done.10 = bf16[64,512]{1,0:T(8,128)(2,1)S(1)} collective-permute-done((bf16[64,512]{1,0:T(8,128)(2,1)S(1)}, bf16[64,512]{1,0:T(8,128)(2,1)S(1)}, u32[]{:S(2)}, u32[]{:S(2)}) %collective-permute-start.10) | collective-permute-done | bytes 65568 | tf_op jit(solution)/shard_map/ppermute | solution.py:297
  119.4 3.0 %collective-permute-done.11 = bf16[64,512]{1,0:T(8,128)(2,1)S(1)} collective-permute-done((bf16[64,512]{1,0:T(8,128)(2,1)S(1)}, bf16[64,512]{1,0:T(8,128)(2,1)S(1)}, u32[]{:S(2)}, u32[]{:S(2)}) %collective-permute-start.11) | collective-permute-done | bytes 65568 | tf_op jit(solution)/shard_map/ppermute | solution.py:297
  122.4 0.6 collective-permute-start.12
  123.0 3.0 %collective-permute-start.14 = (bf16[256,512]{1,0:T(8,128)(2,1)S(1)}, bf16[256,512]{1,0:T(8,128)(2,1)S(1)}, u32[]{:S(2)}, u32[]{:S(2)}) collective-permute-start(bf16[256,512]{1,0:T(8,128)(2,1)S(1)} %constant_dynamic-update-slice_fusion.4), channel_id=1, source_target_pairs={{6,0},{4,2},{2,4},{0,6},{14,8},{12,10},{10,12},{8,14},{22,16},{20,... | collective-permute-start | bytes 786440 | tf_op jit(solution)/shard_map/ppermute | solution.py:297
  125.9 0.1 broadcast_in_dim.8
  126.0 4.0 %collective-permute-done.12 = bf16[256,512]{1,0:T(8,128)(2,1)S(1)} collective-permute-done((bf16[256,512]{1,0:T(8,128)(2,1)S(1)}, bf16[256,512]{1,0:T(8,128)(2,1)S(1)}, u32[]{:S(2)}, u32[]{:S(2)}) %collective-permute-start.12) | collective-permute-done | bytes 262176 | tf_op jit(solution)/shard_map/ppermute | solution.py:297
  130.1 4.9 %collective-permute-done.13 = bf16[256,512]{1,0:T(8,128)(2,1)S(1)} collective-permute-done((bf16[256,512]{1,0:T(8,128)(2,1)S(1)}, bf16[256,512]{1,0:T(8,128)(2,1)S(1)}, u32[]{:S(2)}, u32[]{:S(2)}) %collective-permute-start.13) | collective-permute-done | bytes 262176 | tf_op jit(solution)/shard_map/ppermute | solution.py:297
  135.0 0.3 convert_multiply_fusion
  135.3 1.5 %fusion.10 = (f32[1024,256]{1,0:T(8,128)}, f32[1024,256]{1,0:T(8,128)}) fusion(f32[1024,512]{1,0:T(8,128)S(1)} %convert_multiply_fusion), kind=kLoop, calls=%fused_computation.41 | loop fusion | bytes 4194304 | tf_op jit(solution)/shard_map/slice | solution.py:348
  136.8 1.9 %shard_map.131 = (bf16[1024,256]{1,0:T(8,128)(2,1)}, f32[4,128]{1,0:T(4,128)}) custom-call(s32[1]{0:T(128)} %bitcast.9.share_ref, bf16[1024,256]{1,0:T(8,128)(2,1)S(1)} %copy-done.3, bf16[1024,256]{1,0:T(8,128)(2,1)S(1)} %fusion.mine_ref, bf16[1024,256]{1,0:T(8,128)(2,1)S(1)} %collective-permute-done.15.other_ref, f32[8,128]{1,0:T(8,128)S(1)} %bitcast.23), custom_call_target="tpu_custom_call" | custom-call | flops 2097152 | bytes 2097152 | tf_op jit(solution)/shard_map/pallas_call | solution.py:230
  (44 shorter events, 0.3 us)
Async XLA Ops:
  16.9 1.0 copy-start.2
  18.0 10.0 %copy-start.9 = (bf16[2048]{0:T(1024)(128)(2,1)S(1)}, bf16[2048]{0:T(1024)(128)(2,1)}, u32[]{:S(2)}) copy-start(bf16[2048]{0:T(1024)(128)(2,1)} %param.14) | copy-start | bytes 12292
  23.7 26.9 %all-to-all-start.1 = ((bf16[16,128,256]{2,1,0:T(8,128)(2,1)}), bf16[16,128,256]{2,1,0:T(8,128)(2,1)S(1)}, u32[]{:S(2)}, u32[]{:S(2)}) async-start(bf16[16,128,256]{2,1,0:T(8,128)(2,1)} %bitcast.1), calls=%async_computation.1 | async-start | bytes 2097152 | tf_op jit(solution)/shard_map/all_to_all | solution.py:321
  27.4 8.1 %collective-permute-start.1 = (bf16[1024,256]{1,0:T(8,128)(2,1)}, bf16[1024,256]{1,0:T(8,128)(2,1)}, u32[]{:S(2)}, u32[]{:S(2)}) collective-permute-start(bf16[1024,256]{1,0:T(8,128)(2,1)} %param.12), channel_id=1, source_target_pairs={{1,0},{0,1},{3,2},{2,3},{5,4},{4,5},{7,6},{6,7},{9,8},{8,9},{11,10... | collective-permute-start | bytes 1572872 | tf_op jit(solution)/shard_map/ppermute | solution.py:297
  27.5 9.2 %collective-permute-start = (bf16[1024,256]{1,0:T(8,128)(2,1)}, bf16[1024,256]{1,0:T(8,128)(2,1)}, u32[]{:S(2)}, u32[]{:S(2)}) collective-permute-start(bf16[1024,256]{1,0:T(8,128)(2,1)} %param.11), channel_id=1, source_target_pairs={{1,0},{0,1},{3,2},{2,3},{5,4},{4,5},{7,6},{6,7},{9,8},{8,9},{11,10... | collective-permute-start | bytes 1572872 | tf_op jit(solution)/shard_map/ppermute | solution.py:297
  28.0 2.3 %copy-start.8 = (s32[16,128]{1,0:T(8,128)S(1)}, s32[16,128]{1,0:T(8,128)}, u32[]{:S(2)}) copy-start(s32[16,128]{1,0:T(8,128)} %param.17) | copy-start | bytes 24580
  35.5 15.1 %copy-start.4 = (f32[2048]{0:T(1024)S(1)}, f32[2048]{0:T(1024)}, u32[]{:S(2)}) copy-start(f32[2048]{0:T(1024)} %param.13) | copy-start | bytes 24580
  35.5 15.1 %copy-start.6 = (f32[128]{0:T(128)S(1)}, f32[128]{0:T(128)}, u32[]{:S(2)}) copy-start(f32[128]{0:T(128)} %param.15) | copy-start | bytes 1540
  58.9 1.8 %copy-start.1 = (bf16[2048,256]{1,0:T(8,128)(2,1)}, bf16[2048,256]{1,0:T(8,128)(2,1)S(1)}, u32[]{:S(2)}) copy-start(bf16[2048,256]{1,0:T(8,128)(2,1)S(1)} %get-tuple-element.14) | copy-start | bytes 3145732
  58.9 7.9 %copy-start.7 = (bf16[2048,512]{1,0:T(8,128)(2,1)S(1)}, bf16[2048,512]{1,0:T(8,128)(2,1)}, u32[]{:S(2)}) copy-start(bf16[2048,512]{1,0:T(8,128)(2,1)} %get-tuple-element.13) | copy-start | bytes 6291460
  60.6 6.2 %collective-permute-start.2 = (bf16[1024,512]{1,0:T(8,128)(2,1)S(1)}, bf16[1024,512]{1,0:T(8,128)(2,1)}, u32[]{:S(2)}, u32[]{:S(2)}) collective-permute-start(bf16[1024,512]{1,0:T(8,128)(2,1)S(1)} %constant_dynamic-slice_fusion.6), channel_id=1, source_target_pairs={{1,0},{0,1},{3,2},{2,3},{5,4},{4,5},{7,6},{6,7},{9,8},{8,9},{11,10... | collective-permute-start | bytes 3145736 | tf_op jit(solution)/shard_map/ppermute | solution.py:283
  60.7 48.8 %all-to-all-start.2 = ((bf16[16,128,256]{2,1,0:T(8,128)(2,1)}), bf16[16,128,256]{2,1,0:T(8,128)(2,1)}, u32[]{:S(2)}, u32[]{:S(2)}) async-start(bf16[16,128,256]{2,1,0:T(8,128)(2,1)} %bitcast.19), calls=%async_computation.2 | async-start | bytes 2097152 | tf_op jit(solution)/shard_map/all_to_all | solution.py:333
  68.4 11.9 %collective-permute-start.3 = (bf16[256,512]{1,0:T(8,128)(2,1)S(1)}, bf16[256,512]{1,0:T(8,128)(2,1)S(1)}, u32[]{:S(2)}, u32[]{:S(2)}) collective-permute-start(bf16[256,512]{1,0:T(8,128)(2,1)S(1)} %get-tuple-element.21), channel_id=1, source_target_pairs={{2,0},{0,2},{6,4},{4,6},{10,8},{8,10},{14,12},{12,14},{18,16},{16,... | collective-permute-start | bytes 786440 | tf_op jit(solution)/shard_map/ppermute | solution.py:283
  70.1 18.4 %collective-permute-start.4 = (bf16[256,512]{1,0:T(8,128)(2,1)S(1)}, bf16[256,512]{1,0:T(8,128)(2,1)S(1)}, u32[]{:S(2)}, u32[]{:S(2)}) collective-permute-start(bf16[256,512]{1,0:T(8,128)(2,1)S(1)} %get-tuple-element.23), channel_id=1, source_target_pairs={{4,0},{6,2},{0,4},{2,6},{12,8},{14,10},{8,12},{10,14},{20,16},{22,... | collective-permute-start | bytes 786440 | tf_op jit(solution)/shard_map/ppermute | solution.py:283
  71.6 21.9 %collective-permute-start.5 = (bf16[256,512]{1,0:T(8,128)(2,1)S(1)}, bf16[256,512]{1,0:T(8,128)(2,1)S(1)}, u32[]{:S(2)}, u32[]{:S(2)}) collective-permute-start(bf16[256,512]{1,0:T(8,128)(2,1)S(1)} %get-tuple-element.22), channel_id=1, source_target_pairs={{6,0},{4,2},{2,4},{0,6},{14,8},{12,10},{10,12},{8,14},{22,16},{20,... | collective-permute-start | bytes 786440 | tf_op jit(solution)/shard_map/ppermute | solution.py:283
  93.6 15.8 %collective-permute-start.6 = (bf16[64,512]{1,0:T(8,128)(2,1)S(1)}, bf16[64,512]{1,0:T(8,128)(2,1)S(1)}, u32[]{:S(2)}, u32[]{:S(2)}) collective-permute-start(bf16[64,512]{1,0:T(8,128)(2,1)S(1)} %get-tuple-element.24), channel_id=1, source_target_pairs={{8,0},{10,2},{12,4},{14,6},{0,8},{2,10},{4,12},{6,14},{24,16},{26,... | collective-permute-start | bytes 196616 | tf_op jit(solution)/shard_map/ppermute | solution.py:283
  93.7 15.7 %collective-permute-start.7 = (bf16[64,512]{1,0:T(8,128)(2,1)S(1)}, bf16[64,512]{1,0:T(8,128)(2,1)S(1)}, u32[]{:S(2)}, u32[]{:S(2)}) collective-permute-start(bf16[64,512]{1,0:T(8,128)(2,1)S(1)} %get-tuple-element.26), channel_id=1, source_target_pairs={{16,0},{18,2},{20,4},{22,6},{24,8},{26,10},{28,12},{30,14},{0,16},... | collective-permute-start | bytes 196616 | tf_op jit(solution)/shard_map/ppermute | solution.py:283
  96.9 12.5 %collective-permute-start.8 = (bf16[64,512]{1,0:T(8,128)(2,1)S(1)}, bf16[64,512]{1,0:T(8,128)(2,1)S(1)}, u32[]{:S(2)}, u32[]{:S(2)}) collective-permute-start(bf16[64,512]{1,0:T(8,128)(2,1)S(1)} %get-tuple-element.25), channel_id=1, source_target_pairs={{24,0},{26,2},{28,4},{30,6},{16,8},{18,10},{20,12},{22,14},{8,16},... | collective-permute-start | bytes 196616 | tf_op jit(solution)/shard_map/ppermute | solution.py:283
  107.5 2.0 %copy-start = (bf16[1024,2048]{1,0:T(8,128)(2,1)}, bf16[1024,2048]{1,0:T(8,128)(2,1)S(1)}, u32[]{:S(2)}) copy-start(bf16[1024,2048]{1,0:T(8,128)(2,1)S(1)} %shard_map.130) | copy-start | bytes 12582916
  113.2 4.5 %collective-permute-start.9 = (bf16[64,512]{1,0:T(8,128)(2,1)S(1)}, bf16[64,512]{1,0:T(8,128)(2,1)S(1)}, u32[]{:S(2)}, u32[]{:S(2)}) collective-permute-start(bf16[64,512]{1,0:T(8,128)(2,1)S(1)} %add_convert_fusion.2), channel_id=1, source_target_pairs={{8,0},{10,2},{12,4},{14,6},{0,8},{2,10},{4,12},{6,14},{24,16},{26,... | collective-permute-start | bytes 196616 | tf_op jit(solution)/shard_map/ppermute | solution.py:297
  113.9 5.5 %collective-permute-start.10 = (bf16[64,512]{1,0:T(8,128)(2,1)S(1)}, bf16[64,512]{1,0:T(8,128)(2,1)S(1)}, u32[]{:S(2)}, u32[]{:S(2)}) collective-permute-start(bf16[64,512]{1,0:T(8,128)(2,1)S(1)} %add_convert_fusion.2), channel_id=1, source_target_pairs={{16,0},{18,2},{20,4},{22,6},{24,8},{26,10},{28,12},{30,14},{0,16},... | collective-permute-start | bytes 196616 | tf_op jit(solution)/shard_map/ppermute | solution.py:297
  116.3 6.1 %collective-permute-start.11 = (bf16[64,512]{1,0:T(8,128)(2,1)S(1)}, bf16[64,512]{1,0:T(8,128)(2,1)S(1)}, u32[]{:S(2)}, u32[]{:S(2)}) collective-permute-start(bf16[64,512]{1,0:T(8,128)(2,1)S(1)} %add_convert_fusion.2), channel_id=1, source_target_pairs={{24,0},{26,2},{28,4},{30,6},{16,8},{18,10},{20,12},{22,14},{8,16},... | collective-permute-start | bytes 196616 | tf_op jit(solution)/shard_map/ppermute | solution.py:297
  122.4 7.7 %collective-permute-start.12 = (bf16[256,512]{1,0:T(8,128)(2,1)S(1)}, bf16[256,512]{1,0:T(8,128)(2,1)S(1)}, u32[]{:S(2)}, u32[]{:S(2)}) collective-permute-start(bf16[256,512]{1,0:T(8,128)(2,1)S(1)} %constant_dynamic-update-slice_fusion.4), channel_id=1, source_target_pairs={{2,0},{0,2},{6,4},{4,6},{10,8},{8,10},{14,12},{12,14},{18,16},{16,... | collective-permute-start | bytes 786440 | tf_op jit(solution)/shard_map/ppermute | solution.py:297
  123.0 12.0 %collective-permute-start.13 = (bf16[256,512]{1,0:T(8,128)(2,1)S(1)}, bf16[256,512]{1,0:T(8,128)(2,1)S(1)}, u32[]{:S(2)}, u32[]{:S(2)}) collective-permute-start(bf16[256,512]{1,0:T(8,128)(2,1)S(1)} %constant_dynamic-update-slice_fusion.4), channel_id=1, source_target_pairs={{4,0},{6,2},{0,4},{2,6},{12,8},{14,10},{8,12},{10,14},{20,16},{22,... | collective-permute-start | bytes 786440 | tf_op jit(solution)/shard_map/ppermute | solution.py:297
  123.0 13.8 %collective-permute-start.15 = (bf16[1024,256]{1,0:T(8,128)(2,1)S(1)}, bf16[1024,256]{1,0:T(8,128)(2,1)S(1)}, u32[]{:S(2)}, u32[]{:S(2)}) collective-permute-start(bf16[1024,256]{1,0:T(8,128)(2,1)S(1)} %fusion.mine_ref), channel_id=1, source_target_pairs={{1,0},{0,1},{3,2},{2,3},{5,4},{4,5},{7,6},{6,7},{9,8},{8,9},{11,10... | collective-permute-start | bytes 1572872 | tf_op jit(solution)/shard_map/ppermute | solution.py:351
  123.0 12.0 %collective-permute-start.14 = (bf16[256,512]{1,0:T(8,128)(2,1)S(1)}, bf16[256,512]{1,0:T(8,128)(2,1)S(1)}, u32[]{:S(2)}, u32[]{:S(2)}) collective-permute-start(bf16[256,512]{1,0:T(8,128)(2,1)S(1)} %constant_dynamic-update-slice_fusion.4), channel_id=1, source_target_pairs={{6,0},{4,2},{2,4},{0,6},{14,8},{12,10},{10,12},{8,14},{22,16},{20,... | collective-permute-start | bytes 786440 | tf_op jit(solution)/shard_map/ppermute | solution.py:297
  135.3 1.5 %copy-start.3 = (bf16[1024,256]{1,0:T(8,128)(2,1)S(1)}, bf16[1024,256]{1,0:T(8,128)(2,1)}, u32[]{:S(2)}) copy-start(bf16[1024,256]{1,0:T(8,128)(2,1)} %rows_ref.3) | copy-start | bytes 1572868
  135.3 1.5 %copy-start.5 = (f32[1024]{0:T(1024)S(1)}, f32[1024]{0:T(1024)}, u32[]{:S(2)}) copy-start(f32[1024]{0:T(1024)} %param.10) | copy-start | bytes 12292

commit v3 on v2

v3 whole, which is shorter than its diff:
```python
import functools
import math

import jax
import jax.numpy as jnp
from jax import lax
from jax.experimental import pallas as pl
from jax.experimental.pallas import tpu as pltpu
from jax.sharding import PartitionSpec as P

FEAT = 8
HOT = 4


LEARN_RATE = 0.2
LOSS_SCALE = 32.0
ADA_EPS = 1e-06


SLOTS = 128
VMEM_BYTES = 48 * 1024 * 1024


def matmul(left, right):
    return jnp.dot(left, right, preferred_element_type=jnp.float32)


def transposed_dot(left, right):
    return lax.dot_general(
        left, right, (((0,), (0,)), ((), ())), preferred_element_type=jnp.float32
    )


def rows_dot(left, right):
    return lax.dot_general(
        left, right, (((1,), (1,)), ((), ())), preferred_element_type=jnp.float32
    )


def kernel_call(kernel, out_shape, cost, scratch=(), flags=0, operands=0):
    flops, moved = cost
    smem = pl.BlockSpec(memory_space=pltpu.SMEM)
    vmem = pl.BlockSpec(memory_space=pltpu.VMEM)
    return pl.pallas_call(
        kernel,
        in_specs=[smem] * flags + [vmem] * operands,
        out_shape=out_shape,
        scratch_shapes=scratch,
        compiler_params=pltpu.CompilerParams(vmem_limit_bytes=VMEM_BYTES),
        cost_estimate=pl.CostEstimate(flops=flops, bytes_accessed=moved, transcendentals=0),
    )


def split_ids(ids):
    shifted = ids + 1
    high = lax.shift_right_logical(shifted, 5).astype(jnp.float32).astype(jnp.bfloat16)
    low = (shifted & 31).astype(jnp.float32).astype(jnp.bfloat16)
    return high, low


def lookup_choice():
    shape = (HOT * SLOTS, HOT * SLOTS)
    row = lax.broadcasted_iota(jnp.int32, shape, 0)
    column = lax.broadcasted_iota(jnp.int32, shape, 1)
    wanted = (row & (SLOTS - 1)) * HOT + lax.shift_right_logical(row, 7)
    return jnp.where(wanted == column, 1.0, 0.0).astype(jnp.bfloat16)


def joined(digits):
    high, low = digits
    return (high * 32.0 + low - 1.0).astype(jnp.int32)


def ones_where(mask):
    return jnp.where(mask, jnp.asarray(1, jnp.bfloat16), jnp.asarray(0, jnp.bfloat16))


def pool_kernel(offset, swap_ref, ids_ref, first_ref, second_ref, out_ref, counts_ref):
    blocks = ids_ref.shape[0]
    half = first_ref.shape[0]
    high, low = split_ids(ids_ref[:, offset : offset + HOT * SLOTS])
    choice = lookup_choice()
    columns = joined((rows_dot(choice, high), rows_dot(choice, low))).astype(jnp.int16)
    position = lax.broadcasted_iota(jnp.int32, (SLOTS, 2 * half), 1)
    shifted = position + swap_ref[0] * half
    position = jnp.where(shifted >= 2 * half, shifted - 2 * half, shifted).astype(jnp.int16)
    for block in range(blocks):
        counts = None
        for lookup in range(HOT):
            column = columns[lookup * SLOTS : (lookup + 1) * SLOTS, block : block + 1]
            found = ones_where(column == position)
            counts = found if counts is None else counts + found
        counts_ref[block * SLOTS : (block + 1) * SLOTS, :] = counts
    sums = matmul(counts_ref[:, :half], first_ref[...])
    sums = sums + matmul(counts_ref[:, half:], second_ref[...])
    out_ref[...] = sums.astype(jnp.bfloat16)


def pool_lookups(ids, offset, swap, first, second):
    blocks = ids.shape[0]
    half, width = first.shape
    slots = blocks * SLOTS
    return kernel_call(
        functools.partial(pool_kernel, offset),
        jax.ShapeDtypeStruct((slots, width), jnp.bfloat16),
        (4 * slots * half * width, 4 * half * width + 2 * slots * width),
        [pltpu.VMEM((slots, 2 * half), jnp.bfloat16)],
        flags=1,
        operands=3,
    )(swap, ids, first, second)


def counts_kernel(ids_ref, out_ref):
    blocks = ids_ref.shape[0]
    row_dev = out_ref.shape[0]
    tile = 64
    high, low = split_ids(ids_ref[...])
    choice = lookup_choice()
    lines = joined((rows_dot(high, choice), rows_dot(low, choice)))
    position = lax.broadcasted_iota(jnp.int32, (tile, SLOTS), 0).astype(jnp.int16)
    for block in range(blocks):
        spread = []
        for lookup in range(HOT):
            line = lines[block : block + 1, lookup * SLOTS : (lookup + 1) * SLOTS]
            spread.append(jnp.broadcast_to(line, (tile, SLOTS)).astype(jnp.int16))
        for start in range(0, row_dev, tile):
            counts = None
            for lookup in range(HOT):
                found = ones_where(spread[lookup] - jnp.asarray(start, jnp.int16) == position)
                counts = found if counts is None else counts + found
            out_ref[start : start + tile, block * SLOTS : (block + 1) * SLOTS] = counts


def lookup_counts(ids, row_dev):
    slot_count = ids.size // HOT
    return kernel_call(
        counts_kernel,
        jax.ShapeDtypeStruct((row_dev, slot_count), jnp.bfloat16),
        (8 * row_dev * slot_count, 2 * row_dev * slot_count),
        operands=1,
    )(ids)


def diagonal(size):
    row = lax.broadcasted_iota(jnp.int32, (size, size), 0)
    return row == lax.broadcasted_iota(jnp.int32, (size, size), 1)


def as_column(line):
    return jnp.sum(jnp.where(diagonal(line.shape[1]), line, 0.0), axis=1, keepdims=True)


def as_line(column):
    return jnp.sum(jnp.where(diagonal(column.shape[0]), column, 0.0), axis=0, keepdims=True)


def dense_kernel(
    swap_ref,
    goals_ref,
    near_ref,
    far_ref,
    down_a_ref,
    down_b_ref,
    up_a_ref,
    up_b_ref,
    bias_ref,
    weight_ref,
    target_ref,
    logits_ref,
    grads_ref,
    kept_ref,
    sent_ref,
    place_ref,
    wide_ref,
    cross_ref,
    down_ref,
    up_ref,
):
    samples = target_ref.shape[1]
    width, rank = down_ref.shape
    emb = width // FEAT
    slots = near_ref.shape[0]
    half = width // 2
    swapped = swap_ref[0] == 1
    down_ref[:half, :] = jnp.where(swapped, down_b_ref[...], down_a_ref[...])
    down_ref[half:, :] = jnp.where(swapped, down_a_ref[...], down_b_ref[...])
    up_ref[:half, :] = jnp.where(swapped, up_b_ref[...], up_a_ref[...])
    up_ref[half:, :] = jnp.where(swapped, up_a_ref[...], up_b_ref[...])
    features = [slice(f * emb, (f + 1) * emb) for f in range(FEAT)]
    chunk = 512
    first_bag = lax.broadcasted_iota(jnp.int32, (samples, chunk), 0) * FEAT
    for start in range(0, goals_ref.shape[1], chunk):
        line = goals_ref[:, start : start + chunk]
        nth = (jnp.broadcast_to(line, (samples, chunk)) - first_bag).astype(jnp.int16)
        for f in range(FEAT):
            place_ref[f * samples : (f + 1) * samples, start : start + chunk] = ones_where(
                nth == jnp.asarray(f, jnp.int16)
            )
    pooled = matmul(place_ref[:, :slots], near_ref[...])
    pooled = (pooled + matmul(place_ref[:, slots:], far_ref[...])).astype(jnp.bfloat16)
    for f, part in enumerate(features):
        wide_ref[:, part] = pooled[f * samples : (f + 1) * samples, :]
    hidden = matmul(wide_ref[...], down_ref[...]).astype(jnp.bfloat16)
    summed = jnp.zeros((samples, emb), jnp.float32)
    for part in features:
        shifted = rows_dot(hidden, up_ref[part, :]) + bias_ref[:, part]
        cross_ref[:, part] = shifted
        feats = wide_ref[:, part].astype(jnp.float32)
        summed = summed + (feats * shifted + feats) * weight_ref[:, part].astype(jnp.float32)
    logits = jnp.sum(summed, axis=1, keepdims=True)
    logits_ref[...] = as_line(logits)
    dlogit = LOSS_SCALE * (jax.nn.sigmoid(logits) - as_column(target_ref[...]))
    dcross = []
    for part in features:
        dmixed = dlogit * weight_ref[:, part].astype(jnp.float32)
        dcross.append((dmixed * wide_ref[:, part].astype(jnp.float32)).astype(jnp.bfloat16))
    dhidden = matmul(jnp.concatenate(dcross, axis=1), up_ref[...]).astype(jnp.bfloat16)
    for f, part in enumerate(features):
        dmixed = dlogit * weight_ref[:, part].astype(jnp.float32)
        back_term = rows_dot(dhidden, down_ref[part, :])
        grads = dmixed * (cross_ref[:, part] + 1.0) + back_term
        grads_ref[f * samples : (f + 1) * samples, :] = grads.astype(jnp.bfloat16)
    for f, part in enumerate(features):
        down_term = transposed_dot(wide_ref[:, part], dhidden).astype(jnp.bfloat16)
        up_term = transposed_dot(dcross[f], hidden).astype(jnp.bfloat16)
        spot = slice((f * emb) % half, (f * emb) % half + emb)
        keep = swapped if f * emb >= half else jnp.logical_not(swapped)

        @pl.when(keep)
        def _():
            kept_ref[spot, :rank] = down_term
            kept_ref[spot, rank:] = up_term

        @pl.when(jnp.logical_not(keep))
        def _():
            sent_ref[spot, :rank] = down_term
            sent_ref[spot, rank:] = up_term


def dense_step(swap, goals, near, far, downs, ups, bias, weight, target):
    samples = target.shape[0]
    slots, emb = near.shape
    width, rank = 2 * downs[0].shape[0], downs[0].shape[1]
    flops = 4 * slots * samples * width + 12 * samples * width * rank
    logits, grads, kept, sent = kernel_call(
        dense_kernel,
        (
            jax.ShapeDtypeStruct((1, samples), jnp.float32),
            jax.ShapeDtypeStruct((samples * FEAT, emb), jnp.bfloat16),
            jax.ShapeDtypeStruct((width // 2, 2 * rank), jnp.bfloat16),
            jax.ShapeDtypeStruct((width // 2, 2 * rank), jnp.bfloat16),
        ),
        (flops, 4 * near.size + 8 * width * rank),
        [
            pltpu.VMEM((samples * FEAT, 2 * slots), jnp.bfloat16),
            pltpu.VMEM((samples, width), jnp.bfloat16),
            pltpu.VMEM((samples, width), jnp.float32),
            pltpu.VMEM((width, rank), jnp.bfloat16),
            pltpu.VMEM((width, rank), jnp.bfloat16),
        ],
        flags=1,
        operands=10,
    )(
        swap,
        goals.reshape(1, 2 * slots),
        near,
        far,
        *downs,
        *ups,
        bias.reshape(1, width),
        weight.reshape(1, width),
        target.reshape(1, samples),
    )
    return logits.reshape(samples), grads, kept, sent


def return_kernel(goals_ref, grads_ref, out_ref, pick_ref):
    blocks = goals_ref.shape[0]
    bags = grads_ref.shape[0]
    samples = bags // FEAT
    high, low = split_ids(goals_ref[...])
    unit = ones_where(diagonal(SLOTS))
    columns = joined((rows_dot(unit, high), rows_dot(unit, low))).astype(jnp.int16)
    place = lax.broadcasted_iota(jnp.int32, (SLOTS, bags), 1)
    order = ((place % samples) * FEAT + place // samples).astype(jnp.int16)
    for block in range(blocks):
        pick_ref[block * SLOTS : (block + 1) * SLOTS, :] = ones_where(
            columns[:, block : block + 1] == order
        )
    out_ref[...] = matmul(pick_ref[...], grads_ref[...]).astype(jnp.bfloat16)


def return_grads(goals, grads):
    bags, emb = grads.shape
    slot_count = goals.size
    return kernel_call(
        return_kernel,
        jax.ShapeDtypeStruct((slot_count, emb), jnp.bfloat16),
        (2 * slot_count * bags * emb, 2 * grads.size + 2 * slot_count * emb),
        [pltpu.VMEM((slot_count, bags), jnp.bfloat16)],
        operands=2,
    )(goals.reshape(slot_count // SLOTS, SLOTS), grads)


def update_kernel(share_ref, rows_ref, mine_ref, other_ref, accum_ref, rows_out_ref, accum_out_ref):
    chunks = accum_ref.shape[0]
    per_share = accum_out_ref.shape[0]
    for chunk in range(chunks):
        part = slice(chunk * SLOTS, (chunk + 1) * SLOTS)
        row_grad = mine_ref[part, :].astype(jnp.float32) + other_ref[part, :].astype(jnp.float32)
        squares = jnp.mean(row_grad * row_grad, axis=1, keepdims=True)
        accum = as_column(accum_ref[chunk : chunk + 1, :]) + squares
        step = LEARN_RATE * row_grad * lax.rsqrt(accum + ADA_EPS)
        rows_out_ref[part, :] = (rows_ref[part, :].astype(jnp.float32) - step).astype(jnp.bfloat16)

        @pl.when(share_ref[0] == chunk // per_share)
        def _():
            accum_out_ref[chunk % per_share : chunk % per_share + 1, :] = as_line(accum)


def update_rows(share, rows, mine, other, accum, narrows):
    row_dev, emb = rows.shape
    chunks = row_dev // SLOTS
    new_rows, new_accum = kernel_call(
        update_kernel,
        (
            jax.ShapeDtypeStruct((row_dev, emb), jnp.bfloat16),
            jax.ShapeDtypeStruct((chunks // narrows, SLOTS), jnp.float32),
        ),
        (8 * rows.size, 8 * rows.size),
        flags=1,
        operands=4,
    )(share, rows, mine, other, accum.reshape(chunks, SLOTS))
    return new_rows, new_accum.reshape(row_dev // narrows)


def group_levels(size):
    levels = []
    stride = 1
    while size % 4 == 0:
        levels.append((stride, 4))
        stride, size = stride * 4, size // 4
    if size > 1:
        levels.append((stride, size))
    return levels


def partner_index(index, stride, group, step):
    place = (index // stride) % group
    if group & (group - 1) == 0:
        other = place ^ step
    else:
        other = (place + step) % group
    return index + (other - place) * stride


def sent_from(axis, stride, group, step):
    size = lax.axis_size(axis)
    return [(partner_index(i, stride, group, step), i) for i in range(size)]


def scatter_sum(blocks, axis, levels):
    index = lax.axis_index(axis)
    for stride, group in levels:
        rows = blocks.shape[0] // group
        place = (index // stride) % group
        total = lax.dynamic_slice_in_dim(blocks, place * rows, rows, 0).astype(jnp.float32)
        for step in range(1, group):
            pairs = sent_from(axis, stride, group, step)
            if group & (group - 1) == 0:
                goal = place ^ step
            else:
                goal = (place + group - step) % group
            outgoing = lax.dynamic_slice_in_dim(blocks, goal * rows, rows, 0)
            total = total + lax.ppermute(outgoing, axis, pairs).astype(jnp.float32)
        blocks = total.astype(jnp.bfloat16)
    return blocks


def gather_blocks(block, axis, levels):
    index = lax.axis_index(axis)
    for stride, group in reversed(levels):
        rows = block.shape[0]
        place = (index // stride) % group
        whole = jnp.zeros((group * rows,) + block.shape[1:], block.dtype)
        whole = lax.dynamic_update_slice_in_dim(whole, block, place * rows, 0)
        for step in range(1, group):
            origin = partner_index(index, stride, group, step)
            came = lax.ppermute(block, axis, sent_from(axis, stride, group, step))
            spot = (origin // stride) % group
            whole = lax.dynamic_update_slice_in_dim(whole, came, spot * rows, 0)
        block = whole
    return block


def local(
    table_rows, accum, factor_down, factor_up, cross_bias, out_weight, target, bag_rows, slot_target
):
    tables = lax.axis_size("table")
    narrows = lax.axis_size("narrow")
    row_dev, emb_width = table_rows.shape
    pools_per = slot_target.shape[1]
    samples = target.shape[0]
    bag_count = samples * FEAT
    slot_count = tables * pools_per
    narrow_levels = group_levels(narrows)
    table_levels = group_levels(tables)
    table_index = lax.axis_index("table")
    narrow_index = lax.axis_index("narrow")
    near_count = tables // 2
    far_half = table_index // near_count
    halves = [list(range(near_count)), list(range(near_count, tables))]
    across = [(i, (i + near_count) % tables) for i in range(tables)]
    paired = narrows == 2
    swap = (narrow_index if paired else narrow_index * 0).reshape(1)

    def near_first(rows):
        return jnp.where(far_half == 0, rows, jnp.roll(rows, near_count, axis=0))

    def both_halves(block):
        if paired:
            return block, lax.ppermute(block, "narrow", sent_from("narrow", 1, 2, 1))
        whole = gather_blocks(block, "narrow", narrow_levels)
        return tuple(jnp.split(whole, 2, axis=0))

    share_rows = row_dev // narrows
    own_share = lax.dynamic_slice_in_dim(table_rows, narrow_index * share_rows, share_rows, 0)
    far_rows = both_halves(lax.ppermute(own_share, "table", across))
    downs = both_halves(factor_down)
    ups = both_halves(factor_up)

    per_window = bag_rows.shape[1]
    asked = near_first(bag_rows)
    asked = jnp.concatenate([asked[:near_count], asked[near_count:]], axis=1)
    asked = lax.all_to_all(
        asked, "table", split_axis=0, concat_axis=0, tiled=True, axis_index_groups=halves
    )
    near_ids, far_ids = asked[:, :per_window], asked[:, per_window:]

    def pooled_for(part, plain_ids, flag, rows):
        if per_window == SLOTS * HOT:
            sums = pool_lookups(asked, part * per_window, flag, *rows)
        else:
            sums = pool_lookups(plain_ids.reshape(-1, SLOTS * HOT), 0, flag, *rows)
        return lax.all_to_all(
            sums.reshape(near_count, pools_per, emb_width),
            "table",
            split_axis=0,
            concat_axis=0,
            tiled=True,
            axis_index_groups=halves,
        ).reshape(slot_count // 2, emb_width)

    own_rows = tuple(jnp.split(table_rows, 2, axis=0))
    near = pooled_for(0, near_ids, swap * 0, own_rows)
    far = pooled_for(1, far_ids, swap, far_rows)
    other_ids = lax.ppermute(far_ids, "table", across)
    all_ids = near_first(jnp.concatenate([near_ids, other_ids], axis=0))
    counts = lookup_counts(all_ids.reshape(-1, SLOTS * HOT), row_dev)
    near, far, counts = lax.optimization_barrier((near, far, counts))
    logits, bag_grads, kept, sent = dense_step(
        swap, near_first(slot_target), near, far, downs, ups, cross_bias, out_weight, target
    )
    if paired:
        came = lax.ppermute(sent, "narrow", sent_from("narrow", 1, 2, 1))
        narrow_sum = (kept.astype(jnp.float32) + came.astype(jnp.float32)).astype(jnp.bfloat16)
    else:
        narrow_sum = scatter_sum(jnp.concatenate([kept, sent], axis=0), "narrow", narrow_levels)
    slot_grads = return_grads(slot_target, bag_grads)
    returned = lax.all_to_all(
        slot_grads.reshape(tables, pools_per, emb_width),
        "table",
        split_axis=0,
        concat_axis=0,
        tiled=True,
    ).reshape(slot_count, emb_width)
    table_sum = scatter_sum(narrow_sum, "table", table_levels)
    sent_grad = matmul(counts, returned).astype(jnp.bfloat16)
    table_sum, sent_grad = lax.optimization_barrier((table_sum, sent_grad))
    grand_total = gather_blocks(table_sum, "table", table_levels).astype(jnp.float32)
    batch_all = samples * tables * narrows
    grand_total = grand_total * (1.0 / math.sqrt(batch_all))
    rank_size = factor_down.shape[1]
    down_grad = grand_total[:, :rank_size]
    up_grad = grand_total[:, rank_size:]
    if paired:
        mine = sent_grad
        other = lax.ppermute(sent_grad, "narrow", sent_from("narrow", 1, 2, 1))
    else:
        share = scatter_sum(sent_grad, "narrow", narrow_levels)
        mine = gather_blocks(share, "narrow", narrow_levels)
        other = jnp.zeros_like(mine)
    new_rows, new_accum = update_rows(
        narrow_index.reshape(1), table_rows, mine, other, accum, narrows
    )
    return (logits, down_grad, up_grad, new_rows, new_accum)


def solution(mesh):
    in_specs = (
        P("table", None),
        P("table"),
        P("narrow", None),
        P("narrow", None),
        P(),
        P(),
        P(("table", "narrow")),
        P(("table", "narrow"), None),
        P(("table", "narrow"), None),
    )
    out_specs = (
        P(("table", "narrow")),
        P("narrow", None),
        P("narrow", None),
        P("table", None),
        P(("table", "narrow")),
    )
    return jax.shard_map(local, mesh=mesh, in_specs=in_specs, out_specs=out_specs, check_vma=False)
```

time: 139 us -> 141 us (1.014)
  starting transfers between devices: 26.6 us -> 45.2 us
  blocking collectives: 15.5 us -> 0 us
  waiting for transfers between devices: 47.9 us -> 57.8 us
  Pallas kernels: 25 us -> 19.3 us
  other arithmetic: 7.13 us -> 2.75 us
  local copies, waits for them, and re-layouts: 11.8 us -> 10.2 us
    all_to_all x1 -> x0, blocking collectives: 15.5 us -> none  [local(): lax.all_to_all(bag_rows, 'table', split_axis=0, concat_axis=0, tiled=True)]
    all_to_all x1 -> x3, starting transfers between devices: 3.66 us -> 16.9 us  [the longest x2 10.7 us: pooled_for(): lax.all_to_all(sums.reshape(near_count, pools_per, emb_width), 'table', s...]
    ppermute x0 -> x6, waiting for transfers between devices: none -> 13.1 us  [the longest x1 8.33 us: local(): far_rows = both_halves(lax.ppermute(own_share, 'table', across))]
    all_to_all x1 -> x3, waiting for transfers between devices: 12.9 us -> 4.54 us  [the longest x1 4.54 us: local(): lax.all_to_all(asked, 'table', split_axis=0, concat_axis=0, tiled=True, a...]
    pallas_call x1, Pallas kernels: 9.16 us -> 2.77 us  [lookup_counts(): kernel_call(counts_kernel, jax.ShapeDtypeStruct((row_dev, slot_count), jn...]
    ppermute x7 -> x6, waiting for transfers between devices: 21.5 us -> 27.2 us  [scatter_sum(): total = total + lax.ppermute(outgoing, axis, pairs).astype(jnp.float32)]
    ppermute x0 -> x6, starting transfers between devices: none -> 5.02 us  [the longest x1 2.55 us: local(): other_ids = lax.ppermute(far_ids, 'table', across)]
    convert_element_type x2 -> x1, other arithmetic: 5.15 us -> 1.51 us  [local(): (kept.astype(jnp.float32) + came.astype(jnp.float32)).astype(jnp.bfloat16)]
  transfers between devices with their start and end apart: 18 -> 23, of which waited for: 8 -> 13; matrix products, arithmetic and copies ran while one was open for 10% -> 4% of each run, Pallas kernels for 7% -> 5%
where the time goes in v3:
time: 141 us; the launch traced here: 140 us
  waiting for transfers between devices  57.8 us (41%)
  starting transfers between devices  45.2 us (32%)
  Pallas kernels  19.3 us (14%)
  local copies, waits for them, and re-layouts  10.2 us (7%)
  matrix products  3.73 us (3%)
  other arithmetic  2.75 us (2%)
    ppermute x6, waiting for transfers between devices, scatter_sum(): total = total + lax.ppermute(outgoing, axis, pairs).astype(jnp.float32)  27.2 us
    ppermute x6, waiting for transfers between devices, gather_blocks(): came = lax.ppermute(block, axis, sent_from(axis, stride, group, step))  12.9 us
    all_to_all x2, starting transfers between devices, pooled_for(): lax.all_to_all(sums.reshape(near_count, pools_per, emb_width), 'table', s...  10.7 us
    ppermute x1, waiting for transfers between devices, local(): far_rows = both_halves(lax.ppermute(own_share, 'table', across))  8.33 us
    ppermute x6, starting transfers between devices, gather_blocks(): came = lax.ppermute(block, axis, sent_from(axis, stride, group, step))  8 us
    all_to_all x1, starting transfers between devices, local(): lax.all_to_all(slot_grads.reshape(tables, pools_per, emb_width), 'table',...  7.93 us
    pallas_call x1, Pallas kernels, dense_step(): kernel_call(dense_kernel, (jax.ShapeDtypeStruct((1, samples), jnp.float32...  7.89 us
    ppermute x6, starting transfers between devices, scatter_sum(): total = total + lax.ppermute(outgoing, axis, pairs).astype(jnp.float32)  7.38 us
  transfers between devices with their start and end apart: 23, of which 13 were waited for; matrix products, arithmetic and copies ran while one was open for 4% of the time, Pallas kernels for 5%

profile of v3, /device:TPU:0, one launch (start us, length us, event | category | flops | bytes accessed | tf_op | source)
XLA Modules:
  0.0 140.0 jit_solution(11459791129580663582)
XLA Ops:
  0.6 0.7 fusion.3
  1.4 0.8 add_select_fusion
  2.2 0.6 copy.14
  2.8 6.2 %all-to-all-start = ((s32[8,1,1024]{2,1,0:T(1,128)}), s32[8,1,1024]{2,1,0:T(1,128)S(1)}, u32[]{:S(2)}, u32[]{:S(2)}) async-start(s32[8,1,1024]{2,1,0:T(1,128)} %copy.14), calls=%async_computation | async-start | bytes 65536 | tf_op jit(solution)/shard_map/all_to_all | solution.py:435
  9.0 1.2 constant_dynamic-slice_fusion.6
  10.2 4.5 %all-to-all-done = s32[8,1,1024]{2,1,0:T(1,128)S(1)} async-done(((s32[8,1,1024]{2,1,0:T(1,128)}), s32[8,1,1024]{2,1,0:T(1,128)S(1)}, u32[]{:S(2)}, u32[]{:S(2)}) %all-to-all-start) | async-done | bytes 32800 | tf_op jit(solution)/shard_map/all_to_all | solution.py:435
  14.7 2.2 %shard_map.128 = bf16[1024,256]{1,0:T(8,128)(2,1)} custom-call(s32[1]{0:T(128)} %constant.164.clone.1.swap_ref, s32[8,1024]{1,0:T(8,128)S(1)} %bitcast.22, bf16[512,256]{1,0:T(8,128)(2,1)S(1)} %get-tuple-element.34.first_ref, bf16[512,256]{1,0:T(8,128)(2,1)S(1)} %get-tuple-element.33.second_ref), custom_call_target="tpu_custom_call" | custom-call | flops 536870912 | bytes 1048576 | tf_op jit(solution)/shard_map/pallas_call | solution.py:103
  16.9 3.6 %all-to-all-start.1 = ((bf16[8,128,256]{2,1,0:T(8,128)(2,1)}), bf16[8,128,256]{2,1,0:T(8,128)(2,1)S(1)}, u32[]{:S(2)}, u32[]{:S(2)}) async-start(bf16[8,128,256]{2,1,0:T(8,128)(2,1)} %bitcast.3), calls=%async_computation.1 | async-start | bytes 1048576 | tf_op jit(solution)/shard_map/all_to_all | solution.py:445
  20.5 1.9 %collective-permute-start = (bf16[512,256]{1,0:T(8,128)(2,1)S(1)}, bf16[512,256]{1,0:T(8,128)(2,1)S(1)}, u32[]{:S(2)}, u32[]{:S(2)}) collective-permute-start(bf16[512,256]{1,0:T(8,128)(2,1)S(1)} %get-tuple-element.32), channel_id=1, source_target_pairs={{0,16},{2,18},{4,20},{6,22},{8,24},{10,26},{12,28},{14,30},{16,0},... | collective-permute-start | bytes 786440 | tf_op jit(solution)/shard_map/ppermute | solution.py:428
  22.4 8.3 %collective-permute-done.first_ref = bf16[512,256]{1,0:T(8,128)(2,1)S(1)} collective-permute-done((bf16[512,256]{1,0:T(8,128)(2,1)S(1)}, bf16[512,256]{1,0:T(8,128)(2,1)S(1)}, u32[]{:S(2)}, u32[]{:S(2)}) %collective-permute-start) | collective-permute-done | bytes 262176 | tf_op jit(solution)/shard_map/ppermute | solution.py:428
  30.8 1.5 %collective-permute-done.1.second_ref = bf16[512,256]{1,0:T(8,128)(2,1)S(1)} collective-permute-done((bf16[512,256]{1,0:T(8,128)(2,1)S(1)}, bf16[512,256]{1,0:T(8,128)(2,1)S(1)}, u32[]{:S(2)}, u32[]{:S(2)}) %collective-permute-start.1) | collective-permute-done | bytes 262176 | tf_op jit(solution)/shard_map/ppermute | solution.py:422
  32.3 2.2 %shard_map.129 = bf16[1024,256]{1,0:T(8,128)(2,1)} custom-call(s32[1]{0:T(128)} %bitcast.swap_ref.share_ref, s32[8,1024]{1,0:T(8,128)S(1)} %bitcast.23, bf16[512,256]{1,0:T(8,128)(2,1)S(1)} %collective-permute-done.first_ref, bf16[512,256]{1,0:T(8,128)(2,1)S(1)} %collective-permute-done.1.second_ref), custom_call_target="tpu_custom_call" | custom-call | flops 536870912 | bytes 1048576 | tf_op jit(solution)/shard_map/pallas_call | solution.py:103
  34.5 7.0 %all-to-all-start.2 = ((bf16[8,128,256]{2,1,0:T(8,128)(2,1)}), bf16[8,128,256]{2,1,0:T(8,128)(2,1)S(1)}, u32[]{:S(2)}, u32[]{:S(2)}) async-start(bf16[8,128,256]{2,1,0:T(8,128)(2,1)} %bitcast.5), calls=%async_computation.2 | async-start | bytes 1048576 | tf_op jit(solution)/shard_map/all_to_all | solution.py:445
  41.6 0.5 collective-permute-start.4
  42.1 2.5 %collective-permute-start.2 = (s32[8,512]{1,0:T(8,128)S(1)}, s32[8,512]{1,0:T(8,128)S(1)}, u32[]{:S(2)}, u32[]{:S(2)}) collective-permute-start(s32[8,512]{1,0:T(8,128)S(1)} %get-tuple-element.39), channel_id=1, source_target_pairs={{0,16},{2,18},{4,20},{6,22},{8,24},{10,26},{12,28},{14,30},{16,0},... | collective-permute-start | bytes 49160 | tf_op jit(solution)/shard_map/ppermute | solution.py:457
  44.7 3.3 %collective-permute-done.2 = s32[8,512]{1,0:T(8,128)S(1)} collective-permute-done((s32[8,512]{1,0:T(8,128)S(1)}, s32[8,512]{1,0:T(8,128)S(1)}, u32[]{:S(2)}, u32[]{:S(2)}) %collective-permute-start.2) | collective-permute-done | bytes 16416 | tf_op jit(solution)/shard_map/ppermute | solution.py:457
  48.0 2.8 %shard_map.130 = bf16[1024,2048]{1,0:T(8,128)(2,1)S(1)} custom-call(s32[16,512]{1,0:T(8,128)S(1)} %add_select_fusion.1.ids_ref), custom_call_target="tpu_custom_call" | custom-call | flops 16777216 | bytes 4194304 | tf_op jit(solution)/shard_map/pallas_call | solution.py:136
  50.7 1.9 %copy-done = bf16[1024,2048]{1,0:T(8,128)(2,1)} copy-done((bf16[1024,2048]{1,0:T(8,128)(2,1)}, bf16[1024,2048]{1,0:T(8,128)(2,1)S(1)}, u32[]{:S(2)}) %copy-start) | copy-done | bytes 4194328
  52.7 0.8 copy-done.8
  53.5 1.0 copy-done.5
  54.6 1.0 copy-done.7
  55.6 1.0 copy-done.9
  56.6 7.9 %shard_map.131 = (f32[1,128]{1,0:T(1,128)}, bf16[1024,256]{1,0:T(8,128)(2,1)S(1)}, bf16[1024,512]{1,0:T(8,128)(2,1)S(1)}, bf16[1024,512]{1,0:T(8,128)(2,1)S(1)}) custom-call(s32[1]{0:T(128)} %bitcast.swap_ref.share_ref, s32[1,2048]{1,0:T(1,128)S(1)} %bitcast.25, bf16[1024,256]{1,0:T(8,128)(2,1)S(1)} %bitcast.20, bf16[1024,256]{1,0:T(8,128)(2,1)S(1)} %bitcast.21, ...), custom_call_target="tpu_custom_call" | custom-call | flops 1879048192 | bytes 5242880 | tf_op jit(solution)/shard_map/pallas_call | solution.py:245
  64.5 2.4 %shard_map.132 = bf16[2048,256]{1,0:T(8,128)(2,1)} custom-call(s32[16,128]{1,0:T(8,128)S(1)} %copy-done.2, bf16[1024,256]{1,0:T(8,128)(2,1)S(1)} %get-tuple-element.22.grads_ref), custom_call_target="tpu_custom_call" | custom-call | flops 1073741824 | bytes 1572864 | tf_op jit(solution)/shard_map/pallas_call | solution.py:296
  66.9 7.9 %all-to-all-start.3 = ((bf16[16,128,256]{2,1,0:T(8,128)(2,1)}), bf16[16,128,256]{2,1,0:T(8,128)(2,1)}, u32[]{:S(2)}, u32[]{:S(2)}) async-start(bf16[16,128,256]{2,1,0:T(8,128)(2,1)} %bitcast.10), calls=%async_computation.3 | async-start | bytes 2097152 | tf_op jit(solution)/shard_map/all_to_all | solution.py:470
  74.9 1.5 %add_convert_fusion = bf16[1024,512]{1,0:T(8,128)(2,1)S(1)} fusion(bf16[1024,512]{1,0:T(8,128)(2,1)} %collective-permute-done.5, bf16[1024,512]{1,0:T(8,128)(2,1)S(1)} %get-tuple-element.19), kind=kLoop, calls=%fused_computation.1 | loop fusion | flops 2097152 | bytes 3145728 | tf_op jit(solution)/shard_map/convert_element_type | solution.py:466
  76.5 1.9 %collective-permute-start.6 = (bf16[256,512]{1,0:T(8,128)(2,1)S(1)}, bf16[256,512]{1,0:T(8,128)(2,1)S(1)}, u32[]{:S(2)}, u32[]{:S(2)}) collective-permute-start(bf16[256,512]{1,0:T(8,128)(2,1)S(1)} %get-tuple-element.29), channel_id=1, source_target_pairs={{2,0},{0,2},{6,4},{4,6},{10,8},{8,10},{14,12},{12,14},{18,16},{16,... | collective-permute-start | bytes 786440 | tf_op jit(solution)/shard_map/ppermute | solution.py:375
  78.4 1.5 %collective-permute-start.7 = (bf16[256,512]{1,0:T(8,128)(2,1)S(1)}, bf16[256,512]{1,0:T(8,128)(2,1)S(1)}, u32[]{:S(2)}, u32[]{:S(2)}) collective-permute-start(bf16[256,512]{1,0:T(8,128)(2,1)S(1)} %get-tuple-element.31), channel_id=1, source_target_pairs={{4,0},{6,2},{0,4},{2,6},{12,8},{14,10},{8,12},{10,14},{20,16},{22,... | collective-permute-start | bytes 786440 | tf_op jit(solution)/shard_map/ppermute | solution.py:375
  80.1 8.2 %collective-permute-done.6 = bf16[256,512]{1,0:T(8,128)(2,1)S(1)} collective-permute-done((bf16[256,512]{1,0:T(8,128)(2,1)S(1)}, bf16[256,512]{1,0:T(8,128)(2,1)S(1)}, u32[]{:S(2)}, u32[]{:S(2)}) %collective-permute-start.6) | collective-permute-done | bytes 262176 | tf_op jit(solution)/shard_map/ppermute | solution.py:375
  88.3 8.6 %collective-permute-done.7 = bf16[256,512]{1,0:T(8,128)(2,1)S(1)} collective-permute-done((bf16[256,512]{1,0:T(8,128)(2,1)S(1)}, bf16[256,512]{1,0:T(8,128)(2,1)S(1)}, u32[]{:S(2)}, u32[]{:S(2)}) %collective-permute-start.7) | collective-permute-done | bytes 262176 | tf_op jit(solution)/shard_map/ppermute | solution.py:375
  96.9 4.9 %collective-permute-done.8 = bf16[256,512]{1,0:T(8,128)(2,1)S(1)} collective-permute-done((bf16[256,512]{1,0:T(8,128)(2,1)S(1)}, bf16[256,512]{1,0:T(8,128)(2,1)S(1)}, u32[]{:S(2)}, u32[]{:S(2)}) %collective-permute-start.8) | collective-permute-done | bytes 262176 | tf_op jit(solution)/shard_map/ppermute | solution.py:375
  102.0 3.2 %collective-permute-start.10 = (bf16[64,512]{1,0:T(8,128)(2,1)S(1)}, bf16[64,512]{1,0:T(8,128)(2,1)S(1)}, u32[]{:S(2)}, u32[]{:S(2)}) collective-permute-start(bf16[64,512]{1,0:T(8,128)(2,1)S(1)} %get-tuple-element.37), channel_id=1, source_target_pairs={{16,0},{18,2},{20,4},{22,6},{24,8},{26,10},{28,12},{30,14},{0,16},... | collective-permute-start | bytes 196616 | tf_op jit(solution)/shard_map/ppermute | solution.py:375
  105.2 0.6 collective-permute-start.9
  105.8 2.4 %collective-permute-done.10 = bf16[64,512]{1,0:T(8,128)(2,1)S(1)} collective-permute-done((bf16[64,512]{1,0:T(8,128)(2,1)S(1)}, bf16[64,512]{1,0:T(8,128)(2,1)S(1)}, u32[]{:S(2)}, u32[]{:S(2)}) %collective-permute-start.10) | collective-permute-done | bytes 65568 | tf_op jit(solution)/shard_map/ppermute | solution.py:375
  108.2 3.0 %collective-permute-done.11 = bf16[64,512]{1,0:T(8,128)(2,1)S(1)} collective-permute-done((bf16[64,512]{1,0:T(8,128)(2,1)S(1)}, bf16[64,512]{1,0:T(8,128)(2,1)S(1)}, u32[]{:S(2)}, u32[]{:S(2)}) %collective-permute-start.11) | collective-permute-done | bytes 65568 | tf_op jit(solution)/shard_map/ppermute | solution.py:375
  111.3 3.7 %convolution_convert_fusion.mine_ref = bf16[1024,256]{1,0:T(8,128)(2,1)S(1)} fusion(bf16[1024,2048]{1,0:T(8,128)(2,1)} %copy-done, bf16[2048,256]{1,0:T(8,128)(2,1)} %bitcast.11), kind=kOutput, calls=%fused_computation.2 | convolution fusion | flops 1074003968 | bytes 5767168 | tf_op jit(solution)/shard_map/dot_general | solution.py:25
  115.1 2.6 %collective-permute-start.13 = (bf16[64,512]{1,0:T(8,128)(2,1)S(1)}, bf16[64,512]{1,0:T(8,128)(2,1)S(1)}, u32[]{:S(2)}, u32[]{:S(2)}) collective-permute-start(bf16[64,512]{1,0:T(8,128)(2,1)S(1)} %add_convert_fusion.2), channel_id=1, source_target_pairs={{16,0},{18,2},{20,4},{22,6},{24,8},{26,10},{28,12},{30,14},{0,16},... | collective-permute-start | bytes 196616 | tf_op jit(solution)/shard_map/ppermute | solution.py:389
  117.7 1.8 %collective-permute-start.14 = (bf16[64,512]{1,0:T(8,128)(2,1)S(1)}, bf16[64,512]{1,0:T(8,128)(2,1)S(1)}, u32[]{:S(2)}, u32[]{:S(2)}) collective-permute-start(bf16[64,512]{1,0:T(8,128)(2,1)S(1)} %add_convert_fusion.2), channel_id=1, source_target_pairs={{24,0},{26,2},{28,4},{30,6},{16,8},{18,10},{20,12},{22,14},{8,16},... | collective-permute-start | bytes 196616 | tf_op jit(solution)/shard_map/ppermute | solution.py:389
  119.6 2.2 %collective-permute-done.13 = bf16[64,512]{1,0:T(8,128)(2,1)S(1)} collective-permute-done((bf16[64,512]{1,0:T(8,128)(2,1)S(1)}, bf16[64,512]{1,0:T(8,128)(2,1)S(1)}, u32[]{:S(2)}, u32[]{:S(2)}) %collective-permute-start.13) | collective-permute-done | bytes 65568 | tf_op jit(solution)/shard_map/ppermute | solution.py:389
  121.8 2.0 %collective-permute-done.14 = bf16[64,512]{1,0:T(8,128)(2,1)S(1)} collective-permute-done((bf16[64,512]{1,0:T(8,128)(2,1)S(1)}, bf16[64,512]{1,0:T(8,128)(2,1)S(1)}, u32[]{:S(2)}, u32[]{:S(2)}) %collective-permute-start.14) | collective-permute-done | bytes 65568 | tf_op jit(solution)/shard_map/ppermute | solution.py:389
  123.8 0.5 collective-permute-start.15
  124.2 0.3 collective-permute-start.16
  124.6 2.8 %collective-permute-start.17 = (bf16[256,512]{1,0:T(8,128)(2,1)S(1)}, bf16[256,512]{1,0:T(8,128)(2,1)S(1)}, u32[]{:S(2)}, u32[]{:S(2)}) collective-permute-start(bf16[256,512]{1,0:T(8,128)(2,1)S(1)} %constant_dynamic-update-slice_fusion.4), channel_id=1, source_target_pairs={{6,0},{4,2},{2,4},{0,6},{14,8},{12,10},{10,12},{8,14},{22,16},{20,... | collective-permute-start | bytes 786440 | tf_op jit(solution)/shard_map/ppermute | solution.py:389
  127.4 4.1 %collective-permute-done.15 = bf16[256,512]{1,0:T(8,128)(2,1)S(1)} collective-permute-done((bf16[256,512]{1,0:T(8,128)(2,1)S(1)}, bf16[256,512]{1,0:T(8,128)(2,1)S(1)}, u32[]{:S(2)}, u32[]{:S(2)}) %collective-permute-start.15) | collective-permute-done | bytes 262176 | tf_op jit(solution)/shard_map/ppermute | solution.py:389
  131.6 4.6 %collective-permute-done.16 = bf16[256,512]{1,0:T(8,128)(2,1)S(1)} collective-permute-done((bf16[256,512]{1,0:T(8,128)(2,1)S(1)}, bf16[256,512]{1,0:T(8,128)(2,1)S(1)}, u32[]{:S(2)}, u32[]{:S(2)}) %collective-permute-start.16) | collective-permute-done | bytes 262176 | tf_op jit(solution)/shard_map/ppermute | solution.py:389
  136.3 0.3 convert_multiply_fusion
  136.6 1.5 %fusion = (f32[1024,256]{1,0:T(8,128)}, f32[1024,256]{1,0:T(8,128)}) fusion(f32[1024,512]{1,0:T(8,128)S(1)} %convert_multiply_fusion), kind=kLoop, calls=%fused_computation.25 | loop fusion | bytes 4194304 | tf_op jit(solution)/shard_map/slice | solution.py:485
  138.0 1.9 %shard_map.133 = (bf16[1024,256]{1,0:T(8,128)(2,1)}, f32[4,128]{1,0:T(4,128)}) custom-call(s32[1]{0:T(128)} %bitcast.swap_ref.share_ref, bf16[1024,256]{1,0:T(8,128)(2,1)S(1)} %copy-done.1, bf16[1024,256]{1,0:T(8,128)(2,1)S(1)} %convolution_convert_fusion.mine_ref, bf16[1024,256]{1,0:T(8,128)(2,1)S(1)} %collective-permute-done.18.other_ref, ...), custom_call_target="tpu_custom_call" | custom-call | flops 2097152 | bytes 2097152 | tf_op jit(solution)/shard_map/pallas_call | solution.py:324
  (60 shorter events, 1.0 us)
Async XLA Ops:
  2.8 11.9 %all-to-all-start = ((s32[8,1,1024]{2,1,0:T(1,128)}), s32[8,1,1024]{2,1,0:T(1,128)S(1)}, u32[]{:S(2)}, u32[]{:S(2)}) async-start(s32[8,1,1024]{2,1,0:T(1,128)} %copy.14), calls=%async_computation | async-start | bytes 65536 | tf_op jit(solution)/shard_map/all_to_all | solution.py:435
  16.9 24.6 %copy-start.4 = (bf16[1024,256]{1,0:T(8,128)(2,1)S(1)}, bf16[1024,256]{1,0:T(8,128)(2,1)}, u32[]{:S(2)}) copy-start(bf16[1024,256]{1,0:T(8,128)(2,1)} %down_a_ref.1) | copy-start | bytes 1572868
  16.9 24.7 %copy-start.6 = (bf16[1024,256]{1,0:T(8,128)(2,1)S(1)}, bf16[1024,256]{1,0:T(8,128)(2,1)}, u32[]{:S(2)}) copy-start(bf16[1024,256]{1,0:T(8,128)(2,1)} %up_a_ref.1) | copy-start | bytes 1572868
  16.9 25.2 %copy-start.2 = (s32[16,128]{1,0:T(8,128)S(1)}, s32[16,128]{1,0:T(8,128)}, u32[]{:S(2)}) copy-start(s32[16,128]{1,0:T(8,128)} %goals_ref.1) | copy-start | bytes 24580
  16.9 27.8 %copy-start.12 = (bf16[2048]{0:T(1024)(128)(2,1)S(1)}, bf16[2048]{0:T(1024)(128)(2,1)}, u32[]{:S(2)}) copy-start(bf16[2048]{0:T(1024)(128)(2,1)} %param.14) | copy-start | bytes 12292
  16.9 17.6 %all-to-all-start.1 = ((bf16[8,128,256]{2,1,0:T(8,128)(2,1)}), bf16[8,128,256]{2,1,0:T(8,128)(2,1)S(1)}, u32[]{:S(2)}, u32[]{:S(2)}) async-start(bf16[8,128,256]{2,1,0:T(8,128)(2,1)} %bitcast.3), calls=%async_computation.1 | async-start | bytes 1048576 | tf_op jit(solution)/shard_map/all_to_all | solution.py:445
  20.5 10.2 %collective-permute-start = (bf16[512,256]{1,0:T(8,128)(2,1)S(1)}, bf16[512,256]{1,0:T(8,128)(2,1)S(1)}, u32[]{:S(2)}, u32[]{:S(2)}) collective-permute-start(bf16[512,256]{1,0:T(8,128)(2,1)S(1)} %get-tuple-element.32), channel_id=1, source_target_pairs={{0,16},{2,18},{4,20},{6,22},{8,24},{10,26},{12,28},{14,30},{16,0},... | collective-permute-start | bytes 786440 | tf_op jit(solution)/shard_map/ppermute | solution.py:428
  30.8 1.5 %collective-permute-start.1 = (bf16[512,256]{1,0:T(8,128)(2,1)S(1)}, bf16[512,256]{1,0:T(8,128)(2,1)S(1)}, u32[]{:S(2)}, u32[]{:S(2)}) collective-permute-start(bf16[512,256]{1,0:T(8,128)(2,1)S(1)} %collective-permute-done.first_ref), channel_id=1, source_target_pairs={{1,0},{0,1},{3,2},{2,3},{5,4},{4,5},{7,6},{6,7},{9,8},{8,9},{11,10... | collective-permute-start | bytes 786440 | tf_op jit(solution)/shard_map/ppermute | solution.py:422
  34.5 18.2 %all-to-all-start.2 = ((bf16[8,128,256]{2,1,0:T(8,128)(2,1)}), bf16[8,128,256]{2,1,0:T(8,128)(2,1)S(1)}, u32[]{:S(2)}, u32[]{:S(2)}) async-start(bf16[8,128,256]{2,1,0:T(8,128)(2,1)} %bitcast.5), calls=%async_computation.2 | async-start | bytes 1048576 | tf_op jit(solution)/shard_map/all_to_all | solution.py:445
  41.5 11.2 %collective-permute-start.3 = (bf16[1024,256]{1,0:T(8,128)(2,1)S(1)}, bf16[1024,256]{1,0:T(8,128)(2,1)S(1)}, u32[]{:S(2)}, u32[]{:S(2)}) collective-permute-start(bf16[1024,256]{1,0:T(8,128)(2,1)S(1)} %copy-done.4), channel_id=1, source_target_pairs={{1,0},{0,1},{3,2},{2,3},{5,4},{4,5},{7,6},{6,7},{9,8},{8,9},{11,10... | collective-permute-start | bytes 1572872 | tf_op jit(solution)/shard_map/ppermute | solution.py:422
  41.6 11.9 %collective-permute-start.4 = (bf16[1024,256]{1,0:T(8,128)(2,1)S(1)}, bf16[1024,256]{1,0:T(8,128)(2,1)}, u32[]{:S(2)}, u32[]{:S(2)}) collective-permute-start(bf16[1024,256]{1,0:T(8,128)(2,1)S(1)} %copy-done.6), channel_id=1, source_target_pairs={{1,0},{0,1},{3,2},{2,3},{5,4},{4,5},{7,6},{6,7},{9,8},{8,9},{11,10... | collective-permute-start | bytes 1572872 | tf_op jit(solution)/shard_map/ppermute | solution.py:422
  42.1 5.8 %collective-permute-start.2 = (s32[8,512]{1,0:T(8,128)S(1)}, s32[8,512]{1,0:T(8,128)S(1)}, u32[]{:S(2)}, u32[]{:S(2)}) collective-permute-start(s32[8,512]{1,0:T(8,128)S(1)} %get-tuple-element.39), channel_id=1, source_target_pairs={{0,16},{2,18},{4,20},{6,22},{8,24},{10,26},{12,28},{14,30},{16,0},... | collective-permute-start | bytes 49160 | tf_op jit(solution)/shard_map/ppermute | solution.py:457
  47.9 5.6 %copy-start.10 = (f32[2048]{0:T(1024)S(1)}, f32[2048]{0:T(1024)}, u32[]{:S(2)}) copy-start(f32[2048]{0:T(1024)} %param.13) | copy-start | bytes 24580
  47.9 5.6 %copy-start.11 = (f32[128]{0:T(128)S(1)}, f32[128]{0:T(128)}, u32[]{:S(2)}) copy-start(f32[128]{0:T(128)} %param.15) | copy-start | bytes 1540
  50.7 2.0 %copy-start = (bf16[1024,2048]{1,0:T(8,128)(2,1)}, bf16[1024,2048]{1,0:T(8,128)(2,1)S(1)}, u32[]{:S(2)}) copy-start(bf16[1024,2048]{1,0:T(8,128)(2,1)S(1)} %shard_map.130) | copy-start | bytes 12582916
  52.7 0.8 copy-start.8
  53.5 1.0 copy-start.5
  54.6 1.0 copy-start.7
  55.6 1.0 copy-start.9
  64.5 10.4 %collective-permute-start.5 = (bf16[1024,512]{1,0:T(8,128)(2,1)S(1)}, bf16[1024,512]{1,0:T(8,128)(2,1)}, u32[]{:S(2)}, u32[]{:S(2)}) collective-permute-start(bf16[1024,512]{1,0:T(8,128)(2,1)S(1)} %get-tuple-element.20), channel_id=1, source_target_pairs={{1,0},{0,1},{3,2},{2,3},{5,4},{4,5},{7,6},{6,7},{9,8},{8,9},{11,10... | collective-permute-start | bytes 3145736 | tf_op jit(solution)/shard_map/ppermute | solution.py:465
  66.9 44.3 %all-to-all-start.3 = ((bf16[16,128,256]{2,1,0:T(8,128)(2,1)}), bf16[16,128,256]{2,1,0:T(8,128)(2,1)}, u32[]{:S(2)}, u32[]{:S(2)}) async-start(bf16[16,128,256]{2,1,0:T(8,128)(2,1)} %bitcast.10), calls=%async_computation.3 | async-start | bytes 2097152 | tf_op jit(solution)/shard_map/all_to_all | solution.py:470
  76.5 11.8 %collective-permute-start.6 = (bf16[256,512]{1,0:T(8,128)(2,1)S(1)}, bf16[256,512]{1,0:T(8,128)(2,1)S(1)}, u32[]{:S(2)}, u32[]{:S(2)}) collective-permute-start(bf16[256,512]{1,0:T(8,128)(2,1)S(1)} %get-tuple-element.29), channel_id=1, source_target_pairs={{2,0},{0,2},{6,4},{4,6},{10,8},{8,10},{14,12},{12,14},{18,16},{16,... | collective-permute-start | bytes 786440 | tf_op jit(solution)/shard_map/ppermute | solution.py:375
  78.4 18.5 %collective-permute-start.7 = (bf16[256,512]{1,0:T(8,128)(2,1)S(1)}, bf16[256,512]{1,0:T(8,128)(2,1)S(1)}, u32[]{:S(2)}, u32[]{:S(2)}) collective-permute-start(bf16[256,512]{1,0:T(8,128)(2,1)S(1)} %get-tuple-element.31), channel_id=1, source_target_pairs={{4,0},{6,2},{0,4},{2,6},{12,8},{14,10},{8,12},{10,14},{20,16},{22,... | collective-permute-start | bytes 786440 | tf_op jit(solution)/shard_map/ppermute | solution.py:375
  79.9 21.9 %collective-permute-start.8 = (bf16[256,512]{1,0:T(8,128)(2,1)S(1)}, bf16[256,512]{1,0:T(8,128)(2,1)S(1)}, u32[]{:S(2)}, u32[]{:S(2)}) collective-permute-start(bf16[256,512]{1,0:T(8,128)(2,1)S(1)} %get-tuple-element.30), channel_id=1, source_target_pairs={{6,0},{4,2},{2,4},{0,6},{14,8},{12,10},{10,12},{8,14},{22,16},{20,... | collective-permute-start | bytes 786440 | tf_op jit(solution)/shard_map/ppermute | solution.py:375
  102.0 6.2 %collective-permute-start.10 = (bf16[64,512]{1,0:T(8,128)(2,1)S(1)}, bf16[64,512]{1,0:T(8,128)(2,1)S(1)}, u32[]{:S(2)}, u32[]{:S(2)}) collective-permute-start(bf16[64,512]{1,0:T(8,128)(2,1)S(1)} %get-tuple-element.37), channel_id=1, source_target_pairs={{16,0},{18,2},{20,4},{22,6},{24,8},{26,10},{28,12},{30,14},{0,16},... | collective-permute-start | bytes 196616 | tf_op jit(solution)/shard_map/ppermute | solution.py:375
  105.2 6.1 %collective-permute-start.11 = (bf16[64,512]{1,0:T(8,128)(2,1)S(1)}, bf16[64,512]{1,0:T(8,128)(2,1)S(1)}, u32[]{:S(2)}, u32[]{:S(2)}) collective-permute-start(bf16[64,512]{1,0:T(8,128)(2,1)S(1)} %get-tuple-element.36), channel_id=1, source_target_pairs={{24,0},{26,2},{28,4},{30,6},{16,8},{18,10},{20,12},{22,14},{8,16},... | collective-permute-start | bytes 196616 | tf_op jit(solution)/shard_map/ppermute | solution.py:375
  105.2 6.1 %collective-permute-start.9 = (bf16[64,512]{1,0:T(8,128)(2,1)S(1)}, bf16[64,512]{1,0:T(8,128)(2,1)S(1)}, u32[]{:S(2)}, u32[]{:S(2)}) collective-permute-start(bf16[64,512]{1,0:T(8,128)(2,1)S(1)} %get-tuple-element.35), channel_id=1, source_target_pairs={{8,0},{10,2},{12,4},{14,6},{0,8},{2,10},{4,12},{6,14},{24,16},{26,... | collective-permute-start | bytes 196616 | tf_op jit(solution)/shard_map/ppermute | solution.py:375
  115.0 4.5 %collective-permute-start.12 = (bf16[64,512]{1,0:T(8,128)(2,1)S(1)}, bf16[64,512]{1,0:T(8,128)(2,1)S(1)}, u32[]{:S(2)}, u32[]{:S(2)}) collective-permute-start(bf16[64,512]{1,0:T(8,128)(2,1)S(1)} %add_convert_fusion.2), channel_id=1, source_target_pairs={{8,0},{10,2},{12,4},{14,6},{0,8},{2,10},{4,12},{6,14},{24,16},{26,... | collective-permute-start | bytes 196616 | tf_op jit(solution)/shard_map/ppermute | solution.py:389
  115.1 6.6 %collective-permute-start.13 = (bf16[64,512]{1,0:T(8,128)(2,1)S(1)}, bf16[64,512]{1,0:T(8,128)(2,1)S(1)}, u32[]{:S(2)}, u32[]{:S(2)}) collective-permute-start(bf16[64,512]{1,0:T(8,128)(2,1)S(1)} %add_convert_fusion.2), channel_id=1, source_target_pairs={{16,0},{18,2},{20,4},{22,6},{24,8},{26,10},{28,12},{30,14},{0,16},... | collective-permute-start | bytes 196616 | tf_op jit(solution)/shard_map/ppermute | solution.py:389
  117.7 6.1 %collective-permute-start.14 = (bf16[64,512]{1,0:T(8,128)(2,1)S(1)}, bf16[64,512]{1,0:T(8,128)(2,1)S(1)}, u32[]{:S(2)}, u32[]{:S(2)}) collective-permute-start(bf16[64,512]{1,0:T(8,128)(2,1)S(1)} %add_convert_fusion.2), channel_id=1, source_target_pairs={{24,0},{26,2},{28,4},{30,6},{16,8},{18,10},{20,12},{22,14},{8,16},... | collective-permute-start | bytes 196616 | tf_op jit(solution)/shard_map/ppermute | solution.py:389
  123.8 7.8 %collective-permute-start.15 = (bf16[256,512]{1,0:T(8,128)(2,1)S(1)}, bf16[256,512]{1,0:T(8,128)(2,1)S(1)}, u32[]{:S(2)}, u32[]{:S(2)}) collective-permute-start(bf16[256,512]{1,0:T(8,128)(2,1)S(1)} %constant_dynamic-update-slice_fusion.4), channel_id=1, source_target_pairs={{2,0},{0,2},{6,4},{4,6},{10,8},{8,10},{14,12},{12,14},{18,16},{16,... | collective-permute-start | bytes 786440 | tf_op jit(solution)/shard_map/ppermute | solution.py:389
  124.2 12.0 %collective-permute-start.16 = (bf16[256,512]{1,0:T(8,128)(2,1)S(1)}, bf16[256,512]{1,0:T(8,128)(2,1)S(1)}, u32[]{:S(2)}, u32[]{:S(2)}) collective-permute-start(bf16[256,512]{1,0:T(8,128)(2,1)S(1)} %constant_dynamic-update-slice_fusion.4), channel_id=1, source_target_pairs={{4,0},{6,2},{0,4},{2,6},{12,8},{14,10},{8,12},{10,14},{20,16},{22,... | collective-permute-start | bytes 786440 | tf_op jit(solution)/shard_map/ppermute | solution.py:389
  124.6 13.5 %collective-permute-start.18 = (bf16[1024,256]{1,0:T(8,128)(2,1)S(1)}, bf16[1024,256]{1,0:T(8,128)(2,1)S(1)}, u32[]{:S(2)}, u32[]{:S(2)}) collective-permute-start(bf16[1024,256]{1,0:T(8,128)(2,1)S(1)} %convolution_convert_fusion.mine_ref), channel_id=1, source_target_pairs={{1,0},{0,1},{3,2},{2,3},{5,4},{4,5},{7,6},{6,7},{9,8},{8,9},{11,10... | collective-permute-start | bytes 1572872 | tf_op jit(solution)/shard_map/ppermute | solution.py:488
  124.6 11.7 %collective-permute-start.17 = (bf16[256,512]{1,0:T(8,128)(2,1)S(1)}, bf16[256,512]{1,0:T(8,128)(2,1)S(1)}, u32[]{:S(2)}, u32[]{:S(2)}) collective-permute-start(bf16[256,512]{1,0:T(8,128)(2,1)S(1)} %constant_dynamic-update-slice_fusion.4), channel_id=1, source_target_pairs={{6,0},{4,2},{2,4},{0,6},{14,8},{12,10},{10,12},{8,14},{22,16},{20,... | collective-permute-start | bytes 786440 | tf_op jit(solution)/shard_map/ppermute | solution.py:389
  136.6 1.5 %copy-start.1 = (bf16[1024,256]{1,0:T(8,128)(2,1)S(1)}, bf16[1024,256]{1,0:T(8,128)(2,1)}, u32[]{:S(2)}) copy-start(bf16[1024,256]{1,0:T(8,128)(2,1)} %rows_ref.1) | copy-start | bytes 1572868
  136.6 1.5 %copy-start.3 = (f32[1024]{0:T(1024)S(1)}, f32[1024]{0:T(1024)}, u32[]{:S(2)}) copy-start(f32[1024]{0:T(1024)} %param.10) | copy-start | bytes 12292

commit v4 on v3

--- a/solution.py
+++ b/solution.py
@@ -18,7 +18,7 @@
 
 
 SLOTS = 128
-VMEM_BYTES = 48 * 1024 * 1024
+MIB = 1024 * 1024
 
 
 def matmul(left, right):
@@ -37,16 +37,17 @@
     )
 
 
-def kernel_call(kernel, out_shape, cost, scratch=(), flags=0, operands=0):
+def kernel_call(kernel, out_shape, cost, scratch=(), flags=0, operands=0, room=8):
     flops, moved = cost
     smem = pl.BlockSpec(memory_space=pltpu.SMEM)
     vmem = pl.BlockSpec(memory_space=pltpu.VMEM)
     return pl.pallas_call(
         kernel,
         in_specs=[smem] * flags + [vmem] * operands,
+        out_specs=jax.tree.map(lambda _: vmem, out_shape),
         out_shape=out_shape,
         scratch_shapes=scratch,
-        compiler_params=pltpu.CompilerParams(vmem_limit_bytes=VMEM_BYTES),
+        compiler_params=pltpu.CompilerParams(vmem_limit_bytes=room * MIB),
         cost_estimate=pl.CostEstimate(flops=flops, bytes_accessed=moved, transcendentals=0),
     )
 
@@ -154,9 +155,73 @@
     return jnp.sum(jnp.where(diagonal(column.shape[0]), column, 0.0), axis=0, keepdims=True)
 
 
+def place_kernel(goals_ref, out_ref):
+    samples = out_ref.shape[0] // FEAT
+    chunk = 512
+    first_bag = lax.broadcasted_iota(jnp.int32, (samples, chunk), 0) * FEAT
+    for start in range(0, goals_ref.shape[1], chunk):
+        line = goals_ref[:, start : start + chunk]
+        nth = (jnp.broadcast_to(line, (samples, chunk)) - first_bag).astype(jnp.int16)
+        for f in range(FEAT):
+            out_ref[f * samples : (f + 1) * samples, start : start + chunk] = ones_where(
+                nth == jnp.asarray(f, jnp.int16)
+            )
+
+
+def place_slots(goals, samples):
+    slot_count = goals.size
+    size = samples * FEAT * slot_count
+    return kernel_call(
+        place_kernel,
+        jax.ShapeDtypeStruct((samples * FEAT, slot_count), jnp.bfloat16),
+        (2 * size, 2 * size),
+        operands=1,
+    )(goals.reshape(1, slot_count))
+
+
+def pick_kernel(goals_ref, out_ref):
+    blocks = goals_ref.shape[0]
+    bags = out_ref.shape[1]
+    samples = bags // FEAT
+    high, low = split_ids(goals_ref[...])
+    unit = ones_where(diagonal(SLOTS))
+    columns = joined((rows_dot(unit, high), rows_dot(unit, low))).astype(jnp.int16)
+    place = lax.broadcasted_iota(jnp.int32, (SLOTS, bags), 1)
+    order = ((place % samples) * FEAT + place // samples).astype(jnp.int16)
+    for block in range(blocks):
+        out_ref[block * SLOTS : (block + 1) * SLOTS, :] = ones_where(
+            columns[:, block : block + 1] == order
+        )
+
+
+def pick_bags(goals, samples):
+    slot_count = goals.size
+    size = samples * FEAT * slot_count
+    return kernel_call(
+        pick_kernel,
+        jax.ShapeDtypeStruct((slot_count, samples * FEAT), jnp.bfloat16),
+        (2 * size, 2 * size),
+        operands=1,
+    )(goals.reshape(slot_count // SLOTS, SLOTS))
+
+
+def product_kernel(left_ref, right_ref, out_ref):
+    out_ref[...] = matmul(left_ref[...], right_ref[...]).astype(jnp.bfloat16)
+
+
+def product(left, right):
+    shape = (left.shape[0], right.shape[1])
+    return kernel_call(
+        product_kernel,
+        jax.ShapeDtypeStruct(shape, jnp.bfloat16),
+        (2 * left.size * right.shape[1], 2 * left.size + 2 * right.size),
+        operands=2,
+    )(left, right)
+
+
 def dense_kernel(
     swap_ref,
-    goals_ref,
+    place_ref,
     near_ref,
     far_ref,
     down_a_ref,
@@ -170,7 +235,6 @@
     grads_ref,
     kept_ref,
     sent_ref,
-    place_ref,
     wide_ref,
     cross_ref,
     down_ref,
@@ -187,15 +251,6 @@
     up_ref[:half, :] = jnp.where(swapped, up_b_ref[...], up_a_ref[...])
     up_ref[half:, :] = jnp.where(swapped, up_a_ref[...], up_b_ref[...])
     features = [slice(f * emb, (f + 1) * emb) for f in range(FEAT)]
-    chunk = 512
-    first_bag = lax.broadcasted_iota(jnp.int32, (samples, chunk), 0) * FEAT
-    for start in range(0, goals_ref.shape[1], chunk):
-        line = goals_ref[:, start : start + chunk]
-        nth = (jnp.broadcast_to(line, (samples, chunk)) - first_bag).astype(jnp.int16)
-        for f in range(FEAT):
-            place_ref[f * samples : (f + 1) * samples, start : start + chunk] = ones_where(
-                nth == jnp.asarray(f, jnp.int16)
-            )
     pooled = matmul(place_ref[:, :slots], near_ref[...])
     pooled = (pooled + matmul(place_ref[:, slots:], far_ref[...])).astype(jnp.bfloat16)
     for f, part in enumerate(features):
@@ -220,9 +275,12 @@
         back_term = rows_dot(dhidden, down_ref[part, :])
         grads = dmixed * (cross_ref[:, part] + 1.0) + back_term
         grads_ref[f * samples : (f + 1) * samples, :] = grads.astype(jnp.bfloat16)
+    unit = ones_where(diagonal(emb))
     for f, part in enumerate(features):
-        down_term = transposed_dot(wide_ref[:, part], dhidden).astype(jnp.bfloat16)
-        up_term = transposed_dot(dcross[f], hidden).astype(jnp.bfloat16)
+        feats_t = rows_dot(unit, wide_ref[:, part]).astype(jnp.bfloat16)
+        down_term = matmul(feats_t, dhidden).astype(jnp.bfloat16)
+        cross_t = rows_dot(unit, dcross[f]).astype(jnp.bfloat16)
+        up_term = matmul(cross_t, hidden).astype(jnp.bfloat16)
         spot = slice((f * emb) % half, (f * emb) % half + emb)
         keep = swapped if f * emb >= half else jnp.logical_not(swapped)
 
@@ -237,7 +295,7 @@
             sent_ref[spot, rank:] = up_term
 
 
-def dense_step(swap, goals, near, far, downs, ups, bias, weight, target):
+def dense_step(swap, place, near, far, downs, ups, bias, weight, target):
     samples = target.shape[0]
     slots, emb = near.shape
     width, rank = 2 * downs[0].shape[0], downs[0].shape[1]
@@ -252,7 +310,6 @@
         ),
         (flops, 4 * near.size + 8 * width * rank),
         [
-            pltpu.VMEM((samples * FEAT, 2 * slots), jnp.bfloat16),
             pltpu.VMEM((samples, width), jnp.bfloat16),
             pltpu.VMEM((samples, width), jnp.float32),
             pltpu.VMEM((width, rank), jnp.bfloat16),
@@ -260,9 +317,10 @@
         ],
         flags=1,
         operands=10,
+        room=16,
     )(
         swap,
-        goals.reshape(1, 2 * slots),
+        place,
         near,
         far,
         *downs,
@@ -272,34 +330,6 @@
         target.reshape(1, samples),
     )
     return logits.reshape(samples), grads, kept, sent
-
-
-def return_kernel(goals_ref, grads_ref, out_ref, pick_ref):
-    blocks = goals_ref.shape[0]
-    bags = grads_ref.shape[0]
-    samples = bags // FEAT
-    high, low = split_ids(goals_ref[...])
-    unit = ones_where(diagonal(SLOTS))
-    columns = joined((rows_dot(unit, high), rows_dot(unit, low))).astype(jnp.int16)
-    place = lax.broadcasted_iota(jnp.int32, (SLOTS, bags), 1)
-    order = ((place % samples) * FEAT + place // samples).astype(jnp.int16)
-    for block in range(blocks):
-        pick_ref[block * SLOTS : (block + 1) * SLOTS, :] = ones_where(
-            columns[:, block : block + 1] == order
-        )
-    out_ref[...] = matmul(pick_ref[...], grads_ref[...]).astype(jnp.bfloat16)
-
-
-def return_grads(goals, grads):
-    bags, emb = grads.shape
-    slot_count = goals.size
-    return kernel_call(
-        return_kernel,
-        jax.ShapeDtypeStruct((slot_count, emb), jnp.bfloat16),
-        (2 * slot_count * bags * emb, 2 * grads.size + 2 * slot_count * emb),
-        [pltpu.VMEM((slot_count, bags), jnp.bfloat16)],
-        operands=2,
-    )(goals.reshape(slot_count // SLOTS, SLOTS), grads)
 
 
 def update_kernel(share_ref, rows_ref, mine_ref, other_ref, accum_ref, rows_out_ref, accum_out_ref):
@@ -377,19 +407,24 @@
     return blocks
 
 
+def gathered_pieces(block, axis, level):
+    stride, group = level
+    index = lax.axis_index(axis)
+    pieces = [((index // stride) % group, block)]
+    for step in range(1, group):
+        origin = partner_index(index, stride, group, step)
+        came = lax.ppermute(block, axis, sent_from(axis, stride, group, step))
+        pieces.append(((origin // stride) % group, came))
+    return pieces
+
+
 def gather_blocks(block, axis, levels):
-    index = lax.axis_index(axis)
-    for stride, group in reversed(levels):
+    for level in reversed(levels):
         rows = block.shape[0]
-        place = (index // stride) % group
-        whole = jnp.zeros((group * rows,) + block.shape[1:], block.dtype)
-        whole = lax.dynamic_update_slice_in_dim(whole, block, place * rows, 0)
-        for step in range(1, group):
-            origin = partner_index(index, stride, group, step)
-            came = lax.ppermute(block, axis, sent_from(axis, stride, group, step))
-            spot = (origin // stride) % group
-            whole = lax.dynamic_update_slice_in_dim(whole, came, spot * rows, 0)
-        block = whole
+        pieces = gathered_pieces(block, axis, level)
+        block = jnp.zeros((len(pieces) * rows,) + block.shape[1:], block.dtype)
+        for place, piece in pieces:
+            block = lax.dynamic_update_slice_in_dim(block, piece, place * rows, 0)
     return block
 
 
@@ -414,8 +449,16 @@
     paired = narrows == 2
     swap = (narrow_index if paired else narrow_index * 0).reshape(1)
 
-    def near_first(rows):
-        return jnp.where(far_half == 0, rows, jnp.roll(rows, near_count, axis=0))
+    def near_and_far(rows):
+        return tuple(
+            lax.dynamic_slice_in_dim(rows, half * near_count, near_count, 0)
+            for half in (far_half, 1 - far_half)
+        )
+
+    def in_order(near, far):
+        return jnp.where(
+            far_half == 0, jnp.concatenate([near, far]), jnp.concatenate([far, near])
+        )
 
     def both_halves(block):
         if paired:
@@ -425,16 +468,17 @@
 
     share_rows = row_dev // narrows
     own_share = lax.dynamic_slice_in_dim(table_rows, narrow_index * share_rows, share_rows, 0)
-    far_rows = both_halves(lax.ppermute(own_share, "table", across))
+    far_share = lax.ppermute(own_share, "table", across)
     downs = both_halves(factor_down)
     ups = both_halves(factor_up)
 
     per_window = bag_rows.shape[1]
-    asked = near_first(bag_rows)
-    asked = jnp.concatenate([asked[:near_count], asked[near_count:]], axis=1)
+    asked = jnp.concatenate(near_and_far(bag_rows), axis=1)
     asked = lax.all_to_all(
         asked, "table", split_axis=0, concat_axis=0, tiled=True, axis_index_groups=halves
     )
+    asked, far_share = lax.optimization_barrier((asked, far_share))
+    far_rows = both_halves(far_share)
     near_ids, far_ids = asked[:, :per_window], asked[:, per_window:]
 
     def pooled_for(part, plain_ids, flag, rows):
@@ -455,18 +499,21 @@
     near = pooled_for(0, near_ids, swap * 0, own_rows)
     far = pooled_for(1, far_ids, swap, far_rows)
     other_ids = lax.ppermute(far_ids, "table", across)
-    all_ids = near_first(jnp.concatenate([near_ids, other_ids], axis=0))
+    all_ids = in_order(near_ids, other_ids)
     counts = lookup_counts(all_ids.reshape(-1, SLOTS * HOT), row_dev)
-    near, far, counts = lax.optimization_barrier((near, far, counts))
+    place = place_slots(jnp.concatenate(near_and_far(slot_target)), samples)
+    pick = pick_bags(slot_target, samples)
+    near, far, counts, place, pick = lax.optimization_barrier((near, far, counts, place, pick))
     logits, bag_grads, kept, sent = dense_step(
-        swap, near_first(slot_target), near, far, downs, ups, cross_bias, out_weight, target
+        swap, place, near, far, downs, ups, cross_bias, out_weight, target
     )
     if paired:
         came = lax.ppermute(sent, "narrow", sent_from("narrow", 1, 2, 1))
         narrow_sum = (kept.astype(jnp.float32) + came.astype(jnp.float32)).astype(jnp.bfloat16)
     else:
         narrow_sum = scatter_sum(jnp.concatenate([kept, sent], axis=0), "narrow", narrow_levels)
-    slot_grads = return_grads(slot_target, bag_grads)
+    slot_grads = product(pick, bag_grads)
+    slot_grads, narrow_sum = lax.optimization_barrier((slot_grads, narrow_sum))
     returned = lax.all_to_all(
         slot_grads.reshape(tables, pools_per, emb_width),
         "table",
@@ -475,14 +522,9 @@
         tiled=True,
     ).reshape(slot_count, emb_width)
     table_sum = scatter_sum(narrow_sum, "table", table_levels)
-    sent_grad = matmul(counts, returned).astype(jnp.bfloat16)
-    table_sum, sent_grad = lax.optimization_barrier((table_sum, sent_grad))
-    grand_total = gather_blocks(table_sum, "table", table_levels).astype(jnp.float32)
-    batch_all = samples * tables * narrows
-    grand_total = grand_total * (1.0 / math.sqrt(batch_all))
-    rank_size = factor_down.shape[1]
-    down_grad = grand_total[:, :rank_size]
-    up_grad = grand_total[:, rank_size:]
+    sent_grad = product(counts, returned)
+    level_sum = gather_blocks(table_sum, "table", table_levels[1:])
+    level_sum, sent_grad = lax.optimization_barrier((level_sum, sent_grad))
     if paired:
         mine = sent_grad
         other = lax.ppermute(sent_grad, "narrow", sent_from("narrow", 1, 2, 1))
@@ -493,6 +535,18 @@
     new_rows, new_accum = update_rows(
         narrow_index.reshape(1), table_rows, mine, other, accum, narrows
     )
+    rank = factor_down.shape[1]
+    scale = 1.0 / math.sqrt(samples * tables * narrows)
+    down_grad = jnp.zeros(factor_down.shape, jnp.float32)
+    up_grad = jnp.zeros(factor_up.shape, jnp.float32)
+    pieces = gathered_pieces(level_sum, "table", table_levels[0])
+    spot, last = pieces[-1]
+    last, new_rows, new_accum = lax.optimization_barrier((last, new_rows, new_accum))
+    for spot, piece in pieces[:-1] + [(spot, last)]:
+        spot = spot * piece.shape[0]
+        scaled = piece.astype(jnp.float32) * scale
+        down_grad = lax.dynamic_update_slice_in_dim(down_grad, scaled[:, :rank], spot, 0)
+        up_grad = lax.dynamic_update_slice_in_dim(up_grad, scaled[:, rank:], spot, 0)
     return (logits, down_grad, up_grad, new_rows, new_accum)
 
 

time: 141 us -> 135 us (0.957)
  blocking collectives: 0 us -> 13.2 us
  waiting for transfers between devices: 57.8 us -> 46.3 us
  starting transfers between devices: 45.2 us -> 35.4 us
  local copies, waits for them, and re-layouts: 10.2 us -> 14.4 us
  matrix products: 3.73 us -> 0 us
  Pallas kernels: 19.3 us -> 21.8 us
    all_to_all x0 -> x1, blocking collectives: none -> 13.2 us  [local(): lax.all_to_all(asked, 'table', split_axis=0, concat_axis=0, tiled=True, a...]
    ppermute x7, waiting for transfers between devices: 21.3 us -> 12 us  [the longest x6 12 us: gathered_pieces(): came = lax.ppermute(block, axis, sent_from(axis, stride, group, step))]
    all_to_all x1 -> x0, starting transfers between devices: 6.18 us -> none  [local(): lax.all_to_all(asked, 'table', split_axis=0, concat_axis=0, tiled=True, a...]
    unnamed x27 -> x33, local copies, waits for them, and re-layouts: 5.9 us -> 11.9 us
    all_to_all x1 -> x0, waiting for transfers between devices: 4.54 us -> none  [local(): lax.all_to_all(asked, 'table', split_axis=0, concat_axis=0, tiled=True, a...]
    all_to_all x2, waiting for transfers between devices: 0.01 us -> 3.86 us  [pooled_for(): lax.all_to_all(sums.reshape(near_count, pools_per, emb_width), 'table', s...]
    dot_general x1 -> x0, matrix products: 3.73 us -> none  [matmul(): return jnp.dot(left, right, preferred_element_type=jnp.float32)]
    all_to_all x2, starting transfers between devices: 10.7 us -> 6.99 us  [pooled_for(): lax.all_to_all(sums.reshape(near_count, pools_per, emb_width), 'table', s...]
  transfers between devices with their start and end apart: 23 -> 22, of which waited for: 13 -> 12; matrix products, arithmetic and copies ran while one was open for 4% -> 2% of each run, Pallas kernels for 5% -> 8%
where the time goes in v4:
time: 135 us; the launch traced here: 134 us
  waiting for transfers between devices  46.3 us (34%)
  starting transfers between devices  35.4 us (26%)
  Pallas kernels  21.8 us (16%)
  local copies, waits for them, and re-layouts  14.4 us (11%)
  blocking collectives  13.2 us (10%)
  other arithmetic  1.65 us (1%)
    ppermute x6, waiting for transfers between devices, scatter_sum(): total = total + lax.ppermute(outgoing, axis, pairs).astype(jnp.float32)  28.6 us
    all_to_all x1, blocking collectives, local(): lax.all_to_all(asked, 'table', split_axis=0, concat_axis=0, tiled=True, a...  13.2 us
    ppermute x6, waiting for transfers between devices, gathered_pieces(): came = lax.ppermute(block, axis, sent_from(axis, stride, group, step))  12 us
    unnamed x33, local copies, waits for them, and re-layouts  11.9 us
    pallas_call x1, Pallas kernels, dense_step(): kernel_call(dense_kernel, (jax.ShapeDtypeStruct((1, samples), jnp.float32...  8.25 us
    ppermute x6, starting transfers between devices, gathered_pieces(): came = lax.ppermute(block, axis, sent_from(axis, stride, group, step))  7.85 us
    ppermute x6, starting transfers between devices, scatter_sum(): total = total + lax.ppermute(outgoing, axis, pairs).astype(jnp.float32)  7.27 us
    all_to_all x2, starting transfers between devices, pooled_for(): lax.all_to_all(sums.reshape(near_count, pools_per, emb_width), 'table', s...  6.99 us
  transfers between devices with their start and end apart: 22, of which 12 were waited for; matrix products, arithmetic and copies ran while one was open for 2% of the time, Pallas kernels for 8%

profile of v4, /device:TPU:0, one launch (start us, length us, event | category | flops | bytes accessed | tf_op | source)
XLA Modules:
  0.0 134.0 jit_solution(12606165847246430659)
XLA Ops:
  0.7 1.2 fusion
  1.9 4.1 %collective-permute-start = (bf16[512,256]{1,0:T(8,128)(2,1)S(1)}, bf16[512,256]{1,0:T(8,128)(2,1)S(1)}, u32[]{:S(2)}, u32[]{:S(2)}) collective-permute-start(bf16[512,256]{1,0:T(8,128)(2,1)S(1)} %get-tuple-element.58), channel_id=1, source_target_pairs={{0,16},{2,18},{4,20},{6,22},{8,24},{10,26},{12,28},{14,30},{16,0},... | collective-permute-start | bytes 786440 | tf_op jit(solution)/shard_map/ppermute | solution.py:471
  6.0 0.7 constant_dynamic-slice_fusion.10
  6.8 13.2 %all_to_all.27 = s32[8,1,1024]{2,1,0:T(1,128)S(1)} all-to-all(s32[8,1,1024]{2,1,0:T(1,128)S(1)} %all_to_all.17), channel_id=1, replica_groups={{0,2,4,6,8,10,12,14},{16,18,20,22,24,26,28,30},{1,3,5,7,9,11,13,15},{17..., dimensions={0} | all-to-all | bytes 65536 | tf_op jit(solution)/shard_map/all_to_all | solution.py:477
  20.0 2.1 %shard_map.128 = bf16[1024,256]{1,0:T(8,128)(2,1)} custom-call(s32[1]{0:T(128)} %constant.159.clone.1.swap_ref, s32[8,1024]{1,0:T(8,128)S(1)} %bitcast.19, bf16[512,256]{1,0:T(8,128)(2,1)S(1)} %get-tuple-element.57.first_ref, bf16[512,256]{1,0:T(8,128)(2,1)S(1)} %get-tuple-element.56.second_ref), custom_call_target="tpu_custom_call" | custom-call | flops 536870912 | bytes 1048576 | tf_op jit(solution)/shard_map/pallas_call | solution.py:104
  22.2 3.5 %all-to-all-start.1 = ((bf16[8,128,256]{2,1,0:T(8,128)(2,1)}), bf16[8,128,256]{2,1,0:T(8,128)(2,1)S(1)}, u32[]{:S(2)}, u32[]{:S(2)}) async-start(bf16[8,128,256]{2,1,0:T(8,128)(2,1)} %bitcast.1), calls=%async_computation.1 | async-start | bytes 1048576 | tf_op jit(solution)/shard_map/all_to_all | solution.py:489
  25.8 1.5 %collective-permute-done.1.second_ref = bf16[512,256]{1,0:T(8,128)(2,1)S(1)} collective-permute-done((bf16[512,256]{1,0:T(8,128)(2,1)S(1)}, bf16[512,256]{1,0:T(8,128)(2,1)S(1)}, u32[]{:S(2)}, u32[]{:S(2)}) %collective-permute-start.1) | collective-permute-done | bytes 262176 | tf_op jit(solution)/shard_map/ppermute | solution.py:465
  27.3 2.1 %shard_map.129 = bf16[1024,256]{1,0:T(8,128)(2,1)} custom-call(s32[1]{0:T(128)} %bitcast.swap_ref.share_ref, s32[8,1024]{1,0:T(8,128)S(1)} %bitcast.20, bf16[512,256]{1,0:T(8,128)(2,1)S(1)} %collective-permute-done.first_ref, bf16[512,256]{1,0:T(8,128)(2,1)S(1)} %collective-permute-done.1.second_ref), custom_call_target="tpu_custom_call" | custom-call | flops 536870912 | bytes 1048576 | tf_op jit(solution)/shard_map/pallas_call | solution.py:104
  29.4 3.9 %all-to-all-done.1 = bf16[8,128,256]{2,1,0:T(8,128)(2,1)S(1)} async-done(((bf16[8,128,256]{2,1,0:T(8,128)(2,1)}), bf16[8,128,256]{2,1,0:T(8,128)(2,1)S(1)}, u32[]{:S(2)}, u32[]{:S(2)}) %all-to-all-start.1) | async-done | bytes 524320 | tf_op jit(solution)/shard_map/all_to_all | solution.py:489
  33.3 3.5 %all-to-all-start.2 = ((bf16[8,128,256]{2,1,0:T(8,128)(2,1)}), bf16[8,128,256]{2,1,0:T(8,128)(2,1)S(1)}, u32[]{:S(2)}, u32[]{:S(2)}) async-start(bf16[8,128,256]{2,1,0:T(8,128)(2,1)} %bitcast.3), calls=%async_computation.2 | async-start | bytes 1048576 | tf_op jit(solution)/shard_map/all_to_all | solution.py:489
  36.9 0.5 collective-permute-start.4
  37.4 3.4 %collective-permute-start.2 = (s32[8,512]{1,0:T(8,128)S(1)}, s32[8,512]{1,0:T(8,128)S(1)}, u32[]{:S(2)}, u32[]{:S(2)}) collective-permute-start(s32[8,512]{1,0:T(8,128)S(1)} %get-tuple-element.63), channel_id=1, source_target_pairs={{0,16},{2,18},{4,20},{6,22},{8,24},{10,26},{12,28},{14,30},{16,0},... | collective-permute-start | bytes 49160 | tf_op jit(solution)/shard_map/ppermute | solution.py:501
  40.8 0.6 shard_map.132.left_ref
  41.5 2.0 %copy-done.2 = bf16[2048,1024]{1,0:T(8,128)(2,1)} copy-done((bf16[2048,1024]{1,0:T(8,128)(2,1)}, bf16[2048,1024]{1,0:T(8,128)(2,1)S(1)}, u32[]{:S(2)}) %copy-start.2) | copy-done | bytes 4194328
  43.5 0.5 shard_map.131.place_ref
  44.0 2.0 %copy-done.4 = bf16[1024,2048]{1,0:T(8,128)(2,1)} copy-done((bf16[1024,2048]{1,0:T(8,128)(2,1)}, bf16[1024,2048]{1,0:T(8,128)(2,1)S(1)}, u32[]{:S(2)}) %copy-start.4) | copy-done | bytes 4194328
  46.0 2.8 %shard_map.130.left_ref = bf16[1024,2048]{1,0:T(8,128)(2,1)S(1)} custom-call(s32[16,512]{1,0:T(8,128)S(1)} %add_select_fusion.ids_ref), custom_call_target="tpu_custom_call" | custom-call | flops 16777216 | bytes 4194304 | tf_op jit(solution)/shard_map/pallas_call | solution.py:137
  48.8 2.0 %copy-done = bf16[1024,2048]{1,0:T(8,128)(2,1)} copy-done((bf16[1024,2048]{1,0:T(8,128)(2,1)}, bf16[1024,2048]{1,0:T(8,128)(2,1)S(1)}, u32[]{:S(2)}) %copy-start) | copy-done | bytes 4194328
  50.8 2.3 %copy-done.5 = bf16[1024,2048]{1,0:T(8,128)(2,1)S(1)} copy-done((bf16[1024,2048]{1,0:T(8,128)(2,1)S(1)}, bf16[1024,2048]{1,0:T(8,128)(2,1)}, u32[]{:S(2)}) %copy-start.5) | copy-done | bytes 4194328
  53.1 8.3 %shard_map.133 = (f32[1,128]{1,0:T(1,128)}, bf16[1024,256]{1,0:T(8,128)(2,1)S(1)}, bf16[1024,512]{1,0:T(8,128)(2,1)S(1)}, bf16[1024,512]{1,0:T(8,128)(2,1)S(1)}) custom-call(s32[1]{0:T(128)} %bitcast.swap_ref.share_ref, bf16[1024,2048]{1,0:T(8,128)(2,1)S(1)} %copy-done.5, bf16[1024,256]{1,0:T(8,128)(2,1)S(1)} %bitcast.17, bf16[1024,256]{1,0:T(8,128)(2,1)S(1)} %bitcast.18, ...), custom_call_target="tpu_custom_call" | custom-call | flops 1879048192 | bytes 5242880 | tf_op jit(solution)/shard_map/pallas_call | solution.py:303
  61.4 2.3 %shard_map.134 = bf16[2048,256]{1,0:T(8,128)(2,1)} custom-call(bf16[2048,1024]{1,0:T(8,128)(2,1)S(1)} %copy-done.3, bf16[1024,256]{1,0:T(8,128)(2,1)S(1)} %get-tuple-element.32.right_ref), custom_call_target="tpu_custom_call" | custom-call | flops 1073741824 | bytes 4718592 | tf_op jit(solution)/shard_map/pallas_call | solution.py:214
  63.7 0.4 collective-permute-done.5
  64.1 0.3 add_convert_fusion
  64.4 5.1 %all-to-all-start.3 = ((bf16[16,128,256]{2,1,0:T(8,128)(2,1)}), bf16[16,128,256]{2,1,0:T(8,128)(2,1)S(1)}, u32[]{:S(2)}, u32[]{:S(2)}) async-start(bf16[16,128,256]{2,1,0:T(8,128)(2,1)} %bitcast.9), calls=%async_computation.3 | async-start | bytes 2097152 | tf_op jit(solution)/shard_map/all_to_all | solution.py:517
  69.6 2.0 %collective-permute-start.6 = (bf16[256,512]{1,0:T(8,128)(2,1)S(1)}, bf16[256,512]{1,0:T(8,128)(2,1)S(1)}, u32[]{:S(2)}, u32[]{:S(2)}) collective-permute-start(bf16[256,512]{1,0:T(8,128)(2,1)S(1)} %get-tuple-element.47), channel_id=1, source_target_pairs={{2,0},{0,2},{6,4},{4,6},{10,8},{8,10},{14,12},{12,14},{18,16},{16,... | collective-permute-start | bytes 786440 | tf_op jit(solution)/shard_map/ppermute | solution.py:405
  71.5 1.5 %collective-permute-start.7 = (bf16[256,512]{1,0:T(8,128)(2,1)S(1)}, bf16[256,512]{1,0:T(8,128)(2,1)S(1)}, u32[]{:S(2)}, u32[]{:S(2)}) collective-permute-start(bf16[256,512]{1,0:T(8,128)(2,1)S(1)} %get-tuple-element.49), channel_id=1, source_target_pairs={{4,0},{6,2},{0,4},{2,6},{12,8},{14,10},{8,12},{10,14},{20,16},{22,... | collective-permute-start | bytes 786440 | tf_op jit(solution)/shard_map/ppermute | solution.py:405
  73.0 0.1 collective-permute-start.8
  73.1 14.1 %collective-permute-done.6 = bf16[256,512]{1,0:T(8,128)(2,1)S(1)} collective-permute-done((bf16[256,512]{1,0:T(8,128)(2,1)S(1)}, bf16[256,512]{1,0:T(8,128)(2,1)S(1)}, u32[]{:S(2)}, u32[]{:S(2)}) %collective-permute-start.6) | collective-permute-done | bytes 262176 | tf_op jit(solution)/shard_map/ppermute | solution.py:405
  87.2 2.3 %collective-permute-done.7 = bf16[256,512]{1,0:T(8,128)(2,1)S(1)} collective-permute-done((bf16[256,512]{1,0:T(8,128)(2,1)S(1)}, bf16[256,512]{1,0:T(8,128)(2,1)S(1)}, u32[]{:S(2)}, u32[]{:S(2)}) %collective-permute-start.7) | collective-permute-done | bytes 262176 | tf_op jit(solution)/shard_map/ppermute | solution.py:405
  89.4 6.8 %collective-permute-done.8 = bf16[256,512]{1,0:T(8,128)(2,1)} collective-permute-done((bf16[256,512]{1,0:T(8,128)(2,1)S(1)}, bf16[256,512]{1,0:T(8,128)(2,1)}, u32[]{:S(2)}, u32[]{:S(2)}) %collective-permute-start.8) | collective-permute-done | bytes 262176 | tf_op jit(solution)/shard_map/ppermute | solution.py:405
  96.2 1.1 add_convert_fusion.1
  97.4 3.1 %collective-permute-start.10 = (bf16[64,512]{1,0:T(8,128)(2,1)S(1)}, bf16[64,512]{1,0:T(8,128)(2,1)S(1)}, u32[]{:S(2)}, u32[]{:S(2)}) collective-permute-start(bf16[64,512]{1,0:T(8,128)(2,1)S(1)} %get-tuple-element.61), channel_id=1, source_target_pairs={{16,0},{18,2},{20,4},{22,6},{24,8},{26,10},{28,12},{30,14},{0,16},... | collective-permute-start | bytes 196616 | tf_op jit(solution)/shard_map/ppermute | solution.py:405
  100.4 0.6 collective-permute-start.9
  101.1 3.0 %collective-permute-done.10 = bf16[64,512]{1,0:T(8,128)(2,1)S(1)} collective-permute-done((bf16[64,512]{1,0:T(8,128)(2,1)S(1)}, bf16[64,512]{1,0:T(8,128)(2,1)S(1)}, u32[]{:S(2)}, u32[]{:S(2)}) %collective-permute-start.10) | collective-permute-done | bytes 65568 | tf_op jit(solution)/shard_map/ppermute | solution.py:405
  104.0 2.5 %collective-permute-done.11 = bf16[64,512]{1,0:T(8,128)(2,1)S(1)} collective-permute-done((bf16[64,512]{1,0:T(8,128)(2,1)S(1)}, bf16[64,512]{1,0:T(8,128)(2,1)S(1)}, u32[]{:S(2)}, u32[]{:S(2)}) %collective-permute-start.11) | collective-permute-done | bytes 65568 | tf_op jit(solution)/shard_map/ppermute | solution.py:405
  106.9 2.4 %collective-permute-start.13 = (bf16[64,512]{1,0:T(8,128)(2,1)S(1)}, bf16[64,512]{1,0:T(8,128)(2,1)S(1)}, u32[]{:S(2)}, u32[]{:S(2)}) collective-permute-start(bf16[64,512]{1,0:T(8,128)(2,1)S(1)} %get-tuple-element.46), channel_id=1, source_target_pairs={{16,0},{18,2},{20,4},{22,6},{24,8},{26,10},{28,12},{30,14},{0,16},... | collective-permute-start | bytes 196616 | tf_op jit(solution)/shard_map/ppermute | solution.py:416
  109.2 1.8 %collective-permute-start.14 = (bf16[64,512]{1,0:T(8,128)(2,1)S(1)}, bf16[64,512]{1,0:T(8,128)(2,1)S(1)}, u32[]{:S(2)}, u32[]{:S(2)}) collective-permute-start(bf16[64,512]{1,0:T(8,128)(2,1)S(1)} %get-tuple-element.46), channel_id=1, source_target_pairs={{24,0},{26,2},{28,4},{30,6},{16,8},{18,10},{20,12},{22,14},{8,16},... | collective-permute-start | bytes 196616 | tf_op jit(solution)/shard_map/ppermute | solution.py:416
  111.0 2.3 %collective-permute-done.13 = bf16[64,512]{1,0:T(8,128)(2,1)S(1)} collective-permute-done((bf16[64,512]{1,0:T(8,128)(2,1)S(1)}, bf16[64,512]{1,0:T(8,128)(2,1)S(1)}, u32[]{:S(2)}, u32[]{:S(2)}) %collective-permute-start.13) | collective-permute-done | bytes 65568 | tf_op jit(solution)/shard_map/ppermute | solution.py:416
  113.3 2.0 %collective-permute-done.14 = bf16[64,512]{1,0:T(8,128)(2,1)S(1)} collective-permute-done((bf16[64,512]{1,0:T(8,128)(2,1)S(1)}, bf16[64,512]{1,0:T(8,128)(2,1)S(1)}, u32[]{:S(2)}, u32[]{:S(2)}) %collective-permute-start.14) | collective-permute-done | bytes 65568 | tf_op jit(solution)/shard_map/ppermute | solution.py:416
  115.3 2.2 %copy-done.1 = bf16[1024,2048]{1,0:T(8,128)(2,1)S(1)} copy-done((bf16[1024,2048]{1,0:T(8,128)(2,1)S(1)}, bf16[1024,2048]{1,0:T(8,128)(2,1)}, u32[]{:S(2)}) %copy-start.1) | copy-done | bytes 4194328
  117.5 1.2 shard_map.135.mine_ref
  118.9 1.1 collective-permute-start.15
  120.0 2.4 %collective-permute-start.16 = (bf16[256,512]{1,0:T(8,128)(2,1)S(1)}, bf16[256,512]{1,0:T(8,128)(2,1)S(1)}, u32[]{:S(2)}, u32[]{:S(2)}) collective-permute-start(bf16[256,512]{1,0:T(8,128)(2,1)S(1)} %constant_dynamic-update-slice_fusion), channel_id=1, source_target_pairs={{4,0},{6,2},{0,4},{2,6},{12,8},{14,10},{8,12},{10,14},{20,16},{22,... | collective-permute-start | bytes 786440 | tf_op jit(solution)/shard_map/ppermute | solution.py:416
  122.7 5.7 %collective-permute-done.15 = bf16[256,512]{1,0:T(8,128)(2,1)S(1)} collective-permute-done((bf16[256,512]{1,0:T(8,128)(2,1)S(1)}, bf16[256,512]{1,0:T(8,128)(2,1)S(1)}, u32[]{:S(2)}, u32[]{:S(2)}) %collective-permute-start.15) | collective-permute-done | bytes 262176 | tf_op jit(solution)/shard_map/ppermute | solution.py:416
  128.5 2.0 %collective-permute-done.16 = bf16[256,512]{1,0:T(8,128)(2,1)S(1)} collective-permute-done((bf16[256,512]{1,0:T(8,128)(2,1)S(1)}, bf16[256,512]{1,0:T(8,128)(2,1)S(1)}, u32[]{:S(2)}, u32[]{:S(2)}) %collective-permute-start.16) | collective-permute-done | bytes 262176 | tf_op jit(solution)/shard_map/ppermute | solution.py:416
  130.7 1.9 %shard_map.136 = (bf16[1024,256]{1,0:T(8,128)(2,1)}, f32[4,128]{1,0:T(4,128)}) custom-call(s32[1]{0:T(128)} %bitcast.swap_ref.share_ref, bf16[1024,256]{1,0:T(8,128)(2,1)S(1)} %copy-done.6, bf16[1024,256]{1,0:T(8,128)(2,1)S(1)} %shard_map.135.mine_ref, bf16[1024,256]{1,0:T(8,128)(2,1)S(1)} %collective-permute-done.18.other_ref, f32[8,128]{1,0:T(8,128)S(1)} %bitcast.24), custom_call_target="tpu_custom_call" | custom-call | flops 2097152 | bytes 2097152 | tf_op jit(solution)/shard_map/pallas_call | solution.py:354
  132.7 0.9 copy-done.13
  133.7 0.3 copy-done.14
  (68 shorter events, 1.1 us)
Async XLA Ops:
  0.6 36.2 %copy-start.7 = (bf16[1024,256]{1,0:T(8,128)(2,1)S(1)}, bf16[1024,256]{1,0:T(8,128)(2,1)}, u32[]{:S(2)}) copy-start(bf16[1024,256]{1,0:T(8,128)(2,1)} %down_a_ref.1) | copy-start | bytes 1572868
  0.6 36.2 %copy-start.8 = (bf16[1024,256]{1,0:T(8,128)(2,1)S(1)}, bf16[1024,256]{1,0:T(8,128)(2,1)}, u32[]{:S(2)}) copy-start(bf16[1024,256]{1,0:T(8,128)(2,1)} %up_a_ref.1) | copy-start | bytes 1572868
  0.7 36.7 %copy-start.9 = (s32[16,128]{1,0:T(8,128)S(1)}, s32[16,128]{1,0:T(8,128)}, u32[]{:S(2)}) copy-start(s32[16,128]{1,0:T(8,128)} %goals_ref.1) | copy-start | bytes 24580
  0.7 40.2 %copy-start.15 = (bf16[2048]{0:T(1024)(128)(2,1)S(1)}, bf16[2048]{0:T(1024)(128)(2,1)}, u32[]{:S(2)}) copy-start(bf16[2048]{0:T(1024)(128)(2,1)} %param.14) | copy-start | bytes 12292
  1.9 18.1 %collective-permute-start = (bf16[512,256]{1,0:T(8,128)(2,1)S(1)}, bf16[512,256]{1,0:T(8,128)(2,1)S(1)}, u32[]{:S(2)}, u32[]{:S(2)}) collective-permute-start(bf16[512,256]{1,0:T(8,128)(2,1)S(1)} %get-tuple-element.58), channel_id=1, source_target_pairs={{0,16},{2,18},{4,20},{6,22},{8,24},{10,26},{12,28},{14,30},{16,0},... | collective-permute-start | bytes 786440 | tf_op jit(solution)/shard_map/ppermute | solution.py:471
  22.2 11.1 %all-to-all-start.1 = ((bf16[8,128,256]{2,1,0:T(8,128)(2,1)}), bf16[8,128,256]{2,1,0:T(8,128)(2,1)S(1)}, u32[]{:S(2)}, u32[]{:S(2)}) async-start(bf16[8,128,256]{2,1,0:T(8,128)(2,1)} %bitcast.1), calls=%async_computation.1 | async-start | bytes 1048576 | tf_op jit(solution)/shard_map/all_to_all | solution.py:489
  25.7 1.6 %collective-permute-start.1 = (bf16[512,256]{1,0:T(8,128)(2,1)S(1)}, bf16[512,256]{1,0:T(8,128)(2,1)S(1)}, u32[]{:S(2)}, u32[]{:S(2)}) collective-permute-start(bf16[512,256]{1,0:T(8,128)(2,1)S(1)} %collective-permute-done.first_ref), channel_id=1, source_target_pairs={{1,0},{0,1},{3,2},{2,3},{5,4},{4,5},{7,6},{6,7},{9,8},{8,9},{11,10... | collective-permute-start | bytes 786440 | tf_op jit(solution)/shard_map/ppermute | solution.py:465
  33.3 17.5 %all-to-all-start.2 = ((bf16[8,128,256]{2,1,0:T(8,128)(2,1)}), bf16[8,128,256]{2,1,0:T(8,128)(2,1)S(1)}, u32[]{:S(2)}, u32[]{:S(2)}) async-start(bf16[8,128,256]{2,1,0:T(8,128)(2,1)} %bitcast.3), calls=%async_computation.2 | async-start | bytes 1048576 | tf_op jit(solution)/shard_map/all_to_all | solution.py:489
  36.8 14.0 %collective-permute-start.3 = (bf16[1024,256]{1,0:T(8,128)(2,1)S(1)}, bf16[1024,256]{1,0:T(8,128)(2,1)S(1)}, u32[]{:S(2)}, u32[]{:S(2)}) collective-permute-start(bf16[1024,256]{1,0:T(8,128)(2,1)S(1)} %copy-done.7), channel_id=1, source_target_pairs={{1,0},{0,1},{3,2},{2,3},{5,4},{4,5},{7,6},{6,7},{9,8},{8,9},{11,10... | collective-permute-start | bytes 1572872 | tf_op jit(solution)/shard_map/ppermute | solution.py:465
  36.9 13.9 %collective-permute-start.4 = (bf16[1024,256]{1,0:T(8,128)(2,1)S(1)}, bf16[1024,256]{1,0:T(8,128)(2,1)S(1)}, u32[]{:S(2)}, u32[]{:S(2)}) collective-permute-start(bf16[1024,256]{1,0:T(8,128)(2,1)S(1)} %copy-done.8), channel_id=1, source_target_pairs={{1,0},{0,1},{3,2},{2,3},{5,4},{4,5},{7,6},{6,7},{9,8},{8,9},{11,10... | collective-permute-start | bytes 1572872 | tf_op jit(solution)/shard_map/ppermute | solution.py:465
  37.4 8.6 %collective-permute-start.2 = (s32[8,512]{1,0:T(8,128)S(1)}, s32[8,512]{1,0:T(8,128)S(1)}, u32[]{:S(2)}, u32[]{:S(2)}) collective-permute-start(s32[8,512]{1,0:T(8,128)S(1)} %get-tuple-element.63), channel_id=1, source_target_pairs={{0,16},{2,18},{4,20},{6,22},{8,24},{10,26},{12,28},{14,30},{16,0},... | collective-permute-start | bytes 49160 | tf_op jit(solution)/shard_map/ppermute | solution.py:501
  41.5 2.0 %copy-start.2 = (bf16[2048,1024]{1,0:T(8,128)(2,1)}, bf16[2048,1024]{1,0:T(8,128)(2,1)S(1)}, u32[]{:S(2)}) copy-start(bf16[2048,1024]{1,0:T(8,128)(2,1)S(1)} %shard_map.132.left_ref) | copy-start | bytes 12582916
  43.5 7.3 %copy-start.10 = (f32[2048]{0:T(1024)S(1)}, f32[2048]{0:T(1024)}, u32[]{:S(2)}) copy-start(f32[2048]{0:T(1024)} %param.13) | copy-start | bytes 24580
  43.5 7.3 %copy-start.12 = (f32[128]{0:T(128)S(1)}, f32[128]{0:T(128)}, u32[]{:S(2)}) copy-start(f32[128]{0:T(128)} %param.15) | copy-start | bytes 1540
  44.0 2.1 %copy-start.4 = (bf16[1024,2048]{1,0:T(8,128)(2,1)}, bf16[1024,2048]{1,0:T(8,128)(2,1)S(1)}, u32[]{:S(2)}) copy-start(bf16[1024,2048]{1,0:T(8,128)(2,1)S(1)} %shard_map.131.place_ref) | copy-start | bytes 12582916
  48.8 2.0 %copy-start = (bf16[1024,2048]{1,0:T(8,128)(2,1)}, bf16[1024,2048]{1,0:T(8,128)(2,1)S(1)}, u32[]{:S(2)}) copy-start(bf16[1024,2048]{1,0:T(8,128)(2,1)S(1)} %shard_map.130.left_ref) | copy-start | bytes 12582916
  50.8 10.6 %copy-start.3 = (bf16[2048,1024]{1,0:T(8,128)(2,1)S(1)}, bf16[2048,1024]{1,0:T(8,128)(2,1)}, u32[]{:S(2)}) copy-start(bf16[2048,1024]{1,0:T(8,128)(2,1)} %copy-done.2) | copy-start | bytes 12582916
  50.8 2.3 %copy-start.5 = (bf16[1024,2048]{1,0:T(8,128)(2,1)S(1)}, bf16[1024,2048]{1,0:T(8,128)(2,1)}, u32[]{:S(2)}) copy-start(bf16[1024,2048]{1,0:T(8,128)(2,1)} %copy-done.4) | copy-start | bytes 12582916
  61.4 2.7 %collective-permute-start.5 = (bf16[1024,512]{1,0:T(8,128)(2,1)S(1)}, bf16[1024,512]{1,0:T(8,128)(2,1)S(1)}, u32[]{:S(2)}, u32[]{:S(2)}) collective-permute-start(bf16[1024,512]{1,0:T(8,128)(2,1)S(1)} %get-tuple-element.34), channel_id=1, source_target_pairs={{1,0},{0,1},{3,2},{2,3},{5,4},{4,5},{7,6},{6,7},{9,8},{8,9},{11,10... | collective-permute-start | bytes 3145736 | tf_op jit(solution)/shard_map/ppermute | solution.py:511
  64.4 50.9 %all-to-all-start.3 = ((bf16[16,128,256]{2,1,0:T(8,128)(2,1)}), bf16[16,128,256]{2,1,0:T(8,128)(2,1)S(1)}, u32[]{:S(2)}, u32[]{:S(2)}) async-start(bf16[16,128,256]{2,1,0:T(8,128)(2,1)} %bitcast.9), calls=%async_computation.3 | async-start | bytes 2097152 | tf_op jit(solution)/shard_map/all_to_all | solution.py:517
  69.6 17.6 %collective-permute-start.6 = (bf16[256,512]{1,0:T(8,128)(2,1)S(1)}, bf16[256,512]{1,0:T(8,128)(2,1)S(1)}, u32[]{:S(2)}, u32[]{:S(2)}) collective-permute-start(bf16[256,512]{1,0:T(8,128)(2,1)S(1)} %get-tuple-element.47), channel_id=1, source_target_pairs={{2,0},{0,2},{6,4},{4,6},{10,8},{8,10},{14,12},{12,14},{18,16},{16,... | collective-permute-start | bytes 786440 | tf_op jit(solution)/shard_map/ppermute | solution.py:405
  71.5 17.9 %collective-permute-start.7 = (bf16[256,512]{1,0:T(8,128)(2,1)S(1)}, bf16[256,512]{1,0:T(8,128)(2,1)S(1)}, u32[]{:S(2)}, u32[]{:S(2)}) collective-permute-start(bf16[256,512]{1,0:T(8,128)(2,1)S(1)} %get-tuple-element.49), channel_id=1, source_target_pairs={{4,0},{6,2},{0,4},{2,6},{12,8},{14,10},{8,12},{10,14},{20,16},{22,... | collective-permute-start | bytes 786440 | tf_op jit(solution)/shard_map/ppermute | solution.py:405
  73.0 23.3 %collective-permute-start.8 = (bf16[256,512]{1,0:T(8,128)(2,1)S(1)}, bf16[256,512]{1,0:T(8,128)(2,1)}, u32[]{:S(2)}, u32[]{:S(2)}) collective-permute-start(bf16[256,512]{1,0:T(8,128)(2,1)S(1)} %get-tuple-element.48), channel_id=1, source_target_pairs={{6,0},{4,2},{2,4},{0,6},{14,8},{12,10},{10,12},{8,14},{22,16},{20,... | collective-permute-start | bytes 786440 | tf_op jit(solution)/shard_map/ppermute | solution.py:405
  97.4 6.7 %collective-permute-start.10 = (bf16[64,512]{1,0:T(8,128)(2,1)S(1)}, bf16[64,512]{1,0:T(8,128)(2,1)S(1)}, u32[]{:S(2)}, u32[]{:S(2)}) collective-permute-start(bf16[64,512]{1,0:T(8,128)(2,1)S(1)} %get-tuple-element.61), channel_id=1, source_target_pairs={{16,0},{18,2},{20,4},{22,6},{24,8},{26,10},{28,12},{30,14},{0,16},... | collective-permute-start | bytes 196616 | tf_op jit(solution)/shard_map/ppermute | solution.py:405
  100.4 6.1 %collective-permute-start.11 = (bf16[64,512]{1,0:T(8,128)(2,1)S(1)}, bf16[64,512]{1,0:T(8,128)(2,1)S(1)}, u32[]{:S(2)}, u32[]{:S(2)}) collective-permute-start(bf16[64,512]{1,0:T(8,128)(2,1)S(1)} %get-tuple-element.60), channel_id=1, source_target_pairs={{24,0},{26,2},{28,4},{30,6},{16,8},{18,10},{20,12},{22,14},{8,16},... | collective-permute-start | bytes 196616 | tf_op jit(solution)/shard_map/ppermute | solution.py:405
  100.4 6.1 %collective-permute-start.9 = (bf16[64,512]{1,0:T(8,128)(2,1)S(1)}, bf16[64,512]{1,0:T(8,128)(2,1)S(1)}, u32[]{:S(2)}, u32[]{:S(2)}) collective-permute-start(bf16[64,512]{1,0:T(8,128)(2,1)S(1)} %get-tuple-element.59), channel_id=1, source_target_pairs={{8,0},{10,2},{12,4},{14,6},{0,8},{2,10},{4,12},{6,14},{24,16},{26,... | collective-permute-start | bytes 196616 | tf_op jit(solution)/shard_map/ppermute | solution.py:405
  106.6 4.5 %collective-permute-start.12 = (bf16[64,512]{1,0:T(8,128)(2,1)S(1)}, bf16[64,512]{1,0:T(8,128)(2,1)S(1)}, u32[]{:S(2)}, u32[]{:S(2)}) collective-permute-start(bf16[64,512]{1,0:T(8,128)(2,1)S(1)} %get-tuple-element.46), channel_id=1, source_target_pairs={{8,0},{10,2},{12,4},{14,6},{0,8},{2,10},{4,12},{6,14},{24,16},{26,... | collective-permute-start | bytes 196616 | tf_op jit(solution)/shard_map/ppermute | solution.py:416
  106.9 6.5 %collective-permute-start.13 = (bf16[64,512]{1,0:T(8,128)(2,1)S(1)}, bf16[64,512]{1,0:T(8,128)(2,1)S(1)}, u32[]{:S(2)}, u32[]{:S(2)}) collective-permute-start(bf16[64,512]{1,0:T(8,128)(2,1)S(1)} %get-tuple-element.46), channel_id=1, source_target_pairs={{16,0},{18,2},{20,4},{22,6},{24,8},{26,10},{28,12},{30,14},{0,16},... | collective-permute-start | bytes 196616 | tf_op jit(solution)/shard_map/ppermute | solution.py:416
  109.2 6.1 %collective-permute-start.14 = (bf16[64,512]{1,0:T(8,128)(2,1)S(1)}, bf16[64,512]{1,0:T(8,128)(2,1)S(1)}, u32[]{:S(2)}, u32[]{:S(2)}) collective-permute-start(bf16[64,512]{1,0:T(8,128)(2,1)S(1)} %get-tuple-element.46), channel_id=1, source_target_pairs={{24,0},{26,2},{28,4},{30,6},{16,8},{18,10},{20,12},{22,14},{8,16},... | collective-permute-start | bytes 196616 | tf_op jit(solution)/shard_map/ppermute | solution.py:416
  115.3 2.2 %copy-start.1 = (bf16[1024,2048]{1,0:T(8,128)(2,1)S(1)}, bf16[1024,2048]{1,0:T(8,128)(2,1)}, u32[]{:S(2)}) copy-start(bf16[1024,2048]{1,0:T(8,128)(2,1)} %copy-done) | copy-start | bytes 12582916
  118.8 11.9 %copy-start.6 = (bf16[1024,256]{1,0:T(8,128)(2,1)S(1)}, bf16[1024,256]{1,0:T(8,128)(2,1)}, u32[]{:S(2)}) copy-start(bf16[1024,256]{1,0:T(8,128)(2,1)} %rows_ref.1) | copy-start | bytes 1572868
  118.8 11.9 %copy-start.11 = (f32[1024]{0:T(1024)S(1)}, f32[1024]{0:T(1024)}, u32[]{:S(2)}) copy-start(f32[1024]{0:T(1024)} %param.10) | copy-start | bytes 12292
  118.8 13.8 %collective-permute-start.17 = (bf16[256,512]{1,0:T(8,128)(2,1)S(1)}, bf16[256,512]{1,0:T(8,128)(2,1)S(1)}, u32[]{:S(2)}, u32[]{:S(2)}) collective-permute-start(bf16[256,512]{1,0:T(8,128)(2,1)S(1)} %constant_dynamic-update-slice_fusion), channel_id=1, source_target_pairs={{6,0},{4,2},{2,4},{0,6},{14,8},{12,10},{10,12},{8,14},{22,16},{20,... | collective-permute-start | bytes 786440 | tf_op jit(solution)/shard_map/ppermute | solution.py:416
  118.9 9.5 %collective-permute-start.15 = (bf16[256,512]{1,0:T(8,128)(2,1)S(1)}, bf16[256,512]{1,0:T(8,128)(2,1)S(1)}, u32[]{:S(2)}, u32[]{:S(2)}) collective-permute-start(bf16[256,512]{1,0:T(8,128)(2,1)S(1)} %constant_dynamic-update-slice_fusion), channel_id=1, source_target_pairs={{2,0},{0,2},{6,4},{4,6},{10,8},{8,10},{14,12},{12,14},{18,16},{16,... | collective-permute-start | bytes 786440 | tf_op jit(solution)/shard_map/ppermute | solution.py:416
  120.0 10.5 %collective-permute-start.16 = (bf16[256,512]{1,0:T(8,128)(2,1)S(1)}, bf16[256,512]{1,0:T(8,128)(2,1)S(1)}, u32[]{:S(2)}, u32[]{:S(2)}) collective-permute-start(bf16[256,512]{1,0:T(8,128)(2,1)S(1)} %constant_dynamic-update-slice_fusion), channel_id=1, source_target_pairs={{4,0},{6,2},{0,4},{2,6},{12,8},{14,10},{8,12},{10,14},{20,16},{22,... | collective-permute-start | bytes 786440 | tf_op jit(solution)/shard_map/ppermute | solution.py:416
  122.5 8.2 %collective-permute-start.18 = (bf16[1024,256]{1,0:T(8,128)(2,1)S(1)}, bf16[1024,256]{1,0:T(8,128)(2,1)S(1)}, u32[]{:S(2)}, u32[]{:S(2)}) collective-permute-start(bf16[1024,256]{1,0:T(8,128)(2,1)S(1)} %shard_map.135.mine_ref), channel_id=1, source_target_pairs={{1,0},{0,1},{3,2},{2,3},{5,4},{4,5},{7,6},{6,7},{9,8},{8,9},{11,10... | collective-permute-start | bytes 1572872 | tf_op jit(solution)/shard_map/ppermute | solution.py:530
  132.7 1.0 copy-start.13
  132.7 1.3 copy-start.14

commit v5 on v4

v5 whole, which is shorter than its diff:
```python
import functools
import math

import jax
import jax.numpy as jnp
from jax import lax
from jax.experimental import pallas as pl
from jax.experimental.pallas import tpu as pltpu
from jax.sharding import PartitionSpec as P

FEAT = 8
HOT = 4


LEARN_RATE = 0.2
LOSS_SCALE = 32.0
ADA_EPS = 1e-06


SLOTS = 128
MIB = 1024 * 1024
MOST = 56


def matmul(left, right):
    return jnp.dot(left, right, preferred_element_type=jnp.float32)


def transposed_dot(left, right):
    return lax.dot_general(
        left, right, (((0,), (0,)), ((), ())), preferred_element_type=jnp.float32
    )


def rows_dot(left, right):
    return lax.dot_general(
        left, right, (((1,), (1,)), ((), ())), preferred_element_type=jnp.float32
    )


def kernel_call(
    kernel, out_shape, cost, scratch=(), flags=0, operands=0, left=0, left_out=(), aliases=None, room=8
):
    flops, moved = cost
    smem = pl.BlockSpec(memory_space=pltpu.SMEM)
    vmem = pl.BlockSpec(memory_space=pltpu.VMEM)
    hbm = pl.BlockSpec(memory_space=pltpu.HBM)
    if isinstance(out_shape, tuple):
        out_specs = tuple(hbm if i in left_out else vmem for i in range(len(out_shape)))
    else:
        out_specs = hbm if left_out else vmem
    return pl.pallas_call(
        kernel,
        in_specs=[smem] * flags + [vmem] * operands + [hbm] * left,
        out_specs=out_specs,
        input_output_aliases=aliases or {},
        out_shape=out_shape,
        scratch_shapes=scratch,
        compiler_params=pltpu.CompilerParams(vmem_limit_bytes=room * MIB),
        cost_estimate=pl.CostEstimate(flops=flops, bytes_accessed=moved, transcendentals=0),
    )


def split_ids(ids):
    shifted = ids + 1
    high = lax.shift_right_logical(shifted, 5).astype(jnp.float32).astype(jnp.bfloat16)
    low = (shifted & 31).astype(jnp.float32).astype(jnp.bfloat16)
    return high, low


def lookup_choice():
    shape = (HOT * SLOTS, HOT * SLOTS)
    row = lax.broadcasted_iota(jnp.int32, shape, 0)
    column = lax.broadcasted_iota(jnp.int32, shape, 1)
    wanted = (row & (SLOTS - 1)) * HOT + lax.shift_right_logical(row, 7)
    return jnp.where(wanted == column, 1.0, 0.0).astype(jnp.bfloat16)


def joined(digits):
    high, low = digits
    return (high * 32.0 + low - 1.0).astype(jnp.int32)


def ones_where(mask):
    return jnp.where(mask, jnp.asarray(1, jnp.bfloat16), jnp.asarray(0, jnp.bfloat16))


def pool_kernel(
    swap_ref, ids_ref, first_ref, second_ref, rows_ref, out_ref, counts_ref, near_ref, far_ref, sem
):
    half = first_ref.shape[0]
    fetch = pltpu.make_async_copy(rows_ref, near_ref, sem)
    fetch.start()
    for i, given_ref in enumerate((first_ref, second_ref)):
        into_half = 1 - swap_ref[0] if i else swap_ref[0]
        far_ref[pl.ds(pl.multiple_of(into_half * half, half), half), :] = given_ref[...]
    blocks = ids_ref.shape[0]
    sources, _, pools, _ = out_ref.shape
    per_block = HOT * SLOTS
    choice = lookup_choice()
    for part in range(2):
        high, low = split_ids(ids_ref[:, part * per_block : (part + 1) * per_block])
        columns = joined((rows_dot(choice, high), rows_dot(choice, low))).astype(jnp.int16)
        position = lax.broadcasted_iota(jnp.int32, (SLOTS, 2 * half), 1).astype(jnp.int16)
        for block in range(blocks):
            counts = None
            for lookup in range(HOT):
                column = columns[lookup * SLOTS : (lookup + 1) * SLOTS, block : block + 1]
                found = ones_where(column == position)
                counts = found if counts is None else counts + found
            counts_ref[block * SLOTS : (block + 1) * SLOTS, :] = counts
        if part == 0:
            fetch.wait()
        sums = matmul(counts_ref[...], (far_ref if part else near_ref)[...])
        sums = sums.astype(jnp.bfloat16)
        for source in range(sources):
            out_ref[source, part] = sums[source * pools : (source + 1) * pools]


def pool_lookups(ids, swap, near_rows, far_rows, pools):
    slots = ids.shape[0] * SLOTS
    row_dev, width = near_rows.shape
    return kernel_call(
        pool_kernel,
        jax.ShapeDtypeStruct((slots // pools, 2, pools, width), jnp.bfloat16),
        (4 * slots * row_dev * width, 4 * row_dev * width + 4 * slots * width),
        [
            pltpu.VMEM((slots, row_dev), jnp.bfloat16),
            pltpu.VMEM((row_dev, width), jnp.bfloat16),
            pltpu.VMEM((row_dev, width), jnp.bfloat16),
            pltpu.SemaphoreType.DMA,
        ],
        flags=1,
        operands=3,
        left=1,
        room=MOST,
    )(swap, ids, *far_rows, near_rows)


def row_grad_kernel(ids_ref, given_ref, out_ref, counts_ref, grads_ref, sem):
    fetch = pltpu.make_async_copy(given_ref, grads_ref, sem)
    fetch.start()
    blocks = ids_ref.shape[0]
    row_dev = out_ref.shape[0]
    tile = 64
    high, low = split_ids(ids_ref[...])
    choice = lookup_choice()
    lines = joined((rows_dot(high, choice), rows_dot(low, choice)))
    position = lax.broadcasted_iota(jnp.int32, (tile, SLOTS), 0).astype(jnp.int16)
    for block in range(blocks):
        spread = []
        for lookup in range(HOT):
            line = lines[block : block + 1, lookup * SLOTS : (lookup + 1) * SLOTS]
            spread.append(jnp.broadcast_to(line, (tile, SLOTS)).astype(jnp.int16))
        for start in range(0, row_dev, tile):
            counts = None
            for lookup in range(HOT):
                found = ones_where(spread[lookup] - jnp.asarray(start, jnp.int16) == position)
                counts = found if counts is None else counts + found
            counts_ref[start : start + tile, block * SLOTS : (block + 1) * SLOTS] = counts
    fetch.wait()
    out_ref[...] = matmul(counts_ref[...], grads_ref[...]).astype(jnp.bfloat16)


def row_grads(ids, slot_grads, row_dev):
    slot_count, emb = slot_grads.shape
    return kernel_call(
        row_grad_kernel,
        jax.ShapeDtypeStruct((row_dev, emb), jnp.bfloat16),
        (2 * row_dev * slot_count * emb, 2 * slot_grads.size + 2 * row_dev * emb),
        [
            pltpu.VMEM((row_dev, slot_count), jnp.bfloat16),
            pltpu.VMEM((slot_count, emb), jnp.bfloat16),
            pltpu.SemaphoreType.DMA,
        ],
        operands=1,
        left=1,
        room=16,
    )(ids, slot_grads)


def diagonal(size):
    row = lax.broadcasted_iota(jnp.int32, (size, size), 0)
    return row == lax.broadcasted_iota(jnp.int32, (size, size), 1)


def as_column(line):
    return jnp.sum(jnp.where(diagonal(line.shape[1]), line, 0.0), axis=1, keepdims=True)


def as_line(column):
    return jnp.sum(jnp.where(diagonal(column.shape[0]), column, 0.0), axis=0, keepdims=True)


def return_kernel(goals_ref, grads_ref, out_ref, pick_ref):
    blocks = goals_ref.shape[0]
    bags = grads_ref.shape[0]
    samples = bags // FEAT
    high, low = split_ids(goals_ref[...])
    unit = ones_where(diagonal(SLOTS))
    columns = joined((rows_dot(unit, high), rows_dot(unit, low))).astype(jnp.int16)
    place = lax.broadcasted_iota(jnp.int32, (SLOTS, bags), 1)
    order = ((place % samples) * FEAT + place // samples).astype(jnp.int16)
    for block in range(blocks):
        pick_ref[block * SLOTS : (block + 1) * SLOTS, :] = ones_where(
            columns[:, block : block + 1] == order
        )
    out_ref[...] = matmul(pick_ref[...], grads_ref[...]).astype(jnp.bfloat16)


def return_grads(goals, grads):
    bags, emb = grads.shape
    slot_count = goals.size
    return kernel_call(
        return_kernel,
        jax.ShapeDtypeStruct((slot_count, emb), jnp.bfloat16),
        (2 * slot_count * bags * emb, 2 * grads.size + 2 * slot_count * emb),
        [pltpu.VMEM((slot_count, bags), jnp.bfloat16)],
        operands=2,
        room=12,
    )(goals.reshape(slot_count // SLOTS, SLOTS), grads)


def dense_kernel(
    swap_ref,
    goals_ref,
    bias_ref,
    weight_ref,
    target_ref,
    arrived_ref,
    down_a_ref,
    down_b_ref,
    up_a_ref,
    up_b_ref,
    logits_ref,
    grads_ref,
    kept_ref,
    sent_ref,
    place_ref,
    wide_ref,
    dcross_ref,
    shifted_ref,
    down_ref,
    up_ref,
    sems,
):
    samples = target_ref.shape[1]
    width, rank = down_ref.shape
    emb = width // FEAT
    half = width // 2
    fetches = []
    for source_ref, goal_ref, second in (
        (down_a_ref, down_ref, False),
        (down_b_ref, down_ref, True),
        (up_a_ref, up_ref, False),
        (up_b_ref, up_ref, True),
    ):
        into_half = 1 - swap_ref[0] if second else swap_ref[0]
        spot = pl.ds(pl.multiple_of(into_half * half, half), half)
        fetches.append(
            pltpu.make_async_copy(source_ref, goal_ref.at[spot, :], sems.at[len(fetches)])
        )
        fetches[-1].start()
    chunk = 512
    first_bag = lax.broadcasted_iota(jnp.int32, (samples, chunk), 0) * FEAT
    for start in range(0, goals_ref.shape[1], chunk):
        line = goals_ref[:, start : start + chunk]
        nth = (jnp.broadcast_to(line, (samples, chunk)) - first_bag).astype(jnp.int16)
        for f in range(FEAT):
            place_ref[f * samples : (f + 1) * samples, start : start + chunk] = ones_where(
                nth == jnp.asarray(f, jnp.int16)
            )
    features = [slice(f * emb, (f + 1) * emb) for f in range(FEAT)]
    for f, part in enumerate(features):
        spot = slice(f * samples, (f + 1) * samples)
        wide_ref[:, part] = matmul(place_ref[spot, :], arrived_ref[...]).astype(jnp.bfloat16)
    for fetch in fetches:
        fetch.wait()
    hidden = matmul(wide_ref[...], down_ref[...]).astype(jnp.bfloat16)
    summed = jnp.zeros((samples, emb), jnp.float32)
    for part in features:
        shifted = rows_dot(hidden, up_ref[part, :]) + bias_ref[:, part]
        shifted_ref[:, part] = shifted
        feats = wide_ref[:, part].astype(jnp.float32)
        summed = summed + (feats * shifted + feats) * weight_ref[:, part].astype(jnp.float32)
    logits = jnp.sum(summed, axis=1, keepdims=True)
    logits_ref[...] = as_line(logits)
    dlogit = LOSS_SCALE * (jax.nn.sigmoid(logits) - as_column(target_ref[...]))
    for part in features:
        dmixed = dlogit * weight_ref[:, part].astype(jnp.float32)
        feats = wide_ref[:, part].astype(jnp.float32)
        dcross_ref[:, part] = (dmixed * feats).astype(jnp.bfloat16)
    dhidden = matmul(dcross_ref[...], up_ref[...]).astype(jnp.bfloat16)
    for f, part in enumerate(features):
        dmixed = dlogit * weight_ref[:, part].astype(jnp.float32)
        back_term = rows_dot(dhidden, down_ref[part, :])
        grads = dmixed * (shifted_ref[:, part] + 1.0) + back_term
        grads_ref[f * samples : (f + 1) * samples, :] = grads.astype(jnp.bfloat16)
    for step in range(FEAT):
        into_half = swap_ref[0] if step * emb < half else 1 - swap_ref[0]
        spot = (step * emb) % half
        part = pl.ds(pl.multiple_of(into_half * half + spot, emb), emb)
        out_ref = kept_ref if step * emb < half else sent_ref
        down_term = transposed_dot(wide_ref[:, part], dhidden)
        up_term = transposed_dot(dcross_ref[:, part], hidden)
        out_ref[spot : spot + emb, :rank] = down_term.astype(jnp.bfloat16)
        out_ref[spot : spot + emb, rank:] = up_term.astype(jnp.bfloat16)


def dense_step(swap, goals, arrived, downs, ups, bias, weight, target):
    samples = target.shape[0]
    slots, emb = arrived.shape
    width, rank = 2 * downs[0].shape[0], downs[0].shape[1]
    flops = 2 * slots * samples * width + 12 * samples * width * rank
    logits, grads, kept, sent = kernel_call(
        dense_kernel,
        (
            jax.ShapeDtypeStruct((1, samples), jnp.float32),
            jax.ShapeDtypeStruct((samples * FEAT, emb), jnp.bfloat16),
            jax.ShapeDtypeStruct((width // 2, 2 * rank), jnp.bfloat16),
            jax.ShapeDtypeStruct((width // 2, 2 * rank), jnp.bfloat16),
        ),
        (flops, 2 * arrived.size + 8 * width * rank),
        [
            pltpu.VMEM((samples * FEAT, slots), jnp.bfloat16),
            pltpu.VMEM((samples, width), jnp.bfloat16),
            pltpu.VMEM((samples, width), jnp.bfloat16),
            pltpu.VMEM((samples, width), jnp.float32),
            pltpu.VMEM((width, rank), jnp.bfloat16),
            pltpu.VMEM((width, rank), jnp.bfloat16),
            pltpu.SemaphoreType.DMA((4,)),
        ],
        flags=1,
        operands=5,
        left=4,
        room=MOST,
    )(
        swap,
        goals.reshape(1, slots),
        bias.reshape(1, width),
        weight.reshape(1, width),
        target.reshape(1, samples),
        arrived,
        *downs,
        *ups,
    )
    return logits.reshape(samples), grads, kept, sent


def spread_kernel(count, scale, aliased, spots_ref, *refs):
    piece_refs = refs[:count]
    down_out_ref, up_out_ref, down_ref, up_ref, sems = refs[count + aliased :]
    rows = piece_refs[0].shape[0]
    rank = down_ref.shape[1]
    stores = []
    for i, piece_ref in enumerate(piece_refs):
        here = slice(i * rows, (i + 1) * rows)
        spot = pl.ds(pl.multiple_of(spots_ref[i] * rows, rows), rows)
        for half, (from_ref, to_ref) in enumerate(((down_ref, down_out_ref), (up_ref, up_out_ref))):
            part = slice(half * rank, (half + 1) * rank)
            from_ref[here, :] = piece_ref[:, part].astype(jnp.float32) * scale
            stores.append(
                pltpu.make_async_copy(from_ref.at[here, :], to_ref.at[spot, :], sems.at[len(stores)])
            )
            stores[-1].start()
    for store in stores:
        store.wait()


def spread_pieces(pieces, scale, rows, given=()):
    count = len(pieces)
    spots = jnp.stack([spot for spot, _ in pieces]).astype(jnp.int32)
    arrays = [piece for _, piece in pieces]
    step, both = arrays[0].shape
    rank = both // 2
    shape = jax.ShapeDtypeStruct((rows, rank), jnp.float32)
    block = pltpu.VMEM((count * step, rank), jnp.float32)
    return kernel_call(
        functools.partial(spread_kernel, count, scale, len(given)),
        (shape, shape),
        (count * step * both, 6 * count * step * both),
        [block, block, pltpu.SemaphoreType.DMA((2 * count,))],
        flags=1,
        operands=count,
        left=len(given),
        left_out=(0, 1),
        aliases={1 + count + i: i for i in range(len(given))},
    )(spots, *arrays, *given)


def update_kernel(share_ref, rows_ref, mine_ref, other_ref, accum_ref, rows_out_ref, accum_out_ref):
    chunks = accum_ref.shape[0]
    per_share = accum_out_ref.shape[0]
    for chunk in range(chunks):
        part = slice(chunk * SLOTS, (chunk + 1) * SLOTS)
        row_grad = mine_ref[part, :].astype(jnp.float32) + other_ref[part, :].astype(jnp.float32)
        squares = jnp.mean(row_grad * row_grad, axis=1, keepdims=True)
        accum = as_column(accum_ref[chunk : chunk + 1, :]) + squares
        step = LEARN_RATE * row_grad * lax.rsqrt(accum + ADA_EPS)
        rows_out_ref[part, :] = (rows_ref[part, :].astype(jnp.float32) - step).astype(jnp.bfloat16)

        @pl.when(share_ref[0] == chunk // per_share)
        def _():
            accum_out_ref[chunk % per_share : chunk % per_share + 1, :] = as_line(accum)


def update_rows(share, rows, mine, other, accum, narrows):
    row_dev, emb = rows.shape
    chunks = row_dev // SLOTS
    new_rows, new_accum = kernel_call(
        update_kernel,
        (
            jax.ShapeDtypeStruct((row_dev, emb), jnp.bfloat16),
            jax.ShapeDtypeStruct((chunks // narrows, SLOTS), jnp.float32),
        ),
        (8 * rows.size, 8 * rows.size),
        flags=1,
        operands=4,
    )(share, rows, mine, other, accum.reshape(chunks, SLOTS))
    return new_rows, new_accum.reshape(row_dev // narrows)


def group_levels(size):
    levels = []
    stride = 1
    while size % 4 == 0:
        levels.append((stride, 4))
        stride, size = stride * 4, size // 4
    if size > 1:
        levels.append((stride, size))
    return levels


def partner_index(index, stride, group, step):
    place = (index // stride) % group
    if group & (group - 1) == 0:
        other = place ^ step
    else:
        other = (place + step) % group
    return index + (other - place) * stride


def sent_from(axis, stride, group, step):
    size = lax.axis_size(axis)
    return [(partner_index(i, stride, group, step), i) for i in range(size)]


def scattered_pieces(blocks, axis, level):
    stride, group = level
    rows = blocks.shape[0] // group
    place = (lax.axis_index(axis) // stride) % group
    pieces = [lax.dynamic_slice_in_dim(blocks, place * rows, rows, 0)]
    for step in range(1, group):
        pairs = sent_from(axis, stride, group, step)
        if group & (group - 1) == 0:
            goal = place ^ step
        else:
            goal = (place + group - step) % group
        outgoing = lax.dynamic_slice_in_dim(blocks, goal * rows, rows, 0)
        pieces.append(lax.ppermute(outgoing, axis, pairs))
    return pieces


def summed(pieces):
    total = pieces[0].astype(jnp.float32)
    for piece in pieces[1:]:
        total = total + piece.astype(jnp.float32)
    return total.astype(jnp.bfloat16)


def scatter_sum(blocks, axis, levels):
    for level in levels:
        blocks = summed(scattered_pieces(blocks, axis, level))
    return blocks


def gathered_pieces(block, axis, level):
    stride, group = level
    index = lax.axis_index(axis)
    pieces = [((index // stride) % group, block)]
    for step in range(1, group):
        origin = partner_index(index, stride, group, step)
        came = lax.ppermute(block, axis, sent_from(axis, stride, group, step))
        pieces.append(((origin // stride) % group, came))
    return pieces


def gather_blocks(block, axis, levels):
    for level in reversed(levels):
        rows = block.shape[0]
        pieces = gathered_pieces(block, axis, level)
        block = jnp.zeros((len(pieces) * rows,) + block.shape[1:], block.dtype)
        for place, piece in pieces:
            block = lax.dynamic_update_slice_in_dim(block, piece, place * rows, 0)
    return block


def local(
    table_rows, accum, factor_down, factor_up, cross_bias, out_weight, target, bag_rows, slot_target
):
    tables = lax.axis_size("table")
    narrows = lax.axis_size("narrow")
    row_dev, emb_width = table_rows.shape
    pools_per = slot_target.shape[1]
    samples = target.shape[0]
    bag_count = samples * FEAT
    slot_count = tables * pools_per
    narrow_levels = group_levels(narrows)
    table_levels = group_levels(tables)
    table_index = lax.axis_index("table")
    narrow_index = lax.axis_index("narrow")
    near_count = tables // 2
    far_half = table_index // near_count
    halves = [list(range(near_count)), list(range(near_count, tables))]
    across = [(i, (i + near_count) % tables) for i in range(tables)]
    paired = narrows == 2
    swap = (narrow_index if paired else narrow_index * 0).reshape(1)

    def near_and_far(rows):
        return tuple(
            lax.dynamic_slice_in_dim(rows, half * near_count, near_count, 0)
            for half in (far_half, 1 - far_half)
        )

    def in_order(near, far):
        return jnp.where(
            far_half == 0, jnp.concatenate([near, far]), jnp.concatenate([far, near])
        )

    def both_halves(block):
        if paired:
            return block, lax.ppermute(block, "narrow", sent_from("narrow", 1, 2, 1))
        whole = gather_blocks(block, "narrow", narrow_levels)
        return tuple(jnp.split(whole, 2, axis=0))

    share_rows = row_dev // narrows
    own_share = lax.dynamic_slice_in_dim(table_rows, narrow_index * share_rows, share_rows, 0)
    far_share = lax.ppermute(own_share, "table", across)
    downs = both_halves(factor_down)
    ups = both_halves(factor_up)

    per_window = bag_rows.shape[1]
    asked = jnp.concatenate(near_and_far(bag_rows), axis=1)
    asked = lax.all_to_all(
        asked, "table", split_axis=0, concat_axis=0, tiled=True, axis_index_groups=halves
    )
    asked, far_share = lax.optimization_barrier((asked, far_share))
    far_rows = both_halves(far_share)
    near_ids, far_ids = asked[:, :per_window], asked[:, per_window:]

    if per_window != SLOTS * HOT:
        by_block = (ids.reshape(-1, SLOTS * HOT) for ids in (near_ids, far_ids))
        asked = jnp.concatenate(tuple(by_block), axis=1)
    sums = pool_lookups(asked, swap, table_rows, far_rows, pools_per)
    arrived = lax.all_to_all(
        sums, "table", split_axis=0, concat_axis=0, tiled=True, axis_index_groups=halves
    )
    other_ids = lax.ppermute(far_ids, "table", across)
    arrived, other_ids = lax.optimization_barrier((arrived, other_ids))
    logits, bag_grads, kept, sent = dense_step(
        swap,
        jnp.stack(near_and_far(slot_target), axis=1),
        arrived.reshape(slot_count, emb_width),
        downs,
        ups,
        cross_bias,
        out_weight,
        target,
    )
    if paired:
        came = lax.ppermute(sent, "narrow", sent_from("narrow", 1, 2, 1))
        narrow_sum = (kept.astype(jnp.float32) + came.astype(jnp.float32)).astype(jnp.bfloat16)
    else:
        narrow_sum = scatter_sum(jnp.concatenate([kept, sent], axis=0), "narrow", narrow_levels)
    bag_grads, narrow_sum = lax.optimization_barrier((bag_grads, narrow_sum))
    slot_grads = return_grads(slot_target, bag_grads)
    pieces = scattered_pieces(narrow_sum, "table", table_levels[0])
    slot_grads, *pieces = lax.optimization_barrier((slot_grads, *pieces))
    returned = lax.all_to_all(
        slot_grads.reshape(tables, pools_per, emb_width),
        "table",
        split_axis=0,
        concat_axis=0,
        tiled=True,
    ).reshape(slot_count, emb_width)
    table_sum = scatter_sum(summed(pieces), "table", table_levels[1:])
    level_sum = gather_blocks(table_sum, "table", table_levels[1:])
    pieces = gathered_pieces(level_sum, "table", table_levels[0])
    all_ids = in_order(near_ids, other_ids).reshape(-1, SLOTS * HOT)
    sent_grad = row_grads(all_ids, returned, row_dev)
    spot, first = pieces[1]
    first, sent_grad = lax.optimization_barrier((first, sent_grad))
    pieces[1] = (spot, first)
    if paired:
        mine = sent_grad
        other = lax.ppermute(sent_grad, "narrow", sent_from("narrow", 1, 2, 1))
    else:
        share = scatter_sum(sent_grad, "narrow", narrow_levels)
        mine = gather_blocks(share, "narrow", narrow_levels)
        other = jnp.zeros_like(mine)
    new_rows, new_accum = update_rows(
        narrow_index.reshape(1), table_rows, mine, other, accum, narrows
    )
    scale = 1.0 / math.sqrt(samples * tables * narrows)
    spot, last = pieces[-1]
    grads = spread_pieces(pieces[:-1], scale, factor_down.shape[0])
    last, new_rows, new_accum, *grads = lax.optimization_barrier(
        (last, new_rows, new_accum, *grads)
    )
    down_grad, up_grad = spread_pieces([(spot, last)], scale, factor_down.shape[0], grads)
    return (logits, down_grad, up_grad, new_rows, new_accum)


def solution(mesh):
    in_specs = (
        P("table", None),
        P("table"),
        P("narrow", None),
        P("narrow", None),
        P(),
        P(),
        P(("table", "narrow")),
        P(("table", "narrow"), None),
        P(("table", "narrow"), None),
    )
    out_specs = (
        P(("table", "narrow")),
        P("narrow", None),
        P("narrow", None),
        P("table", None),
        P(("table", "narrow")),
    )
    return jax.shard_map(local, mesh=mesh, in_specs=in_specs, out_specs=out_specs, check_vma=False)
```

time: 135 us -> 143 us (1.059)
  waiting for transfers between devices: 46.3 us -> 67.6 us
  local copies, waits for them, and re-layouts: 14.4 us -> 4.99 us
  starting transfers between devices: 35.4 us -> 30.2 us
    ppermute x1, waiting for transfers between devices: 0.01 us -> 9.48 us  [local(): other_ids = lax.ppermute(far_ids, 'table', across)]
    unnamed x33 -> x25, local copies, waits for them, and re-layouts: 11.9 us -> 2.5 us
    ppermute x6, waiting for transfers between devices: 28.6 us -> 35 us  [scattered_pieces(): pieces.append(lax.ppermute(outgoing, axis, pairs))]
    ppermute x6, waiting for transfers between devices: 12 us -> 15.7 us  [gathered_pieces(): came = lax.ppermute(block, axis, sent_from(axis, stride, group, step))]
    all_to_all x2 -> x1, starting transfers between devices: 6.99 us -> 3.7 us  [local(): lax.all_to_all(sums, 'table', split_axis=0, concat_axis=0, tiled=True, ax...]
    pallas_call x7 -> x5, Pallas kernels: 11.6 us -> 14.1 us  [the longest x1 5.05 us: pool_lookups(): kernel_call(pool_kernel, jax.ShapeDtypeStruct((slots // pools, 2, pools,...]
    ppermute x1, waiting for transfers between devices: 0.4 us -> 2.82 us  [local(): came = lax.ppermute(sent, 'narrow', sent_from('narrow', 1, 2, 1))]
    ppermute x1, starting transfers between devices: 3.42 us -> 1.07 us  [local(): other_ids = lax.ppermute(far_ids, 'table', across)]
  transfers between devices with their start and end apart: 22 -> 21, of which waited for: 12 -> 12; matrix products, arithmetic and copies ran while one was open for 2% -> 2% of each run, Pallas kernels for 8% -> 7%
where the time goes in v5:
time: 143 us; the launch traced here: 142 us
  waiting for transfers between devices  67.6 us (47%)
  starting transfers between devices  30.2 us (21%)
  Pallas kernels  22.6 us (16%)
  blocking collectives  13.2 us (9%)
  local copies, waits for them, and re-layouts  4.99 us (3%)
  other arithmetic  2.37 us (2%)
    ppermute x6, waiting for transfers between devices, scattered_pieces(): pieces.append(lax.ppermute(outgoing, axis, pairs))  35 us
    ppermute x6, waiting for transfers between devices, gathered_pieces(): came = lax.ppermute(block, axis, sent_from(axis, stride, group, step))  15.7 us
    all_to_all x1, blocking collectives, local(): lax.all_to_all(asked, 'table', split_axis=0, concat_axis=0, tiled=True, a...  13.2 us
    ppermute x1, waiting for transfers between devices, local(): other_ids = lax.ppermute(far_ids, 'table', across)  9.48 us
    ppermute x6, starting transfers between devices, gathered_pieces(): came = lax.ppermute(block, axis, sent_from(axis, stride, group, step))  8.77 us
    ppermute x6, starting transfers between devices, scattered_pieces(): pieces.append(lax.ppermute(outgoing, axis, pairs))  8.01 us
    pallas_call x1, Pallas kernels, dense_step(): kernel_call(dense_kernel, (jax.ShapeDtypeStruct((1, samples), jnp.float32...  6.5 us
    pallas_call x1, Pallas kernels, pool_lookups(): kernel_call(pool_kernel, jax.ShapeDtypeStruct((slots // pools, 2, pools,...  5.05 us
  transfers between devices with their start and end apart: 21, of which 12 were waited for; matrix products, arithmetic and copies ran while one was open for 2% of the time, Pallas kernels for 7%

profile of v5, /device:TPU:0, one launch (start us, length us, event | category | flops | bytes accessed | tf_op | source)
XLA Modules:
  0.0 142.2 jit_solution(2204728122235673118)
XLA Ops:
  0.6 1.0 constant_dynamic-slice_fusion.7
  1.6 4.1 %collective-permute-start = (bf16[512,256]{1,0:T(8,128)(2,1)S(1)}, bf16[512,256]{1,0:T(8,128)(2,1)S(1)}, u32[]{:S(2)}, u32[]{:S(2)}) collective-permute-start(bf16[512,256]{1,0:T(8,128)(2,1)S(1)} %constant_dynamic-slice_fusion.7), channel_id=1, source_target_pairs={{0,16},{2,18},{4,20},{6,22},{8,24},{10,26},{12,28},{14,30},{16,0},... | collective-permute-start | bytes 786440 | tf_op jit(solution)/shard_map/ppermute | solution.py:538
  5.7 0.7 constant_dynamic-slice_fusion.9
  6.5 13.2 %all_to_all.22 = s32[8,1,1024]{2,1,0:T(1,128)S(1)} all-to-all(s32[8,1,1024]{2,1,0:T(1,128)S(1)} %all_to_all.14), channel_id=1, replica_groups={{0,2,4,6,8,10,12,14},{16,18,20,22,24,26,28,30},{1,3,5,7,9,11,13,15},{17..., dimensions={0} | all-to-all | bytes 65536 | tf_op jit(solution)/shard_map/all_to_all | solution.py:544
  19.7 0.6 copy.18
  20.3 1.5 %collective-permute-done.1.second_ref = bf16[512,256]{1,0:T(8,128)(2,1)S(1)} collective-permute-done((bf16[512,256]{1,0:T(8,128)(2,1)S(1)}, bf16[512,256]{1,0:T(8,128)(2,1)S(1)}, u32[]{:S(2)}, u32[]{:S(2)}) %collective-permute-start.1) | collective-permute-done | bytes 262176 | tf_op jit(solution)/shard_map/ppermute | solution.py:532
  21.9 0.7 copy-done.11
  22.6 5.0 %shard_map.128 = bf16[8,2,128,256]{3,2,1,0:T(8,128)(2,1)} custom-call(s32[1]{0:T(128)} %bitcast.swap_ref.share_ref, s32[8,1024]{1,0:T(8,128)} %bitcast.22, bf16[512,256]{1,0:T(8,128)(2,1)} %copy-done.10, bf16[512,256]{1,0:T(8,128)(2,1)} %copy-done.11, bf16[1024,256]{1,0:T(8,128)(2,1)} %rows_ref.3), custom_call_target="tpu_custom_call" | custom-call | flops 1073741824 | bytes 2097152 | tf_op jit(solution)/shard_map/pallas_call | solution.py:123
  27.7 3.7 %all-to-all-start.1 = ((bf16[8,2,128,256]{3,2,1,0:T(8,128)(2,1)}), bf16[8,2,128,256]{3,2,1,0:T(8,128)(2,1)S(1)}, u32[]{:S(2)}, u32[]{:S(2)}) async-start(bf16[8,2,128,256]{3,2,1,0:T(8,128)(2,1)} %shard_map.128), calls=%async_computation.1 | async-start | bytes 2097152 | tf_op jit(solution)/shard_map/all_to_all | solution.py:555
  31.4 0.2 collective-permute-start.3
  31.6 0.4 collective-permute-start.4
  32.0 1.1 collective-permute-start.2
  33.1 0.6 pad_add_fusion.1
  33.7 0.6 reshape.49.weight_ref
  34.3 9.5 %collective-permute-done.2 = s32[8,512]{1,0:T(8,128)S(1)} collective-permute-done((s32[8,512]{1,0:T(8,128)S(1)}, s32[8,512]{1,0:T(8,128)S(1)}, u32[]{:S(2)}, u32[]{:S(2)}) %collective-permute-start.2) | collective-permute-done | bytes 16416 | tf_op jit(solution)/shard_map/ppermute | solution.py:558
  43.8 3.1 %all-to-all-done.1 = bf16[8,2,128,256]{3,2,1,0:T(8,128)(2,1)S(1)} async-done(((bf16[8,2,128,256]{3,2,1,0:T(8,128)(2,1)}), bf16[8,2,128,256]{3,2,1,0:T(8,128)(2,1)S(1)}, u32[]{:S(2)}, u32[]{:S(2)}) %all-to-all-start.1) | async-done | bytes 1048608 | tf_op jit(solution)/shard_map/all_to_all | solution.py:555
  46.8 1.0 copy-done.4
  47.8 0.2 copy-done.9
  48.0 6.5 %shard_map.129 = (f32[1,128]{1,0:T(1,128)}, bf16[1024,256]{1,0:T(8,128)(2,1)}, bf16[1024,512]{1,0:T(8,128)(2,1)}, bf16[1024,512]{1,0:T(8,128)(2,1)}) custom-call(s32[1]{0:T(128)} %bitcast.swap_ref.share_ref, s32[1,2048]{1,0:T(1,128)} %bitcast.26, f32[1,2048]{1,0:T(1,128)} %bitcast.27, bf16[1,2048]{1,0:T(2,128)(2,1)} %reshape.49.weight_ref, ...), custom_call_target="tpu_custom_call" | custom-call | flops 1879048192 | bytes 5242880 | tf_op jit(solution)/shard_map/pallas_call | solution.py:315
  54.6 2.8 %collective-permute-done.5 = bf16[1024,512]{1,0:T(8,128)(2,1)S(1)} collective-permute-done((bf16[1024,512]{1,0:T(8,128)(2,1)}, bf16[1024,512]{1,0:T(8,128)(2,1)S(1)}, u32[]{:S(2)}, u32[]{:S(2)}) %collective-permute-start.5) | collective-permute-done | bytes 1048608 | tf_op jit(solution)/shard_map/ppermute | solution.py:571
  57.4 1.5 %add_convert_fusion = bf16[1024,512]{1,0:T(8,128)(2,1)S(1)} fusion(bf16[1024,512]{1,0:T(8,128)(2,1)S(1)} %collective-permute-done.5, bf16[1024,512]{1,0:T(8,128)(2,1)} %get-tuple-element.38), kind=kLoop, calls=%fused_computation | loop fusion | flops 2097152 | bytes 3145728 | tf_op jit(solution)/shard_map/convert_element_type | solution.py:572
  58.9 0.1 constant_dynamic-slice_fusion.3
  59.0 1.3 collective-permute-start.6
  60.3 1.5 %collective-permute-start.7 = (bf16[256,512]{1,0:T(8,128)(2,1)S(1)}, bf16[256,512]{1,0:T(8,128)(2,1)S(1)}, u32[]{:S(2)}, u32[]{:S(2)}) collective-permute-start(bf16[256,512]{1,0:T(8,128)(2,1)S(1)} %get-tuple-element.64), channel_id=1, source_target_pairs={{4,0},{6,2},{0,4},{2,6},{12,8},{14,10},{8,12},{10,14},{20,16},{22,... | collective-permute-start | bytes 786440 | tf_op jit(solution)/shard_map/ppermute | solution.py:460
  61.8 0.7 collective-permute-start.8
  62.6 2.4 %shard_map.130 = bf16[2048,256]{1,0:T(8,128)(2,1)} custom-call(s32[16,128]{1,0:T(8,128)S(1)} %copy-done.1, bf16[1024,256]{1,0:T(8,128)(2,1)S(1)} %copy-done.3), custom_call_target="tpu_custom_call" | custom-call | flops 1073741824 | bytes 1572864 | tf_op jit(solution)/shard_map/pallas_call | solution.py:214
  65.0 3.3 %collective-permute-done.6 = bf16[256,512]{1,0:T(8,128)(2,1)S(1)} collective-permute-done((bf16[256,512]{1,0:T(8,128)(2,1)S(1)}, bf16[256,512]{1,0:T(8,128)(2,1)S(1)}, u32[]{:S(2)}, u32[]{:S(2)}) %collective-permute-start.6) | collective-permute-done | bytes 262176 | tf_op jit(solution)/shard_map/ppermute | solution.py:460
  68.2 5.8 %collective-permute-done.7 = bf16[256,512]{1,0:T(8,128)(2,1)S(1)} collective-permute-done((bf16[256,512]{1,0:T(8,128)(2,1)S(1)}, bf16[256,512]{1,0:T(8,128)(2,1)S(1)}, u32[]{:S(2)}, u32[]{:S(2)}) %collective-permute-start.7) | collective-permute-done | bytes 262176 | tf_op jit(solution)/shard_map/ppermute | solution.py:460
  74.0 3.9 %all-to-all-start.2 = ((bf16[16,128,256]{2,1,0:T(8,128)(2,1)}), bf16[16,128,256]{2,1,0:T(8,128)(2,1)S(1)}, u32[]{:S(2)}, u32[]{:S(2)}) async-start(bf16[16,128,256]{2,1,0:T(8,128)(2,1)} %bitcast.9), calls=%async_computation.2 | async-start | bytes 2097152 | tf_op jit(solution)/shard_map/all_to_all | solution.py:579
  78.0 0.1 add_convert_fusion.1
  78.1 3.7 %collective-permute-start.11 = (bf16[64,512]{1,0:T(8,128)(2,1)S(1)}, bf16[64,512]{1,0:T(8,128)(2,1)S(1)}, u32[]{:S(2)}, u32[]{:S(2)}) collective-permute-start(bf16[64,512]{1,0:T(8,128)(2,1)S(1)} %get-tuple-element.68), channel_id=1, source_target_pairs={{24,0},{26,2},{28,4},{30,6},{16,8},{18,10},{20,12},{22,14},{8,16},... | collective-permute-start | bytes 196616 | tf_op jit(solution)/shard_map/ppermute | solution.py:460
  81.9 0.7 collective-permute-start.9
  82.6 18.5 %collective-permute-done.11 = bf16[64,512]{1,0:T(8,128)(2,1)S(1)} collective-permute-done((bf16[64,512]{1,0:T(8,128)(2,1)S(1)}, bf16[64,512]{1,0:T(8,128)(2,1)S(1)}, u32[]{:S(2)}, u32[]{:S(2)}) %collective-permute-start.11) | collective-permute-done | bytes 65568 | tf_op jit(solution)/shard_map/ppermute | solution.py:460
  101.1 7.4 %collective-permute-done.10 = bf16[64,512]{1,0:T(8,128)(2,1)S(1)} collective-permute-done((bf16[64,512]{1,0:T(8,128)(2,1)S(1)}, bf16[64,512]{1,0:T(8,128)(2,1)S(1)}, u32[]{:S(2)}, u32[]{:S(2)}) %collective-permute-start.10) | collective-permute-done | bytes 65568 | tf_op jit(solution)/shard_map/ppermute | solution.py:460
  108.8 1.8 %collective-permute-start.13 = (bf16[64,512]{1,0:T(8,128)(2,1)S(1)}, bf16[64,512]{1,0:T(8,128)(2,1)S(1)}, u32[]{:S(2)}, u32[]{:S(2)}) collective-permute-start(bf16[64,512]{1,0:T(8,128)(2,1)S(1)} %get-tuple-element.62), channel_id=1, source_target_pairs={{16,0},{18,2},{20,4},{22,6},{24,8},{26,10},{28,12},{30,14},{0,16},... | collective-permute-start | bytes 196616 | tf_op jit(solution)/shard_map/ppermute | solution.py:483
  110.6 2.5 %collective-permute-start.14 = (bf16[64,512]{1,0:T(8,128)(2,1)S(1)}, bf16[64,512]{1,0:T(8,128)(2,1)S(1)}, u32[]{:S(2)}, u32[]{:S(2)}) collective-permute-start(bf16[64,512]{1,0:T(8,128)(2,1)S(1)} %get-tuple-element.62), channel_id=1, source_target_pairs={{24,0},{26,2},{28,4},{30,6},{16,8},{18,10},{20,12},{22,14},{8,16},... | collective-permute-start | bytes 196616 | tf_op jit(solution)/shard_map/ppermute | solution.py:483
  113.1 1.6 %collective-permute-done.13 = bf16[64,512]{1,0:T(8,128)(2,1)S(1)} collective-permute-done((bf16[64,512]{1,0:T(8,128)(2,1)S(1)}, bf16[64,512]{1,0:T(8,128)(2,1)S(1)}, u32[]{:S(2)}, u32[]{:S(2)}) %collective-permute-start.13) | collective-permute-done | bytes 65568 | tf_op jit(solution)/shard_map/ppermute | solution.py:483
  114.6 2.1 %collective-permute-done.14 = bf16[64,512]{1,0:T(8,128)(2,1)S(1)} collective-permute-done((bf16[64,512]{1,0:T(8,128)(2,1)S(1)}, bf16[64,512]{1,0:T(8,128)(2,1)S(1)}, u32[]{:S(2)}, u32[]{:S(2)}) %collective-permute-start.14) | collective-permute-done | bytes 65568 | tf_op jit(solution)/shard_map/ppermute | solution.py:483
  116.7 1.5 %collective-permute-start.16 = (bf16[256,512]{1,0:T(8,128)(2,1)S(1)}, bf16[256,512]{1,0:T(8,128)(2,1)S(1)}, u32[]{:S(2)}, u32[]{:S(2)}) collective-permute-start(bf16[256,512]{1,0:T(8,128)(2,1)S(1)} %constant_dynamic-update-slice_fusion.refs_0_), channel_id=1, source_target_pairs={{2,0},{0,2},{6,4},{4,6},{10,8},{8,10},{14,12},{12,14},{18,16},{16,... | collective-permute-start | bytes 786440 | tf_op jit(solution)/shard_map/ppermute | solution.py:483
  118.3 4.1 %shard_map.131.mine_ref = bf16[1024,256]{1,0:T(8,128)(2,1)S(1)} custom-call(s32[16,512]{1,0:T(8,128)S(1)} %add_select_fusion.ids_ref, bf16[2048,256]{1,0:T(8,128)(2,1)S(1)} %bitcast.19), custom_call_target="tpu_custom_call" | custom-call | flops 1073741824 | bytes 1572864 | tf_op jit(solution)/shard_map/pallas_call | solution.py:167
  122.4 0.7 collective-permute-done.16.refs_1_
  123.2 1.5 %collective-permute-start.18 = (bf16[256,512]{1,0:T(8,128)(2,1)S(1)}, bf16[256,512]{1,0:T(8,128)(2,1)S(1)}, u32[]{:S(2)}, u32[]{:S(2)}) collective-permute-start(bf16[256,512]{1,0:T(8,128)(2,1)S(1)} %constant_dynamic-update-slice_fusion.refs_0_), channel_id=1, source_target_pairs={{4,0},{6,2},{0,4},{2,6},{12,8},{14,10},{8,12},{10,14},{20,16},{22,... | collective-permute-start | bytes 786440 | tf_op jit(solution)/shard_map/ppermute | solution.py:483
  124.7 1.4 collective-permute-start.15
  126.1 0.1 pad_add_fusion.2.spots_ref
  126.2 11.3 %collective-permute-done.18.refs_2_ = bf16[256,512]{1,0:T(8,128)(2,1)S(1)} collective-permute-done((bf16[256,512]{1,0:T(8,128)(2,1)S(1)}, bf16[256,512]{1,0:T(8,128)(2,1)S(1)}, u32[]{:S(2)}, u32[]{:S(2)}) %collective-permute-start.18) | collective-permute-done | bytes 262176 | tf_op jit(solution)/shard_map/ppermute | solution.py:483
  137.5 1.7 %shard_map.133 = (f32[1024,256]{1,0:T(8,128)}, f32[1024,256]{1,0:T(8,128)}) custom-call(s32[3]{0:T(128)S(1)} %pad_add_fusion.2.spots_ref, bf16[256,512]{1,0:T(8,128)(2,1)S(1)} %constant_dynamic-update-slice_fusion.refs_0_, bf16[256,512]{1,0:T(8,128)(2,1)S(1)} %collective-permute-done.16.refs_1_, bf16[256,512]{1,0:T(8,128)(2,1)S(1)} %collective-permute-done.18.refs_2_), custom_call_target="tpu_custom_call" | custom-call | flops 393216 | bytes 2359296 | tf_op jit(solution)/shard_map/pallas_call | solution.py:378
  139.3 1.9 %shard_map.132 = (bf16[1024,256]{1,0:T(8,128)(2,1)}, f32[4,128]{1,0:T(4,128)}) custom-call(s32[1]{0:T(128)} %bitcast.swap_ref.share_ref, bf16[1024,256]{1,0:T(8,128)(2,1)S(1)} %copy-done, bf16[1024,256]{1,0:T(8,128)(2,1)S(1)} %shard_map.131.mine_ref, bf16[1024,256]{1,0:T(8,128)(2,1)S(1)} %collective-permute-done.17.other_ref, f32[8,128]{1,0:T(8,128)S(1)} %bitcast.20), custom_call_target="tpu_custom_call" | custom-call | flops 2097152 | bytes 2097152 | tf_op jit(solution)/shard_map/pallas_call | solution.py:410
  141.2 0.8 shard_map.134
  (46 shorter events, 0.4 us)
Async XLA Ops:
  1.6 18.7 %collective-permute-start = (bf16[512,256]{1,0:T(8,128)(2,1)S(1)}, bf16[512,256]{1,0:T(8,128)(2,1)S(1)}, u32[]{:S(2)}, u32[]{:S(2)}) collective-permute-start(bf16[512,256]{1,0:T(8,128)(2,1)S(1)} %constant_dynamic-slice_fusion.7), channel_id=1, source_target_pairs={{0,16},{2,18},{4,20},{6,22},{8,24},{10,26},{12,28},{14,30},{16,0},... | collective-permute-start | bytes 786440 | tf_op jit(solution)/shard_map/ppermute | solution.py:538
  20.3 1.5 %copy-start.10 = (bf16[512,256]{1,0:T(8,128)(2,1)}, bf16[512,256]{1,0:T(8,128)(2,1)S(1)}, u32[]{:S(2)}) copy-start(bf16[512,256]{1,0:T(8,128)(2,1)S(1)} %collective-permute-done.first_ref) | copy-start | bytes 786436
  20.3 1.5 %collective-permute-start.1 = (bf16[512,256]{1,0:T(8,128)(2,1)S(1)}, bf16[512,256]{1,0:T(8,128)(2,1)S(1)}, u32[]{:S(2)}, u32[]{:S(2)}) collective-permute-start(bf16[512,256]{1,0:T(8,128)(2,1)S(1)} %collective-permute-done.first_ref), channel_id=1, source_target_pairs={{1,0},{0,1},{3,2},{2,3},{5,4},{4,5},{7,6},{6,7},{9,8},{8,9},{11,10... | collective-permute-start | bytes 786440 | tf_op jit(solution)/shard_map/ppermute | solution.py:532
  21.9 0.7 copy-start.11
  27.6 3.8 %copy-start.7 = (bf16[1024,256]{1,0:T(8,128)(2,1)S(1)}, bf16[1024,256]{1,0:T(8,128)(2,1)}, u32[]{:S(2)}) copy-start(bf16[1024,256]{1,0:T(8,128)(2,1)} %down_a_ref.1) | copy-start | bytes 1572868
  27.6 4.0 %copy-start.8 = (bf16[1024,256]{1,0:T(8,128)(2,1)S(1)}, bf16[1024,256]{1,0:T(8,128)(2,1)}, u32[]{:S(2)}) copy-start(bf16[1024,256]{1,0:T(8,128)(2,1)} %up_a_ref.1) | copy-start | bytes 1572868
  27.6 4.3 %copy-start.1 = (s32[16,128]{1,0:T(8,128)S(1)}, s32[16,128]{1,0:T(8,128)}, u32[]{:S(2)}) copy-start(s32[16,128]{1,0:T(8,128)} %goals_ref.1) | copy-start | bytes 24580
  27.7 4.3 %copy-start.5 = (s32[8,1,1024]{2,0,1:T(8,128)S(1)}, s32[8,1,1024]{2,0,1:T(8,128)}, u32[]{:S(2)}) copy-start(s32[8,1,1024]{2,0,1:T(8,128)} %copy.18) | copy-start | bytes 98308
  27.7 6.0 %copy-start.6 = (bf16[2048]{0:T(1024)(128)(2,1)S(1)}, bf16[2048]{0:T(1024)(128)(2,1)}, u32[]{:S(2)}) copy-start(bf16[2048]{0:T(1024)(128)(2,1)} %param.14) | copy-start | bytes 12292
  27.7 19.1 %all-to-all-start.1 = ((bf16[8,2,128,256]{3,2,1,0:T(8,128)(2,1)}), bf16[8,2,128,256]{3,2,1,0:T(8,128)(2,1)S(1)}, u32[]{:S(2)}, u32[]{:S(2)}) async-start(bf16[8,2,128,256]{3,2,1,0:T(8,128)(2,1)} %shard_map.128), calls=%async_computation.1 | async-start | bytes 2097152 | tf_op jit(solution)/shard_map/all_to_all | solution.py:555
  31.4 15.4 %collective-permute-start.3 = (bf16[1024,256]{1,0:T(8,128)(2,1)S(1)}, bf16[1024,256]{1,0:T(8,128)(2,1)S(1)}, u32[]{:S(2)}, u32[]{:S(2)}) collective-permute-start(bf16[1024,256]{1,0:T(8,128)(2,1)S(1)} %copy-done.7), channel_id=1, source_target_pairs={{1,0},{0,1},{3,2},{2,3},{5,4},{4,5},{7,6},{6,7},{9,8},{8,9},{11,10... | collective-permute-start | bytes 1572872 | tf_op jit(solution)/shard_map/ppermute | solution.py:532
  31.6 15.2 %collective-permute-start.4 = (bf16[1024,256]{1,0:T(8,128)(2,1)S(1)}, bf16[1024,256]{1,0:T(8,128)(2,1)}, u32[]{:S(2)}, u32[]{:S(2)}) collective-permute-start(bf16[1024,256]{1,0:T(8,128)(2,1)S(1)} %copy-done.8), channel_id=1, source_target_pairs={{1,0},{0,1},{3,2},{2,3},{5,4},{4,5},{7,6},{6,7},{9,8},{8,9},{11,10... | collective-permute-start | bytes 1572872 | tf_op jit(solution)/shard_map/ppermute | solution.py:532
  32.0 11.8 %collective-permute-start.2 = (s32[8,512]{1,0:T(8,128)S(1)}, s32[8,512]{1,0:T(8,128)S(1)}, u32[]{:S(2)}, u32[]{:S(2)}) collective-permute-start(s32[8,512]{1,0:T(8,128)S(1)} %get-tuple-element.71), channel_id=1, source_target_pairs={{0,16},{2,18},{4,20},{6,22},{8,24},{10,26},{12,28},{14,30},{16,0},... | collective-permute-start | bytes 49160 | tf_op jit(solution)/shard_map/ppermute | solution.py:558
  46.8 1.0 copy-start.4
  46.8 1.1 copy-start.9
  54.5 2.9 %collective-permute-start.5 = (bf16[1024,512]{1,0:T(8,128)(2,1)}, bf16[1024,512]{1,0:T(8,128)(2,1)S(1)}, u32[]{:S(2)}, u32[]{:S(2)}) collective-permute-start(bf16[1024,512]{1,0:T(8,128)(2,1)} %get-tuple-element.39), channel_id=1, source_target_pairs={{1,0},{0,1},{3,2},{2,3},{5,4},{4,5},{7,6},{6,7},{9,8},{8,9},{11,10... | collective-permute-start | bytes 3145736 | tf_op jit(solution)/shard_map/ppermute | solution.py:571
  58.9 3.7 %copy-start.3 = (bf16[1024,256]{1,0:T(8,128)(2,1)S(1)}, bf16[1024,256]{1,0:T(8,128)(2,1)}, u32[]{:S(2)}) copy-start(bf16[1024,256]{1,0:T(8,128)(2,1)} %get-tuple-element.40.grads_ref) | copy-start | bytes 1572868
  59.0 9.2 %collective-permute-start.6 = (bf16[256,512]{1,0:T(8,128)(2,1)S(1)}, bf16[256,512]{1,0:T(8,128)(2,1)S(1)}, u32[]{:S(2)}, u32[]{:S(2)}) collective-permute-start(bf16[256,512]{1,0:T(8,128)(2,1)S(1)} %get-tuple-element.65), channel_id=1, source_target_pairs={{2,0},{0,2},{6,4},{4,6},{10,8},{8,10},{14,12},{12,14},{18,16},{16,... | collective-permute-start | bytes 786440 | tf_op jit(solution)/shard_map/ppermute | solution.py:460
  60.3 13.7 %collective-permute-start.7 = (bf16[256,512]{1,0:T(8,128)(2,1)S(1)}, bf16[256,512]{1,0:T(8,128)(2,1)S(1)}, u32[]{:S(2)}, u32[]{:S(2)}) collective-permute-start(bf16[256,512]{1,0:T(8,128)(2,1)S(1)} %get-tuple-element.64), channel_id=1, source_target_pairs={{4,0},{6,2},{0,4},{2,6},{12,8},{14,10},{8,12},{10,14},{20,16},{22,... | collective-permute-start | bytes 786440 | tf_op jit(solution)/shard_map/ppermute | solution.py:460
  61.8 12.2 %collective-permute-start.8 = (bf16[256,512]{1,0:T(8,128)(2,1)S(1)}, bf16[256,512]{1,0:T(8,128)(2,1)S(1)}, u32[]{:S(2)}, u32[]{:S(2)}) collective-permute-start(bf16[256,512]{1,0:T(8,128)(2,1)S(1)} %get-tuple-element.63), channel_id=1, source_target_pairs={{6,0},{4,2},{2,4},{0,6},{14,8},{12,10},{10,12},{8,14},{22,16},{20,... | collective-permute-start | bytes 786440 | tf_op jit(solution)/shard_map/ppermute | solution.py:460
  74.0 44.2 %all-to-all-start.2 = ((bf16[16,128,256]{2,1,0:T(8,128)(2,1)}), bf16[16,128,256]{2,1,0:T(8,128)(2,1)S(1)}, u32[]{:S(2)}, u32[]{:S(2)}) async-start(bf16[16,128,256]{2,1,0:T(8,128)(2,1)} %bitcast.9), calls=%async_computation.2 | async-start | bytes 2097152 | tf_op jit(solution)/shard_map/all_to_all | solution.py:579
  78.1 23.0 %collective-permute-start.11 = (bf16[64,512]{1,0:T(8,128)(2,1)S(1)}, bf16[64,512]{1,0:T(8,128)(2,1)S(1)}, u32[]{:S(2)}, u32[]{:S(2)}) collective-permute-start(bf16[64,512]{1,0:T(8,128)(2,1)S(1)} %get-tuple-element.68), channel_id=1, source_target_pairs={{24,0},{26,2},{28,4},{30,6},{16,8},{18,10},{20,12},{22,14},{8,16},... | collective-permute-start | bytes 196616 | tf_op jit(solution)/shard_map/ppermute | solution.py:460
  81.8 26.7 %collective-permute-start.10 = (bf16[64,512]{1,0:T(8,128)(2,1)S(1)}, bf16[64,512]{1,0:T(8,128)(2,1)S(1)}, u32[]{:S(2)}, u32[]{:S(2)}) collective-permute-start(bf16[64,512]{1,0:T(8,128)(2,1)S(1)} %get-tuple-element.69), channel_id=1, source_target_pairs={{16,0},{18,2},{20,4},{22,6},{24,8},{26,10},{28,12},{30,14},{0,16},... | collective-permute-start | bytes 196616 | tf_op jit(solution)/shard_map/ppermute | solution.py:460
  81.9 26.7 %collective-permute-start.9 = (bf16[64,512]{1,0:T(8,128)(2,1)S(1)}, bf16[64,512]{1,0:T(8,128)(2,1)S(1)}, u32[]{:S(2)}, u32[]{:S(2)}) collective-permute-start(bf16[64,512]{1,0:T(8,128)(2,1)S(1)} %get-tuple-element.67), channel_id=1, source_target_pairs={{8,0},{10,2},{12,4},{14,6},{0,8},{2,10},{4,12},{6,14},{24,16},{26,... | collective-permute-start | bytes 196616 | tf_op jit(solution)/shard_map/ppermute | solution.py:460
  108.6 4.5 %collective-permute-start.12 = (bf16[64,512]{1,0:T(8,128)(2,1)S(1)}, bf16[64,512]{1,0:T(8,128)(2,1)S(1)}, u32[]{:S(2)}, u32[]{:S(2)}) collective-permute-start(bf16[64,512]{1,0:T(8,128)(2,1)S(1)} %get-tuple-element.62), channel_id=1, source_target_pairs={{8,0},{10,2},{12,4},{14,6},{0,8},{2,10},{4,12},{6,14},{24,16},{26,... | collective-permute-start | bytes 196616 | tf_op jit(solution)/shard_map/ppermute | solution.py:483
  108.8 5.8 %collective-permute-start.13 = (bf16[64,512]{1,0:T(8,128)(2,1)S(1)}, bf16[64,512]{1,0:T(8,128)(2,1)S(1)}, u32[]{:S(2)}, u32[]{:S(2)}) collective-permute-start(bf16[64,512]{1,0:T(8,128)(2,1)S(1)} %get-tuple-element.62), channel_id=1, source_target_pairs={{16,0},{18,2},{20,4},{22,6},{24,8},{26,10},{28,12},{30,14},{0,16},... | collective-permute-start | bytes 196616 | tf_op jit(solution)/shard_map/ppermute | solution.py:483
  110.6 6.1 %collective-permute-start.14 = (bf16[64,512]{1,0:T(8,128)(2,1)S(1)}, bf16[64,512]{1,0:T(8,128)(2,1)S(1)}, u32[]{:S(2)}, u32[]{:S(2)}) collective-permute-start(bf16[64,512]{1,0:T(8,128)(2,1)S(1)} %get-tuple-element.62), channel_id=1, source_target_pairs={{24,0},{26,2},{28,4},{30,6},{16,8},{18,10},{20,12},{22,14},{8,16},... | collective-permute-start | bytes 196616 | tf_op jit(solution)/shard_map/ppermute | solution.py:483
  116.7 6.4 %collective-permute-start.16 = (bf16[256,512]{1,0:T(8,128)(2,1)S(1)}, bf16[256,512]{1,0:T(8,128)(2,1)S(1)}, u32[]{:S(2)}, u32[]{:S(2)}) collective-permute-start(bf16[256,512]{1,0:T(8,128)(2,1)S(1)} %constant_dynamic-update-slice_fusion.refs_0_), channel_id=1, source_target_pairs={{2,0},{0,2},{6,4},{4,6},{10,8},{8,10},{14,12},{12,14},{18,16},{16,... | collective-permute-start | bytes 786440 | tf_op jit(solution)/shard_map/ppermute | solution.py:483
  118.3 21.0 %copy-start.2 = (f32[1024]{0:T(1024)S(1)}, f32[1024]{0:T(1024)}, u32[]{:S(2)}) copy-start(f32[1024]{0:T(1024)} %param.10) | copy-start | bytes 12292
  122.4 16.9 %copy-start = (bf16[1024,256]{1,0:T(8,128)(2,1)S(1)}, bf16[1024,256]{1,0:T(8,128)(2,1)}, u32[]{:S(2)}) copy-start(bf16[1024,256]{1,0:T(8,128)(2,1)} %rows_ref.3) | copy-start | bytes 1572868
  123.2 16.1 %collective-permute-start.17 = (bf16[1024,256]{1,0:T(8,128)(2,1)S(1)}, bf16[1024,256]{1,0:T(8,128)(2,1)S(1)}, u32[]{:S(2)}, u32[]{:S(2)}) collective-permute-start(bf16[1024,256]{1,0:T(8,128)(2,1)S(1)} %shard_map.131.mine_ref), channel_id=1, source_target_pairs={{1,0},{0,1},{3,2},{2,3},{5,4},{4,5},{7,6},{6,7},{9,8},{8,9},{11,10... | collective-permute-start | bytes 1572872 | tf_op jit(solution)/shard_map/ppermute | solution.py:596
  123.2 14.3 %collective-permute-start.18 = (bf16[256,512]{1,0:T(8,128)(2,1)S(1)}, bf16[256,512]{1,0:T(8,128)(2,1)S(1)}, u32[]{:S(2)}, u32[]{:S(2)}) collective-permute-start(bf16[256,512]{1,0:T(8,128)(2,1)S(1)} %constant_dynamic-update-slice_fusion.refs_0_), channel_id=1, source_target_pairs={{4,0},{6,2},{0,4},{2,6},{12,8},{14,10},{8,12},{10,14},{20,16},{22,... | collective-permute-start | bytes 786440 | tf_op jit(solution)/shard_map/ppermute | solution.py:483
  124.7 16.5 %collective-permute-start.15 = (bf16[256,512]{1,0:T(8,128)(2,1)S(1)}, bf16[256,512]{1,0:T(8,128)(2,1)S(1)}, u32[]{:S(2)}, u32[]{:S(2)}) collective-permute-start(bf16[256,512]{1,0:T(8,128)(2,1)S(1)} %constant_dynamic-update-slice_fusion.refs_0_), channel_id=1, source_target_pairs={{6,0},{4,2},{2,4},{0,6},{14,8},{12,10},{10,12},{8,14},{22,16},{20,... | collective-permute-start | bytes 786440 | tf_op jit(solution)/shard_map/ppermute | solution.py:483

commit v6 on v5

--- a/solution.py
+++ b/solution.py
@@ -19,7 +19,6 @@
 
 SLOTS = 128
 MIB = 1024 * 1024
-MOST = 56
 
 
 def matmul(left, right):
@@ -85,56 +84,52 @@
     return jnp.where(mask, jnp.asarray(1, jnp.bfloat16), jnp.asarray(0, jnp.bfloat16))
 
 
-def pool_kernel(
-    swap_ref, ids_ref, first_ref, second_ref, rows_ref, out_ref, counts_ref, near_ref, far_ref, sem
-):
-    half = first_ref.shape[0]
-    fetch = pltpu.make_async_copy(rows_ref, near_ref, sem)
-    fetch.start()
-    for i, given_ref in enumerate((first_ref, second_ref)):
-        into_half = 1 - swap_ref[0] if i else swap_ref[0]
-        far_ref[pl.ds(pl.multiple_of(into_half * half, half), half), :] = given_ref[...]
-    blocks = ids_ref.shape[0]
+def pool_kernel(part, ids_ref, rows_ref, *refs):
+    out_ref, counts_ref, sums_ref, sem = refs[-4:]
+    slots = counts_ref.shape[0]
     sources, _, pools, _ = out_ref.shape
     per_block = HOT * SLOTS
+    if len(ids_ref.shape) == 3:
+        ids = ids_ref[:, 0, part * per_block : (part + 1) * per_block]
+    else:
+        ids = ids_ref[:, part * per_block : (part + 1) * per_block]
     choice = lookup_choice()
-    for part in range(2):
-        high, low = split_ids(ids_ref[:, part * per_block : (part + 1) * per_block])
-        columns = joined((rows_dot(choice, high), rows_dot(choice, low))).astype(jnp.int16)
-        position = lax.broadcasted_iota(jnp.int32, (SLOTS, 2 * half), 1).astype(jnp.int16)
-        for block in range(blocks):
-            counts = None
-            for lookup in range(HOT):
-                column = columns[lookup * SLOTS : (lookup + 1) * SLOTS, block : block + 1]
-                found = ones_where(column == position)
-                counts = found if counts is None else counts + found
-            counts_ref[block * SLOTS : (block + 1) * SLOTS, :] = counts
-        if part == 0:
-            fetch.wait()
-        sums = matmul(counts_ref[...], (far_ref if part else near_ref)[...])
-        sums = sums.astype(jnp.bfloat16)
-        for source in range(sources):
-            out_ref[source, part] = sums[source * pools : (source + 1) * pools]
-
-
-def pool_lookups(ids, swap, near_rows, far_rows, pools):
+    high, low = split_ids(ids)
+    columns = joined((rows_dot(choice, high), rows_dot(choice, low))).astype(jnp.int16)
+    position = lax.broadcasted_iota(jnp.int32, (SLOTS, rows_ref.shape[0]), 1).astype(jnp.int16)
+    for block in range(slots // SLOTS):
+        counts = None
+        for lookup in range(HOT):
+            column = columns[lookup * SLOTS : (lookup + 1) * SLOTS, block : block + 1]
+            found = ones_where(column == position)
+            counts = found if counts is None else counts + found
+        counts_ref[block * SLOTS : (block + 1) * SLOTS, :] = counts
+    sums = matmul(counts_ref[...], rows_ref[...]).astype(jnp.bfloat16)
+    for source in range(sources):
+        sums_ref[source] = sums[source * pools : (source + 1) * pools]
+    store = pltpu.make_async_copy(sums_ref, out_ref.at[:, part], sem)
+    store.start()
+    store.wait()
+
+
+def pool_lookups(part, ids, rows, pools, given=()):
     slots = ids.shape[0] * SLOTS
-    row_dev, width = near_rows.shape
+    row_dev, width = rows.shape
     return kernel_call(
-        pool_kernel,
+        functools.partial(pool_kernel, part),
         jax.ShapeDtypeStruct((slots // pools, 2, pools, width), jnp.bfloat16),
-        (4 * slots * row_dev * width, 4 * row_dev * width + 4 * slots * width),
+        (2 * slots * row_dev * width, 2 * row_dev * width + 2 * slots * width),
         [
             pltpu.VMEM((slots, row_dev), jnp.bfloat16),
-            pltpu.VMEM((row_dev, width), jnp.bfloat16),
-            pltpu.VMEM((row_dev, width), jnp.bfloat16),
+            pltpu.VMEM((slots // pools, pools, width), jnp.bfloat16),
             pltpu.SemaphoreType.DMA,
         ],
-        flags=1,
-        operands=3,
-        left=1,
-        room=MOST,
-    )(swap, ids, *far_rows, near_rows)
+        operands=2,
+        left=len(given),
+        left_out=(0,),
+        aliases={2: 0} if given else None,
+        room=12,
+    )(ids, rows, *given)
 
 
 def row_grad_kernel(ids_ref, given_ref, out_ref, counts_ref, grads_ref, sem):
@@ -228,10 +223,8 @@
     weight_ref,
     target_ref,
     arrived_ref,
-    down_a_ref,
-    down_b_ref,
-    up_a_ref,
-    up_b_ref,
+    down_ref,
+    up_ref,
     logits_ref,
     grads_ref,
     kept_ref,
@@ -240,27 +233,11 @@
     wide_ref,
     dcross_ref,
     shifted_ref,
-    down_ref,
-    up_ref,
-    sems,
 ):
     samples = target_ref.shape[1]
     width, rank = down_ref.shape
     emb = width // FEAT
     half = width // 2
-    fetches = []
-    for source_ref, goal_ref, second in (
-        (down_a_ref, down_ref, False),
-        (down_b_ref, down_ref, True),
-        (up_a_ref, up_ref, False),
-        (up_b_ref, up_ref, True),
-    ):
-        into_half = 1 - swap_ref[0] if second else swap_ref[0]
-        spot = pl.ds(pl.multiple_of(into_half * half, half), half)
-        fetches.append(
-            pltpu.make_async_copy(source_ref, goal_ref.at[spot, :], sems.at[len(fetches)])
-        )
-        fetches[-1].start()
     chunk = 512
     first_bag = lax.broadcasted_iota(jnp.int32, (samples, chunk), 0) * FEAT
     for start in range(0, goals_ref.shape[1], chunk):
@@ -274,8 +251,6 @@
     for f, part in enumerate(features):
         spot = slice(f * samples, (f + 1) * samples)
         wide_ref[:, part] = matmul(place_ref[spot, :], arrived_ref[...]).astype(jnp.bfloat16)
-    for fetch in fetches:
-        fetch.wait()
     hidden = matmul(wide_ref[...], down_ref[...]).astype(jnp.bfloat16)
     summed = jnp.zeros((samples, emb), jnp.float32)
     for part in features:
@@ -307,10 +282,10 @@
         out_ref[spot : spot + emb, rank:] = up_term.astype(jnp.bfloat16)
 
 
-def dense_step(swap, goals, arrived, downs, ups, bias, weight, target):
+def dense_step(swap, goals, arrived, down_full, up_full, bias, weight, target):
     samples = target.shape[0]
     slots, emb = arrived.shape
-    width, rank = 2 * downs[0].shape[0], downs[0].shape[1]
+    width, rank = down_full.shape
     flops = 2 * slots * samples * width + 12 * samples * width * rank
     logits, grads, kept, sent = kernel_call(
         dense_kernel,
@@ -326,14 +301,10 @@
             pltpu.VMEM((samples, width), jnp.bfloat16),
             pltpu.VMEM((samples, width), jnp.bfloat16),
             pltpu.VMEM((samples, width), jnp.float32),
-            pltpu.VMEM((width, rank), jnp.bfloat16),
-            pltpu.VMEM((width, rank), jnp.bfloat16),
-            pltpu.SemaphoreType.DMA((4,)),
         ],
         flags=1,
-        operands=5,
-        left=4,
-        room=MOST,
+        operands=7,
+        room=20,
     )(
         swap,
         goals.reshape(1, slots),
@@ -341,8 +312,8 @@
         weight.reshape(1, width),
         target.reshape(1, samples),
         arrived,
-        *downs,
-        *ups,
+        down_full,
+        up_full,
     )
     return logits.reshape(samples), grads, kept, sent
 
@@ -527,42 +498,46 @@
             far_half == 0, jnp.concatenate([near, far]), jnp.concatenate([far, near])
         )
 
-    def both_halves(block):
-        if paired:
-            return block, lax.ppermute(block, "narrow", sent_from("narrow", 1, 2, 1))
-        whole = gather_blocks(block, "narrow", narrow_levels)
-        return tuple(jnp.split(whole, 2, axis=0))
+    def narrow_whole(block):
+        if not paired:
+            return gather_blocks(block, "narrow", narrow_levels)
+        came = lax.ppermute(block, "narrow", sent_from("narrow", 1, 2, 1))
+        first = jnp.where(narrow_index == 0, block, came)
+        second = jnp.where(narrow_index == 0, came, block)
+        return jnp.concatenate([first, second], axis=0)
 
     share_rows = row_dev // narrows
     own_share = lax.dynamic_slice_in_dim(table_rows, narrow_index * share_rows, share_rows, 0)
     far_share = lax.ppermute(own_share, "table", across)
-    downs = both_halves(factor_down)
-    ups = both_halves(factor_up)
+    down_full = narrow_whole(factor_down)
+    up_full = narrow_whole(factor_up)
 
     per_window = bag_rows.shape[1]
-    asked = jnp.concatenate(near_and_far(bag_rows), axis=1)
+    asked = jnp.concatenate(near_and_far(bag_rows), axis=1)[:, None, :]
     asked = lax.all_to_all(
         asked, "table", split_axis=0, concat_axis=0, tiled=True, axis_index_groups=halves
     )
-    asked, far_share = lax.optimization_barrier((asked, far_share))
-    far_rows = both_halves(far_share)
-    near_ids, far_ids = asked[:, :per_window], asked[:, per_window:]
-
+    near_ids, far_ids = asked[:, 0, :per_window], asked[:, 0, per_window:]
     if per_window != SLOTS * HOT:
         by_block = (ids.reshape(-1, SLOTS * HOT) for ids in (near_ids, far_ids))
         asked = jnp.concatenate(tuple(by_block), axis=1)
-    sums = pool_lookups(asked, swap, table_rows, far_rows, pools_per)
+    sums = pool_lookups(0, asked, table_rows, pools_per)
+    sums, far_share = lax.optimization_barrier((sums, far_share))
+    sums = pool_lookups(1, asked, narrow_whole(far_share), pools_per, (sums,))
     arrived = lax.all_to_all(
         sums, "table", split_axis=0, concat_axis=0, tiled=True, axis_index_groups=halves
     )
     other_ids = lax.ppermute(far_ids, "table", across)
-    arrived, other_ids = lax.optimization_barrier((arrived, other_ids))
+    goals = jnp.stack(near_and_far(slot_target), axis=1)
+    arrived, other_ids, down_full, up_full, goals = lax.optimization_barrier(
+        (arrived, other_ids, down_full, up_full, goals)
+    )
     logits, bag_grads, kept, sent = dense_step(
         swap,
-        jnp.stack(near_and_far(slot_target), axis=1),
+        goals,
         arrived.reshape(slot_count, emb_width),
-        downs,
-        ups,
+        down_full,
+        up_full,
         cross_bias,
         out_weight,
         target,
@@ -572,10 +547,8 @@
         narrow_sum = (kept.astype(jnp.float32) + came.astype(jnp.float32)).astype(jnp.bfloat16)
     else:
         narrow_sum = scatter_sum(jnp.concatenate([kept, sent], axis=0), "narrow", narrow_levels)
-    bag_grads, narrow_sum = lax.optimization_barrier((bag_grads, narrow_sum))
     slot_grads = return_grads(slot_target, bag_grads)
-    pieces = scattered_pieces(narrow_sum, "table", table_levels[0])
-    slot_grads, *pieces = lax.optimization_barrier((slot_grads, *pieces))
+    slot_grads, narrow_sum = lax.optimization_barrier((slot_grads, narrow_sum))
     returned = lax.all_to_all(
         slot_grads.reshape(tables, pools_per, emb_width),
         "table",
@@ -583,14 +556,12 @@
         concat_axis=0,
         tiled=True,
     ).reshape(slot_count, emb_width)
-    table_sum = scatter_sum(summed(pieces), "table", table_levels[1:])
-    level_sum = gather_blocks(table_sum, "table", table_levels[1:])
-    pieces = gathered_pieces(level_sum, "table", table_levels[0])
+    level_sum = scatter_sum(narrow_sum, "table", table_levels[:1])
+    table_sum = scatter_sum(level_sum, "table", table_levels[1:-1])
     all_ids = in_order(near_ids, other_ids).reshape(-1, SLOTS * HOT)
     sent_grad = row_grads(all_ids, returned, row_dev)
-    spot, first = pieces[1]
-    first, sent_grad = lax.optimization_barrier((first, sent_grad))
-    pieces[1] = (spot, first)
+    pieces = scattered_pieces(table_sum, "table", table_levels[-1])
+    sent_grad, *pieces = lax.optimization_barrier((sent_grad, *pieces))
     if paired:
         mine = sent_grad
         other = lax.ppermute(sent_grad, "narrow", sent_from("narrow", 1, 2, 1))
@@ -598,6 +569,9 @@
         share = scatter_sum(sent_grad, "narrow", narrow_levels)
         mine = gather_blocks(share, "narrow", narrow_levels)
         other = jnp.zeros_like(mine)
+    level_sum = gather_blocks(summed(pieces), "table", table_levels[1:])
+    level_sum, other = lax.optimization_barrier((level_sum, other))
+    pieces = gathered_pieces(level_sum, "table", table_levels[0])
     new_rows, new_accum = update_rows(
         narrow_index.reshape(1), table_rows, mine, other, accum, narrows
     )

time: 143 us -> 121 us (0.85)
  waiting for transfers between devices: 67.6 us -> 53 us
  Pallas kernels: 22.6 us -> 19.2 us
  local copies, waits for them, and re-layouts: 4.99 us -> 3 us
    ppermute x6, waiting for transfers between devices: 35 us -> 24.7 us  [scattered_pieces(): pieces.append(lax.ppermute(outgoing, axis, pairs))]
    ppermute x6, waiting for transfers between devices: 15.7 us -> 12.2 us  [gathered_pieces(): came = lax.ppermute(block, axis, sent_from(axis, stride, group, step))]
    pallas_call x1, Pallas kernels: 6.5 us -> 3.76 us  [dense_step(): kernel_call(dense_kernel, (jax.ShapeDtypeStruct((1, samples), jnp.float32...]
    ppermute x1, waiting for transfers between devices: 2.82 us -> 0.24 us  [local(): came = lax.ppermute(sent, 'narrow', sent_from('narrow', 1, 2, 1))]
    ppermute x3, waiting for transfers between devices: 1.54 us -> 3.5 us  [narrow_whole(): came = lax.ppermute(block, 'narrow', sent_from('narrow', 1, 2, 1))]
    pallas_call x1 -> x2, Pallas kernels: 5.05 us -> 4.4 us  [pool_lookups(): kernel_call(functools.partial(pool_kernel, part), jax.ShapeDtypeStruct((s...]
  transfers between devices with their start and end apart: 21 -> 21, of which waited for: 12 -> 14; matrix products, arithmetic and copies ran while one was open for 2% -> 2% of each run, Pallas kernels for 7% -> 10%
where the time goes in v6:
time: 121 us
  waiting for transfers between devices  53 us (44%)
  starting transfers between devices  29 us (24%)
  Pallas kernels  19.2 us (16%)
  blocking collectives  13.2 us (11%)
  local copies, waits for them, and re-layouts  3 us (2%)
  other arithmetic  1.9 us (2%)
  between operations  1.33 us (1%)
    ppermute x6, waiting for transfers between devices, scattered_pieces(): pieces.append(lax.ppermute(outgoing, axis, pairs))  24.7 us
    all_to_all x1, blocking collectives, local(): lax.all_to_all(asked, 'table', split_axis=0, concat_axis=0, tiled=True, a...  13.2 us
    ppermute x6, waiting for transfers between devices, gathered_pieces(): came = lax.ppermute(block, axis, sent_from(axis, stride, group, step))  12.2 us
    ppermute x1, waiting for transfers between devices, local(): other_ids = lax.ppermute(far_ids, 'table', across)  9.27 us
    ppermute x6, starting transfers between devices, scattered_pieces(): pieces.append(lax.ppermute(outgoing, axis, pairs))  8 us
    ppermute x6, starting transfers between devices, gathered_pieces(): came = lax.ppermute(block, axis, sent_from(axis, stride, group, step))  7.86 us
    all_to_all x1, starting transfers between devices, local(): lax.all_to_all(slot_grads.reshape(tables, pools_per, emb_width), 'table',...  4.57 us
    pallas_call x2, Pallas kernels, pool_lookups(): kernel_call(functools.partial(pool_kernel, part), jax.ShapeDtypeStruct((s...  4.4 us
  transfers between devices with their start and end apart: 21, of which 14 were waited for; matrix products, arithmetic and copies ran while one was open for 2% of the time, Pallas kernels for 10%

profile of v6, /device:TPU:0, one launch (start us, length us, event | category | flops | bytes accessed | tf_op | source)
XLA Modules:
  0.0 120.6 jit_solution(2810903908426185025)
XLA Ops:
  0.6 1.0 constant_dynamic-slice_fusion.9
  1.6 4.1 %collective-permute-start = (bf16[512,256]{1,0:T(8,128)(2,1)S(1)}, bf16[512,256]{1,0:T(8,128)(2,1)S(1)}, u32[]{:S(2)}, u32[]{:S(2)}) collective-permute-start(bf16[512,256]{1,0:T(8,128)(2,1)S(1)} %constant_dynamic-slice_fusion.9), channel_id=1, source_target_pairs={{0,16},{2,18},{4,20},{6,22},{8,24},{10,26},{12,28},{14,30},{16,0},... | collective-permute-start | bytes 786440 | tf_op jit(solution)/shard_map/ppermute | solution.py:511
  5.7 0.7 constant_dynamic-slice_fusion.11
  6.5 13.2 %all_to_all.15.ids_ref = s32[8,1,1024]{2,1,0:T(1,128)S(1)} all-to-all(s32[8,1,1024]{2,1,0:T(1,128)S(1)} %broadcast_in_dim.6), channel_id=1, replica_groups={{0,2,4,6,8,10,12,14},{16,18,20,22,24,26,28,30},{1,3,5,7,9,11,13,15},{17..., dimensions={0} | all-to-all | bytes 65536 | tf_op jit(solution)/shard_map/all_to_all | solution.py:517
  19.7 1.0 copy-done
  20.7 2.2 %shard_map.128.refs_0_ = bf16[8,2,128,256]{3,2,1,0:T(8,128)(2,1)} custom-call(s32[8,1,1024]{2,1,0:T(1,128)S(1)} %all_to_all.15.ids_ref, bf16[1024,256]{1,0:T(8,128)(2,1)S(1)} %copy-done), custom_call_target="tpu_custom_call" | custom-call | flops 536870912 | bytes 1048576 | tf_op jit(solution)/shard_map/pallas_call | solution.py:118
  23.0 0.1 collective-permute-start.1
  23.0 1.5 %collective-permute-done.1 = bf16[512,256]{1,0:T(8,128)(2,1)S(1)} collective-permute-done((bf16[512,256]{1,0:T(8,128)(2,1)S(1)}, bf16[512,256]{1,0:T(8,128)(2,1)S(1)}, u32[]{:S(2)}, u32[]{:S(2)}) %collective-permute-start.1) | collective-permute-done | bytes 262176 | tf_op jit(solution)/shard_map/ppermute | solution.py:504
  24.6 2.2 %shard_map.129 = bf16[8,2,128,256]{3,2,1,0:T(8,128)(2,1)} custom-call(s32[8,1,1024]{2,1,0:T(1,128)S(1)} %all_to_all.15.ids_ref, bf16[1024,256]{1,0:T(8,128)(2,1)S(1)} %pad_maximum_fusion.2.rows_ref, bf16[8,2,128,256]{3,2,1,0:T(8,128)(2,1)} %shard_map.128.refs_0_), custom_call_target="tpu_custom_call", output_to_operand_aliasing={{}: (2, {})} | custom-call | flops 536870912 | bytes 1048576 | tf_op jit(solution)/shard_map/pallas_call | solution.py:118
  26.9 3.7 %all-to-all-start.1 = ((bf16[8,2,128,256]{3,2,1,0:T(8,128)(2,1)}), bf16[8,2,128,256]{3,2,1,0:T(8,128)(2,1)S(1)}, u32[]{:S(2)}, u32[]{:S(2)}) async-start(bf16[8,2,128,256]{3,2,1,0:T(8,128)(2,1)} %shard_map.129), calls=%async_computation.1 | async-start | bytes 2097152 | tf_op jit(solution)/shard_map/all_to_all | solution.py:527
  30.6 0.2 collective-permute-start.4
  30.8 0.4 collective-permute-start.3
  31.3 0.1 collective-permute-start.2
  31.4 1.2 %collective-permute-done.4 = bf16[1024,256]{1,0:T(8,128)(2,1)S(1)} collective-permute-done((bf16[1024,256]{1,0:T(8,128)(2,1)S(1)}, bf16[1024,256]{1,0:T(8,128)(2,1)S(1)}, u32[]{:S(2)}, u32[]{:S(2)}) %collective-permute-start.4) | collective-permute-done | bytes 524320 | tf_op jit(solution)/shard_map/ppermute | solution.py:504
  32.6 0.7 collective-permute-done.3
  33.4 0.2 broadcast_select_fusion.1
  33.7 9.3 %collective-permute-done.2 = s32[8,512]{1,0:T(8,128)S(1)} collective-permute-done((s32[8,512]{1,0:T(8,128)S(1)}, s32[8,512]{1,0:T(8,128)S(1)}, u32[]{:S(2)}, u32[]{:S(2)}) %collective-permute-start.2) | collective-permute-done | bytes 16416 | tf_op jit(solution)/shard_map/ppermute | solution.py:530
  43.0 3.1 %all-to-all-done.1 = bf16[8,2,128,256]{3,2,1,0:T(8,128)(2,1)S(1)} async-done(((bf16[8,2,128,256]{3,2,1,0:T(8,128)(2,1)}), bf16[8,2,128,256]{3,2,1,0:T(8,128)(2,1)S(1)}, u32[]{:S(2)}, u32[]{:S(2)}) %all-to-all-start.1) | async-done | bytes 1048608 | tf_op jit(solution)/shard_map/all_to_all | solution.py:527
  46.1 3.8 %shard_map.130 = (f32[1,128]{1,0:T(1,128)}, bf16[1024,256]{1,0:T(8,128)(2,1)S(1)}, bf16[1024,512]{1,0:T(8,128)(2,1)S(1)}, bf16[1024,512]{1,0:T(8,128)(2,1)S(1)}) custom-call(s32[1]{0:T(128)} %bitcast.swap_ref.share_ref, s32[1,2048]{1,0:T(1,128)S(1)} %bitcast.24, f32[1,2048]{1,0:T(1,128)S(1)} %bitcast.26, bf16[1,2048]{1,0:T(2,128)(2,1)S(1)} %reshape.47.weight_ref, ...), custom_call_target="tpu_custom_call" | custom-call | flops 1879048192 | bytes 5242880 | tf_op jit(solution)/shard_map/pallas_call | solution.py:290
  49.8 0.1 collective-permute-start.5
  49.9 2.4 %shard_map.131 = bf16[2048,256]{1,0:T(8,128)(2,1)} custom-call(s32[16,128]{1,0:T(8,128)S(1)} %copy-done.2, bf16[1024,256]{1,0:T(8,128)(2,1)S(1)} %get-tuple-element.44.grads_ref), custom_call_target="tpu_custom_call" | custom-call | flops 1073741824 | bytes 1572864 | tf_op jit(solution)/shard_map/pallas_call | solution.py:209
  52.3 0.2 collective-permute-done.5
  52.5 0.3 add_convert_fusion
  52.8 4.6 %all-to-all-start.2 = ((bf16[16,128,256]{2,1,0:T(8,128)(2,1)}), bf16[16,128,256]{2,1,0:T(8,128)(2,1)S(1)}, u32[]{:S(2)}, u32[]{:S(2)}) async-start(bf16[16,128,256]{2,1,0:T(8,128)(2,1)} %bitcast.11), calls=%async_computation.2 | async-start | bytes 2097152 | tf_op jit(solution)/shard_map/all_to_all | solution.py:552
  57.5 2.9 %collective-permute-start.8 = (bf16[256,512]{1,0:T(8,128)(2,1)S(1)}, bf16[256,512]{1,0:T(8,128)(2,1)S(1)}, u32[]{:S(2)}, u32[]{:S(2)}) collective-permute-start(bf16[256,512]{1,0:T(8,128)(2,1)S(1)} %get-tuple-element.70), channel_id=1, source_target_pairs={{6,0},{4,2},{2,4},{0,6},{14,8},{12,10},{10,12},{8,14},{22,16},{20,... | collective-permute-start | bytes 786440 | tf_op jit(solution)/shard_map/ppermute | solution.py:431
  60.4 0.6 collective-permute-start.7
  60.9 0.1 collective-permute-start.6
  61.1 15.8 %collective-permute-done.8 = bf16[256,512]{1,0:T(8,128)(2,1)S(1)} collective-permute-done((bf16[256,512]{1,0:T(8,128)(2,1)S(1)}, bf16[256,512]{1,0:T(8,128)(2,1)S(1)}, u32[]{:S(2)}, u32[]{:S(2)}) %collective-permute-start.8) | collective-permute-done | bytes 262176 | tf_op jit(solution)/shard_map/ppermute | solution.py:431
  76.9 5.8 %collective-permute-done.7 = bf16[256,512]{1,0:T(8,128)(2,1)S(1)} collective-permute-done((bf16[256,512]{1,0:T(8,128)(2,1)S(1)}, bf16[256,512]{1,0:T(8,128)(2,1)S(1)}, u32[]{:S(2)}, u32[]{:S(2)}) %collective-permute-start.7) | collective-permute-done | bytes 262176 | tf_op jit(solution)/shard_map/ppermute | solution.py:431
  82.8 1.5 %collective-permute-done.6 = bf16[256,512]{1,0:T(8,128)(2,1)} collective-permute-done((bf16[256,512]{1,0:T(8,128)(2,1)S(1)}, bf16[256,512]{1,0:T(8,128)(2,1)}, u32[]{:S(2)}, u32[]{:S(2)}) %collective-permute-start.6) | collective-permute-done | bytes 262176 | tf_op jit(solution)/shard_map/ppermute | solution.py:431
  84.3 1.1 add_convert_fusion.1
  85.5 4.0 %collective-permute-start.10 = (bf16[64,512]{1,0:T(8,128)(2,1)S(1)}, bf16[64,512]{1,0:T(8,128)(2,1)S(1)}, u32[]{:S(2)}, u32[]{:S(2)}) collective-permute-start(bf16[64,512]{1,0:T(8,128)(2,1)S(1)} %get-tuple-element.79), channel_id=1, source_target_pairs={{16,0},{18,2},{20,4},{22,6},{24,8},{26,10},{28,12},{30,14},{0,16},... | collective-permute-start | bytes 196616 | tf_op jit(solution)/shard_map/ppermute | solution.py:431
  89.5 0.3 collective-permute-start.11
  89.8 4.1 %shard_map.132.mine_ref = bf16[1024,256]{1,0:T(8,128)(2,1)S(1)} custom-call(s32[16,512]{1,0:T(8,128)S(1)} %add_select_fusion.ids_ref, bf16[2048,256]{1,0:T(8,128)(2,1)S(1)} %bitcast.22), custom_call_target="tpu_custom_call" | custom-call | flops 1073741824 | bytes 1572864 | tf_op jit(solution)/shard_map/pallas_call | solution.py:162
  94.0 1.6 %collective-permute-done.11 = bf16[64,512]{1,0:T(8,128)(2,1)S(1)} collective-permute-done((bf16[64,512]{1,0:T(8,128)(2,1)S(1)}, bf16[64,512]{1,0:T(8,128)(2,1)S(1)}, u32[]{:S(2)}, u32[]{:S(2)}) %collective-permute-start.11) | collective-permute-done | bytes 65568 | tf_op jit(solution)/shard_map/ppermute | solution.py:431
  95.9 2.4 %collective-permute-start.13 = (bf16[64,512]{1,0:T(8,128)(2,1)S(1)}, bf16[64,512]{1,0:T(8,128)(2,1)S(1)}, u32[]{:S(2)}, u32[]{:S(2)}) collective-permute-start(bf16[64,512]{1,0:T(8,128)(2,1)S(1)} %get-tuple-element.68), channel_id=1, source_target_pairs={{16,0},{18,2},{20,4},{22,6},{24,8},{26,10},{28,12},{30,14},{0,16},... | collective-permute-start | bytes 196616 | tf_op jit(solution)/shard_map/ppermute | solution.py:454
  98.3 1.8 %collective-permute-start.14 = (bf16[64,512]{1,0:T(8,128)(2,1)S(1)}, bf16[64,512]{1,0:T(8,128)(2,1)S(1)}, u32[]{:S(2)}, u32[]{:S(2)}) collective-permute-start(bf16[64,512]{1,0:T(8,128)(2,1)S(1)} %get-tuple-element.68), channel_id=1, source_target_pairs={{24,0},{26,2},{28,4},{30,6},{16,8},{18,10},{20,12},{22,14},{8,16},... | collective-permute-start | bytes 196616 | tf_op jit(solution)/shard_map/ppermute | solution.py:454
  100.1 1.2 collective-permute-done.12
  101.3 3.3 %collective-permute-done.13 = bf16[64,512]{1,0:T(8,128)(2,1)S(1)} collective-permute-done((bf16[64,512]{1,0:T(8,128)(2,1)S(1)}, bf16[64,512]{1,0:T(8,128)(2,1)S(1)}, u32[]{:S(2)}, u32[]{:S(2)}) %collective-permute-start.13) | collective-permute-done | bytes 65568 | tf_op jit(solution)/shard_map/ppermute | solution.py:454
  104.6 0.8 collective-permute-start.17
  105.3 2.2 %collective-permute-start.18 = (bf16[256,512]{1,0:T(8,128)(2,1)S(1)}, bf16[256,512]{1,0:T(8,128)(2,1)S(1)}, u32[]{:S(2)}, u32[]{:S(2)}) collective-permute-start(bf16[256,512]{1,0:T(8,128)(2,1)S(1)} %constant_dynamic-update-slice_fusion.refs_0_), channel_id=1, source_target_pairs={{4,0},{6,2},{0,4},{2,6},{12,8},{14,10},{8,12},{10,14},{20,16},{22,... | collective-permute-start | bytes 786440 | tf_op jit(solution)/shard_map/ppermute | solution.py:454
  107.5 0.6 collective-permute-start.16
  108.1 0.1 pad_add_fusion.2.spots_ref
  108.2 1.9 %shard_map.133 = (bf16[1024,256]{1,0:T(8,128)(2,1)}, f32[4,128]{1,0:T(4,128)}) custom-call(s32[1]{0:T(128)} %bitcast.swap_ref.share_ref, bf16[1024,256]{1,0:T(8,128)(2,1)S(1)} %copy-done.1, bf16[1024,256]{1,0:T(8,128)(2,1)S(1)} %shard_map.132.mine_ref, bf16[1024,256]{1,0:T(8,128)(2,1)S(1)} %collective-permute-done.15.other_ref, f32[8,128]{1,0:T(8,128)S(1)} %bitcast.25), custom_call_target="tpu_custom_call" | custom-call | flops 2097152 | bytes 2097152 | tf_op jit(solution)/shard_map/pallas_call | solution.py:381
  110.1 3.8 %collective-permute-done.17.refs_1_ = bf16[256,512]{1,0:T(8,128)(2,1)S(1)} collective-permute-done((bf16[256,512]{1,0:T(8,128)(2,1)S(1)}, bf16[256,512]{1,0:T(8,128)(2,1)S(1)}, u32[]{:S(2)}, u32[]{:S(2)}) %collective-permute-start.17) | collective-permute-done | bytes 262176 | tf_op jit(solution)/shard_map/ppermute | solution.py:454
  113.9 4.0 %collective-permute-done.18.refs_2_ = bf16[256,512]{1,0:T(8,128)(2,1)S(1)} collective-permute-done((bf16[256,512]{1,0:T(8,128)(2,1)S(1)}, bf16[256,512]{1,0:T(8,128)(2,1)S(1)}, u32[]{:S(2)}, u32[]{:S(2)}) %collective-permute-start.18) | collective-permute-done | bytes 262176 | tf_op jit(solution)/shard_map/ppermute | solution.py:454
  117.9 1.7 %shard_map.134 = (f32[1024,256]{1,0:T(8,128)}, f32[1024,256]{1,0:T(8,128)}) custom-call(s32[3]{0:T(128)S(1)} %pad_add_fusion.2.spots_ref, bf16[256,512]{1,0:T(8,128)(2,1)S(1)} %constant_dynamic-update-slice_fusion.refs_0_, bf16[256,512]{1,0:T(8,128)(2,1)S(1)} %collective-permute-done.17.refs_1_, bf16[256,512]{1,0:T(8,128)(2,1)S(1)} %collective-permute-done.18.refs_2_), custom_call_target="tpu_custom_call" | custom-call | flops 393216 | bytes 2359296 | tf_op jit(solution)/shard_map/pallas_call | solution.py:349
  119.7 0.8 shard_map.135
  (47 shorter events, 0.7 us)
Async XLA Ops:
  1.6 21.3 %collective-permute-start = (bf16[512,256]{1,0:T(8,128)(2,1)S(1)}, bf16[512,256]{1,0:T(8,128)(2,1)S(1)}, u32[]{:S(2)}, u32[]{:S(2)}) collective-permute-start(bf16[512,256]{1,0:T(8,128)(2,1)S(1)} %constant_dynamic-slice_fusion.9), channel_id=1, source_target_pairs={{0,16},{2,18},{4,20},{6,22},{8,24},{10,26},{12,28},{14,30},{16,0},... | collective-permute-start | bytes 786440 | tf_op jit(solution)/shard_map/ppermute | solution.py:511
  19.7 1.0 copy-start
  23.0 1.6 %collective-permute-start.1 = (bf16[512,256]{1,0:T(8,128)(2,1)S(1)}, bf16[512,256]{1,0:T(8,128)(2,1)S(1)}, u32[]{:S(2)}, u32[]{:S(2)}) collective-permute-start(bf16[512,256]{1,0:T(8,128)(2,1)S(1)} %collective-permute-done), channel_id=1, source_target_pairs={{1,0},{0,1},{3,2},{2,3},{5,4},{4,5},{7,6},{6,7},{9,8},{8,9},{11,10... | collective-permute-start | bytes 786440 | tf_op jit(solution)/shard_map/ppermute | solution.py:504
  26.9 3.8 %copy-start.6 = (bf16[1024,256]{1,0:T(8,128)(2,1)S(1)}, bf16[1024,256]{1,0:T(8,128)(2,1)}, u32[]{:S(2)}) copy-start(bf16[1024,256]{1,0:T(8,128)(2,1)} %param.12) | copy-start | bytes 1572868
  26.9 4.0 %copy-start.7 = (bf16[1024,256]{1,0:T(8,128)(2,1)S(1)}, bf16[1024,256]{1,0:T(8,128)(2,1)}, u32[]{:S(2)}) copy-start(bf16[1024,256]{1,0:T(8,128)(2,1)} %param.11) | copy-start | bytes 1572868
  26.9 4.3 %copy-start.8 = (bf16[2048]{0:T(1024)(128)(2,1)S(1)}, bf16[2048]{0:T(1024)(128)(2,1)}, u32[]{:S(2)}) copy-start(bf16[2048]{0:T(1024)(128)(2,1)} %param.14) | copy-start | bytes 12292
  26.9 4.3 %copy-start.2 = (s32[16,128]{1,0:T(8,128)S(1)}, s32[16,128]{1,0:T(8,128)}, u32[]{:S(2)}) copy-start(s32[16,128]{1,0:T(8,128)} %goals_ref.1) | copy-start | bytes 24580
  26.9 19.1 %all-to-all-start.1 = ((bf16[8,2,128,256]{3,2,1,0:T(8,128)(2,1)}), bf16[8,2,128,256]{3,2,1,0:T(8,128)(2,1)S(1)}, u32[]{:S(2)}, u32[]{:S(2)}) async-start(bf16[8,2,128,256]{3,2,1,0:T(8,128)(2,1)} %shard_map.129), calls=%async_computation.1 | async-start | bytes 2097152 | tf_op jit(solution)/shard_map/all_to_all | solution.py:527
  30.6 2.0 %collective-permute-start.4 = (bf16[1024,256]{1,0:T(8,128)(2,1)S(1)}, bf16[1024,256]{1,0:T(8,128)(2,1)S(1)}, u32[]{:S(2)}, u32[]{:S(2)}) collective-permute-start(bf16[1024,256]{1,0:T(8,128)(2,1)S(1)} %copy-done.6), channel_id=1, source_target_pairs={{1,0},{0,1},{3,2},{2,3},{5,4},{4,5},{7,6},{6,7},{9,8},{8,9},{11,10... | collective-permute-start | bytes 1572872 | tf_op jit(solution)/shard_map/ppermute | solution.py:504
  30.8 2.5 %collective-permute-start.3 = (bf16[1024,256]{1,0:T(8,128)(2,1)S(1)}, bf16[1024,256]{1,0:T(8,128)(2,1)S(1)}, u32[]{:S(2)}, u32[]{:S(2)}) collective-permute-start(bf16[1024,256]{1,0:T(8,128)(2,1)S(1)} %copy-done.7), channel_id=1, source_target_pairs={{1,0},{0,1},{3,2},{2,3},{5,4},{4,5},{7,6},{6,7},{9,8},{8,9},{11,10... | collective-permute-start | bytes 1572872 | tf_op jit(solution)/shard_map/ppermute | solution.py:504
  31.3 11.7 %collective-permute-start.2 = (s32[8,512]{1,0:T(8,128)S(1)}, s32[8,512]{1,0:T(8,128)S(1)}, u32[]{:S(2)}, u32[]{:S(2)}) collective-permute-start(s32[8,512]{1,0:T(8,128)S(1)} %bitcast.29), channel_id=1, source_target_pairs={{0,16},{2,18},{4,20},{6,22},{8,24},{10,26},{12,28},{14,30},{16,0},... | collective-permute-start | bytes 49160 | tf_op jit(solution)/shard_map/ppermute | solution.py:530
  33.6 12.4 %copy-start.4 = (f32[2048]{0:T(1024)S(1)}, f32[2048]{0:T(1024)}, u32[]{:S(2)}) copy-start(f32[2048]{0:T(1024)} %param.13) | copy-start | bytes 24580
  33.6 12.4 %copy-start.5 = (f32[128]{0:T(128)S(1)}, f32[128]{0:T(128)}, u32[]{:S(2)}) copy-start(f32[128]{0:T(128)} %param.15) | copy-start | bytes 1540
  49.8 2.7 %collective-permute-start.5 = (bf16[1024,512]{1,0:T(8,128)(2,1)S(1)}, bf16[1024,512]{1,0:T(8,128)(2,1)S(1)}, u32[]{:S(2)}, u32[]{:S(2)}) collective-permute-start(bf16[1024,512]{1,0:T(8,128)(2,1)S(1)} %get-tuple-element.46), channel_id=1, source_target_pairs={{1,0},{0,1},{3,2},{2,3},{5,4},{4,5},{7,6},{6,7},{9,8},{8,9},{11,10... | collective-permute-start | bytes 3145736 | tf_op jit(solution)/shard_map/ppermute | solution.py:546
  52.8 37.0 %all-to-all-start.2 = ((bf16[16,128,256]{2,1,0:T(8,128)(2,1)}), bf16[16,128,256]{2,1,0:T(8,128)(2,1)S(1)}, u32[]{:S(2)}, u32[]{:S(2)}) async-start(bf16[16,128,256]{2,1,0:T(8,128)(2,1)} %bitcast.11), calls=%async_computation.2 | async-start | bytes 2097152 | tf_op jit(solution)/shard_map/all_to_all | solution.py:552
  57.5 19.4 %collective-permute-start.8 = (bf16[256,512]{1,0:T(8,128)(2,1)S(1)}, bf16[256,512]{1,0:T(8,128)(2,1)S(1)}, u32[]{:S(2)}, u32[]{:S(2)}) collective-permute-start(bf16[256,512]{1,0:T(8,128)(2,1)S(1)} %get-tuple-element.70), channel_id=1, source_target_pairs={{6,0},{4,2},{2,4},{0,6},{14,8},{12,10},{10,12},{8,14},{22,16},{20,... | collective-permute-start | bytes 786440 | tf_op jit(solution)/shard_map/ppermute | solution.py:431
  60.4 22.4 %collective-permute-start.7 = (bf16[256,512]{1,0:T(8,128)(2,1)S(1)}, bf16[256,512]{1,0:T(8,128)(2,1)S(1)}, u32[]{:S(2)}, u32[]{:S(2)}) collective-permute-start(bf16[256,512]{1,0:T(8,128)(2,1)S(1)} %get-tuple-element.71), channel_id=1, source_target_pairs={{4,0},{6,2},{0,4},{2,6},{12,8},{14,10},{8,12},{10,14},{20,16},{22,... | collective-permute-start | bytes 786440 | tf_op jit(solution)/shard_map/ppermute | solution.py:431
  60.9 23.3 %collective-permute-start.6 = (bf16[256,512]{1,0:T(8,128)(2,1)S(1)}, bf16[256,512]{1,0:T(8,128)(2,1)}, u32[]{:S(2)}, u32[]{:S(2)}) collective-permute-start(bf16[256,512]{1,0:T(8,128)(2,1)S(1)} %get-tuple-element.69), channel_id=1, source_target_pairs={{2,0},{0,2},{6,4},{4,6},{10,8},{8,10},{14,12},{12,14},{18,16},{16,... | collective-permute-start | bytes 786440 | tf_op jit(solution)/shard_map/ppermute | solution.py:431
  85.4 8.6 %collective-permute-start.9 = (bf16[64,512]{1,0:T(8,128)(2,1)S(1)}, bf16[64,512]{1,0:T(8,128)(2,1)S(1)}, u32[]{:S(2)}, u32[]{:S(2)}) collective-permute-start(bf16[64,512]{1,0:T(8,128)(2,1)S(1)} %get-tuple-element.80), channel_id=1, source_target_pairs={{8,0},{10,2},{12,4},{14,6},{0,8},{2,10},{4,12},{6,14},{24,16},{26,... | collective-permute-start | bytes 196616 | tf_op jit(solution)/shard_map/ppermute | solution.py:431
  85.5 8.5 %collective-permute-start.10 = (bf16[64,512]{1,0:T(8,128)(2,1)S(1)}, bf16[64,512]{1,0:T(8,128)(2,1)S(1)}, u32[]{:S(2)}, u32[]{:S(2)}) collective-permute-start(bf16[64,512]{1,0:T(8,128)(2,1)S(1)} %get-tuple-element.79), channel_id=1, source_target_pairs={{16,0},{18,2},{20,4},{22,6},{24,8},{26,10},{28,12},{30,14},{0,16},... | collective-permute-start | bytes 196616 | tf_op jit(solution)/shard_map/ppermute | solution.py:431
  89.5 6.1 %collective-permute-start.11 = (bf16[64,512]{1,0:T(8,128)(2,1)S(1)}, bf16[64,512]{1,0:T(8,128)(2,1)S(1)}, u32[]{:S(2)}, u32[]{:S(2)}) collective-permute-start(bf16[64,512]{1,0:T(8,128)(2,1)S(1)} %get-tuple-element.78), channel_id=1, source_target_pairs={{24,0},{26,2},{28,4},{30,6},{16,8},{18,10},{20,12},{22,14},{8,16},... | collective-permute-start | bytes 196616 | tf_op jit(solution)/shard_map/ppermute | solution.py:431
  94.0 14.2 %copy-start.1 = (bf16[1024,256]{1,0:T(8,128)(2,1)S(1)}, bf16[1024,256]{1,0:T(8,128)(2,1)}, u32[]{:S(2)}) copy-start(bf16[1024,256]{1,0:T(8,128)(2,1)} %rows_ref.3) | copy-start | bytes 1572868
  94.0 14.2 %copy-start.3 = (f32[1024]{0:T(1024)S(1)}, f32[1024]{0:T(1024)}, u32[]{:S(2)}) copy-start(f32[1024]{0:T(1024)} %param.10) | copy-start | bytes 12292
  95.6 9.0 %collective-permute-start.15 = (bf16[1024,256]{1,0:T(8,128)(2,1)S(1)}, bf16[1024,256]{1,0:T(8,128)(2,1)S(1)}, u32[]{:S(2)}, u32[]{:S(2)}) collective-permute-start(bf16[1024,256]{1,0:T(8,128)(2,1)S(1)} %shard_map.132.mine_ref), channel_id=1, source_target_pairs={{1,0},{0,1},{3,2},{2,3},{5,4},{4,5},{7,6},{6,7},{9,8},{8,9},{11,10... | collective-permute-start | bytes 1572872 | tf_op jit(solution)/shard_map/ppermute | solution.py:567
  95.6 5.6 %collective-permute-start.12 = (bf16[64,512]{1,0:T(8,128)(2,1)S(1)}, bf16[64,512]{1,0:T(8,128)(2,1)S(1)}, u32[]{:S(2)}, u32[]{:S(2)}) collective-permute-start(bf16[64,512]{1,0:T(8,128)(2,1)S(1)} %get-tuple-element.68), channel_id=1, source_target_pairs={{8,0},{10,2},{12,4},{14,6},{0,8},{2,10},{4,12},{6,14},{24,16},{26,... | collective-permute-start | bytes 196616 | tf_op jit(solution)/shard_map/ppermute | solution.py:454
  95.9 8.7 %collective-permute-start.13 = (bf16[64,512]{1,0:T(8,128)(2,1)S(1)}, bf16[64,512]{1,0:T(8,128)(2,1)S(1)}, u32[]{:S(2)}, u32[]{:S(2)}) collective-permute-start(bf16[64,512]{1,0:T(8,128)(2,1)S(1)} %get-tuple-element.68), channel_id=1, source_target_pairs={{16,0},{18,2},{20,4},{22,6},{24,8},{26,10},{28,12},{30,14},{0,16},... | collective-permute-start | bytes 196616 | tf_op jit(solution)/shard_map/ppermute | solution.py:454
  98.3 6.2 %collective-permute-start.14 = (bf16[64,512]{1,0:T(8,128)(2,1)S(1)}, bf16[64,512]{1,0:T(8,128)(2,1)S(1)}, u32[]{:S(2)}, u32[]{:S(2)}) collective-permute-start(bf16[64,512]{1,0:T(8,128)(2,1)S(1)} %get-tuple-element.68), channel_id=1, source_target_pairs={{24,0},{26,2},{28,4},{30,6},{16,8},{18,10},{20,12},{22,14},{8,16},... | collective-permute-start | bytes 196616 | tf_op jit(solution)/shard_map/ppermute | solution.py:454
  104.6 9.3 %collective-permute-start.17 = (bf16[256,512]{1,0:T(8,128)(2,1)S(1)}, bf16[256,512]{1,0:T(8,128)(2,1)S(1)}, u32[]{:S(2)}, u32[]{:S(2)}) collective-permute-start(bf16[256,512]{1,0:T(8,128)(2,1)S(1)} %constant_dynamic-update-slice_fusion.refs_0_), channel_id=1, source_target_pairs={{2,0},{0,2},{6,4},{4,6},{10,8},{8,10},{14,12},{12,14},{18,16},{16,... | collective-permute-start | bytes 786440 | tf_op jit(solution)/shard_map/ppermute | solution.py:454
  105.3 12.6 %collective-permute-start.18 = (bf16[256,512]{1,0:T(8,128)(2,1)S(1)}, bf16[256,512]{1,0:T(8,128)(2,1)S(1)}, u32[]{:S(2)}, u32[]{:S(2)}) collective-permute-start(bf16[256,512]{1,0:T(8,128)(2,1)S(1)} %constant_dynamic-update-slice_fusion.refs_0_), channel_id=1, source_target_pairs={{4,0},{6,2},{0,4},{2,6},{12,8},{14,10},{8,12},{10,14},{20,16},{22,... | collective-permute-start | bytes 786440 | tf_op jit(solution)/shard_map/ppermute | solution.py:454
  107.5 12.1 %collective-permute-start.16 = (bf16[256,512]{1,0:T(8,128)(2,1)S(1)}, bf16[256,512]{1,0:T(8,128)(2,1)S(1)}, u32[]{:S(2)}, u32[]{:S(2)}) collective-permute-start(bf16[256,512]{1,0:T(8,128)(2,1)S(1)} %constant_dynamic-update-slice_fusion.refs_0_), channel_id=1, source_target_pairs={{6,0},{4,2},{2,4},{0,6},{14,8},{12,10},{10,12},{8,14},{22,16},{20,... | collective-permute-start | bytes 786440 | tf_op jit(solution)/shard_map/ppermute | solution.py:454

commit v7 on v6

--- a/solution.py
+++ b/solution.py
@@ -84,10 +84,14 @@
     return jnp.where(mask, jnp.asarray(1, jnp.bfloat16), jnp.asarray(0, jnp.bfloat16))
 
 
-def pool_kernel(part, ids_ref, rows_ref, *refs):
-    out_ref, counts_ref, sums_ref, sem = refs[-4:]
+def pool_kernel(part, far, ids_ref, rows_ref, *refs):
+    if far:
+        out_ref, counts_ref = refs
+    else:
+        out_ref, counts_ref, held_ref, sem = refs
+        fetch = pltpu.make_async_copy(rows_ref, held_ref, sem)
+        fetch.start()
     slots = counts_ref.shape[0]
-    sources, _, pools, _ = out_ref.shape
     per_block = HOT * SLOTS
     if len(ids_ref.shape) == 3:
         ids = ids_ref[:, 0, part * per_block : (part + 1) * per_block]
@@ -104,32 +108,30 @@
             found = ones_where(column == position)
             counts = found if counts is None else counts + found
         counts_ref[block * SLOTS : (block + 1) * SLOTS, :] = counts
-    sums = matmul(counts_ref[...], rows_ref[...]).astype(jnp.bfloat16)
-    for source in range(sources):
-        sums_ref[source] = sums[source * pools : (source + 1) * pools]
-    store = pltpu.make_async_copy(sums_ref, out_ref.at[:, part], sem)
-    store.start()
-    store.wait()
-
-
-def pool_lookups(part, ids, rows, pools, given=()):
+    if far:
+        rows = rows_ref[...]
+    else:
+        fetch.wait()
+        rows = held_ref[...]
+    out_ref[...] = matmul(counts_ref[...], rows).astype(jnp.bfloat16)
+
+
+def pool_lookups(part, ids, rows):
+    far = part == 1
     slots = ids.shape[0] * SLOTS
     row_dev, width = rows.shape
+    scratch = [pltpu.VMEM((slots, row_dev), jnp.bfloat16)]
+    if not far:
+        scratch += [pltpu.VMEM((row_dev, width), jnp.bfloat16), pltpu.SemaphoreType.DMA]
     return kernel_call(
-        functools.partial(pool_kernel, part),
-        jax.ShapeDtypeStruct((slots // pools, 2, pools, width), jnp.bfloat16),
+        functools.partial(pool_kernel, part, far),
+        jax.ShapeDtypeStruct((slots, width), jnp.bfloat16),
         (2 * slots * row_dev * width, 2 * row_dev * width + 2 * slots * width),
-        [
-            pltpu.VMEM((slots, row_dev), jnp.bfloat16),
-            pltpu.VMEM((slots // pools, pools, width), jnp.bfloat16),
-            pltpu.SemaphoreType.DMA,
-        ],
-        operands=2,
-        left=len(given),
-        left_out=(0,),
-        aliases={2: 0} if given else None,
-        room=12,
-    )(ids, rows, *given)
+        scratch,
+        operands=2 if far else 1,
+        left=0 if far else 1,
+        room=12 if far else 56,
+    )(ids, rows)
 
 
 def row_grad_kernel(ids_ref, given_ref, out_ref, counts_ref, grads_ref, sem):
@@ -222,7 +224,8 @@
     bias_ref,
     weight_ref,
     target_ref,
-    arrived_ref,
+    near_ref,
+    far_ref,
     down_ref,
     up_ref,
     logits_ref,
@@ -248,9 +251,12 @@
                 nth == jnp.asarray(f, jnp.int16)
             )
     features = [slice(f * emb, (f + 1) * emb) for f in range(FEAT)]
+    slots = near_ref.shape[0]
     for f, part in enumerate(features):
         spot = slice(f * samples, (f + 1) * samples)
-        wide_ref[:, part] = matmul(place_ref[spot, :], arrived_ref[...]).astype(jnp.bfloat16)
+        pooled = matmul(place_ref[spot, :slots], near_ref[...])
+        pooled = pooled + matmul(place_ref[spot, slots:], far_ref[...])
+        wide_ref[:, part] = pooled.astype(jnp.bfloat16)
     hidden = matmul(wide_ref[...], down_ref[...]).astype(jnp.bfloat16)
     summed = jnp.zeros((samples, emb), jnp.float32)
     for part in features:
@@ -282,9 +288,9 @@
         out_ref[spot : spot + emb, rank:] = up_term.astype(jnp.bfloat16)
 
 
-def dense_step(swap, goals, arrived, down_full, up_full, bias, weight, target):
+def dense_step(swap, goals, near, far, down_full, up_full, bias, weight, target):
     samples = target.shape[0]
-    slots, emb = arrived.shape
+    slots, emb = 2 * near.shape[0], near.shape[1]
     width, rank = down_full.shape
     flops = 2 * slots * samples * width + 12 * samples * width * rank
     logits, grads, kept, sent = kernel_call(
@@ -295,7 +301,7 @@
             jax.ShapeDtypeStruct((width // 2, 2 * rank), jnp.bfloat16),
             jax.ShapeDtypeStruct((width // 2, 2 * rank), jnp.bfloat16),
         ),
-        (flops, 2 * arrived.size + 8 * width * rank),
+        (flops, 4 * near.size + 8 * width * rank),
         [
             pltpu.VMEM((samples * FEAT, slots), jnp.bfloat16),
             pltpu.VMEM((samples, width), jnp.bfloat16),
@@ -303,7 +309,7 @@
             pltpu.VMEM((samples, width), jnp.float32),
         ],
         flags=1,
-        operands=7,
+        operands=8,
         room=20,
     )(
         swap,
@@ -311,7 +317,8 @@
         bias.reshape(1, width),
         weight.reshape(1, width),
         target.reshape(1, samples),
-        arrived,
+        near,
+        far,
         down_full,
         up_full,
     )
@@ -521,21 +528,31 @@
     if per_window != SLOTS * HOT:
         by_block = (ids.reshape(-1, SLOTS * HOT) for ids in (near_ids, far_ids))
         asked = jnp.concatenate(tuple(by_block), axis=1)
-    sums = pool_lookups(0, asked, table_rows, pools_per)
+
+    def answered(sums):
+        return lax.all_to_all(
+            sums.reshape(near_count, pools_per, emb_width),
+            "table",
+            split_axis=0,
+            concat_axis=0,
+            tiled=True,
+            axis_index_groups=halves,
+        ).reshape(slot_count // 2, emb_width)
+
+    sums = pool_lookups(0, asked, table_rows)
     sums, far_share = lax.optimization_barrier((sums, far_share))
-    sums = pool_lookups(1, asked, narrow_whole(far_share), pools_per, (sums,))
-    arrived = lax.all_to_all(
-        sums, "table", split_axis=0, concat_axis=0, tiled=True, axis_index_groups=halves
-    )
+    near = answered(sums)
+    far = answered(pool_lookups(1, asked, narrow_whole(far_share)))
     other_ids = lax.ppermute(far_ids, "table", across)
-    goals = jnp.stack(near_and_far(slot_target), axis=1)
-    arrived, other_ids, down_full, up_full, goals = lax.optimization_barrier(
-        (arrived, other_ids, down_full, up_full, goals)
+    goals = jnp.concatenate(near_and_far(slot_target))
+    near, far, other_ids, down_full, up_full, goals = lax.optimization_barrier(
+        (near, far, other_ids, down_full, up_full, goals)
     )
     logits, bag_grads, kept, sent = dense_step(
         swap,
         goals,
-        arrived.reshape(slot_count, emb_width),
+        near,
+        far,
         down_full,
         up_full,
         cross_bias,
@@ -570,7 +587,6 @@
         mine = gather_blocks(share, "narrow", narrow_levels)
         other = jnp.zeros_like(mine)
     level_sum = gather_blocks(summed(pieces), "table", table_levels[1:])
-    level_sum, other = lax.optimization_barrier((level_sum, other))
     pieces = gathered_pieces(level_sum, "table", table_levels[0])
     new_rows, new_accum = update_rows(
         narrow_index.reshape(1), table_rows, mine, other, accum, narrows

time: 121 us -> 122 us (level)
  waiting for transfers between devices: 53 us -> 48.7 us
  starting transfers between devices: 29 us -> 31.6 us
  other arithmetic: 1.9 us -> 3.86 us
  Pallas kernels: 19.2 us -> 20.5 us
    ppermute x1, waiting for transfers between devices: 9.27 us -> 3.76 us  [local(): other_ids = lax.ppermute(far_ids, 'table', across)]
    all_to_all x1 -> x2, starting transfers between devices: 3.7 us -> 7 us  [answered(): lax.all_to_all(sums.reshape(near_count, pools_per, emb_width), 'table', s...]
    all_to_all x1 -> x2, waiting for transfers between devices: 3.07 us -> 5.94 us  [answered(): lax.all_to_all(sums.reshape(near_count, pools_per, emb_width), 'table', s...]
    ppermute x3, waiting for transfers between devices: 3.5 us -> 1.01 us  [narrow_whole(): came = lax.ppermute(block, 'narrow', sent_from('narrow', 1, 2, 1))]
    select_n x2, other arithmetic: 0.21 us -> 2.18 us  [narrow_whole(): first = jnp.where(narrow_index == 0, block, came)]
    pallas_call x2, Pallas kernels: 4.4 us -> 5.76 us  [pool_lookups(): kernel_call(functools.partial(pool_kernel, part, far), jax.ShapeDtypeStru...]
  transfers between devices with their start and end apart: 21 -> 22, of which waited for: 14 -> 13; matrix products, arithmetic and copies ran while one was open for 2% -> 4% of each run, Pallas kernels for 10% -> 13%
where the time goes in v7:
time: 122 us; the launch traced here: 121 us
  waiting for transfers between devices  48.7 us (40%)
  starting transfers between devices  31.6 us (26%)
  Pallas kernels  20.5 us (17%)
  blocking collectives  13.3 us (11%)
  other arithmetic  3.86 us (3%)
  local copies, waits for them, and re-layouts  1.95 us (2%)
  between operations  1.31 us (1%)
    ppermute x6, waiting for transfers between devices, scattered_pieces(): pieces.append(lax.ppermute(outgoing, axis, pairs))  25.6 us
    all_to_all x1, blocking collectives, local(): lax.all_to_all(asked, 'table', split_axis=0, concat_axis=0, tiled=True, a...  13.3 us
    ppermute x6, waiting for transfers between devices, gathered_pieces(): came = lax.ppermute(block, axis, sent_from(axis, stride, group, step))  12.1 us
    ppermute x6, starting transfers between devices, scattered_pieces(): pieces.append(lax.ppermute(outgoing, axis, pairs))  8 us
    ppermute x6, starting transfers between devices, gathered_pieces(): came = lax.ppermute(block, axis, sent_from(axis, stride, group, step))  7.86 us
    all_to_all x2, starting transfers between devices, answered(): lax.all_to_all(sums.reshape(near_count, pools_per, emb_width), 'table', s...  7 us
    all_to_all x2, waiting for transfers between devices, answered(): lax.all_to_all(sums.reshape(near_count, pools_per, emb_width), 'table', s...  5.94 us
    pallas_call x2, Pallas kernels, pool_lookups(): kernel_call(functools.partial(pool_kernel, part, far), jax.ShapeDtypeStru...  5.76 us
  transfers between devices with their start and end apart: 22, of which 13 were waited for; matrix products, arithmetic and copies ran while one was open for 4% of the time, Pallas kernels for 13%

profile of v7, /device:TPU:0, one launch (start us, length us, event | category | flops | bytes accessed | tf_op | source)
XLA Modules:
  0.0 121.2 jit_solution(13027657521884903049)
XLA Ops:
  0.6 1.0 constant_dynamic-slice_fusion.9
  1.6 4.1 %collective-permute-start = (bf16[512,256]{1,0:T(8,128)(2,1)S(1)}, bf16[512,256]{1,0:T(8,128)(2,1)S(1)}, u32[]{:S(2)}, u32[]{:S(2)}) collective-permute-start(bf16[512,256]{1,0:T(8,128)(2,1)S(1)} %constant_dynamic-slice_fusion.9), channel_id=1, source_target_pairs={{0,16},{2,18},{4,20},{6,22},{8,24},{10,26},{12,28},{14,30},{16,0},... | collective-permute-start | bytes 786440 | tf_op jit(solution)/shard_map/ppermute | solution.py:518
  5.7 0.7 constant_dynamic-slice_fusion.11
  6.5 13.3 %all_to_all.20.ids_ref = s32[8,1,1024]{2,1,0:T(1,128)} all-to-all(s32[8,1,1024]{2,1,0:T(1,128)S(1)} %broadcast_in_dim.6), channel_id=1, replica_groups={{0,2,4,6,8,10,12,14},{16,18,20,22,24,26,28,30},{1,3,5,7,9,11,13,15},{17..., dimensions={0} | all-to-all | bytes 65536 | tf_op jit(solution)/shard_map/all_to_all | solution.py:524
  19.8 3.6 %shard_map.128 = bf16[1024,256]{1,0:T(8,128)(2,1)} custom-call(s32[8,1,1024]{2,1,0:T(1,128)} %all_to_all.20.ids_ref, bf16[1024,256]{1,0:T(8,128)(2,1)} %rows_ref.3), custom_call_target="tpu_custom_call" | custom-call | flops 536870912 | bytes 1048576 | tf_op jit(solution)/shard_map/pallas_call | solution.py:126
  23.4 3.5 %all-to-all-start.1 = ((bf16[8,128,256]{2,1,0:T(8,128)(2,1)}), bf16[8,128,256]{2,1,0:T(8,128)(2,1)S(1)}, u32[]{:S(2)}, u32[]{:S(2)}) async-start(bf16[8,128,256]{2,1,0:T(8,128)(2,1)} %bitcast.30), calls=%async_computation.1 | async-start | bytes 1048576 | tf_op jit(solution)/shard_map/all_to_all | solution.py:533
  26.9 0.1 collective-permute-start.1
  27.0 0.5 collective-permute-start.4
  27.5 0.1 collective-permute-start.3
  27.7 1.0 collective-permute-done.1
  28.7 1.0 broadcast_select_fusion.5
  29.7 2.2 %shard_map.129 = bf16[1024,256]{1,0:T(8,128)(2,1)} custom-call(s32[8,1,1024]{2,1,0:T(1,128)S(1)} %copy-done.1, bf16[1024,256]{1,0:T(8,128)(2,1)S(1)} %pad_maximum_fusion.2.rows_ref), custom_call_target="tpu_custom_call" | custom-call | flops 536870912 | bytes 1048576 | tf_op jit(solution)/shard_map/pallas_call | solution.py:126
  31.9 2.6 %all-to-all-done.1 = bf16[8,128,256]{2,1,0:T(8,128)(2,1)S(1)} async-done(((bf16[8,128,256]{2,1,0:T(8,128)(2,1)}), bf16[8,128,256]{2,1,0:T(8,128)(2,1)S(1)}, u32[]{:S(2)}, u32[]{:S(2)}) %all-to-all-start.1) | async-done | bytes 524320 | tf_op jit(solution)/shard_map/all_to_all | solution.py:533
  34.5 3.5 %all-to-all-start.2 = ((bf16[8,128,256]{2,1,0:T(8,128)(2,1)}), bf16[8,128,256]{2,1,0:T(8,128)(2,1)S(1)}, u32[]{:S(2)}, u32[]{:S(2)}) async-start(bf16[8,128,256]{2,1,0:T(8,128)(2,1)} %bitcast.3), calls=%async_computation.2 | async-start | bytes 1048576 | tf_op jit(solution)/shard_map/all_to_all | solution.py:533
  38.2 1.2 broadcast_select_fusion.1
  39.5 3.8 %collective-permute-done.2 = s32[8,512]{1,0:T(8,128)S(1)} collective-permute-done((s32[8,512]{1,0:T(8,128)S(1)}, s32[8,512]{1,0:T(8,128)S(1)}, u32[]{:S(2)}, u32[]{:S(2)}) %collective-permute-start.2) | collective-permute-done | bytes 16416 | tf_op jit(solution)/shard_map/ppermute | solution.py:546
  43.3 3.3 %all-to-all-done.2 = bf16[8,128,256]{2,1,0:T(8,128)(2,1)S(1)} async-done(((bf16[8,128,256]{2,1,0:T(8,128)(2,1)}), bf16[8,128,256]{2,1,0:T(8,128)(2,1)S(1)}, u32[]{:S(2)}, u32[]{:S(2)}) %all-to-all-start.2) | async-done | bytes 524320 | tf_op jit(solution)/shard_map/all_to_all | solution.py:533
  46.6 3.8 %shard_map.130 = (f32[1,128]{1,0:T(1,128)}, bf16[1024,256]{1,0:T(8,128)(2,1)S(1)}, bf16[1024,512]{1,0:T(8,128)(2,1)S(1)}, bf16[1024,512]{1,0:T(8,128)(2,1)S(1)}) custom-call(s32[1]{0:T(128)} %bitcast.swap_ref.share_ref, s32[1,2048]{1,0:T(1,128)S(1)} %bitcast.26, f32[1,2048]{1,0:T(1,128)S(1)} %bitcast.28, bf16[1,2048]{1,0:T(2,128)(2,1)S(1)} %reshape.60.weight_ref, ...), custom_call_target="tpu_custom_call" | custom-call | flops 1879048192 | bytes 5242880 | tf_op jit(solution)/shard_map/pallas_call | solution.py:296
  50.4 0.1 collective-permute-start.5
  50.4 2.4 %shard_map.131 = bf16[2048,256]{1,0:T(8,128)(2,1)} custom-call(s32[16,128]{1,0:T(8,128)S(1)} %copy-done.2, bf16[1024,256]{1,0:T(8,128)(2,1)S(1)} %get-tuple-element.44.grads_ref), custom_call_target="tpu_custom_call" | custom-call | flops 1073741824 | bytes 1572864 | tf_op jit(solution)/shard_map/pallas_call | solution.py:211
  52.9 0.2 collective-permute-done.5
  53.1 0.3 add_convert_fusion
  53.4 3.8 %all-to-all-start.3 = ((bf16[16,128,256]{2,1,0:T(8,128)(2,1)}), bf16[16,128,256]{2,1,0:T(8,128)(2,1)S(1)}, u32[]{:S(2)}, u32[]{:S(2)}) async-start(bf16[16,128,256]{2,1,0:T(8,128)(2,1)} %bitcast.12), calls=%async_computation.3 | async-start | bytes 2097152 | tf_op jit(solution)/shard_map/all_to_all | solution.py:569
  57.3 2.6 %collective-permute-start.8 = (bf16[256,512]{1,0:T(8,128)(2,1)S(1)}, bf16[256,512]{1,0:T(8,128)(2,1)S(1)}, u32[]{:S(2)}, u32[]{:S(2)}) collective-permute-start(bf16[256,512]{1,0:T(8,128)(2,1)S(1)} %get-tuple-element.68), channel_id=1, source_target_pairs={{6,0},{4,2},{2,4},{0,6},{14,8},{12,10},{10,12},{8,14},{22,16},{20,... | collective-permute-start | bytes 786440 | tf_op jit(solution)/shard_map/ppermute | solution.py:438
  59.9 0.6 collective-permute-start.7
  60.5 0.4 collective-permute-start.6
  60.9 15.7 %collective-permute-done.8 = bf16[256,512]{1,0:T(8,128)(2,1)S(1)} collective-permute-done((bf16[256,512]{1,0:T(8,128)(2,1)S(1)}, bf16[256,512]{1,0:T(8,128)(2,1)S(1)}, u32[]{:S(2)}, u32[]{:S(2)}) %collective-permute-start.8) | collective-permute-done | bytes 262176 | tf_op jit(solution)/shard_map/ppermute | solution.py:438
  76.6 5.7 %collective-permute-done.7 = bf16[256,512]{1,0:T(8,128)(2,1)S(1)} collective-permute-done((bf16[256,512]{1,0:T(8,128)(2,1)S(1)}, bf16[256,512]{1,0:T(8,128)(2,1)S(1)}, u32[]{:S(2)}, u32[]{:S(2)}) %collective-permute-start.7) | collective-permute-done | bytes 262176 | tf_op jit(solution)/shard_map/ppermute | solution.py:438
  82.4 2.3 %collective-permute-done.6 = bf16[256,512]{1,0:T(8,128)(2,1)} collective-permute-done((bf16[256,512]{1,0:T(8,128)(2,1)S(1)}, bf16[256,512]{1,0:T(8,128)(2,1)}, u32[]{:S(2)}, u32[]{:S(2)}) %collective-permute-start.6) | collective-permute-done | bytes 262176 | tf_op jit(solution)/shard_map/ppermute | solution.py:438
  84.7 1.1 add_convert_fusion.1
  85.9 4.2 %collective-permute-start.10 = (bf16[64,512]{1,0:T(8,128)(2,1)S(1)}, bf16[64,512]{1,0:T(8,128)(2,1)S(1)}, u32[]{:S(2)}, u32[]{:S(2)}) collective-permute-start(bf16[64,512]{1,0:T(8,128)(2,1)S(1)} %get-tuple-element.77), channel_id=1, source_target_pairs={{16,0},{18,2},{20,4},{22,6},{24,8},{26,10},{28,12},{30,14},{0,16},... | collective-permute-start | bytes 196616 | tf_op jit(solution)/shard_map/ppermute | solution.py:438
  90.2 0.1 collective-permute-start.11
  90.3 4.1 %shard_map.132.mine_ref = bf16[1024,256]{1,0:T(8,128)(2,1)S(1)} custom-call(s32[16,512]{1,0:T(8,128)S(1)} %add_select_fusion.ids_ref, bf16[2048,256]{1,0:T(8,128)(2,1)S(1)} %bitcast.23), custom_call_target="tpu_custom_call" | custom-call | flops 1073741824 | bytes 1572864 | tf_op jit(solution)/shard_map/pallas_call | solution.py:164
  94.4 1.8 %collective-permute-done.11 = bf16[64,512]{1,0:T(8,128)(2,1)S(1)} collective-permute-done((bf16[64,512]{1,0:T(8,128)(2,1)S(1)}, bf16[64,512]{1,0:T(8,128)(2,1)S(1)}, u32[]{:S(2)}, u32[]{:S(2)}) %collective-permute-start.11) | collective-permute-done | bytes 65568 | tf_op jit(solution)/shard_map/ppermute | solution.py:438
  96.3 0.1 collective-permute-start.12
  96.5 2.3 %collective-permute-start.13 = (bf16[64,512]{1,0:T(8,128)(2,1)S(1)}, bf16[64,512]{1,0:T(8,128)(2,1)S(1)}, u32[]{:S(2)}, u32[]{:S(2)}) collective-permute-start(bf16[64,512]{1,0:T(8,128)(2,1)S(1)} %get-tuple-element.66), channel_id=1, source_target_pairs={{16,0},{18,2},{20,4},{22,6},{24,8},{26,10},{28,12},{30,14},{0,16},... | collective-permute-start | bytes 196616 | tf_op jit(solution)/shard_map/ppermute | solution.py:461
  98.9 1.9 %collective-permute-start.14 = (bf16[64,512]{1,0:T(8,128)(2,1)S(1)}, bf16[64,512]{1,0:T(8,128)(2,1)S(1)}, u32[]{:S(2)}, u32[]{:S(2)}) collective-permute-start(bf16[64,512]{1,0:T(8,128)(2,1)S(1)} %get-tuple-element.66), channel_id=1, source_target_pairs={{24,0},{26,2},{28,4},{30,6},{16,8},{18,10},{20,12},{22,14},{8,16},... | collective-permute-start | bytes 196616 | tf_op jit(solution)/shard_map/ppermute | solution.py:461
  100.8 2.4 %collective-permute-done.13 = bf16[64,512]{1,0:T(8,128)(2,1)S(1)} collective-permute-done((bf16[64,512]{1,0:T(8,128)(2,1)S(1)}, bf16[64,512]{1,0:T(8,128)(2,1)S(1)}, u32[]{:S(2)}, u32[]{:S(2)}) %collective-permute-start.13) | collective-permute-done | bytes 65568 | tf_op jit(solution)/shard_map/ppermute | solution.py:461
  103.2 1.8 %collective-permute-done.14 = bf16[64,512]{1,0:T(8,128)(2,1)S(1)} collective-permute-done((bf16[64,512]{1,0:T(8,128)(2,1)S(1)}, bf16[64,512]{1,0:T(8,128)(2,1)S(1)}, u32[]{:S(2)}, u32[]{:S(2)}) %collective-permute-start.14) | collective-permute-done | bytes 65568 | tf_op jit(solution)/shard_map/ppermute | solution.py:461
  104.9 0.4 collective-permute-start.17
  105.4 1.9 %collective-permute-start.18 = (bf16[256,512]{1,0:T(8,128)(2,1)S(1)}, bf16[256,512]{1,0:T(8,128)(2,1)S(1)}, u32[]{:S(2)}, u32[]{:S(2)}) collective-permute-start(bf16[256,512]{1,0:T(8,128)(2,1)S(1)} %constant_dynamic-update-slice_fusion.refs_0_), channel_id=1, source_target_pairs={{4,0},{6,2},{0,4},{2,6},{12,8},{14,10},{8,12},{10,14},{20,16},{22,... | collective-permute-start | bytes 786440 | tf_op jit(solution)/shard_map/ppermute | solution.py:461
  107.3 1.2 %collective-permute-start.15 = (bf16[256,512]{1,0:T(8,128)(2,1)S(1)}, bf16[256,512]{1,0:T(8,128)(2,1)S(1)}, u32[]{:S(2)}, u32[]{:S(2)}) collective-permute-start(bf16[256,512]{1,0:T(8,128)(2,1)S(1)} %constant_dynamic-update-slice_fusion.refs_0_), channel_id=1, source_target_pairs={{6,0},{4,2},{2,4},{0,6},{14,8},{12,10},{10,12},{8,14},{22,16},{20,... | collective-permute-start | bytes 786440 | tf_op jit(solution)/shard_map/ppermute | solution.py:461
  108.5 0.1 pad_add_fusion.2.spots_ref
  108.6 4.5 %collective-permute-done.17.refs_1_ = bf16[256,512]{1,0:T(8,128)(2,1)S(1)} collective-permute-done((bf16[256,512]{1,0:T(8,128)(2,1)S(1)}, bf16[256,512]{1,0:T(8,128)(2,1)S(1)}, u32[]{:S(2)}, u32[]{:S(2)}) %collective-permute-start.17) | collective-permute-done | bytes 262176 | tf_op jit(solution)/shard_map/ppermute | solution.py:461
  113.1 3.5 %collective-permute-done.18.refs_2_ = bf16[256,512]{1,0:T(8,128)(2,1)S(1)} collective-permute-done((bf16[256,512]{1,0:T(8,128)(2,1)S(1)}, bf16[256,512]{1,0:T(8,128)(2,1)S(1)}, u32[]{:S(2)}, u32[]{:S(2)}) %collective-permute-start.18) | collective-permute-done | bytes 262176 | tf_op jit(solution)/shard_map/ppermute | solution.py:461
  116.5 1.7 %shard_map.134 = (f32[1024,256]{1,0:T(8,128)}, f32[1024,256]{1,0:T(8,128)}) custom-call(s32[3]{0:T(128)S(1)} %pad_add_fusion.2.spots_ref, bf16[256,512]{1,0:T(8,128)(2,1)S(1)} %constant_dynamic-update-slice_fusion.refs_0_, bf16[256,512]{1,0:T(8,128)(2,1)S(1)} %collective-permute-done.17.refs_1_, bf16[256,512]{1,0:T(8,128)(2,1)S(1)} %collective-permute-done.18.refs_2_), custom_call_target="tpu_custom_call" | custom-call | flops 393216 | bytes 2359296 | tf_op jit(solution)/shard_map/pallas_call | solution.py:356
  118.3 1.9 %shard_map.133 = (bf16[1024,256]{1,0:T(8,128)(2,1)}, f32[4,128]{1,0:T(4,128)}) custom-call(s32[1]{0:T(128)} %bitcast.swap_ref.share_ref, bf16[1024,256]{1,0:T(8,128)(2,1)S(1)} %copy-done, bf16[1024,256]{1,0:T(8,128)(2,1)S(1)} %shard_map.132.mine_ref, bf16[1024,256]{1,0:T(8,128)(2,1)S(1)} %collective-permute-done.16.other_ref, f32[8,128]{1,0:T(8,128)S(1)} %bitcast.27), custom_call_target="tpu_custom_call" | custom-call | flops 2097152 | bytes 2097152 | tf_op jit(solution)/shard_map/pallas_call | solution.py:388
  120.3 0.8 shard_map.135
  (49 shorter events, 0.6 us)
Async XLA Ops:
  1.6 21.8 %collective-permute-start = (bf16[512,256]{1,0:T(8,128)(2,1)S(1)}, bf16[512,256]{1,0:T(8,128)(2,1)S(1)}, u32[]{:S(2)}, u32[]{:S(2)}) collective-permute-start(bf16[512,256]{1,0:T(8,128)(2,1)S(1)} %constant_dynamic-slice_fusion.9), channel_id=1, source_target_pairs={{0,16},{2,18},{4,20},{6,22},{8,24},{10,26},{12,28},{14,30},{16,0},... | collective-permute-start | bytes 786440 | tf_op jit(solution)/shard_map/ppermute | solution.py:518
  19.8 7.2 %copy-start.6 = (bf16[1024,256]{1,0:T(8,128)(2,1)S(1)}, bf16[1024,256]{1,0:T(8,128)(2,1)}, u32[]{:S(2)}) copy-start(bf16[1024,256]{1,0:T(8,128)(2,1)} %param.12) | copy-start | bytes 1572868
  19.8 7.7 %copy-start.7 = (bf16[1024,256]{1,0:T(8,128)(2,1)S(1)}, bf16[1024,256]{1,0:T(8,128)(2,1)}, u32[]{:S(2)}) copy-start(bf16[1024,256]{1,0:T(8,128)(2,1)} %param.11) | copy-start | bytes 1572868
  19.8 7.8 %copy-start.8 = (bf16[2048]{0:T(1024)(128)(2,1)S(1)}, bf16[2048]{0:T(1024)(128)(2,1)}, u32[]{:S(2)}) copy-start(bf16[2048]{0:T(1024)(128)(2,1)} %param.14) | copy-start | bytes 12292
  19.8 7.8 %copy-start.2 = (s32[16,128]{1,0:T(8,128)S(1)}, s32[16,128]{1,0:T(8,128)}, u32[]{:S(2)}) copy-start(s32[16,128]{1,0:T(8,128)} %goals_ref.1) | copy-start | bytes 24580
  23.4 11.1 %all-to-all-start.1 = ((bf16[8,128,256]{2,1,0:T(8,128)(2,1)}), bf16[8,128,256]{2,1,0:T(8,128)(2,1)S(1)}, u32[]{:S(2)}, u32[]{:S(2)}) async-start(bf16[8,128,256]{2,1,0:T(8,128)(2,1)} %bitcast.30), calls=%async_computation.1 | async-start | bytes 1048576 | tf_op jit(solution)/shard_map/all_to_all | solution.py:533
  26.9 1.7 %collective-permute-start.1 = (bf16[512,256]{1,0:T(8,128)(2,1)S(1)}, bf16[512,256]{1,0:T(8,128)(2,1)}, u32[]{:S(2)}, u32[]{:S(2)}) collective-permute-start(bf16[512,256]{1,0:T(8,128)(2,1)S(1)} %collective-permute-done), channel_id=1, source_target_pairs={{1,0},{0,1},{3,2},{2,3},{5,4},{4,5},{7,6},{6,7},{9,8},{8,9},{11,10... | collective-permute-start | bytes 786440 | tf_op jit(solution)/shard_map/ppermute | solution.py:511
  27.0 11.1 %collective-permute-start.4 = (bf16[1024,256]{1,0:T(8,128)(2,1)S(1)}, bf16[1024,256]{1,0:T(8,128)(2,1)S(1)}, u32[]{:S(2)}, u32[]{:S(2)}) collective-permute-start(bf16[1024,256]{1,0:T(8,128)(2,1)S(1)} %copy-done.6), channel_id=1, source_target_pairs={{1,0},{0,1},{3,2},{2,3},{5,4},{4,5},{7,6},{6,7},{9,8},{8,9},{11,10... | collective-permute-start | bytes 1572872 | tf_op jit(solution)/shard_map/ppermute | solution.py:511
  27.5 10.7 %collective-permute-start.3 = (bf16[1024,256]{1,0:T(8,128)(2,1)S(1)}, bf16[1024,256]{1,0:T(8,128)(2,1)S(1)}, u32[]{:S(2)}, u32[]{:S(2)}) collective-permute-start(bf16[1024,256]{1,0:T(8,128)(2,1)S(1)} %copy-done.7), channel_id=1, source_target_pairs={{1,0},{0,1},{3,2},{2,3},{5,4},{4,5},{7,6},{6,7},{9,8},{8,9},{11,10... | collective-permute-start | bytes 1572872 | tf_op jit(solution)/shard_map/ppermute | solution.py:511
  27.7 2.1 %copy-start.1 = (s32[8,1,1024]{2,1,0:T(1,128)S(1)}, s32[8,1,1024]{2,1,0:T(1,128)}, u32[]{:S(2)}) copy-start(s32[8,1,1024]{2,1,0:T(1,128)} %all_to_all.20.ids_ref) | copy-start | bytes 98308
  34.5 12.1 %all-to-all-start.2 = ((bf16[8,128,256]{2,1,0:T(8,128)(2,1)}), bf16[8,128,256]{2,1,0:T(8,128)(2,1)S(1)}, u32[]{:S(2)}, u32[]{:S(2)}) async-start(bf16[8,128,256]{2,1,0:T(8,128)(2,1)} %bitcast.3), calls=%async_computation.2 | async-start | bytes 1048576 | tf_op jit(solution)/shard_map/all_to_all | solution.py:533
  38.1 5.2 %collective-permute-start.2 = (s32[8,512]{1,0:T(8,128)S(1)}, s32[8,512]{1,0:T(8,128)S(1)}, u32[]{:S(2)}, u32[]{:S(2)}) collective-permute-start(s32[8,512]{1,0:T(8,128)S(1)} %bitcast.32), channel_id=1, source_target_pairs={{0,16},{2,18},{4,20},{6,22},{8,24},{10,26},{12,28},{14,30},{16,0},... | collective-permute-start | bytes 49160 | tf_op jit(solution)/shard_map/ppermute | solution.py:546
  39.4 7.2 %copy-start.4 = (f32[2048]{0:T(1024)S(1)}, f32[2048]{0:T(1024)}, u32[]{:S(2)}) copy-start(f32[2048]{0:T(1024)} %param.13) | copy-start | bytes 24580
  39.4 7.1 %copy-start.5 = (f32[128]{0:T(128)S(1)}, f32[128]{0:T(128)}, u32[]{:S(2)}) copy-start(f32[128]{0:T(128)} %param.15) | copy-start | bytes 1540
  50.4 2.7 %collective-permute-start.5 = (bf16[1024,512]{1,0:T(8,128)(2,1)S(1)}, bf16[1024,512]{1,0:T(8,128)(2,1)S(1)}, u32[]{:S(2)}, u32[]{:S(2)}) collective-permute-start(bf16[1024,512]{1,0:T(8,128)(2,1)S(1)} %get-tuple-element.46), channel_id=1, source_target_pairs={{1,0},{0,1},{3,2},{2,3},{5,4},{4,5},{7,6},{6,7},{9,8},{8,9},{11,10... | collective-permute-start | bytes 3145736 | tf_op jit(solution)/shard_map/ppermute | solution.py:563
  53.4 36.9 %all-to-all-start.3 = ((bf16[16,128,256]{2,1,0:T(8,128)(2,1)}), bf16[16,128,256]{2,1,0:T(8,128)(2,1)S(1)}, u32[]{:S(2)}, u32[]{:S(2)}) async-start(bf16[16,128,256]{2,1,0:T(8,128)(2,1)} %bitcast.12), calls=%async_computation.3 | async-start | bytes 2097152 | tf_op jit(solution)/shard_map/all_to_all | solution.py:569
  57.3 19.3 %collective-permute-start.8 = (bf16[256,512]{1,0:T(8,128)(2,1)S(1)}, bf16[256,512]{1,0:T(8,128)(2,1)S(1)}, u32[]{:S(2)}, u32[]{:S(2)}) collective-permute-start(bf16[256,512]{1,0:T(8,128)(2,1)S(1)} %get-tuple-element.68), channel_id=1, source_target_pairs={{6,0},{4,2},{2,4},{0,6},{14,8},{12,10},{10,12},{8,14},{22,16},{20,... | collective-permute-start | bytes 786440 | tf_op jit(solution)/shard_map/ppermute | solution.py:438
  59.9 22.5 %collective-permute-start.7 = (bf16[256,512]{1,0:T(8,128)(2,1)S(1)}, bf16[256,512]{1,0:T(8,128)(2,1)S(1)}, u32[]{:S(2)}, u32[]{:S(2)}) collective-permute-start(bf16[256,512]{1,0:T(8,128)(2,1)S(1)} %get-tuple-element.69), channel_id=1, source_target_pairs={{4,0},{6,2},{0,4},{2,6},{12,8},{14,10},{8,12},{10,14},{20,16},{22,... | collective-permute-start | bytes 786440 | tf_op jit(solution)/shard_map/ppermute | solution.py:438
  60.5 24.2 %collective-permute-start.6 = (bf16[256,512]{1,0:T(8,128)(2,1)S(1)}, bf16[256,512]{1,0:T(8,128)(2,1)}, u32[]{:S(2)}, u32[]{:S(2)}) collective-permute-start(bf16[256,512]{1,0:T(8,128)(2,1)S(1)} %get-tuple-element.67), channel_id=1, source_target_pairs={{2,0},{0,2},{6,4},{4,6},{10,8},{8,10},{14,12},{12,14},{18,16},{16,... | collective-permute-start | bytes 786440 | tf_op jit(solution)/shard_map/ppermute | solution.py:438
  85.8 8.6 %collective-permute-start.9 = (bf16[64,512]{1,0:T(8,128)(2,1)S(1)}, bf16[64,512]{1,0:T(8,128)(2,1)S(1)}, u32[]{:S(2)}, u32[]{:S(2)}) collective-permute-start(bf16[64,512]{1,0:T(8,128)(2,1)S(1)} %get-tuple-element.78), channel_id=1, source_target_pairs={{8,0},{10,2},{12,4},{14,6},{0,8},{2,10},{4,12},{6,14},{24,16},{26,... | collective-permute-start | bytes 196616 | tf_op jit(solution)/shard_map/ppermute | solution.py:438
  85.9 8.5 %collective-permute-start.10 = (bf16[64,512]{1,0:T(8,128)(2,1)S(1)}, bf16[64,512]{1,0:T(8,128)(2,1)S(1)}, u32[]{:S(2)}, u32[]{:S(2)}) collective-permute-start(bf16[64,512]{1,0:T(8,128)(2,1)S(1)} %get-tuple-element.77), channel_id=1, source_target_pairs={{16,0},{18,2},{20,4},{22,6},{24,8},{26,10},{28,12},{30,14},{0,16},... | collective-permute-start | bytes 196616 | tf_op jit(solution)/shard_map/ppermute | solution.py:438
  90.2 6.1 %collective-permute-start.11 = (bf16[64,512]{1,0:T(8,128)(2,1)S(1)}, bf16[64,512]{1,0:T(8,128)(2,1)S(1)}, u32[]{:S(2)}, u32[]{:S(2)}) collective-permute-start(bf16[64,512]{1,0:T(8,128)(2,1)S(1)} %get-tuple-element.76), channel_id=1, source_target_pairs={{24,0},{26,2},{28,4},{30,6},{16,8},{18,10},{20,12},{22,14},{8,16},... | collective-permute-start | bytes 196616 | tf_op jit(solution)/shard_map/ppermute | solution.py:438
  96.2 22.1 %copy-start = (bf16[1024,256]{1,0:T(8,128)(2,1)S(1)}, bf16[1024,256]{1,0:T(8,128)(2,1)}, u32[]{:S(2)}) copy-start(bf16[1024,256]{1,0:T(8,128)(2,1)} %rows_ref.3) | copy-start | bytes 1572868
  96.2 22.1 %copy-start.3 = (f32[1024]{0:T(1024)S(1)}, f32[1024]{0:T(1024)}, u32[]{:S(2)}) copy-start(f32[1024]{0:T(1024)} %param.10) | copy-start | bytes 12292
  96.3 4.5 %collective-permute-start.12 = (bf16[64,512]{1,0:T(8,128)(2,1)S(1)}, bf16[64,512]{1,0:T(8,128)(2,1)S(1)}, u32[]{:S(2)}, u32[]{:S(2)}) collective-permute-start(bf16[64,512]{1,0:T(8,128)(2,1)S(1)} %get-tuple-element.66), channel_id=1, source_target_pairs={{8,0},{10,2},{12,4},{14,6},{0,8},{2,10},{4,12},{6,14},{24,16},{26,... | collective-permute-start | bytes 196616 | tf_op jit(solution)/shard_map/ppermute | solution.py:461
  96.5 6.6 %collective-permute-start.13 = (bf16[64,512]{1,0:T(8,128)(2,1)S(1)}, bf16[64,512]{1,0:T(8,128)(2,1)S(1)}, u32[]{:S(2)}, u32[]{:S(2)}) collective-permute-start(bf16[64,512]{1,0:T(8,128)(2,1)S(1)} %get-tuple-element.66), channel_id=1, source_target_pairs={{16,0},{18,2},{20,4},{22,6},{24,8},{26,10},{28,12},{30,14},{0,16},... | collective-permute-start | bytes 196616 | tf_op jit(solution)/shard_map/ppermute | solution.py:461
  98.9 6.1 %collective-permute-start.14 = (bf16[64,512]{1,0:T(8,128)(2,1)S(1)}, bf16[64,512]{1,0:T(8,128)(2,1)S(1)}, u32[]{:S(2)}, u32[]{:S(2)}) collective-permute-start(bf16[64,512]{1,0:T(8,128)(2,1)S(1)} %get-tuple-element.66), channel_id=1, source_target_pairs={{24,0},{26,2},{28,4},{30,6},{16,8},{18,10},{20,12},{22,14},{8,16},... | collective-permute-start | bytes 196616 | tf_op jit(solution)/shard_map/ppermute | solution.py:461
  100.8 17.5 %collective-permute-start.16 = (bf16[1024,256]{1,0:T(8,128)(2,1)S(1)}, bf16[1024,256]{1,0:T(8,128)(2,1)S(1)}, u32[]{:S(2)}, u32[]{:S(2)}) collective-permute-start(bf16[1024,256]{1,0:T(8,128)(2,1)S(1)} %shard_map.132.mine_ref), channel_id=1, source_target_pairs={{1,0},{0,1},{3,2},{2,3},{5,4},{4,5},{7,6},{6,7},{9,8},{8,9},{11,10... | collective-permute-start | bytes 1572872 | tf_op jit(solution)/shard_map/ppermute | solution.py:584
  104.9 8.1 %collective-permute-start.17 = (bf16[256,512]{1,0:T(8,128)(2,1)S(1)}, bf16[256,512]{1,0:T(8,128)(2,1)S(1)}, u32[]{:S(2)}, u32[]{:S(2)}) collective-permute-start(bf16[256,512]{1,0:T(8,128)(2,1)S(1)} %constant_dynamic-update-slice_fusion.refs_0_), channel_id=1, source_target_pairs={{2,0},{0,2},{6,4},{4,6},{10,8},{8,10},{14,12},{12,14},{18,16},{16,... | collective-permute-start | bytes 786440 | tf_op jit(solution)/shard_map/ppermute | solution.py:461
  105.4 11.2 %collective-permute-start.18 = (bf16[256,512]{1,0:T(8,128)(2,1)S(1)}, bf16[256,512]{1,0:T(8,128)(2,1)S(1)}, u32[]{:S(2)}, u32[]{:S(2)}) collective-permute-start(bf16[256,512]{1,0:T(8,128)(2,1)S(1)} %constant_dynamic-update-slice_fusion.refs_0_), channel_id=1, source_target_pairs={{4,0},{6,2},{0,4},{2,6},{12,8},{14,10},{8,12},{10,14},{20,16},{22,... | collective-permute-start | bytes 786440 | tf_op jit(solution)/shard_map/ppermute | solution.py:461
  107.3 13.0 %collective-permute-start.15 = (bf16[256,512]{1,0:T(8,128)(2,1)S(1)}, bf16[256,512]{1,0:T(8,128)(2,1)S(1)}, u32[]{:S(2)}, u32[]{:S(2)}) collective-permute-start(bf16[256,512]{1,0:T(8,128)(2,1)S(1)} %constant_dynamic-update-slice_fusion.refs_0_), channel_id=1, source_target_pairs={{6,0},{4,2},{2,4},{0,6},{14,8},{12,10},{10,12},{8,14},{22,16},{20,... | collective-permute-start | bytes 786440 | tf_op jit(solution)/shard_map/ppermute | solution.py:461

commit v8 on v6

--- a/solution.py
+++ b/solution.py
@@ -132,46 +132,53 @@
     )(ids, rows, *given)
 
 
-def row_grad_kernel(ids_ref, given_ref, out_ref, counts_ref, grads_ref, sem):
-    fetch = pltpu.make_async_copy(given_ref, grads_ref, sem)
-    fetch.start()
-    blocks = ids_ref.shape[0]
-    row_dev = out_ref.shape[0]
+def row_grad_kernel(swap_ref, ids_ref, grads_ref, kept_ref, sent_ref, counts_ref, sums_ref):
+    sources, _, pools, emb = grads_ref.shape
+    row_dev, slots = counts_ref.shape
+    half = row_dev // 2
+    per_block = HOT * SLOTS
     tile = 64
-    high, low = split_ids(ids_ref[...])
     choice = lookup_choice()
-    lines = joined((rows_dot(high, choice), rows_dot(low, choice)))
     position = lax.broadcasted_iota(jnp.int32, (tile, SLOTS), 0).astype(jnp.int16)
-    for block in range(blocks):
-        spread = []
-        for lookup in range(HOT):
-            line = lines[block : block + 1, lookup * SLOTS : (lookup + 1) * SLOTS]
-            spread.append(jnp.broadcast_to(line, (tile, SLOTS)).astype(jnp.int16))
-        for start in range(0, row_dev, tile):
-            counts = None
+    for part in range(2):
+        lanes = slice(part * per_block, (part + 1) * per_block)
+        ids = ids_ref[:, 0, lanes] if len(ids_ref.shape) == 3 else ids_ref[:, lanes]
+        high, low = split_ids(ids)
+        lines = joined((rows_dot(high, choice), rows_dot(low, choice)))
+        for block in range(slots // SLOTS):
+            spread = []
             for lookup in range(HOT):
-                found = ones_where(spread[lookup] - jnp.asarray(start, jnp.int16) == position)
-                counts = found if counts is None else counts + found
-            counts_ref[start : start + tile, block * SLOTS : (block + 1) * SLOTS] = counts
-    fetch.wait()
-    out_ref[...] = matmul(counts_ref[...], grads_ref[...]).astype(jnp.bfloat16)
-
-
-def row_grads(ids, slot_grads, row_dev):
-    slot_count, emb = slot_grads.shape
+                line = lines[block : block + 1, lookup * SLOTS : (lookup + 1) * SLOTS]
+                spread.append(jnp.broadcast_to(line, (tile, SLOTS)).astype(jnp.int16))
+            for start in range(0, row_dev, tile):
+                counts = None
+                for lookup in range(HOT):
+                    found = ones_where(spread[lookup] - jnp.asarray(start, jnp.int16) == position)
+                    counts = found if counts is None else counts + found
+                counts_ref[start : start + tile, block * SLOTS : (block + 1) * SLOTS] = counts
+        grads = grads_ref[:, part].reshape(sources * pools, emb)
+        where = slice(part * emb, (part + 1) * emb)
+        sums_ref[:, where] = matmul(counts_ref[...], grads).astype(jnp.bfloat16)
+    for out_ref, into_half in ((kept_ref, swap_ref[0]), (sent_ref, 1 - swap_ref[0])):
+        out_ref[...] = sums_ref[pl.ds(pl.multiple_of(into_half * half, half), half), :]
+
+
+def row_grads(swap, ids, slot_grads, row_dev):
+    sources, _, pools, emb = slot_grads.shape
+    slots = sources * pools
+    half = jax.ShapeDtypeStruct((row_dev // 2, 2 * emb), jnp.bfloat16)
     return kernel_call(
         row_grad_kernel,
-        jax.ShapeDtypeStruct((row_dev, emb), jnp.bfloat16),
-        (2 * row_dev * slot_count * emb, 2 * slot_grads.size + 2 * row_dev * emb),
+        (half, half),
+        (4 * row_dev * slots * emb, 2 * slot_grads.size + 4 * row_dev * emb),
         [
-            pltpu.VMEM((row_dev, slot_count), jnp.bfloat16),
-            pltpu.VMEM((slot_count, emb), jnp.bfloat16),
-            pltpu.SemaphoreType.DMA,
+            pltpu.VMEM((row_dev, slots), jnp.bfloat16),
+            pltpu.VMEM((row_dev, 2 * emb), jnp.bfloat16),
         ],
-        operands=1,
-        left=1,
-        room=16,
-    )(ids, slot_grads)
+        flags=1,
+        operands=2,
+        room=12,
+    )(swap, ids, slot_grads)
 
 
 def diagonal(size):
@@ -359,36 +366,58 @@
     )(spots, *arrays, *given)
 
 
-def update_kernel(share_ref, rows_ref, mine_ref, other_ref, accum_ref, rows_out_ref, accum_out_ref):
-    chunks = accum_ref.shape[0]
-    per_share = accum_out_ref.shape[0]
-    for chunk in range(chunks):
+def update_kernel(rows_ref, far_ref, accum_ref, *refs):
+    near_refs = refs[:-2]
+    rows_out_ref, accum_out_ref = refs[-2:]
+    emb = rows_ref.shape[1]
+    for chunk in range(accum_ref.shape[0]):
         part = slice(chunk * SLOTS, (chunk + 1) * SLOTS)
-        row_grad = mine_ref[part, :].astype(jnp.float32) + other_ref[part, :].astype(jnp.float32)
+        row_grad = far_ref[part, :].astype(jnp.float32)
+        for near_ref in near_refs:
+            row_grad = row_grad + near_ref[part, :emb].astype(jnp.float32)
         squares = jnp.mean(row_grad * row_grad, axis=1, keepdims=True)
         accum = as_column(accum_ref[chunk : chunk + 1, :]) + squares
         step = LEARN_RATE * row_grad * lax.rsqrt(accum + ADA_EPS)
         rows_out_ref[part, :] = (rows_ref[part, :].astype(jnp.float32) - step).astype(jnp.bfloat16)
-
-        @pl.when(share_ref[0] == chunk // per_share)
-        def _():
-            accum_out_ref[chunk % per_share : chunk % per_share + 1, :] = as_line(accum)
-
-
-def update_rows(share, rows, mine, other, accum, narrows):
-    row_dev, emb = rows.shape
-    chunks = row_dev // SLOTS
+        accum_out_ref[chunk : chunk + 1, :] = as_line(accum)
+
+
+def update_rows(rows, far, accum, nears):
+    share, emb = rows.shape
+    chunks = share // SLOTS
     new_rows, new_accum = kernel_call(
         update_kernel,
         (
-            jax.ShapeDtypeStruct((row_dev, emb), jnp.bfloat16),
-            jax.ShapeDtypeStruct((chunks // narrows, SLOTS), jnp.float32),
+            jax.ShapeDtypeStruct((share, emb), jnp.bfloat16),
+            jax.ShapeDtypeStruct((chunks, SLOTS), jnp.float32),
         ),
         (8 * rows.size, 8 * rows.size),
+        operands=3 + len(nears),
+    )(rows, far, accum.reshape(chunks, SLOTS), *nears)
+    return new_rows, new_accum.reshape(share)
+
+
+def join_kernel(swap_ref, mine_ref, other_ref, out_ref, sems):
+    half = mine_ref.shape[0]
+    copies = []
+    for i, (from_ref, at) in enumerate(((mine_ref, swap_ref[0]), (other_ref, 1 - swap_ref[0]))):
+        spot = pl.ds(pl.multiple_of(at * half, half), half)
+        copies.append(pltpu.make_async_copy(from_ref, out_ref.at[spot, :], sems.at[i]))
+        copies[-1].start()
+    for copy in copies:
+        copy.wait()
+
+
+def join_halves(swap, mine, other):
+    return kernel_call(
+        join_kernel,
+        jax.ShapeDtypeStruct((2 * mine.shape[0], mine.shape[1]), mine.dtype),
+        (0, 8 * mine.size),
+        [pltpu.SemaphoreType.DMA((2,))],
         flags=1,
-        operands=4,
-    )(share, rows, mine, other, accum.reshape(chunks, SLOTS))
-    return new_rows, new_accum.reshape(row_dev // narrows)
+        operands=2,
+        left_out=(0,),
+    )(swap, mine, other)
 
 
 def group_levels(size):
@@ -527,10 +556,9 @@
     arrived = lax.all_to_all(
         sums, "table", split_axis=0, concat_axis=0, tiled=True, axis_index_groups=halves
     )
-    other_ids = lax.ppermute(far_ids, "table", across)
     goals = jnp.stack(near_and_far(slot_target), axis=1)
-    arrived, other_ids, down_full, up_full, goals = lax.optimization_barrier(
-        (arrived, other_ids, down_full, up_full, goals)
+    arrived, down_full, up_full, goals = lax.optimization_barrier(
+        (arrived, down_full, up_full, goals)
     )
     logits, bag_grads, kept, sent = dense_step(
         swap,
@@ -547,40 +575,40 @@
         narrow_sum = (kept.astype(jnp.float32) + came.astype(jnp.float32)).astype(jnp.bfloat16)
     else:
         narrow_sum = scatter_sum(jnp.concatenate([kept, sent], axis=0), "narrow", narrow_levels)
-    slot_grads = return_grads(slot_target, bag_grads)
+    slot_grads = return_grads(goals, bag_grads)
     slot_grads, narrow_sum = lax.optimization_barrier((slot_grads, narrow_sum))
     returned = lax.all_to_all(
-        slot_grads.reshape(tables, pools_per, emb_width),
+        slot_grads.reshape(near_count, 2, pools_per, emb_width),
         "table",
         split_axis=0,
         concat_axis=0,
         tiled=True,
-    ).reshape(slot_count, emb_width)
+        axis_index_groups=halves,
+    )
     level_sum = scatter_sum(narrow_sum, "table", table_levels[:1])
     table_sum = scatter_sum(level_sum, "table", table_levels[1:-1])
-    all_ids = in_order(near_ids, other_ids).reshape(-1, SLOTS * HOT)
-    sent_grad = row_grads(all_ids, returned, row_dev)
+    mine, passed = row_grads(swap, asked, returned, row_dev)
     pieces = scattered_pieces(table_sum, "table", table_levels[-1])
-    sent_grad, *pieces = lax.optimization_barrier((sent_grad, *pieces))
+    mine, passed, *pieces = lax.optimization_barrier((mine, passed, *pieces))
     if paired:
-        mine = sent_grad
-        other = lax.ppermute(sent_grad, "narrow", sent_from("narrow", 1, 2, 1))
+        nears = [mine, lax.ppermute(passed, "narrow", sent_from("narrow", 1, 2, 1))]
     else:
-        share = scatter_sum(sent_grad, "narrow", narrow_levels)
-        mine = gather_blocks(share, "narrow", narrow_levels)
-        other = jnp.zeros_like(mine)
+        nears = [scatter_sum(jnp.concatenate([mine, passed], axis=0), "narrow", narrow_levels)]
+    far_term = summed([term[:, emb_width:] for term in nears])
     level_sum = gather_blocks(summed(pieces), "table", table_levels[1:])
-    level_sum, other = lax.optimization_barrier((level_sum, other))
     pieces = gathered_pieces(level_sum, "table", table_levels[0])
-    new_rows, new_accum = update_rows(
-        narrow_index.reshape(1), table_rows, mine, other, accum, narrows
-    )
+    far_term = lax.ppermute(far_term, "table", across)
+    own_accum = lax.dynamic_slice_in_dim(accum, narrow_index * share_rows, share_rows, 0)
+    new_share, new_accum = update_rows(own_share, far_term, own_accum, nears)
+    if paired:
+        other_share = lax.ppermute(new_share, "narrow", sent_from("narrow", 1, 2, 1))
+        new_rows = join_halves(swap, new_share, other_share)
+    else:
+        new_rows = gather_blocks(new_share, "narrow", narrow_levels)
     scale = 1.0 / math.sqrt(samples * tables * narrows)
     spot, last = pieces[-1]
     grads = spread_pieces(pieces[:-1], scale, factor_down.shape[0])
-    last, new_rows, new_accum, *grads = lax.optimization_barrier(
-        (last, new_rows, new_accum, *grads)
-    )
+    last, *grads = lax.optimization_barrier((last, *grads))
     down_grad, up_grad = spread_pieces([(spot, last)], scale, factor_down.shape[0], grads)
     return (logits, down_grad, up_grad, new_rows, new_accum)
 

time: 121 us -> 125 us (1.033)
  the two profiles are of different devices: /device:TPU:0 before, /device:TPU:8 now
where the time goes in v8:
time: 125 us; the launch traced here: 124 us
  waiting for transfers between devices  59.6 us (48%)
  starting transfers between devices  30.6 us (24%)
  Pallas kernels  17.9 us (14%)
  blocking collectives  9.26 us (7%)
  local copies, waits for them, and re-layouts  3.74 us (3%)
  other arithmetic  1.95 us (2%)
    ppermute x6, waiting for transfers between devices, scattered_pieces(): pieces.append(lax.ppermute(outgoing, axis, pairs))  22.5 us
    ppermute x6, waiting for transfers between devices, gathered_pieces(): came = lax.ppermute(block, axis, sent_from(axis, stride, group, step))  21.8 us
    all_to_all x1, waiting for transfers between devices, local(): lax.all_to_all(sums, 'table', split_axis=0, concat_axis=0, tiled=True, ax...  11.5 us
    all_to_all x1, blocking collectives, local(): lax.all_to_all(asked, 'table', split_axis=0, concat_axis=0, tiled=True, a...  9.26 us
    all_to_all x1, starting transfers between devices, local(): lax.all_to_all(sums, 'table', split_axis=0, concat_axis=0, tiled=True, ax...  8.02 us
    ppermute x6, starting transfers between devices, gathered_pieces(): came = lax.ppermute(block, axis, sent_from(axis, stride, group, step))  7.54 us
    ppermute x6, starting transfers between devices, scattered_pieces(): pieces.append(lax.ppermute(outgoing, axis, pairs))  7.03 us
    pallas_call x2, Pallas kernels, pool_lookups(): kernel_call(functools.partial(pool_kernel, part), jax.ShapeDtypeStruct((s...  4.4 us
  transfers between devices with their start and end apart: 22, of which 13 were waited for; matrix products, arithmetic and copies ran while one was open for 3% of the time, Pallas kernels for 9%

profile of v8, /device:TPU:8, one launch (start us, length us, event | category | flops | bytes accessed | tf_op | source)
XLA Modules:
  0.0 124.2 jit_solution(8631326390219092879)
XLA Ops:
  0.7 1.0 constant_dynamic-slice_fusion.9.rows_ref
  1.6 2.7 %collective-permute-start = (bf16[512,256]{1,0:T(8,128)(2,1)S(1)}, bf16[512,256]{1,0:T(8,128)(2,1)S(1)}, u32[]{:S(2)}, u32[]{:S(2)}) collective-permute-start(bf16[512,256]{1,0:T(8,128)(2,1)S(1)} %constant_dynamic-slice_fusion.9.rows_ref), channel_id=1, source_target_pairs={{0,16},{2,18},{4,20},{6,22},{8,24},{10,26},{12,28},{14,30},{16,0},... | collective-permute-start | bytes 786440 | tf_op jit(solution)/shard_map/ppermute | solution.py:540
  4.3 0.7 constant_dynamic-slice_fusion.11
  5.1 9.3 %all_to_all.15.ids_ref = s32[8,1,1024]{2,1,0:T(1,128)S(1)} all-to-all(s32[8,1,1024]{2,1,0:T(1,128)S(1)} %broadcast_in_dim.6), channel_id=1, replica_groups={{0,2,4,6,8,10,12,14},{16,18,20,22,24,26,28,30},{1,3,5,7,9,11,13,15},{17..., dimensions={0} | all-to-all | bytes 65536 | tf_op jit(solution)/shard_map/all_to_all | solution.py:546
  14.3 1.0 copy-done.1
  15.4 2.2 %shard_map.128.refs_0_ = bf16[8,2,128,256]{3,2,1,0:T(8,128)(2,1)} custom-call(s32[8,1,1024]{2,1,0:T(1,128)S(1)} %all_to_all.15.ids_ref, bf16[1024,256]{1,0:T(8,128)(2,1)S(1)} %copy-done.1), custom_call_target="tpu_custom_call" | custom-call | flops 536870912 | bytes 1048576 | tf_op jit(solution)/shard_map/pallas_call | solution.py:118
  17.7 1.5 %collective-permute-done.1 = bf16[512,256]{1,0:T(8,128)(2,1)S(1)} collective-permute-done((bf16[512,256]{1,0:T(8,128)(2,1)S(1)}, bf16[512,256]{1,0:T(8,128)(2,1)S(1)}, u32[]{:S(2)}, u32[]{:S(2)}) %collective-permute-start.1) | collective-permute-done | bytes 262176 | tf_op jit(solution)/shard_map/ppermute | solution.py:533
  19.3 2.2 %shard_map.129 = bf16[8,2,128,256]{3,2,1,0:T(8,128)(2,1)} custom-call(s32[8,1,1024]{2,1,0:T(1,128)S(1)} %all_to_all.15.ids_ref, bf16[1024,256]{1,0:T(8,128)(2,1)S(1)} %pad_maximum_fusion.2.rows_ref, bf16[8,2,128,256]{3,2,1,0:T(8,128)(2,1)} %shard_map.128.refs_0_), custom_call_target="tpu_custom_call", output_to_operand_aliasing={{}: (2, {})} | custom-call | flops 536870912 | bytes 1048576 | tf_op jit(solution)/shard_map/pallas_call | solution.py:118
  21.5 8.0 %all-to-all-start.1 = ((bf16[8,2,128,256]{3,2,1,0:T(8,128)(2,1)}), bf16[8,2,128,256]{3,2,1,0:T(8,128)(2,1)S(1)}, u32[]{:S(2)}, u32[]{:S(2)}) async-start(bf16[8,2,128,256]{3,2,1,0:T(8,128)(2,1)} %shard_map.129), calls=%async_computation.1 | async-start | bytes 2097152 | tf_op jit(solution)/shard_map/all_to_all | solution.py:556
  29.6 0.5 collective-permute-start.3
  30.1 1.3 %collective-permute-done.2 = bf16[1024,256]{1,0:T(8,128)(2,1)S(1)} collective-permute-done((bf16[1024,256]{1,0:T(8,128)(2,1)S(1)}, bf16[1024,256]{1,0:T(8,128)(2,1)S(1)}, u32[]{:S(2)}, u32[]{:S(2)}) %collective-permute-start.2) | collective-permute-done | bytes 524320 | tf_op jit(solution)/shard_map/ppermute | solution.py:533
  31.5 0.7 collective-permute-done.3
  32.2 0.1 broadcast_select_fusion.1
  32.5 11.5 %all-to-all-done.1 = bf16[8,2,128,256]{3,2,1,0:T(8,128)(2,1)S(1)} async-done(((bf16[8,2,128,256]{3,2,1,0:T(8,128)(2,1)}), bf16[8,2,128,256]{3,2,1,0:T(8,128)(2,1)S(1)}, u32[]{:S(2)}, u32[]{:S(2)}) %all-to-all-start.1) | async-done | bytes 1048608 | tf_op jit(solution)/shard_map/all_to_all | solution.py:556
  44.1 3.7 %shard_map.130 = (f32[1,128]{1,0:T(1,128)}, bf16[1024,256]{1,0:T(8,128)(2,1)S(1)}, bf16[1024,512]{1,0:T(8,128)(2,1)S(1)}, bf16[1024,512]{1,0:T(8,128)(2,1)S(1)}) custom-call(s32[1]{0:T(128)} %bitcast.swap_ref, s32[1,2048]{1,0:T(1,128)S(1)} %bitcast.18, f32[1,2048]{1,0:T(1,128)S(1)} %bitcast.20, bf16[1,2048]{1,0:T(2,128)(2,1)S(1)} %reshape.46.weight_ref, ...), custom_call_target="tpu_custom_call" | custom-call | flops 1879048192 | bytes 5242880 | tf_op jit(solution)/shard_map/pallas_call | solution.py:297
  47.8 0.1 collective-permute-start.4
  47.9 2.4 %shard_map.131 = bf16[2048,256]{1,0:T(8,128)(2,1)} custom-call(s32[16,128]{1,0:T(8,128)S(1)} %bitcast.19, bf16[1024,256]{1,0:T(8,128)(2,1)S(1)} %get-tuple-element.41.grads_ref), custom_call_target="tpu_custom_call" | custom-call | flops 1073741824 | bytes 1572864 | tf_op jit(solution)/shard_map/pallas_call | solution.py:216
  50.3 0.2 collective-permute-done.4
  50.5 0.3 add_convert_fusion
  50.8 4.2 %all-to-all-start.2 = ((bf16[8,2,128,256]{3,2,1,0:T(8,128)(2,1)}), bf16[8,2,128,256]{3,2,1,0:T(8,128)(2,1)S(1)}, u32[]{:S(2)}, u32[]{:S(2)}) async-start(bf16[8,2,128,256]{3,2,1,0:T(8,128)(2,1)} %bitcast.10), calls=%async_computation.2 | async-start | bytes 2097152 | tf_op jit(solution)/shard_map/all_to_all | solution.py:580
  55.0 0.8 constant_dynamic-slice_fusion.6
  55.8 1.5 %collective-permute-start.5 = (bf16[256,512]{1,0:T(8,128)(2,1)}, bf16[256,512]{1,0:T(8,128)(2,1)S(1)}, u32[]{:S(2)}, u32[]{:S(2)}) collective-permute-start(bf16[256,512]{1,0:T(8,128)(2,1)} %get-tuple-element.65), channel_id=1, source_target_pairs={{2,0},{0,2},{6,4},{4,6},{10,8},{8,10},{14,12},{12,14},{18,16},{16,... | collective-permute-start | bytes 786440 | tf_op jit(solution)/shard_map/ppermute | solution.py:460
  57.3 1.5 %collective-permute-start.6 = (bf16[256,512]{1,0:T(8,128)(2,1)S(1)}, bf16[256,512]{1,0:T(8,128)(2,1)S(1)}, u32[]{:S(2)}, u32[]{:S(2)}) collective-permute-start(bf16[256,512]{1,0:T(8,128)(2,1)S(1)} %get-tuple-element.67), channel_id=1, source_target_pairs={{4,0},{6,2},{0,4},{2,6},{12,8},{14,10},{8,12},{10,14},{20,16},{22,... | collective-permute-start | bytes 786440 | tf_op jit(solution)/shard_map/ppermute | solution.py:460
  58.7 0.6 collective-permute-start.7
  59.3 15.1 %collective-permute-done.5 = bf16[256,512]{1,0:T(8,128)(2,1)S(1)} collective-permute-done((bf16[256,512]{1,0:T(8,128)(2,1)}, bf16[256,512]{1,0:T(8,128)(2,1)S(1)}, u32[]{:S(2)}, u32[]{:S(2)}) %collective-permute-start.5) | collective-permute-done | bytes 262176 | tf_op jit(solution)/shard_map/ppermute | solution.py:460
  74.4 6.6 %collective-permute-done.7 = bf16[256,512]{1,0:T(8,128)(2,1)} collective-permute-done((bf16[256,512]{1,0:T(8,128)(2,1)S(1)}, bf16[256,512]{1,0:T(8,128)(2,1)}, u32[]{:S(2)}, u32[]{:S(2)}) %collective-permute-start.7) | collective-permute-done | bytes 262176 | tf_op jit(solution)/shard_map/ppermute | solution.py:460
  81.0 1.1 add_convert_fusion.2
  82.2 0.8 collective-permute-start.8
  82.9 2.7 %collective-permute-start.9 = (bf16[64,512]{1,0:T(8,128)(2,1)S(1)}, bf16[64,512]{1,0:T(8,128)(2,1)S(1)}, u32[]{:S(2)}, u32[]{:S(2)}) collective-permute-start(bf16[64,512]{1,0:T(8,128)(2,1)S(1)} %get-tuple-element.75), channel_id=1, source_target_pairs={{16,0},{18,2},{20,4},{22,6},{24,8},{26,10},{28,12},{30,14},{0,16},... | collective-permute-start | bytes 196616 | tf_op jit(solution)/shard_map/ppermute | solution.py:460
  85.6 3.2 %shard_map.132 = (bf16[512,512]{1,0:T(8,128)(2,1)S(1)}, bf16[512,512]{1,0:T(8,128)(2,1)S(1)}) custom-call(s32[1]{0:T(128)} %bitcast.swap_ref, s32[8,1,1024]{2,1,0:T(1,128)S(1)} %all_to_all.15.ids_ref, bf16[8,2,128,256]{3,2,1,0:T(8,128)(2,1)S(1)} %all-to-all-done.2.grads_ref), custom_call_target="tpu_custom_call" | custom-call | flops 1073741824 | bytes 2097152 | tf_op jit(solution)/shard_map/pallas_call | solution.py:170
  88.9 0.8 collective-permute-done.9
  89.7 2.3 %collective-permute-start.11 = (bf16[64,512]{1,0:T(8,128)(2,1)S(1)}, bf16[64,512]{1,0:T(8,128)(2,1)S(1)}, u32[]{:S(2)}, u32[]{:S(2)}) collective-permute-start(bf16[64,512]{1,0:T(8,128)(2,1)S(1)} %get-tuple-element.64), channel_id=1, source_target_pairs={{8,0},{10,2},{12,4},{14,6},{0,8},{2,10},{4,12},{6,14},{24,16},{26,... | collective-permute-start | bytes 196616 | tf_op jit(solution)/shard_map/ppermute | solution.py:483
  92.0 0.6 collective-permute-start.12
  92.6 1.1 collective-permute-start.13
  93.7 1.4 %collective-permute-done.11 = bf16[64,512]{1,0:T(8,128)(2,1)S(1)} collective-permute-done((bf16[64,512]{1,0:T(8,128)(2,1)S(1)}, bf16[64,512]{1,0:T(8,128)(2,1)S(1)}, u32[]{:S(2)}, u32[]{:S(2)}) %collective-permute-start.11) | collective-permute-done | bytes 65568 | tf_op jit(solution)/shard_map/ppermute | solution.py:483
  95.1 0.1 add_convert_fusion.1
  95.2 0.4 collective-permute-start.18
  95.6 2.3 %collective-permute-done.12 = bf16[64,512]{1,0:T(8,128)(2,1)S(1)} collective-permute-done((bf16[64,512]{1,0:T(8,128)(2,1)S(1)}, bf16[64,512]{1,0:T(8,128)(2,1)S(1)}, u32[]{:S(2)}, u32[]{:S(2)}) %collective-permute-start.12) | collective-permute-done | bytes 65568 | tf_op jit(solution)/shard_map/ppermute | solution.py:483
  97.9 8.4 %collective-permute-done.13 = bf16[64,512]{1,0:T(8,128)(2,1)S(1)} collective-permute-done((bf16[64,512]{1,0:T(8,128)(2,1)S(1)}, bf16[64,512]{1,0:T(8,128)(2,1)S(1)}, u32[]{:S(2)}, u32[]{:S(2)}) %collective-permute-start.13) | collective-permute-done | bytes 65568 | tf_op jit(solution)/shard_map/ppermute | solution.py:483
  106.4 1.3 %collective-permute-start.15 = (bf16[256,512]{1,0:T(8,128)(2,1)S(1)}, bf16[256,512]{1,0:T(8,128)(2,1)S(1)}, u32[]{:S(2)}, u32[]{:S(2)}) collective-permute-start(bf16[256,512]{1,0:T(8,128)(2,1)S(1)} %constant_dynamic-update-slice_fusion.refs_0_), channel_id=1, source_target_pairs={{2,0},{0,2},{6,4},{4,6},{10,8},{8,10},{14,12},{12,14},{18,16},{16,... | collective-permute-start | bytes 786440 | tf_op jit(solution)/shard_map/ppermute | solution.py:483
  107.7 0.8 collective-permute-start.16
  108.5 1.4 %collective-permute-start.14 = (bf16[256,512]{1,0:T(8,128)(2,1)S(1)}, bf16[256,512]{1,0:T(8,128)(2,1)S(1)}, u32[]{:S(2)}, u32[]{:S(2)}) collective-permute-start(bf16[256,512]{1,0:T(8,128)(2,1)S(1)} %constant_dynamic-update-slice_fusion.refs_0_), channel_id=1, source_target_pairs={{6,0},{4,2},{2,4},{0,6},{14,8},{12,10},{10,12},{8,14},{22,16},{20,... | collective-permute-start | bytes 786440 | tf_op jit(solution)/shard_map/ppermute | solution.py:483
  110.0 0.9 shard_map.135
  111.0 4.7 %collective-permute-done.15.refs_1_ = bf16[256,512]{1,0:T(8,128)(2,1)S(1)} collective-permute-done((bf16[256,512]{1,0:T(8,128)(2,1)S(1)}, bf16[256,512]{1,0:T(8,128)(2,1)S(1)}, u32[]{:S(2)}, u32[]{:S(2)}) %collective-permute-start.15) | collective-permute-done | bytes 262176 | tf_op jit(solution)/shard_map/ppermute | solution.py:483
  115.7 4.9 %collective-permute-done.16.refs_2_ = bf16[256,512]{1,0:T(8,128)(2,1)S(1)} collective-permute-done((bf16[256,512]{1,0:T(8,128)(2,1)S(1)}, bf16[256,512]{1,0:T(8,128)(2,1)S(1)}, u32[]{:S(2)}, u32[]{:S(2)}) %collective-permute-start.16) | collective-permute-done | bytes 262176 | tf_op jit(solution)/shard_map/ppermute | solution.py:483
  120.6 1.7 %shard_map.133 = (f32[1024,256]{1,0:T(8,128)}, f32[1024,256]{1,0:T(8,128)}) custom-call(s32[3]{0:T(128)S(1)} %pad_add_fusion.2.spots_ref, bf16[256,512]{1,0:T(8,128)(2,1)S(1)} %constant_dynamic-update-slice_fusion.refs_0_, bf16[256,512]{1,0:T(8,128)(2,1)S(1)} %collective-permute-done.15.refs_1_, bf16[256,512]{1,0:T(8,128)(2,1)S(1)} %collective-permute-done.16.refs_2_), custom_call_target="tpu_custom_call" | custom-call | flops 393216 | bytes 2359296 | tf_op jit(solution)/shard_map/pallas_call | solution.py:356
  122.4 0.8 shard_map.134
  123.2 0.8 shard_map.136
  (46 shorter events, 0.8 us)
Async XLA Ops:
  0.6 109.3 %copy-start = (f32[1024]{0:T(1024)S(1)}, f32[1024]{0:T(1024)}, u32[]{:S(2)}) copy-start(f32[1024]{0:T(1024)} %param.10) | copy-start | bytes 12292
  1.6 15.9 %collective-permute-start = (bf16[512,256]{1,0:T(8,128)(2,1)S(1)}, bf16[512,256]{1,0:T(8,128)(2,1)S(1)}, u32[]{:S(2)}, u32[]{:S(2)}) collective-permute-start(bf16[512,256]{1,0:T(8,128)(2,1)S(1)} %constant_dynamic-slice_fusion.9.rows_ref), channel_id=1, source_target_pairs={{0,16},{2,18},{4,20},{6,22},{8,24},{10,26},{12,28},{14,30},{16,0},... | collective-permute-start | bytes 786440 | tf_op jit(solution)/shard_map/ppermute | solution.py:540
  14.3 1.0 copy-start.1
  17.6 1.6 %collective-permute-start.1 = (bf16[512,256]{1,0:T(8,128)(2,1)S(1)}, bf16[512,256]{1,0:T(8,128)(2,1)S(1)}, u32[]{:S(2)}, u32[]{:S(2)}) collective-permute-start(bf16[512,256]{1,0:T(8,128)(2,1)S(1)} %collective-permute-done), channel_id=1, source_target_pairs={{1,0},{0,1},{3,2},{2,3},{5,4},{4,5},{7,6},{6,7},{9,8},{8,9},{11,10... | collective-permute-start | bytes 786440 | tf_op jit(solution)/shard_map/ppermute | solution.py:533
  21.5 8.1 %copy-start.5 = (bf16[1024,256]{1,0:T(8,128)(2,1)S(1)}, bf16[1024,256]{1,0:T(8,128)(2,1)}, u32[]{:S(2)}) copy-start(bf16[1024,256]{1,0:T(8,128)(2,1)} %param.11) | copy-start | bytes 1572868
  21.5 8.1 %copy-start.4 = (bf16[1024,256]{1,0:T(8,128)(2,1)S(1)}, bf16[1024,256]{1,0:T(8,128)(2,1)}, u32[]{:S(2)}) copy-start(bf16[1024,256]{1,0:T(8,128)(2,1)} %param.12) | copy-start | bytes 1572868
  21.5 8.6 %copy-start.7 = (bf16[2048]{0:T(1024)(128)(2,1)S(1)}, bf16[2048]{0:T(1024)(128)(2,1)}, u32[]{:S(2)}) copy-start(bf16[2048]{0:T(1024)(128)(2,1)} %param.14) | copy-start | bytes 12292
  21.5 8.6 %copy-start.6 = (s32[16,128]{1,0:T(8,128)S(1)}, s32[16,128]{1,0:T(8,128)}, u32[]{:S(2)}) copy-start(s32[16,128]{1,0:T(8,128)} %param.17) | copy-start | bytes 24580
  21.5 22.5 %all-to-all-start.1 = ((bf16[8,2,128,256]{3,2,1,0:T(8,128)(2,1)}), bf16[8,2,128,256]{3,2,1,0:T(8,128)(2,1)S(1)}, u32[]{:S(2)}, u32[]{:S(2)}) async-start(bf16[8,2,128,256]{3,2,1,0:T(8,128)(2,1)} %shard_map.129), calls=%async_computation.1 | async-start | bytes 2097152 | tf_op jit(solution)/shard_map/all_to_all | solution.py:556
  29.5 1.9 %collective-permute-start.2 = (bf16[1024,256]{1,0:T(8,128)(2,1)S(1)}, bf16[1024,256]{1,0:T(8,128)(2,1)S(1)}, u32[]{:S(2)}, u32[]{:S(2)}) collective-permute-start(bf16[1024,256]{1,0:T(8,128)(2,1)S(1)} %copy-done.5), channel_id=1, source_target_pairs={{1,0},{0,1},{3,2},{2,3},{5,4},{4,5},{7,6},{6,7},{9,8},{8,9},{11,10... | collective-permute-start | bytes 1572872 | tf_op jit(solution)/shard_map/ppermute | solution.py:533
  29.6 2.6 %collective-permute-start.3 = (bf16[1024,256]{1,0:T(8,128)(2,1)S(1)}, bf16[1024,256]{1,0:T(8,128)(2,1)S(1)}, u32[]{:S(2)}, u32[]{:S(2)}) collective-permute-start(bf16[1024,256]{1,0:T(8,128)(2,1)S(1)} %copy-done.4), channel_id=1, source_target_pairs={{1,0},{0,1},{3,2},{2,3},{5,4},{4,5},{7,6},{6,7},{9,8},{8,9},{11,10... | collective-permute-start | bytes 1572872 | tf_op jit(solution)/shard_map/ppermute | solution.py:533
  32.4 11.6 %copy-start.2 = (f32[2048]{0:T(1024)S(1)}, f32[2048]{0:T(1024)}, u32[]{:S(2)}) copy-start(f32[2048]{0:T(1024)} %param.13) | copy-start | bytes 24580
  32.4 11.6 %copy-start.3 = (f32[128]{0:T(128)S(1)}, f32[128]{0:T(128)}, u32[]{:S(2)}) copy-start(f32[128]{0:T(128)} %param.15) | copy-start | bytes 1540
  47.8 2.7 %collective-permute-start.4 = (bf16[1024,512]{1,0:T(8,128)(2,1)S(1)}, bf16[1024,512]{1,0:T(8,128)(2,1)S(1)}, u32[]{:S(2)}, u32[]{:S(2)}) collective-permute-start(bf16[1024,512]{1,0:T(8,128)(2,1)S(1)} %get-tuple-element.43), channel_id=1, source_target_pairs={{1,0},{0,1},{3,2},{2,3},{5,4},{4,5},{7,6},{6,7},{9,8},{8,9},{11,10... | collective-permute-start | bytes 3145736 | tf_op jit(solution)/shard_map/ppermute | solution.py:574
  50.8 34.8 %all-to-all-start.2 = ((bf16[8,2,128,256]{3,2,1,0:T(8,128)(2,1)}), bf16[8,2,128,256]{3,2,1,0:T(8,128)(2,1)S(1)}, u32[]{:S(2)}, u32[]{:S(2)}) async-start(bf16[8,2,128,256]{3,2,1,0:T(8,128)(2,1)} %bitcast.10), calls=%async_computation.2 | async-start | bytes 2097152 | tf_op jit(solution)/shard_map/all_to_all | solution.py:580
  55.8 18.6 %collective-permute-start.5 = (bf16[256,512]{1,0:T(8,128)(2,1)}, bf16[256,512]{1,0:T(8,128)(2,1)S(1)}, u32[]{:S(2)}, u32[]{:S(2)}) collective-permute-start(bf16[256,512]{1,0:T(8,128)(2,1)} %get-tuple-element.65), channel_id=1, source_target_pairs={{2,0},{0,2},{6,4},{4,6},{10,8},{8,10},{14,12},{12,14},{18,16},{16,... | collective-permute-start | bytes 786440 | tf_op jit(solution)/shard_map/ppermute | solution.py:460
  57.3 17.1 %collective-permute-start.6 = (bf16[256,512]{1,0:T(8,128)(2,1)S(1)}, bf16[256,512]{1,0:T(8,128)(2,1)S(1)}, u32[]{:S(2)}, u32[]{:S(2)}) collective-permute-start(bf16[256,512]{1,0:T(8,128)(2,1)S(1)} %get-tuple-element.67), channel_id=1, source_target_pairs={{4,0},{6,2},{0,4},{2,6},{12,8},{14,10},{8,12},{10,14},{20,16},{22,... | collective-permute-start | bytes 786440 | tf_op jit(solution)/shard_map/ppermute | solution.py:460
  58.7 22.2 %collective-permute-start.7 = (bf16[256,512]{1,0:T(8,128)(2,1)S(1)}, bf16[256,512]{1,0:T(8,128)(2,1)}, u32[]{:S(2)}, u32[]{:S(2)}) collective-permute-start(bf16[256,512]{1,0:T(8,128)(2,1)S(1)} %get-tuple-element.66), channel_id=1, source_target_pairs={{6,0},{4,2},{2,4},{0,6},{14,8},{12,10},{10,12},{8,14},{22,16},{20,... | collective-permute-start | bytes 786440 | tf_op jit(solution)/shard_map/ppermute | solution.py:460
  82.1 6.8 %collective-permute-start.10 = (bf16[64,512]{1,0:T(8,128)(2,1)S(1)}, bf16[64,512]{1,0:T(8,128)(2,1)S(1)}, u32[]{:S(2)}, u32[]{:S(2)}) collective-permute-start(bf16[64,512]{1,0:T(8,128)(2,1)S(1)} %get-tuple-element.74), channel_id=1, source_target_pairs={{24,0},{26,2},{28,4},{30,6},{16,8},{18,10},{20,12},{22,14},{8,16},... | collective-permute-start | bytes 196616 | tf_op jit(solution)/shard_map/ppermute | solution.py:460
  82.2 6.7 %collective-permute-start.8 = (bf16[64,512]{1,0:T(8,128)(2,1)S(1)}, bf16[64,512]{1,0:T(8,128)(2,1)S(1)}, u32[]{:S(2)}, u32[]{:S(2)}) collective-permute-start(bf16[64,512]{1,0:T(8,128)(2,1)S(1)} %get-tuple-element.76), channel_id=1, source_target_pairs={{8,0},{10,2},{12,4},{14,6},{0,8},{2,10},{4,12},{6,14},{24,16},{26,... | collective-permute-start | bytes 196616 | tf_op jit(solution)/shard_map/ppermute | solution.py:460
  82.9 6.7 %collective-permute-start.9 = (bf16[64,512]{1,0:T(8,128)(2,1)S(1)}, bf16[64,512]{1,0:T(8,128)(2,1)S(1)}, u32[]{:S(2)}, u32[]{:S(2)}) collective-permute-start(bf16[64,512]{1,0:T(8,128)(2,1)S(1)} %get-tuple-element.75), channel_id=1, source_target_pairs={{16,0},{18,2},{20,4},{22,6},{24,8},{26,10},{28,12},{30,14},{0,16},... | collective-permute-start | bytes 196616 | tf_op jit(solution)/shard_map/ppermute | solution.py:460
  89.6 5.5 %collective-permute-start.17 = (bf16[512,512]{1,0:T(8,128)(2,1)S(1)}, bf16[512,512]{1,0:T(8,128)(2,1)S(1)}, u32[]{:S(2)}, u32[]{:S(2)}) collective-permute-start(bf16[512,512]{1,0:T(8,128)(2,1)S(1)} %get-tuple-element.60), channel_id=1, source_target_pairs={{1,0},{0,1},{3,2},{2,3},{5,4},{4,5},{7,6},{6,7},{9,8},{8,9},{11,10... | collective-permute-start | bytes 1572872 | tf_op jit(solution)/shard_map/ppermute | solution.py:594
  89.7 5.4 %collective-permute-start.11 = (bf16[64,512]{1,0:T(8,128)(2,1)S(1)}, bf16[64,512]{1,0:T(8,128)(2,1)S(1)}, u32[]{:S(2)}, u32[]{:S(2)}) collective-permute-start(bf16[64,512]{1,0:T(8,128)(2,1)S(1)} %get-tuple-element.64), channel_id=1, source_target_pairs={{8,0},{10,2},{12,4},{14,6},{0,8},{2,10},{4,12},{6,14},{24,16},{26,... | collective-permute-start | bytes 196616 | tf_op jit(solution)/shard_map/ppermute | solution.py:483
  92.0 5.9 %collective-permute-start.12 = (bf16[64,512]{1,0:T(8,128)(2,1)S(1)}, bf16[64,512]{1,0:T(8,128)(2,1)S(1)}, u32[]{:S(2)}, u32[]{:S(2)}) collective-permute-start(bf16[64,512]{1,0:T(8,128)(2,1)S(1)} %get-tuple-element.64), channel_id=1, source_target_pairs={{16,0},{18,2},{20,4},{22,6},{24,8},{26,10},{28,12},{30,14},{0,16},... | collective-permute-start | bytes 196616 | tf_op jit(solution)/shard_map/ppermute | solution.py:483
  92.6 13.8 %collective-permute-start.13 = (bf16[64,512]{1,0:T(8,128)(2,1)S(1)}, bf16[64,512]{1,0:T(8,128)(2,1)S(1)}, u32[]{:S(2)}, u32[]{:S(2)}) collective-permute-start(bf16[64,512]{1,0:T(8,128)(2,1)S(1)} %get-tuple-element.64), channel_id=1, source_target_pairs={{24,0},{26,2},{28,4},{30,6},{16,8},{18,10},{20,12},{22,14},{8,16},... | collective-permute-start | bytes 196616 | tf_op jit(solution)/shard_map/ppermute | solution.py:483
  95.2 14.8 %collective-permute-start.18 = (bf16[512,256]{1,0:T(8,128)(2,1)S(1)}, bf16[512,256]{1,0:T(8,128)(2,1)S(1)}, u32[]{:S(2)}, u32[]{:S(2)}) collective-permute-start(bf16[512,256]{1,0:T(8,128)(2,1)S(1)} %add_convert_fusion.1), channel_id=1, source_target_pairs={{0,16},{2,18},{4,20},{6,22},{8,24},{10,26},{12,28},{14,30},{16,0},... | collective-permute-start | bytes 786440 | tf_op jit(solution)/shard_map/ppermute | solution.py:600
  106.4 9.3 %collective-permute-start.15 = (bf16[256,512]{1,0:T(8,128)(2,1)S(1)}, bf16[256,512]{1,0:T(8,128)(2,1)S(1)}, u32[]{:S(2)}, u32[]{:S(2)}) collective-permute-start(bf16[256,512]{1,0:T(8,128)(2,1)S(1)} %constant_dynamic-update-slice_fusion.refs_0_), channel_id=1, source_target_pairs={{2,0},{0,2},{6,4},{4,6},{10,8},{8,10},{14,12},{12,14},{18,16},{16,... | collective-permute-start | bytes 786440 | tf_op jit(solution)/shard_map/ppermute | solution.py:483
  107.7 12.9 %collective-permute-start.16 = (bf16[256,512]{1,0:T(8,128)(2,1)S(1)}, bf16[256,512]{1,0:T(8,128)(2,1)S(1)}, u32[]{:S(2)}, u32[]{:S(2)}) collective-permute-start(bf16[256,512]{1,0:T(8,128)(2,1)S(1)} %constant_dynamic-update-slice_fusion.refs_0_), channel_id=1, source_target_pairs={{4,0},{6,2},{0,4},{2,6},{12,8},{14,10},{8,12},{10,14},{20,16},{22,... | collective-permute-start | bytes 786440 | tf_op jit(solution)/shard_map/ppermute | solution.py:483
  108.5 13.9 %collective-permute-start.14 = (bf16[256,512]{1,0:T(8,128)(2,1)S(1)}, bf16[256,512]{1,0:T(8,128)(2,1)S(1)}, u32[]{:S(2)}, u32[]{:S(2)}) collective-permute-start(bf16[256,512]{1,0:T(8,128)(2,1)S(1)} %constant_dynamic-update-slice_fusion.refs_0_), channel_id=1, source_target_pairs={{6,0},{4,2},{2,4},{0,6},{14,8},{12,10},{10,12},{8,14},{22,16},{20,... | collective-permute-start | bytes 786440 | tf_op jit(solution)/shard_map/ppermute | solution.py:483
  110.9 12.3 %collective-permute-start.19 = (bf16[512,256]{1,0:T(8,128)(2,1)S(1)}, bf16[512,256]{1,0:T(8,128)(2,1)S(1)}, u32[]{:S(2)}, u32[]{:S(2)}) collective-permute-start(bf16[512,256]{1,0:T(8,128)(2,1)S(1)} %get-tuple-element.61.mine_ref), channel_id=1, source_target_pairs={{1,0},{0,1},{3,2},{2,3},{5,4},{4,5},{7,6},{6,7},{9,8},{8,9},{11,10... | collective-permute-start | bytes 786440 | tf_op jit(solution)/shard_map/ppermute | solution.py:604

commit v9 on v8

--- a/solution.py
+++ b/solution.py
@@ -133,8 +133,9 @@
 
 
 def row_grad_kernel(swap_ref, ids_ref, grads_ref, kept_ref, sent_ref, counts_ref, sums_ref):
-    sources, _, pools, emb = grads_ref.shape
+    sources, _, emb = grads_ref.shape
     row_dev, slots = counts_ref.shape
+    pools = slots // sources
     half = row_dev // 2
     per_block = HOT * SLOTS
     tile = 64
@@ -156,15 +157,15 @@
                     found = ones_where(spread[lookup] - jnp.asarray(start, jnp.int16) == position)
                     counts = found if counts is None else counts + found
                 counts_ref[start : start + tile, block * SLOTS : (block + 1) * SLOTS] = counts
-        grads = grads_ref[:, part].reshape(sources * pools, emb)
+        grads = grads_ref[:, part * pools : (part + 1) * pools].reshape(slots, emb)
         where = slice(part * emb, (part + 1) * emb)
         sums_ref[:, where] = matmul(counts_ref[...], grads).astype(jnp.bfloat16)
     for out_ref, into_half in ((kept_ref, swap_ref[0]), (sent_ref, 1 - swap_ref[0])):
         out_ref[...] = sums_ref[pl.ds(pl.multiple_of(into_half * half, half), half), :]
 
 
-def row_grads(swap, ids, slot_grads, row_dev):
-    sources, _, pools, emb = slot_grads.shape
+def row_grads(swap, ids, slot_grads, pools, row_dev):
+    sources, _, emb = slot_grads.shape
     slots = sources * pools
     half = jax.ShapeDtypeStruct((row_dev // 2, 2 * emb), jnp.bfloat16)
     return kernel_call(
@@ -506,10 +507,10 @@
     bag_count = samples * FEAT
     slot_count = tables * pools_per
     narrow_levels = group_levels(narrows)
-    table_levels = group_levels(tables)
     table_index = lax.axis_index("table")
     narrow_index = lax.axis_index("narrow")
     near_count = tables // 2
+    half_levels = group_levels(near_count)
     far_half = table_index // near_count
     halves = [list(range(near_count)), list(range(near_count, tables))]
     across = [(i, (i + near_count) % tables) for i in range(tables)]
@@ -576,27 +577,34 @@
     else:
         narrow_sum = scatter_sum(jnp.concatenate([kept, sent], axis=0), "narrow", narrow_levels)
     slot_grads = return_grads(goals, bag_grads)
-    slot_grads, narrow_sum = lax.optimization_barrier((slot_grads, narrow_sum))
+    groups = [group for _, group in half_levels]
+    share_terms = narrow_sum.reshape(*groups, -1, narrow_sum.shape[1])
+    order = list(range(len(groups)))[::-1] + [len(groups), len(groups) + 1]
+    share_terms = share_terms.transpose(order).reshape(near_count, -1, narrow_sum.shape[1])
+    rank = factor_down.shape[1]
+    outgoing = [slot_grads.reshape(near_count, 2 * pools_per, emb_width)]
+    outgoing += [share_terms[:, :, :rank], share_terms[:, :, rank:]]
     returned = lax.all_to_all(
-        slot_grads.reshape(near_count, 2, pools_per, emb_width),
+        jnp.concatenate(outgoing, axis=1),
         "table",
         split_axis=0,
         concat_axis=0,
         tiled=True,
         axis_index_groups=halves,
     )
-    level_sum = scatter_sum(narrow_sum, "table", table_levels[:1])
-    table_sum = scatter_sum(level_sum, "table", table_levels[1:-1])
-    mine, passed = row_grads(swap, asked, returned, row_dev)
-    pieces = scattered_pieces(table_sum, "table", table_levels[-1])
-    mine, passed, *pieces = lax.optimization_barrier((mine, passed, *pieces))
+    terms = jnp.sum(returned[:, 2 * pools_per :].astype(jnp.float32), axis=0)
+    half_sum = jnp.concatenate(jnp.split(terms, 2, axis=0), axis=1).astype(jnp.bfloat16)
+    other_sum = lax.ppermute(half_sum, "table", across)
+    mine, passed = row_grads(swap, asked, returned, pools_per, row_dev)
+    other_sum, mine, passed = lax.optimization_barrier((other_sum, mine, passed))
+    table_sum = summed([half_sum, other_sum])
     if paired:
         nears = [mine, lax.ppermute(passed, "narrow", sent_from("narrow", 1, 2, 1))]
     else:
         nears = [scatter_sum(jnp.concatenate([mine, passed], axis=0), "narrow", narrow_levels)]
     far_term = summed([term[:, emb_width:] for term in nears])
-    level_sum = gather_blocks(summed(pieces), "table", table_levels[1:])
-    pieces = gathered_pieces(level_sum, "table", table_levels[0])
+    level_sum = gather_blocks(table_sum, "table", half_levels[1:])
+    pieces = gathered_pieces(level_sum, "table", half_levels[0])
     far_term = lax.ppermute(far_term, "table", across)
     own_accum = lax.dynamic_slice_in_dim(accum, narrow_index * share_rows, share_rows, 0)
     new_share, new_accum = update_rows(own_share, far_term, own_accum, nears)

time: 125 us -> 115 us (0.920)
  the two profiles are of different devices: /device:TPU:8 before, /device:TPU:0 now
where the time goes in v9:
time: 115 us; the launch traced here: 114 us
  blocking collectives  43.1 us (37%)
  waiting for transfers between devices  36.7 us (32%)
  Pallas kernels  17 us (15%)
  starting transfers between devices  12.2 us (11%)
  local copies, waits for them, and re-layouts  3.14 us (3%)
  between operations  1.18 us (1%)
    all_to_all x1, blocking collectives, local(): lax.all_to_all(jnp.concatenate(outgoing, axis=1), 'table', split_axis=0,...  29.9 us
    all_to_all x1, blocking collectives, local(): lax.all_to_all(asked, 'table', split_axis=0, concat_axis=0, tiled=True, a...  13.2 us
    all_to_all x1, waiting for transfers between devices, local(): lax.all_to_all(sums, 'table', split_axis=0, concat_axis=0, tiled=True, ax...  12 us
    ppermute x1, waiting for transfers between devices, local(): far_term = lax.ppermute(far_term, 'table', across)  6.99 us
    ppermute x4, waiting for transfers between devices, gathered_pieces(): came = lax.ppermute(block, axis, sent_from(axis, stride, group, step))  6.75 us
    pallas_call x2, Pallas kernels, pool_lookups(): kernel_call(functools.partial(pool_kernel, part), jax.ShapeDtypeStruct((s...  4.39 us
    ppermute x1, waiting for transfers between devices, local(): other_sum = lax.ppermute(half_sum, 'table', across)  4.37 us
    ppermute x1, starting transfers between devices, local(): far_share = lax.ppermute(own_share, 'table', across)  4.1 us
  transfers between devices with their start and end apart: 14, of which 10 were waited for; matrix products, arithmetic and copies ran while one was open for 1% of the time, Pallas kernels for 9%

profile of v9, /device:TPU:0, one launch (start us, length us, event | category | flops | bytes accessed | tf_op | source)
XLA Modules:
  0.0 114.4 jit_solution(26927034584483423)
XLA Ops:
  0.7 1.0 constant_dynamic-slice_fusion.2.rows_ref
  1.6 4.1 %collective-permute-start = (bf16[512,256]{1,0:T(8,128)(2,1)S(1)}, bf16[512,256]{1,0:T(8,128)(2,1)S(1)}, u32[]{:S(2)}, u32[]{:S(2)}) collective-permute-start(bf16[512,256]{1,0:T(8,128)(2,1)S(1)} %constant_dynamic-slice_fusion.2.rows_ref), channel_id=1, source_target_pairs={{0,16},{2,18},{4,20},{6,22},{8,24},{10,26},{12,28},{14,30},{16,0},... | collective-permute-start | bytes 786440 | tf_op jit(solution)/shard_map/ppermute | solution.py:541
  5.7 0.7 constant_dynamic-slice_fusion.4
  6.5 13.2 %all_to_all.15.ids_ref = s32[8,1,1024]{2,1,0:T(1,128)S(1)} all-to-all(s32[8,1,1024]{2,1,0:T(1,128)S(1)} %broadcast_in_dim.6), channel_id=1, replica_groups={{0,2,4,6,8,10,12,14},{16,18,20,22,24,26,28,30},{1,3,5,7,9,11,13,15},{17..., dimensions={0} | all-to-all | bytes 65536 | tf_op jit(solution)/shard_map/all_to_all | solution.py:547
  19.7 1.0 copy-done.1
  20.8 2.2 %shard_map.128.refs_0_ = bf16[8,2,128,256]{3,2,1,0:T(8,128)(2,1)} custom-call(s32[8,1,1024]{2,1,0:T(1,128)S(1)} %all_to_all.15.ids_ref, bf16[1024,256]{1,0:T(8,128)(2,1)S(1)} %copy-done.1), custom_call_target="tpu_custom_call" | custom-call | flops 536870912 | bytes 1048576 | tf_op jit(solution)/shard_map/pallas_call | solution.py:118
  23.0 0.1 collective-permute-start.1
  23.1 1.5 %collective-permute-done.1 = bf16[512,256]{1,0:T(8,128)(2,1)S(1)} collective-permute-done((bf16[512,256]{1,0:T(8,128)(2,1)S(1)}, bf16[512,256]{1,0:T(8,128)(2,1)S(1)}, u32[]{:S(2)}, u32[]{:S(2)}) %collective-permute-start.1) | collective-permute-done | bytes 262176 | tf_op jit(solution)/shard_map/ppermute | solution.py:534
  24.7 2.2 %shard_map.129 = bf16[8,2,128,256]{3,2,1,0:T(8,128)(2,1)} custom-call(s32[8,1,1024]{2,1,0:T(1,128)S(1)} %all_to_all.15.ids_ref, bf16[1024,256]{1,0:T(8,128)(2,1)S(1)} %pad_maximum_fusion.3.rows_ref, bf16[8,2,128,256]{3,2,1,0:T(8,128)(2,1)} %shard_map.128.refs_0_), custom_call_target="tpu_custom_call", output_to_operand_aliasing={{}: (2, {})} | custom-call | flops 536870912 | bytes 1048576 | tf_op jit(solution)/shard_map/pallas_call | solution.py:118
  26.9 3.6 %all-to-all-start.1 = ((bf16[8,2,128,256]{3,2,1,0:T(8,128)(2,1)}), bf16[8,2,128,256]{3,2,1,0:T(8,128)(2,1)S(1)}, u32[]{:S(2)}, u32[]{:S(2)}) async-start(bf16[8,2,128,256]{3,2,1,0:T(8,128)(2,1)} %shard_map.129), calls=%async_computation.1 | async-start | bytes 2097152 | tf_op jit(solution)/shard_map/all_to_all | solution.py:557
  30.5 0.2 collective-permute-start.2
  30.7 0.4 collective-permute-start.3
  31.1 1.3 %collective-permute-done.2 = bf16[1024,256]{1,0:T(8,128)(2,1)S(1)} collective-permute-done((bf16[1024,256]{1,0:T(8,128)(2,1)S(1)}, bf16[1024,256]{1,0:T(8,128)(2,1)S(1)}, u32[]{:S(2)}, u32[]{:S(2)}) %collective-permute-start.2) | collective-permute-done | bytes 524320 | tf_op jit(solution)/shard_map/ppermute | solution.py:534
  32.5 0.7 collective-permute-done.3
  33.2 0.1 broadcast_select_fusion.1
  33.4 0.1 pad_maximum_fusion.1.down_ref
  33.5 0.1 pad_maximum_fusion.2.up_ref
  33.6 12.0 %all-to-all-done.1 = bf16[8,2,128,256]{3,2,1,0:T(8,128)(2,1)S(1)} async-done(((bf16[8,2,128,256]{3,2,1,0:T(8,128)(2,1)}), bf16[8,2,128,256]{3,2,1,0:T(8,128)(2,1)S(1)}, u32[]{:S(2)}, u32[]{:S(2)}) %all-to-all-start.1) | async-done | bytes 1048608 | tf_op jit(solution)/shard_map/all_to_all | solution.py:557
  45.6 3.7 %shard_map.130 = (f32[1,128]{1,0:T(1,128)}, bf16[1024,256]{1,0:T(8,128)(2,1)S(1)}, bf16[1024,512]{1,0:T(8,128)(2,1)S(1)}, bf16[1024,512]{1,0:T(8,128)(2,1)S(1)}) custom-call(s32[1]{0:T(128)} %bitcast.swap_ref, s32[1,2048]{1,0:T(1,128)S(1)} %bitcast.23, f32[1,2048]{1,0:T(1,128)S(1)} %bitcast.25, bf16[1,2048]{1,0:T(2,128)(2,1)S(1)} %reshape.52.weight_ref, ...), custom_call_target="tpu_custom_call" | custom-call | flops 1879048192 | bytes 5242880 | tf_op jit(solution)/shard_map/pallas_call | solution.py:298
  49.3 0.1 collective-permute-start.4
  49.4 1.4 %shard_map.131 = bf16[2048,256]{1,0:T(8,128)(2,1)S(1)} custom-call(s32[16,128]{1,0:T(8,128)S(1)} %bitcast.24, bf16[1024,256]{1,0:T(8,128)(2,1)S(1)} %get-tuple-element.36.grads_ref), custom_call_target="tpu_custom_call" | custom-call | flops 1073741824 | bytes 1572864 | tf_op jit(solution)/shard_map/pallas_call | solution.py:217
  50.8 1.2 %collective-permute-done.4 = bf16[1024,512]{1,0:T(8,128)(2,1)S(1)} collective-permute-done((bf16[1024,512]{1,0:T(8,128)(2,1)S(1)}, bf16[1024,512]{1,0:T(8,128)(2,1)S(1)}, u32[]{:S(2)}, u32[]{:S(2)}) %collective-permute-start.4) | collective-permute-done | bytes 1048608 | tf_op jit(solution)/shard_map/ppermute | solution.py:575
  52.0 0.3 add_convert_fusion
  52.4 0.1 copy.17
  52.4 0.1 fusion
  52.5 0.1 pad_maximum_fusion
  52.7 29.9 %all_to_all.16.grads_ref = bf16[8,512,256]{2,1,0:T(8,128)(2,1)S(1)} all-to-all(bf16[8,512,256]{2,1,0:T(8,128)(2,1)S(1)} %pad_maximum_fusion), channel_id=1, replica_groups={{0,2,4,6,8,10,12,14},{16,18,20,22,24,26,28,30},{1,3,5,7,9,11,13,15},{17..., dimensions={0} | all-to-all | bytes 4194304 | tf_op jit(solution)/shard_map/all_to_all | solution.py:587
  82.6 0.1 slice_reduce_fusion
  82.8 0.1 collective-permute-start.5
  82.8 3.2 %shard_map.132 = (bf16[512,512]{1,0:T(8,128)(2,1)S(1)}, bf16[512,512]{1,0:T(8,128)(2,1)S(1)}) custom-call(s32[1]{0:T(128)} %bitcast.swap_ref, s32[8,1,1024]{2,1,0:T(1,128)S(1)} %all_to_all.15.ids_ref, bf16[8,512,256]{2,1,0:T(8,128)(2,1)S(1)} %all_to_all.16.grads_ref), custom_call_target="tpu_custom_call" | custom-call | flops 1073741824 | bytes 3145728 | tf_op jit(solution)/shard_map/pallas_call | solution.py:171
  86.0 4.4 %collective-permute-done.5 = bf16[128,512]{1,0:T(8,128)(2,1)S(1)} collective-permute-done((bf16[128,512]{1,0:T(8,128)(2,1)S(1)}, bf16[128,512]{1,0:T(8,128)(2,1)S(1)}, u32[]{:S(2)}, u32[]{:S(2)}) %collective-permute-start.5) | collective-permute-done | bytes 131104 | tf_op jit(solution)/shard_map/ppermute | solution.py:597
  90.5 0.1 collective-permute-start.6
  90.6 1.8 %collective-permute-done.10.refs_1_ = bf16[512,512]{1,0:T(8,128)(2,1)S(1)} collective-permute-done((bf16[512,512]{1,0:T(8,128)(2,1)S(1)}, bf16[512,512]{1,0:T(8,128)(2,1)S(1)}, u32[]{:S(2)}, u32[]{:S(2)}) %collective-permute-start.10) | collective-permute-done | bytes 524320 | tf_op jit(solution)/shard_map/ppermute | solution.py:602
  92.3 0.1 add_convert_fusion.1
  92.4 0.1 collective-permute-start.11
  92.5 4.0 %collective-permute-done.6 = bf16[128,512]{1,0:T(8,128)(2,1)S(1)} collective-permute-done((bf16[128,512]{1,0:T(8,128)(2,1)S(1)}, bf16[128,512]{1,0:T(8,128)(2,1)S(1)}, u32[]{:S(2)}, u32[]{:S(2)}) %collective-permute-start.6) | collective-permute-done | bytes 131104 | tf_op jit(solution)/shard_map/ppermute | solution.py:484
  96.5 1.1 collective-permute-start.8
  97.6 0.9 collective-permute-start.9
  98.6 1.5 %collective-permute-start.7 = (bf16[256,512]{1,0:T(8,128)(2,1)S(1)}, bf16[256,512]{1,0:T(8,128)(2,1)S(1)}, u32[]{:S(2)}, u32[]{:S(2)}) collective-permute-start(bf16[256,512]{1,0:T(8,128)(2,1)S(1)} %constant_dynamic-update-slice_fusion.refs_0_), channel_id=1, source_target_pairs={{6,0},{4,2},{2,4},{0,6},{14,8},{12,10},{10,12},{8,14},{22,16},{20,... | collective-permute-start | bytes 786440 | tf_op jit(solution)/shard_map/ppermute | solution.py:484
  100.1 0.1 dynamic-slice_bitcast_fusion.accum_ref
  100.1 7.0 %collective-permute-done.11.far_ref = bf16[512,256]{1,0:T(8,128)(2,1)S(1)} collective-permute-done((bf16[512,256]{1,0:T(8,128)(2,1)S(1)}, bf16[512,256]{1,0:T(8,128)(2,1)S(1)}, u32[]{:S(2)}, u32[]{:S(2)}) %collective-permute-start.11) | collective-permute-done | bytes 262176 | tf_op jit(solution)/shard_map/ppermute | solution.py:608
  107.1 0.9 shard_map.135
  108.0 0.0 collective-permute-start.12
  108.0 0.1 pad_add_fusion.2.spots_ref
  108.1 2.8 %collective-permute-done.9.refs_2_ = bf16[256,512]{1,0:T(8,128)(2,1)S(1)} collective-permute-done((bf16[256,512]{1,0:T(8,128)(2,1)S(1)}, bf16[256,512]{1,0:T(8,128)(2,1)S(1)}, u32[]{:S(2)}, u32[]{:S(2)}) %collective-permute-start.9) | collective-permute-done | bytes 262176 | tf_op jit(solution)/shard_map/ppermute | solution.py:484
  110.9 1.7 %shard_map.133 = (f32[1024,256]{1,0:T(8,128)}, f32[1024,256]{1,0:T(8,128)}) custom-call(s32[3]{0:T(128)S(1)} %pad_add_fusion.2.spots_ref, bf16[256,512]{1,0:T(8,128)(2,1)S(1)} %constant_dynamic-update-slice_fusion.refs_0_, bf16[256,512]{1,0:T(8,128)(2,1)S(1)} %collective-permute-done.8.refs_1_, bf16[256,512]{1,0:T(8,128)(2,1)S(1)} %collective-permute-done.9.refs_2_), custom_call_target="tpu_custom_call" | custom-call | flops 393216 | bytes 2359296 | tf_op jit(solution)/shard_map/pallas_call | solution.py:357
  112.6 0.8 shard_map.134
  113.5 0.8 shard_map.136
  (32 shorter events, 0.3 us)
Async XLA Ops:
  0.6 99.4 %copy-start = (f32[1024]{0:T(1024)S(1)}, f32[1024]{0:T(1024)}, u32[]{:S(2)}) copy-start(f32[1024]{0:T(1024)} %param.10) | copy-start | bytes 12292
  1.6 21.3 %collective-permute-start = (bf16[512,256]{1,0:T(8,128)(2,1)S(1)}, bf16[512,256]{1,0:T(8,128)(2,1)S(1)}, u32[]{:S(2)}, u32[]{:S(2)}) collective-permute-start(bf16[512,256]{1,0:T(8,128)(2,1)S(1)} %constant_dynamic-slice_fusion.2.rows_ref), channel_id=1, source_target_pairs={{0,16},{2,18},{4,20},{6,22},{8,24},{10,26},{12,28},{14,30},{16,0},... | collective-permute-start | bytes 786440 | tf_op jit(solution)/shard_map/ppermute | solution.py:541
  19.7 1.0 copy-start.1
  23.0 1.6 %collective-permute-start.1 = (bf16[512,256]{1,0:T(8,128)(2,1)S(1)}, bf16[512,256]{1,0:T(8,128)(2,1)S(1)}, u32[]{:S(2)}, u32[]{:S(2)}) collective-permute-start(bf16[512,256]{1,0:T(8,128)(2,1)S(1)} %collective-permute-done), channel_id=1, source_target_pairs={{1,0},{0,1},{3,2},{2,3},{5,4},{4,5},{7,6},{6,7},{9,8},{8,9},{11,10... | collective-permute-start | bytes 786440 | tf_op jit(solution)/shard_map/ppermute | solution.py:534
  24.7 5.8 %copy-start.5 = (bf16[1024,256]{1,0:T(8,128)(2,1)S(1)}, bf16[1024,256]{1,0:T(8,128)(2,1)}, u32[]{:S(2)}) copy-start(bf16[1024,256]{1,0:T(8,128)(2,1)} %param.11) | copy-start | bytes 1572868
  24.7 6.0 %copy-start.4 = (bf16[1024,256]{1,0:T(8,128)(2,1)S(1)}, bf16[1024,256]{1,0:T(8,128)(2,1)}, u32[]{:S(2)}) copy-start(bf16[1024,256]{1,0:T(8,128)(2,1)} %param.12) | copy-start | bytes 1572868
  24.7 6.4 %copy-start.7 = (bf16[2048]{0:T(1024)(128)(2,1)S(1)}, bf16[2048]{0:T(1024)(128)(2,1)}, u32[]{:S(2)}) copy-start(bf16[2048]{0:T(1024)(128)(2,1)} %param.14) | copy-start | bytes 12292
  24.7 6.4 %copy-start.6 = (s32[16,128]{1,0:T(8,128)S(1)}, s32[16,128]{1,0:T(8,128)}, u32[]{:S(2)}) copy-start(s32[16,128]{1,0:T(8,128)} %param.17) | copy-start | bytes 24580
  26.9 18.7 %all-to-all-start.1 = ((bf16[8,2,128,256]{3,2,1,0:T(8,128)(2,1)}), bf16[8,2,128,256]{3,2,1,0:T(8,128)(2,1)S(1)}, u32[]{:S(2)}, u32[]{:S(2)}) async-start(bf16[8,2,128,256]{3,2,1,0:T(8,128)(2,1)} %shard_map.129), calls=%async_computation.1 | async-start | bytes 2097152 | tf_op jit(solution)/shard_map/all_to_all | solution.py:557
  30.5 2.0 %collective-permute-start.2 = (bf16[1024,256]{1,0:T(8,128)(2,1)S(1)}, bf16[1024,256]{1,0:T(8,128)(2,1)S(1)}, u32[]{:S(2)}, u32[]{:S(2)}) collective-permute-start(bf16[1024,256]{1,0:T(8,128)(2,1)S(1)} %copy-done.5), channel_id=1, source_target_pairs={{1,0},{0,1},{3,2},{2,3},{5,4},{4,5},{7,6},{6,7},{9,8},{8,9},{11,10... | collective-permute-start | bytes 1572872 | tf_op jit(solution)/shard_map/ppermute | solution.py:534
  30.7 2.5 %collective-permute-start.3 = (bf16[1024,256]{1,0:T(8,128)(2,1)S(1)}, bf16[1024,256]{1,0:T(8,128)(2,1)S(1)}, u32[]{:S(2)}, u32[]{:S(2)}) collective-permute-start(bf16[1024,256]{1,0:T(8,128)(2,1)S(1)} %copy-done.4), channel_id=1, source_target_pairs={{1,0},{0,1},{3,2},{2,3},{5,4},{4,5},{7,6},{6,7},{9,8},{8,9},{11,10... | collective-permute-start | bytes 1572872 | tf_op jit(solution)/shard_map/ppermute | solution.py:534
  33.4 12.2 %copy-start.2 = (f32[2048]{0:T(1024)S(1)}, f32[2048]{0:T(1024)}, u32[]{:S(2)}) copy-start(f32[2048]{0:T(1024)} %param.13) | copy-start | bytes 24580
  33.4 12.2 %copy-start.3 = (f32[128]{0:T(128)S(1)}, f32[128]{0:T(128)}, u32[]{:S(2)}) copy-start(f32[128]{0:T(128)} %param.15) | copy-start | bytes 1540
  49.3 2.7 %collective-permute-start.4 = (bf16[1024,512]{1,0:T(8,128)(2,1)S(1)}, bf16[1024,512]{1,0:T(8,128)(2,1)S(1)}, u32[]{:S(2)}, u32[]{:S(2)}) collective-permute-start(bf16[1024,512]{1,0:T(8,128)(2,1)S(1)} %get-tuple-element.38), channel_id=1, source_target_pairs={{1,0},{0,1},{3,2},{2,3},{5,4},{4,5},{7,6},{6,7},{9,8},{8,9},{11,10... | collective-permute-start | bytes 3145736 | tf_op jit(solution)/shard_map/ppermute | solution.py:575
  82.8 7.6 %collective-permute-start.5 = (bf16[128,512]{1,0:T(8,128)(2,1)S(1)}, bf16[128,512]{1,0:T(8,128)(2,1)S(1)}, u32[]{:S(2)}, u32[]{:S(2)}) collective-permute-start(bf16[128,512]{1,0:T(8,128)(2,1)S(1)} %pad_maximum_fusion.4), channel_id=1, source_target_pairs={{0,16},{2,18},{4,20},{6,22},{8,24},{10,26},{12,28},{14,30},{16,0},... | collective-permute-start | bytes 393224 | tf_op jit(solution)/shard_map/ppermute | solution.py:597
  90.4 1.9 %collective-permute-start.10 = (bf16[512,512]{1,0:T(8,128)(2,1)S(1)}, bf16[512,512]{1,0:T(8,128)(2,1)S(1)}, u32[]{:S(2)}, u32[]{:S(2)}) collective-permute-start(bf16[512,512]{1,0:T(8,128)(2,1)S(1)} %get-tuple-element.50), channel_id=1, source_target_pairs={{1,0},{0,1},{3,2},{2,3},{5,4},{4,5},{7,6},{6,7},{9,8},{8,9},{11,10... | collective-permute-start | bytes 1572872 | tf_op jit(solution)/shard_map/ppermute | solution.py:602
  90.5 6.0 %collective-permute-start.6 = (bf16[128,512]{1,0:T(8,128)(2,1)S(1)}, bf16[128,512]{1,0:T(8,128)(2,1)S(1)}, u32[]{:S(2)}, u32[]{:S(2)}) collective-permute-start(bf16[128,512]{1,0:T(8,128)(2,1)S(1)} %get-tuple-element.54), channel_id=1, source_target_pairs={{8,0},{10,2},{12,4},{14,6},{0,8},{2,10},{4,12},{6,14},{24,16},{26,... | collective-permute-start | bytes 393224 | tf_op jit(solution)/shard_map/ppermute | solution.py:484
  92.4 14.7 %collective-permute-start.11 = (bf16[512,256]{1,0:T(8,128)(2,1)S(1)}, bf16[512,256]{1,0:T(8,128)(2,1)S(1)}, u32[]{:S(2)}, u32[]{:S(2)}) collective-permute-start(bf16[512,256]{1,0:T(8,128)(2,1)S(1)} %add_convert_fusion.1), channel_id=1, source_target_pairs={{0,16},{2,18},{4,20},{6,22},{8,24},{10,26},{12,28},{14,30},{16,0},... | collective-permute-start | bytes 786440 | tf_op jit(solution)/shard_map/ppermute | solution.py:608
  96.5 11.6 %collective-permute-start.8 = (bf16[256,512]{1,0:T(8,128)(2,1)S(1)}, bf16[256,512]{1,0:T(8,128)(2,1)S(1)}, u32[]{:S(2)}, u32[]{:S(2)}) collective-permute-start(bf16[256,512]{1,0:T(8,128)(2,1)S(1)} %constant_dynamic-update-slice_fusion.refs_0_), channel_id=1, source_target_pairs={{2,0},{0,2},{6,4},{4,6},{10,8},{8,10},{14,12},{12,14},{18,16},{16,... | collective-permute-start | bytes 786440 | tf_op jit(solution)/shard_map/ppermute | solution.py:484
  97.6 13.2 %collective-permute-start.9 = (bf16[256,512]{1,0:T(8,128)(2,1)S(1)}, bf16[256,512]{1,0:T(8,128)(2,1)S(1)}, u32[]{:S(2)}, u32[]{:S(2)}) collective-permute-start(bf16[256,512]{1,0:T(8,128)(2,1)S(1)} %constant_dynamic-update-slice_fusion.refs_0_), channel_id=1, source_target_pairs={{4,0},{6,2},{0,4},{2,6},{12,8},{14,10},{8,12},{10,14},{20,16},{22,... | collective-permute-start | bytes 786440 | tf_op jit(solution)/shard_map/ppermute | solution.py:484
  98.6 14.1 %collective-permute-start.7 = (bf16[256,512]{1,0:T(8,128)(2,1)S(1)}, bf16[256,512]{1,0:T(8,128)(2,1)S(1)}, u32[]{:S(2)}, u32[]{:S(2)}) collective-permute-start(bf16[256,512]{1,0:T(8,128)(2,1)S(1)} %constant_dynamic-update-slice_fusion.refs_0_), channel_id=1, source_target_pairs={{6,0},{4,2},{2,4},{0,6},{14,8},{12,10},{10,12},{8,14},{22,16},{20,... | collective-permute-start | bytes 786440 | tf_op jit(solution)/shard_map/ppermute | solution.py:484
  108.0 5.5 %collective-permute-start.12 = (bf16[512,256]{1,0:T(8,128)(2,1)S(1)}, bf16[512,256]{1,0:T(8,128)(2,1)S(1)}, u32[]{:S(2)}, u32[]{:S(2)}) collective-permute-start(bf16[512,256]{1,0:T(8,128)(2,1)S(1)} %get-tuple-element.51.mine_ref), channel_id=1, source_target_pairs={{1,0},{0,1},{3,2},{2,3},{5,4},{4,5},{7,6},{6,7},{9,8},{8,9},{11,10... | collective-permute-start | bytes 786440 | tf_op jit(solution)/shard_map/ppermute | solution.py:612

commit v10 on v9

--- a/solution.py
+++ b/solution.py
@@ -84,7 +84,7 @@
     return jnp.where(mask, jnp.asarray(1, jnp.bfloat16), jnp.asarray(0, jnp.bfloat16))
 
 
-def pool_kernel(part, ids_ref, rows_ref, *refs):
+def pool_kernel(part, swap_ref, ids_ref, first_ref, second_ref, *refs):
     out_ref, counts_ref, sums_ref, sem = refs[-4:]
     slots = counts_ref.shape[0]
     sources, _, pools, _ = out_ref.shape
@@ -96,7 +96,9 @@
     choice = lookup_choice()
     high, low = split_ids(ids)
     columns = joined((rows_dot(choice, high), rows_dot(choice, low))).astype(jnp.int16)
-    position = lax.broadcasted_iota(jnp.int32, (SLOTS, rows_ref.shape[0]), 1).astype(jnp.int16)
+    half = first_ref.shape[0]
+    position = lax.broadcasted_iota(jnp.int32, (SLOTS, 2 * half), 1) + swap_ref[0] * half
+    position = jnp.where(position >= 2 * half, position - 2 * half, position).astype(jnp.int16)
     for block in range(slots // SLOTS):
         counts = None
         for lookup in range(HOT):
@@ -104,7 +106,8 @@
             found = ones_where(column == position)
             counts = found if counts is None else counts + found
         counts_ref[block * SLOTS : (block + 1) * SLOTS, :] = counts
-    sums = matmul(counts_ref[...], rows_ref[...]).astype(jnp.bfloat16)
+    sums = matmul(counts_ref[:, :half], first_ref[...])
+    sums = (sums + matmul(counts_ref[:, half:], second_ref[...])).astype(jnp.bfloat16)
     for source in range(sources):
         sums_ref[source] = sums[source * pools : (source + 1) * pools]
     store = pltpu.make_async_copy(sums_ref, out_ref.at[:, part], sem)
@@ -112,9 +115,9 @@
     store.wait()
 
 
-def pool_lookups(part, ids, rows, pools, given=()):
+def pool_lookups(part, swap, ids, halves, pools, given=()):
     slots = ids.shape[0] * SLOTS
-    row_dev, width = rows.shape
+    row_dev, width = 2 * halves[0].shape[0], halves[0].shape[1]
     return kernel_call(
         functools.partial(pool_kernel, part),
         jax.ShapeDtypeStruct((slots // pools, 2, pools, width), jnp.bfloat16),
@@ -124,12 +127,13 @@
             pltpu.VMEM((slots // pools, pools, width), jnp.bfloat16),
             pltpu.SemaphoreType.DMA,
         ],
-        operands=2,
+        flags=1,
+        operands=3,
         left=len(given),
         left_out=(0,),
-        aliases={2: 0} if given else None,
+        aliases={4: 0} if given else None,
         room=12,
-    )(ids, rows, *given)
+    )(swap, ids, *halves, *given)
 
 
 def row_grad_kernel(swap_ref, ids_ref, grads_ref, kept_ref, sent_ref, counts_ref, sums_ref):
@@ -537,6 +541,10 @@
         return jnp.concatenate([first, second], axis=0)
 
     share_rows = row_dev // narrows
+    own_halves = tuple(
+        lax.dynamic_slice_in_dim(table_rows, half * (row_dev // 2), row_dev // 2, 0)
+        for half in (swap[0], 1 - swap[0])
+    )
     own_share = lax.dynamic_slice_in_dim(table_rows, narrow_index * share_rows, share_rows, 0)
     far_share = lax.ppermute(own_share, "table", across)
     down_full = narrow_whole(factor_down)
@@ -551,9 +559,14 @@
     if per_window != SLOTS * HOT:
         by_block = (ids.reshape(-1, SLOTS * HOT) for ids in (near_ids, far_ids))
         asked = jnp.concatenate(tuple(by_block), axis=1)
-    sums = pool_lookups(0, asked, table_rows, pools_per)
+    sums = pool_lookups(0, swap, asked, own_halves, pools_per)
     sums, far_share = lax.optimization_barrier((sums, far_share))
-    sums = pool_lookups(1, asked, narrow_whole(far_share), pools_per, (sums,))
+    if paired:
+        came = lax.ppermute(far_share, "narrow", sent_from("narrow", 1, 2, 1))
+        far_halves = (far_share, came)
+    else:
+        far_halves = tuple(jnp.split(narrow_whole(far_share), 2, axis=0))
+    sums = pool_lookups(1, swap, asked, far_halves, pools_per, (sums,))
     arrived = lax.all_to_all(
         sums, "table", split_axis=0, concat_axis=0, tiled=True, axis_index_groups=halves
     )
@@ -603,9 +616,20 @@
     else:
         nears = [scatter_sum(jnp.concatenate([mine, passed], axis=0), "narrow", narrow_levels)]
     far_term = summed([term[:, emb_width:] for term in nears])
-    level_sum = gather_blocks(table_sum, "table", half_levels[1:])
-    pieces = gathered_pieces(level_sum, "table", half_levels[0])
+    inner = gather_blocks(table_sum, "table", half_levels[2:])
+    blocks, fan = [(0, inner)], 1
+    if len(half_levels) > 1:
+        blocks, fan = gathered_pieces(inner, "table", half_levels[1]), half_levels[1][1]
+    early, late = [], []
+    for i, (place, block) in enumerate(blocks):
+        pieces = gathered_pieces(block, "table", half_levels[0])
+        pieces = [(spot * fan + place, piece) for spot, piece in pieces]
+        early += pieces if i == 0 else pieces[:1]
+        late += [] if i == 0 else pieces[1:]
     far_term = lax.ppermute(far_term, "table", across)
+    spots, came = zip(*early, *late)
+    far_term, *came = lax.optimization_barrier((far_term, *came))
+    pieces = list(zip(spots, came))
     own_accum = lax.dynamic_slice_in_dim(accum, narrow_index * share_rows, share_rows, 0)
     new_share, new_accum = update_rows(own_share, far_term, own_accum, nears)
     if paired:
@@ -614,10 +638,7 @@
     else:
         new_rows = gather_blocks(new_share, "narrow", narrow_levels)
     scale = 1.0 / math.sqrt(samples * tables * narrows)
-    spot, last = pieces[-1]
-    grads = spread_pieces(pieces[:-1], scale, factor_down.shape[0])
-    last, *grads = lax.optimization_barrier((last, *grads))
-    down_grad, up_grad = spread_pieces([(spot, last)], scale, factor_down.shape[0], grads)
+    down_grad, up_grad = spread_pieces(pieces, scale, factor_down.shape[0])
     return (logits, down_grad, up_grad, new_rows, new_accum)
 
 

time: 115 us -> 111 us (0.965)
  waiting for transfers between devices: 36.7 us -> 28.6 us
  starting transfers between devices: 12.2 us -> 17.1 us
    ppermute x1, waiting for transfers between devices: 6.99 us -> 1.77 us  [local(): far_term = lax.ppermute(far_term, 'table', across)]
    ppermute x4 -> x7, starting transfers between devices: 3.62 us -> 7.42 us  [gathered_pieces(): came = lax.ppermute(block, axis, sent_from(axis, stride, group, step))]
    ppermute x1, waiting for transfers between devices: 1.76 us -> 0.01 us  [local(): nears = [mine, lax.ppermute(passed, 'narrow', sent_from('narrow', 1, 2, 1))]]
    ppermute x0 -> x1, waiting for transfers between devices: none -> 1.52 us  [local(): came = lax.ppermute(far_share, 'narrow', sent_from('narrow', 1, 2, 1))]
    ppermute x3 -> x2, waiting for transfers between devices: 3.6 us -> 2.22 us  [narrow_whole(): came = lax.ppermute(block, 'narrow', sent_from('narrow', 1, 2, 1))]
    all_to_all x1, waiting for transfers between devices: 12 us -> 10.7 us  [local(): lax.all_to_all(sums, 'table', split_axis=0, concat_axis=0, tiled=True, ax...]
    select_n x2 -> x1, other arithmetic: 0.18 us -> 1.37 us  [narrow_whole(): first = jnp.where(narrow_index == 0, block, came)]
    ppermute x1, starting transfers between devices: 0.07 us -> 1.24 us  [local(): far_term = lax.ppermute(far_term, 'table', across)]
  transfers between devices with their start and end apart: 14 -> 17, of which waited for: 10 -> 12; matrix products, arithmetic and copies ran while one was open for 1% -> 2% of each run, Pallas kernels for 9% -> 8%
where the time goes in v10:
time: 111 us
  blocking collectives  43.1 us (39%)
  waiting for transfers between devices  28.6 us (26%)
  starting transfers between devices  17.1 us (15%)
  Pallas kernels  16.4 us (15%)
  local copies, waits for them, and re-layouts  2.24 us (2%)
  other arithmetic  2.23 us (2%)
    all_to_all x1, blocking collectives, local(): lax.all_to_all(jnp.concatenate(outgoing, axis=1), 'table', split_axis=0,...  29.9 us
    all_to_all x1, blocking collectives, local(): lax.all_to_all(asked, 'table', split_axis=0, concat_axis=0, tiled=True, a...  13.2 us
    all_to_all x1, waiting for transfers between devices, local(): lax.all_to_all(sums, 'table', split_axis=0, concat_axis=0, tiled=True, ax...  10.7 us
    ppermute x7, starting transfers between devices, gathered_pieces(): came = lax.ppermute(block, axis, sent_from(axis, stride, group, step))  7.42 us
    ppermute x7, waiting for transfers between devices, gathered_pieces(): came = lax.ppermute(block, axis, sent_from(axis, stride, group, step))  6.88 us
    pallas_call x2, Pallas kernels, pool_lookups(): kernel_call(functools.partial(pool_kernel, part), jax.ShapeDtypeStruct((s...  4.41 us
    ppermute x1, waiting for transfers between devices, local(): other_sum = lax.ppermute(half_sum, 'table', across)  4.37 us
    ppermute x1, starting transfers between devices, local(): far_share = lax.ppermute(own_share, 'table', across)  4.1 us
  transfers between devices with their start and end apart: 17, of which 12 were waited for; matrix products, arithmetic and copies ran while one was open for 2% of the time, Pallas kernels for 8%

profile of v10, /device:TPU:0, one launch (start us, length us, event | category | flops | bytes accessed | tf_op | source)
XLA Modules:
  0.0 110.8 jit_solution(399273255799724246)
XLA Ops:
  0.7 1.1 constant_dynamic-slice_fusion.2
  1.7 4.1 %collective-permute-start = (bf16[512,256]{1,0:T(8,128)(2,1)S(1)}, bf16[512,256]{1,0:T(8,128)(2,1)S(1)}, u32[]{:S(2)}, u32[]{:S(2)}) collective-permute-start(bf16[512,256]{1,0:T(8,128)(2,1)S(1)} %get-tuple-element.68.first_ref.rows_ref), channel_id=1, source_target_pairs={{0,16},{2,18},{4,20},{6,22},{8,24},{10,26},{12,28},{14,30},{16,0},... | collective-permute-start | bytes 786440 | tf_op jit(solution)/shard_map/ppermute | solution.py:549
  5.8 0.7 constant_dynamic-slice_fusion.5
  6.6 13.2 %all_to_all.15.ids_ref = s32[8,1,1024]{2,1,0:T(1,128)S(1)} all-to-all(s32[8,1,1024]{2,1,0:T(1,128)S(1)} %broadcast_in_dim.3), channel_id=1, replica_groups={{0,2,4,6,8,10,12,14},{16,18,20,22,24,26,28,30},{1,3,5,7,9,11,13,15},{17..., dimensions={0} | all-to-all | bytes 65536 | tf_op jit(solution)/shard_map/all_to_all | solution.py:555
  19.8 2.2 %shard_map.128.refs_0_ = bf16[8,2,128,256]{3,2,1,0:T(8,128)(2,1)} custom-call(s32[1]{0:T(128)} %bitcast.swap_ref, s32[8,1,1024]{2,1,0:T(1,128)S(1)} %all_to_all.15.ids_ref, bf16[512,256]{1,0:T(8,128)(2,1)S(1)} %get-tuple-element.68.first_ref.rows_ref, bf16[512,256]{1,0:T(8,128)(2,1)S(1)} %get-tuple-element.67.second_ref), custom_call_target="tpu_custom_call" | custom-call | flops 536870912 | bytes 1048576 | tf_op jit(solution)/shard_map/pallas_call | solution.py:121
  22.1 0.1 collective-permute-start.1
  22.2 1.5 %collective-permute-done.1.second_ref = bf16[512,256]{1,0:T(8,128)(2,1)S(1)} collective-permute-done((bf16[512,256]{1,0:T(8,128)(2,1)S(1)}, bf16[512,256]{1,0:T(8,128)(2,1)S(1)}, u32[]{:S(2)}, u32[]{:S(2)}) %collective-permute-start.1) | collective-permute-done | bytes 262176 | tf_op jit(solution)/shard_map/ppermute | solution.py:565
  23.7 2.2 %shard_map.129 = bf16[8,2,128,256]{3,2,1,0:T(8,128)(2,1)} custom-call(s32[1]{0:T(128)} %bitcast.swap_ref, s32[8,1,1024]{2,1,0:T(1,128)S(1)} %all_to_all.15.ids_ref, bf16[512,256]{1,0:T(8,128)(2,1)S(1)} %collective-permute-done.first_ref, bf16[512,256]{1,0:T(8,128)(2,1)S(1)} %collective-permute-done.1.second_ref, ...), custom_call_target="tpu_custom_call", output_to_operand_aliasing={{}: (4, {})} | custom-call | flops 536870912 | bytes 1048576 | tf_op jit(solution)/shard_map/pallas_call | solution.py:121
  25.9 3.6 %all-to-all-start.1 = ((bf16[8,2,128,256]{3,2,1,0:T(8,128)(2,1)}), bf16[8,2,128,256]{3,2,1,0:T(8,128)(2,1)S(1)}, u32[]{:S(2)}, u32[]{:S(2)}) async-start(bf16[8,2,128,256]{3,2,1,0:T(8,128)(2,1)} %shard_map.129), calls=%async_computation.1 | async-start | bytes 2097152 | tf_op jit(solution)/shard_map/all_to_all | solution.py:570
  29.5 0.2 collective-permute-start.2
  29.7 0.4 collective-permute-start.3
  30.1 1.5 %collective-permute-done.2 = bf16[1024,256]{1,0:T(8,128)(2,1)} collective-permute-done((bf16[1024,256]{1,0:T(8,128)(2,1)S(1)}, bf16[1024,256]{1,0:T(8,128)(2,1)}, u32[]{:S(2)}, u32[]{:S(2)}) %collective-permute-start.2) | collective-permute-done | bytes 524320 | tf_op jit(solution)/shard_map/ppermute | solution.py:538
  31.6 0.7 collective-permute-done.3
  32.3 1.4 %broadcast_select_fusion.1 = (bf16[1024,256]{1,0:T(8,128)(2,1)S(1)}, bf16[1024,256]{1,0:T(8,128)(2,1)S(1)}, bf16[1024,256]{1,0:T(8,128)(2,1)S(1)}, bf16[1024,256]{1,0:T(8,128)(2,1)S(1)}) fusion(bf16[1024,256]{1,0:T(8,128)(2,1)S(1)} %copy-done.3, bf16[1024,256]{1,0:T(8,128)(2,1)} %collective-permute-done.3, pred[]{:T(512)S(6)} %eq.24, ...), kind=kLoop, calls=%fused_computation.7 | loop fusion | flops 1048576 | bytes 4194305 | tf_op jit(solution)/shard_map/jit(_where)/select_n | solution.py:539
  33.7 0.1 pad_maximum_fusion.2.up_ref
  33.8 0.1 pad_maximum_fusion.1.down_ref
  33.9 10.7 %all-to-all-done.1 = bf16[8,2,128,256]{3,2,1,0:T(8,128)(2,1)S(1)} async-done(((bf16[8,2,128,256]{3,2,1,0:T(8,128)(2,1)}), bf16[8,2,128,256]{3,2,1,0:T(8,128)(2,1)S(1)}, u32[]{:S(2)}, u32[]{:S(2)}) %all-to-all-start.1) | async-done | bytes 1048608 | tf_op jit(solution)/shard_map/all_to_all | solution.py:570
  44.6 3.7 %shard_map.130 = (f32[1,128]{1,0:T(1,128)}, bf16[1024,256]{1,0:T(8,128)(2,1)S(1)}, bf16[1024,512]{1,0:T(8,128)(2,1)S(1)}, bf16[1024,512]{1,0:T(8,128)(2,1)S(1)}) custom-call(s32[1]{0:T(128)} %bitcast.swap_ref, s32[1,2048]{1,0:T(1,128)S(1)} %bitcast.27, f32[1,2048]{1,0:T(1,128)S(1)} %bitcast.29, bf16[1,2048]{1,0:T(2,128)(2,1)S(1)} %reshape.52.weight_ref, ...), custom_call_target="tpu_custom_call" | custom-call | flops 1879048192 | bytes 5242880 | tf_op jit(solution)/shard_map/pallas_call | solution.py:302
  48.3 0.1 collective-permute-start.4
  48.4 1.4 %shard_map.131 = bf16[2048,256]{1,0:T(8,128)(2,1)S(1)} custom-call(s32[16,128]{1,0:T(8,128)S(1)} %bitcast.28, bf16[1024,256]{1,0:T(8,128)(2,1)S(1)} %get-tuple-element.40.grads_ref), custom_call_target="tpu_custom_call" | custom-call | flops 1073741824 | bytes 1572864 | tf_op jit(solution)/shard_map/pallas_call | solution.py:221
  49.8 1.2 %collective-permute-done.4 = bf16[1024,512]{1,0:T(8,128)(2,1)S(1)} collective-permute-done((bf16[1024,512]{1,0:T(8,128)(2,1)S(1)}, bf16[1024,512]{1,0:T(8,128)(2,1)S(1)}, u32[]{:S(2)}, u32[]{:S(2)}) %collective-permute-start.4) | collective-permute-done | bytes 1048608 | tf_op jit(solution)/shard_map/ppermute | solution.py:588
  51.0 0.3 add_convert_fusion
  51.4 0.1 fusion
  51.5 0.1 pad_maximum_fusion
  51.7 29.9 %all_to_all.16.grads_ref = bf16[8,512,256]{2,1,0:T(8,128)(2,1)S(1)} all-to-all(bf16[8,512,256]{2,1,0:T(8,128)(2,1)S(1)} %pad_maximum_fusion), channel_id=1, replica_groups={{0,2,4,6,8,10,12,14},{16,18,20,22,24,26,28,30},{1,3,5,7,9,11,13,15},{17..., dimensions={0} | all-to-all | bytes 4194304 | tf_op jit(solution)/shard_map/all_to_all | solution.py:600
  81.6 0.1 slice_reduce_fusion
  81.7 0.1 collective-permute-start.5
  81.8 3.2 %shard_map.132 = (bf16[512,512]{1,0:T(8,128)(2,1)S(1)}, bf16[512,512]{1,0:T(8,128)(2,1)S(1)}) custom-call(s32[1]{0:T(128)} %bitcast.swap_ref, s32[8,1,1024]{2,1,0:T(1,128)S(1)} %all_to_all.15.ids_ref, bf16[8,512,256]{2,1,0:T(8,128)(2,1)S(1)} %all_to_all.16.grads_ref), custom_call_target="tpu_custom_call" | custom-call | flops 1073741824 | bytes 3145728 | tf_op jit(solution)/shard_map/pallas_call | solution.py:175
  85.0 4.4 %collective-permute-done.5 = bf16[128,512]{1,0:T(8,128)(2,1)S(1)} collective-permute-done((bf16[128,512]{1,0:T(8,128)(2,1)S(1)}, bf16[128,512]{1,0:T(8,128)(2,1)S(1)}, u32[]{:S(2)}, u32[]{:S(2)}) %collective-permute-start.5) | collective-permute-done | bytes 131104 | tf_op jit(solution)/shard_map/ppermute | solution.py:610
  89.4 0.1 collective-permute-start.11
  89.5 1.5 %collective-permute-start.10 = (bf16[128,512]{1,0:T(8,128)(2,1)S(1)}, bf16[128,512]{1,0:T(8,128)(2,1)S(1)}, u32[]{:S(2)}, u32[]{:S(2)}) collective-permute-start(bf16[128,512]{1,0:T(8,128)(2,1)S(1)} %add_convert_fusion.2.refs_0_), channel_id=1, source_target_pairs={{6,0},{4,2},{2,4},{0,6},{14,8},{12,10},{10,12},{8,14},{22,16},{20,... | collective-permute-start | bytes 393224 | tf_op jit(solution)/shard_map/ppermute | solution.py:488
  91.0 1.1 collective-permute-start.9
  92.1 0.1 add_convert_fusion.1
  92.2 1.2 %collective-permute-start.7 = (bf16[512,256]{1,0:T(8,128)(2,1)S(1)}, bf16[512,256]{1,0:T(8,128)(2,1)S(1)}, u32[]{:S(2)}, u32[]{:S(2)}) collective-permute-start(bf16[512,256]{1,0:T(8,128)(2,1)S(1)} %add_convert_fusion.1), channel_id=1, source_target_pairs={{0,16},{2,18},{4,20},{6,22},{8,24},{10,26},{12,28},{14,30},{16,0},... | collective-permute-start | bytes 786440 | tf_op jit(solution)/shard_map/ppermute | solution.py:629
  93.4 1.5 %collective-permute-start.8 = (bf16[128,512]{1,0:T(8,128)(2,1)S(1)}, bf16[128,512]{1,0:T(8,128)(2,1)S(1)}, u32[]{:S(2)}, u32[]{:S(2)}) collective-permute-start(bf16[128,512]{1,0:T(8,128)(2,1)S(1)} %add_convert_fusion.2.refs_0_), channel_id=1, source_target_pairs={{2,0},{0,2},{6,4},{4,6},{10,8},{8,10},{14,12},{12,14},{18,16},{16,... | collective-permute-start | bytes 393224 | tf_op jit(solution)/shard_map/ppermute | solution.py:488
  94.9 0.5 collective-permute-done.11.refs_4_
  95.4 2.6 %collective-permute-start.14 = (bf16[128,512]{1,0:T(8,128)(2,1)S(1)}, bf16[128,512]{1,0:T(8,128)(2,1)S(1)}, u32[]{:S(2)}, u32[]{:S(2)}) collective-permute-start(bf16[128,512]{1,0:T(8,128)(2,1)S(1)} %collective-permute-done.11.refs_4_), channel_id=1, source_target_pairs={{6,0},{4,2},{2,4},{0,6},{14,8},{12,10},{10,12},{8,14},{22,16},{20,... | collective-permute-start | bytes 393224 | tf_op jit(solution)/shard_map/ppermute | solution.py:488
  98.0 2.1 %collective-permute-done.9.refs_2_ = bf16[128,512]{1,0:T(8,128)(2,1)S(1)} collective-permute-done((bf16[128,512]{1,0:T(8,128)(2,1)S(1)}, bf16[128,512]{1,0:T(8,128)(2,1)S(1)}, u32[]{:S(2)}, u32[]{:S(2)}) %collective-permute-start.9) | collective-permute-done | bytes 131104 | tf_op jit(solution)/shard_map/ppermute | solution.py:488
  100.1 0.7 collective-permute-start.12
  100.8 0.1 dynamic-slice_bitcast_fusion.accum_ref
  100.8 1.2 %collective-permute-done.14.refs_7_ = bf16[128,512]{1,0:T(8,128)(2,1)S(1)} collective-permute-done((bf16[128,512]{1,0:T(8,128)(2,1)S(1)}, bf16[128,512]{1,0:T(8,128)(2,1)S(1)}, u32[]{:S(2)}, u32[]{:S(2)}) %collective-permute-start.14) | collective-permute-done | bytes 131104 | tf_op jit(solution)/shard_map/ppermute | solution.py:488
  102.1 2.7 %collective-permute-done.13.refs_6_ = bf16[128,512]{1,0:T(8,128)(2,1)S(1)} collective-permute-done((bf16[128,512]{1,0:T(8,128)(2,1)S(1)}, bf16[128,512]{1,0:T(8,128)(2,1)S(1)}, u32[]{:S(2)}, u32[]{:S(2)}) %collective-permute-start.13) | collective-permute-done | bytes 131104 | tf_op jit(solution)/shard_map/ppermute | solution.py:488
  104.8 0.3 collective-permute-done.12.refs_5_
  105.1 1.8 %collective-permute-done.7.far_ref = bf16[512,256]{1,0:T(8,128)(2,1)S(1)} collective-permute-done((bf16[512,256]{1,0:T(8,128)(2,1)S(1)}, bf16[512,256]{1,0:T(8,128)(2,1)S(1)}, u32[]{:S(2)}, u32[]{:S(2)}) %collective-permute-start.7) | collective-permute-done | bytes 262176 | tf_op jit(solution)/shard_map/ppermute | solution.py:629
  106.9 0.9 shard_map.134
  107.8 0.1 stack.47.spots_ref
  107.8 2.0 %shard_map.133 = (f32[1024,256]{1,0:T(8,128)}, f32[1024,256]{1,0:T(8,128)}) custom-call(s32[8]{0:T(128)S(1)} %stack.47.spots_ref, bf16[128,512]{1,0:T(8,128)(2,1)S(1)} %add_convert_fusion.2.refs_0_, bf16[128,512]{1,0:T(8,128)(2,1)S(1)} %collective-permute-done.8.refs_1_, bf16[128,512]{1,0:T(8,128)(2,1)S(1)} %collective-permute-done.9.refs_2_, ...), custom_call_target="tpu_custom_call" | custom-call | flops 524288 | bytes 3145728 | tf_op jit(solution)/shard_map/pallas_call | solution.py:361
  109.9 0.8 shard_map.135
  (31 shorter events, 0.3 us)
Async XLA Ops:
  0.6 100.1 %copy-start = (f32[1024]{0:T(1024)S(1)}, f32[1024]{0:T(1024)}, u32[]{:S(2)}) copy-start(f32[1024]{0:T(1024)} %param.10) | copy-start | bytes 12292
  1.7 20.4 %collective-permute-start = (bf16[512,256]{1,0:T(8,128)(2,1)S(1)}, bf16[512,256]{1,0:T(8,128)(2,1)S(1)}, u32[]{:S(2)}, u32[]{:S(2)}) collective-permute-start(bf16[512,256]{1,0:T(8,128)(2,1)S(1)} %get-tuple-element.68.first_ref.rows_ref), channel_id=1, source_target_pairs={{0,16},{2,18},{4,20},{6,22},{8,24},{10,26},{12,28},{14,30},{16,0},... | collective-permute-start | bytes 786440 | tf_op jit(solution)/shard_map/ppermute | solution.py:549
  22.0 7.5 %copy-start.4 = (bf16[1024,256]{1,0:T(8,128)(2,1)S(1)}, bf16[1024,256]{1,0:T(8,128)(2,1)}, u32[]{:S(2)}) copy-start(bf16[1024,256]{1,0:T(8,128)(2,1)} %param.11) | copy-start | bytes 1572868
  22.0 7.6 %copy-start.3 = (bf16[1024,256]{1,0:T(8,128)(2,1)S(1)}, bf16[1024,256]{1,0:T(8,128)(2,1)}, u32[]{:S(2)}) copy-start(bf16[1024,256]{1,0:T(8,128)(2,1)} %param.12) | copy-start | bytes 1572868
  22.0 8.0 %copy-start.6 = (bf16[2048]{0:T(1024)(128)(2,1)S(1)}, bf16[2048]{0:T(1024)(128)(2,1)}, u32[]{:S(2)}) copy-start(bf16[2048]{0:T(1024)(128)(2,1)} %param.14) | copy-start | bytes 12292
  22.1 8.0 %copy-start.5 = (s32[16,128]{1,0:T(8,128)S(1)}, s32[16,128]{1,0:T(8,128)}, u32[]{:S(2)}) copy-start(s32[16,128]{1,0:T(8,128)} %param.17) | copy-start | bytes 24580
  22.1 1.6 %collective-permute-start.1 = (bf16[512,256]{1,0:T(8,128)(2,1)S(1)}, bf16[512,256]{1,0:T(8,128)(2,1)S(1)}, u32[]{:S(2)}, u32[]{:S(2)}) collective-permute-start(bf16[512,256]{1,0:T(8,128)(2,1)S(1)} %collective-permute-done.first_ref), channel_id=1, source_target_pairs={{1,0},{0,1},{3,2},{2,3},{5,4},{4,5},{7,6},{6,7},{9,8},{8,9},{11,10... | collective-permute-start | bytes 786440 | tf_op jit(solution)/shard_map/ppermute | solution.py:565
  25.9 18.7 %all-to-all-start.1 = ((bf16[8,2,128,256]{3,2,1,0:T(8,128)(2,1)}), bf16[8,2,128,256]{3,2,1,0:T(8,128)(2,1)S(1)}, u32[]{:S(2)}, u32[]{:S(2)}) async-start(bf16[8,2,128,256]{3,2,1,0:T(8,128)(2,1)} %shard_map.129), calls=%async_computation.1 | async-start | bytes 2097152 | tf_op jit(solution)/shard_map/all_to_all | solution.py:570
  29.5 2.1 %collective-permute-start.2 = (bf16[1024,256]{1,0:T(8,128)(2,1)S(1)}, bf16[1024,256]{1,0:T(8,128)(2,1)}, u32[]{:S(2)}, u32[]{:S(2)}) collective-permute-start(bf16[1024,256]{1,0:T(8,128)(2,1)S(1)} %copy-done.4), channel_id=1, source_target_pairs={{1,0},{0,1},{3,2},{2,3},{5,4},{4,5},{7,6},{6,7},{9,8},{8,9},{11,10... | collective-permute-start | bytes 1572872 | tf_op jit(solution)/shard_map/ppermute | solution.py:538
  29.7 2.7 %collective-permute-start.3 = (bf16[1024,256]{1,0:T(8,128)(2,1)S(1)}, bf16[1024,256]{1,0:T(8,128)(2,1)}, u32[]{:S(2)}, u32[]{:S(2)}) collective-permute-start(bf16[1024,256]{1,0:T(8,128)(2,1)S(1)} %copy-done.3), channel_id=1, source_target_pairs={{1,0},{0,1},{3,2},{2,3},{5,4},{4,5},{7,6},{6,7},{9,8},{8,9},{11,10... | collective-permute-start | bytes 1572872 | tf_op jit(solution)/shard_map/ppermute | solution.py:538
  33.7 10.8 %copy-start.1 = (f32[2048]{0:T(1024)S(1)}, f32[2048]{0:T(1024)}, u32[]{:S(2)}) copy-start(f32[2048]{0:T(1024)} %param.13) | copy-start | bytes 24580
  33.7 10.8 %copy-start.2 = (f32[128]{0:T(128)S(1)}, f32[128]{0:T(128)}, u32[]{:S(2)}) copy-start(f32[128]{0:T(128)} %param.15) | copy-start | bytes 1540
  48.3 2.7 %collective-permute-start.4 = (bf16[1024,512]{1,0:T(8,128)(2,1)S(1)}, bf16[1024,512]{1,0:T(8,128)(2,1)S(1)}, u32[]{:S(2)}, u32[]{:S(2)}) collective-permute-start(bf16[1024,512]{1,0:T(8,128)(2,1)S(1)} %get-tuple-element.42), channel_id=1, source_target_pairs={{1,0},{0,1},{3,2},{2,3},{5,4},{4,5},{7,6},{6,7},{9,8},{8,9},{11,10... | collective-permute-start | bytes 3145736 | tf_op jit(solution)/shard_map/ppermute | solution.py:588
  81.7 7.6 %collective-permute-start.5 = (bf16[128,512]{1,0:T(8,128)(2,1)S(1)}, bf16[128,512]{1,0:T(8,128)(2,1)S(1)}, u32[]{:S(2)}, u32[]{:S(2)}) collective-permute-start(bf16[128,512]{1,0:T(8,128)(2,1)S(1)} %pad_maximum_fusion.3), channel_id=1, source_target_pairs={{0,16},{2,18},{4,20},{6,22},{8,24},{10,26},{12,28},{14,30},{16,0},... | collective-permute-start | bytes 393224 | tf_op jit(solution)/shard_map/ppermute | solution.py:610
  89.4 2.7 %collective-permute-start.6 = (bf16[512,512]{1,0:T(8,128)(2,1)S(1)}, bf16[512,512]{1,0:T(8,128)(2,1)S(1)}, u32[]{:S(2)}, u32[]{:S(2)}) collective-permute-start(bf16[512,512]{1,0:T(8,128)(2,1)S(1)} %get-tuple-element.46), channel_id=1, source_target_pairs={{1,0},{0,1},{3,2},{2,3},{5,4},{4,5},{7,6},{6,7},{9,8},{8,9},{11,10... | collective-permute-start | bytes 1572872 | tf_op jit(solution)/shard_map/ppermute | solution.py:615
  89.4 6.0 %collective-permute-start.11 = (bf16[128,512]{1,0:T(8,128)(2,1)S(1)}, bf16[128,512]{1,0:T(8,128)(2,1)S(1)}, u32[]{:S(2)}, u32[]{:S(2)}) collective-permute-start(bf16[128,512]{1,0:T(8,128)(2,1)S(1)} %add_convert_fusion.2.refs_0_), channel_id=1, source_target_pairs={{8,0},{10,2},{12,4},{14,6},{0,8},{2,10},{4,12},{6,14},{24,16},{26,... | collective-permute-start | bytes 393224 | tf_op jit(solution)/shard_map/ppermute | solution.py:488
  89.5 8.5 %collective-permute-start.10 = (bf16[128,512]{1,0:T(8,128)(2,1)S(1)}, bf16[128,512]{1,0:T(8,128)(2,1)S(1)}, u32[]{:S(2)}, u32[]{:S(2)}) collective-permute-start(bf16[128,512]{1,0:T(8,128)(2,1)S(1)} %add_convert_fusion.2.refs_0_), channel_id=1, source_target_pairs={{6,0},{4,2},{2,4},{0,6},{14,8},{12,10},{10,12},{8,14},{22,16},{20,... | collective-permute-start | bytes 393224 | tf_op jit(solution)/shard_map/ppermute | solution.py:488
  91.0 9.1 %collective-permute-start.9 = (bf16[128,512]{1,0:T(8,128)(2,1)S(1)}, bf16[128,512]{1,0:T(8,128)(2,1)S(1)}, u32[]{:S(2)}, u32[]{:S(2)}) collective-permute-start(bf16[128,512]{1,0:T(8,128)(2,1)S(1)} %add_convert_fusion.2.refs_0_), channel_id=1, source_target_pairs={{4,0},{6,2},{0,4},{2,6},{12,8},{14,10},{8,12},{10,14},{20,16},{22,... | collective-permute-start | bytes 393224 | tf_op jit(solution)/shard_map/ppermute | solution.py:488
  92.2 14.7 %collective-permute-start.7 = (bf16[512,256]{1,0:T(8,128)(2,1)S(1)}, bf16[512,256]{1,0:T(8,128)(2,1)S(1)}, u32[]{:S(2)}, u32[]{:S(2)}) collective-permute-start(bf16[512,256]{1,0:T(8,128)(2,1)S(1)} %add_convert_fusion.1), channel_id=1, source_target_pairs={{0,16},{2,18},{4,20},{6,22},{8,24},{10,26},{12,28},{14,30},{16,0},... | collective-permute-start | bytes 786440 | tf_op jit(solution)/shard_map/ppermute | solution.py:629
  93.4 7.4 %collective-permute-start.8 = (bf16[128,512]{1,0:T(8,128)(2,1)S(1)}, bf16[128,512]{1,0:T(8,128)(2,1)S(1)}, u32[]{:S(2)}, u32[]{:S(2)}) collective-permute-start(bf16[128,512]{1,0:T(8,128)(2,1)S(1)} %add_convert_fusion.2.refs_0_), channel_id=1, source_target_pairs={{2,0},{0,2},{6,4},{4,6},{10,8},{8,10},{14,12},{12,14},{18,16},{16,... | collective-permute-start | bytes 393224 | tf_op jit(solution)/shard_map/ppermute | solution.py:488
  95.4 6.7 %collective-permute-start.14 = (bf16[128,512]{1,0:T(8,128)(2,1)S(1)}, bf16[128,512]{1,0:T(8,128)(2,1)S(1)}, u32[]{:S(2)}, u32[]{:S(2)}) collective-permute-start(bf16[128,512]{1,0:T(8,128)(2,1)S(1)} %collective-permute-done.11.refs_4_), channel_id=1, source_target_pairs={{6,0},{4,2},{2,4},{0,6},{14,8},{12,10},{10,12},{8,14},{22,16},{20,... | collective-permute-start | bytes 393224 | tf_op jit(solution)/shard_map/ppermute | solution.py:488
  98.0 6.8 %collective-permute-start.13 = (bf16[128,512]{1,0:T(8,128)(2,1)S(1)}, bf16[128,512]{1,0:T(8,128)(2,1)S(1)}, u32[]{:S(2)}, u32[]{:S(2)}) collective-permute-start(bf16[128,512]{1,0:T(8,128)(2,1)S(1)} %collective-permute-done.11.refs_4_), channel_id=1, source_target_pairs={{4,0},{6,2},{0,4},{2,6},{12,8},{14,10},{8,12},{10,14},{20,16},{22,... | collective-permute-start | bytes 393224 | tf_op jit(solution)/shard_map/ppermute | solution.py:488
  100.1 5.1 %collective-permute-start.12 = (bf16[128,512]{1,0:T(8,128)(2,1)S(1)}, bf16[128,512]{1,0:T(8,128)(2,1)S(1)}, u32[]{:S(2)}, u32[]{:S(2)}) collective-permute-start(bf16[128,512]{1,0:T(8,128)(2,1)S(1)} %collective-permute-done.11.refs_4_), channel_id=1, source_target_pairs={{2,0},{0,2},{6,4},{4,6},{10,8},{8,10},{14,12},{12,14},{18,16},{16,... | collective-permute-start | bytes 393224 | tf_op jit(solution)/shard_map/ppermute | solution.py:488
  107.8 2.1 %collective-permute-start.15 = (bf16[512,256]{1,0:T(8,128)(2,1)S(1)}, bf16[512,256]{1,0:T(8,128)(2,1)S(1)}, u32[]{:S(2)}, u32[]{:S(2)}) collective-permute-start(bf16[512,256]{1,0:T(8,128)(2,1)S(1)} %get-tuple-element.59.mine_ref), channel_id=1, source_target_pairs={{1,0},{0,1},{3,2},{2,3},{5,4},{4,5},{7,6},{6,7},{9,8},{8,9},{11,10... | collective-permute-start | bytes 786440 | tf_op jit(solution)/shard_map/ppermute | solution.py:636

commit v11 on v10

--- a/solution.py
+++ b/solution.py
@@ -555,17 +555,19 @@
     asked = lax.all_to_all(
         asked, "table", split_axis=0, concat_axis=0, tiled=True, axis_index_groups=halves
     )
+    asked, far_share = lax.optimization_barrier((asked, far_share))
+    if paired:
+        came = lax.ppermute(far_share, "narrow", sent_from("narrow", 1, 2, 1))
+        far_halves = (far_share, came)
+    else:
+        far_halves = tuple(jnp.split(narrow_whole(far_share), 2, axis=0))
     near_ids, far_ids = asked[:, 0, :per_window], asked[:, 0, per_window:]
     if per_window != SLOTS * HOT:
         by_block = (ids.reshape(-1, SLOTS * HOT) for ids in (near_ids, far_ids))
         asked = jnp.concatenate(tuple(by_block), axis=1)
     sums = pool_lookups(0, swap, asked, own_halves, pools_per)
-    sums, far_share = lax.optimization_barrier((sums, far_share))
-    if paired:
-        came = lax.ppermute(far_share, "narrow", sent_from("narrow", 1, 2, 1))
-        far_halves = (far_share, came)
-    else:
-        far_halves = tuple(jnp.split(narrow_whole(far_share), 2, axis=0))
+    far_halves = lax.optimization_barrier((sums, *far_halves))
+    sums, far_halves = far_halves[0], far_halves[1:]
     sums = pool_lookups(1, swap, asked, far_halves, pools_per, (sums,))
     arrived = lax.all_to_all(
         sums, "table", split_axis=0, concat_axis=0, tiled=True, axis_index_groups=halves

time: 111 us -> 111 us (level)
  waiting for transfers between devices: 28.6 us -> 25.8 us
  starting transfers between devices: 17.1 us -> 18.8 us
    ppermute x1, waiting for transfers between devices: 1.52 us -> 0.01 us  [local(): came = lax.ppermute(far_share, 'narrow', sent_from('narrow', 1, 2, 1))]
  transfers between devices with their start and end apart: 17 -> 17, of which waited for: 12 -> 10; matrix products, arithmetic and copies ran while one was open for 2% -> 2% of each run, Pallas kernels for 8% -> 8%
where the time goes in v11:
time: 111 us; the launch traced here: 110 us
  blocking collectives  43.8 us (39%)
  waiting for transfers between devices  25.8 us (23%)
  starting transfers between devices  18.8 us (17%)
  Pallas kernels  16.4 us (15%)
  local copies, waits for them, and re-layouts  2.24 us (2%)
  other arithmetic  2.22 us (2%)
    all_to_all x1, blocking collectives, local(): lax.all_to_all(jnp.concatenate(outgoing, axis=1), 'table', split_axis=0,...  30.6 us
    all_to_all x1, blocking collectives, local(): lax.all_to_all(asked, 'table', split_axis=0, concat_axis=0, tiled=True, a...  13.2 us
    all_to_all x1, waiting for transfers between devices, local(): lax.all_to_all(sums, 'table', split_axis=0, concat_axis=0, tiled=True, ax...  10.9 us
    ppermute x7, starting transfers between devices, gathered_pieces(): came = lax.ppermute(block, axis, sent_from(axis, stride, group, step))  7.55 us
    ppermute x7, waiting for transfers between devices, gathered_pieces(): came = lax.ppermute(block, axis, sent_from(axis, stride, group, step))  6.13 us
    pallas_call x2, Pallas kernels, pool_lookups(): kernel_call(functools.partial(pool_kernel, part), jax.ShapeDtypeStruct((s...  4.41 us
    ppermute x1, starting transfers between devices, local(): far_share = lax.ppermute(own_share, 'table', across)  4.1 us
    pallas_call x1, Pallas kernels, dense_step(): kernel_call(dense_kernel, (jax.ShapeDtypeStruct((1, samples), jnp.float32...  3.73 us
  transfers between devices with their start and end apart: 17, of which 10 were waited for; matrix products, arithmetic and copies ran while one was open for 2% of the time, Pallas kernels for 8%

profile of v11, /device:TPU:0, one launch (start us, length us, event | category | flops | bytes accessed | tf_op | source)
XLA Modules:
  0.0 110.3 jit_solution(3095220790633789594)
XLA Ops:
  0.6 0.0 copy-start
  0.7 1.1 constant_dynamic-slice_fusion.2
  1.7 4.1 %collective-permute-start = (bf16[512,256]{1,0:T(8,128)(2,1)S(1)}, bf16[512,256]{1,0:T(8,128)(2,1)S(1)}, u32[]{:S(2)}, u32[]{:S(2)}) collective-permute-start(bf16[512,256]{1,0:T(8,128)(2,1)S(1)} %get-tuple-element.74.first_ref.rows_ref), channel_id=1, source_target_pairs={{0,16},{2,18},{4,20},{6,22},{8,24},{10,26},{12,28},{14,30},{16,0},... | collective-permute-start | bytes 786440 | tf_op jit(solution)/shard_map/ppermute | solution.py:549
  5.8 0.7 constant_dynamic-slice_fusion.5
  6.6 13.2 %all_to_all.15.ids_ref = s32[8,1,1024]{2,1,0:T(1,128)S(1)} all-to-all(s32[8,1,1024]{2,1,0:T(1,128)S(1)} %broadcast_in_dim.3), channel_id=1, replica_groups={{0,2,4,6,8,10,12,14},{16,18,20,22,24,26,28,30},{1,3,5,7,9,11,13,15},{17..., dimensions={0} | all-to-all | bytes 65536 | tf_op jit(solution)/shard_map/all_to_all | solution.py:555
  19.8 2.2 %shard_map.128.refs_0_ = bf16[8,2,128,256]{3,2,1,0:T(8,128)(2,1)} custom-call(s32[1]{0:T(128)} %bitcast.swap_ref, s32[8,1,1024]{2,1,0:T(1,128)S(1)} %all_to_all.15.ids_ref, bf16[512,256]{1,0:T(8,128)(2,1)S(1)} %get-tuple-element.74.first_ref.rows_ref, bf16[512,256]{1,0:T(8,128)(2,1)S(1)} %get-tuple-element.73.second_ref), custom_call_target="tpu_custom_call" | custom-call | flops 536870912 | bytes 1048576 | tf_op jit(solution)/shard_map/pallas_call | solution.py:121
  22.1 0.0 copy-start.6
  22.1 2.2 %shard_map.129 = bf16[8,2,128,256]{3,2,1,0:T(8,128)(2,1)} custom-call(s32[1]{0:T(128)} %bitcast.swap_ref, s32[8,1,1024]{2,1,0:T(1,128)S(1)} %all_to_all.15.ids_ref, bf16[512,256]{1,0:T(8,128)(2,1)S(1)} %collective-permute-done.first_ref, bf16[512,256]{1,0:T(8,128)(2,1)S(1)} %collective-permute-done.1.second_ref, ...), custom_call_target="tpu_custom_call", output_to_operand_aliasing={{}: (4, {})} | custom-call | flops 536870912 | bytes 1048576 | tf_op jit(solution)/shard_map/pallas_call | solution.py:121
  24.3 3.6 %all-to-all-start.1 = ((bf16[8,2,128,256]{3,2,1,0:T(8,128)(2,1)}), bf16[8,2,128,256]{3,2,1,0:T(8,128)(2,1)S(1)}, u32[]{:S(2)}, u32[]{:S(2)}) async-start(bf16[8,2,128,256]{3,2,1,0:T(8,128)(2,1)} %shard_map.129), calls=%async_computation.1 | async-start | bytes 2097152 | tf_op jit(solution)/shard_map/all_to_all | solution.py:572
  27.9 0.6 collective-permute-start.2
  28.5 0.1 collective-permute-start.3
  28.6 1.5 %collective-permute-done.2 = bf16[1024,256]{1,0:T(8,128)(2,1)} collective-permute-done((bf16[1024,256]{1,0:T(8,128)(2,1)S(1)}, bf16[1024,256]{1,0:T(8,128)(2,1)}, u32[]{:S(2)}, u32[]{:S(2)}) %collective-permute-start.2) | collective-permute-done | bytes 524320 | tf_op jit(solution)/shard_map/ppermute | solution.py:538
  30.1 0.7 collective-permute-done.3
  30.9 1.4 %broadcast_select_fusion.1 = (bf16[1024,256]{1,0:T(8,128)(2,1)S(1)}, bf16[1024,256]{1,0:T(8,128)(2,1)S(1)}, bf16[1024,256]{1,0:T(8,128)(2,1)S(1)}, bf16[1024,256]{1,0:T(8,128)(2,1)S(1)}) fusion(bf16[1024,256]{1,0:T(8,128)(2,1)S(1)} %copy-done.3, bf16[1024,256]{1,0:T(8,128)(2,1)} %collective-permute-done.3, pred[]{:T(512)S(6)} %eq.24, ...), kind=kLoop, calls=%fused_computation.7 | loop fusion | flops 1048576 | bytes 4194305 | tf_op jit(solution)/shard_map/jit(_where)/select_n | solution.py:539
  32.3 0.1 pad_maximum_fusion.2.up_ref
  32.4 0.1 pad_maximum_fusion.1.down_ref
  32.4 10.9 %all-to-all-done.1 = bf16[8,2,128,256]{3,2,1,0:T(8,128)(2,1)S(1)} async-done(((bf16[8,2,128,256]{3,2,1,0:T(8,128)(2,1)}), bf16[8,2,128,256]{3,2,1,0:T(8,128)(2,1)S(1)}, u32[]{:S(2)}, u32[]{:S(2)}) %all-to-all-start.1) | async-done | bytes 1048608 | tf_op jit(solution)/shard_map/all_to_all | solution.py:572
  43.4 3.7 %shard_map.130 = (f32[1,128]{1,0:T(1,128)}, bf16[1024,256]{1,0:T(8,128)(2,1)S(1)}, bf16[1024,512]{1,0:T(8,128)(2,1)S(1)}, bf16[1024,512]{1,0:T(8,128)(2,1)S(1)}) custom-call(s32[1]{0:T(128)} %bitcast.swap_ref, s32[1,2048]{1,0:T(1,128)S(1)} %bitcast.27, f32[1,2048]{1,0:T(1,128)S(1)} %bitcast.29, bf16[1,2048]{1,0:T(2,128)(2,1)S(1)} %reshape.52.weight_ref, ...), custom_call_target="tpu_custom_call" | custom-call | flops 1879048192 | bytes 5242880 | tf_op jit(solution)/shard_map/pallas_call | solution.py:302
  47.1 0.1 collective-permute-start.4
  47.2 1.4 %shard_map.131 = bf16[2048,256]{1,0:T(8,128)(2,1)S(1)} custom-call(s32[16,128]{1,0:T(8,128)S(1)} %bitcast.28, bf16[1024,256]{1,0:T(8,128)(2,1)S(1)} %get-tuple-element.46.grads_ref), custom_call_target="tpu_custom_call" | custom-call | flops 1073741824 | bytes 1572864 | tf_op jit(solution)/shard_map/pallas_call | solution.py:221
  48.6 1.2 %collective-permute-done.4 = bf16[1024,512]{1,0:T(8,128)(2,1)S(1)} collective-permute-done((bf16[1024,512]{1,0:T(8,128)(2,1)S(1)}, bf16[1024,512]{1,0:T(8,128)(2,1)S(1)}, u32[]{:S(2)}, u32[]{:S(2)}) %collective-permute-start.4) | collective-permute-done | bytes 1048608 | tf_op jit(solution)/shard_map/ppermute | solution.py:590
  49.8 0.3 add_convert_fusion
  50.1 0.1 copy.15
  50.2 0.1 fusion
  50.3 0.1 pad_maximum_fusion
  50.5 30.6 %all_to_all.16.grads_ref = bf16[8,512,256]{2,1,0:T(8,128)(2,1)S(1)} all-to-all(bf16[8,512,256]{2,1,0:T(8,128)(2,1)S(1)} %pad_maximum_fusion), channel_id=1, replica_groups={{0,2,4,6,8,10,12,14},{16,18,20,22,24,26,28,30},{1,3,5,7,9,11,13,15},{17..., dimensions={0} | all-to-all | bytes 4194304 | tf_op jit(solution)/shard_map/all_to_all | solution.py:602
  81.1 0.1 slice_reduce_fusion
  81.2 1.0 collective-permute-start.5
  82.2 3.2 %shard_map.132 = (bf16[512,512]{1,0:T(8,128)(2,1)S(1)}, bf16[512,512]{1,0:T(8,128)(2,1)S(1)}) custom-call(s32[1]{0:T(128)} %bitcast.swap_ref, s32[8,1,1024]{2,1,0:T(1,128)S(1)} %all_to_all.15.ids_ref, bf16[8,512,256]{2,1,0:T(8,128)(2,1)S(1)} %all_to_all.16.grads_ref), custom_call_target="tpu_custom_call" | custom-call | flops 1073741824 | bytes 3145728 | tf_op jit(solution)/shard_map/pallas_call | solution.py:175
  85.4 3.5 %collective-permute-done.5 = bf16[128,512]{1,0:T(8,128)(2,1)S(1)} collective-permute-done((bf16[128,512]{1,0:T(8,128)(2,1)S(1)}, bf16[128,512]{1,0:T(8,128)(2,1)S(1)}, u32[]{:S(2)}, u32[]{:S(2)}) %collective-permute-start.5) | collective-permute-done | bytes 131104 | tf_op jit(solution)/shard_map/ppermute | solution.py:612
  88.9 0.1 collective-permute-start.11
  89.0 1.5 %collective-permute-start.10 = (bf16[128,512]{1,0:T(8,128)(2,1)S(1)}, bf16[128,512]{1,0:T(8,128)(2,1)S(1)}, u32[]{:S(2)}, u32[]{:S(2)}) collective-permute-start(bf16[128,512]{1,0:T(8,128)(2,1)S(1)} %add_convert_fusion.2.refs_0_), channel_id=1, source_target_pairs={{6,0},{4,2},{2,4},{0,6},{14,8},{12,10},{10,12},{8,14},{22,16},{20,... | collective-permute-start | bytes 393224 | tf_op jit(solution)/shard_map/ppermute | solution.py:488
  90.5 1.1 collective-permute-start.9
  91.6 0.1 add_convert_fusion.1
  91.7 1.8 %collective-permute-start.7 = (bf16[512,256]{1,0:T(8,128)(2,1)S(1)}, bf16[512,256]{1,0:T(8,128)(2,1)S(1)}, u32[]{:S(2)}, u32[]{:S(2)}) collective-permute-start(bf16[512,256]{1,0:T(8,128)(2,1)S(1)} %add_convert_fusion.1), channel_id=1, source_target_pairs={{0,16},{2,18},{4,20},{6,22},{8,24},{10,26},{12,28},{14,30},{16,0},... | collective-permute-start | bytes 786440 | tf_op jit(solution)/shard_map/ppermute | solution.py:631
  93.5 1.5 %collective-permute-start.8 = (bf16[128,512]{1,0:T(8,128)(2,1)S(1)}, bf16[128,512]{1,0:T(8,128)(2,1)S(1)}, u32[]{:S(2)}, u32[]{:S(2)}) collective-permute-start(bf16[128,512]{1,0:T(8,128)(2,1)S(1)} %add_convert_fusion.2.refs_0_), channel_id=1, source_target_pairs={{2,0},{0,2},{6,4},{4,6},{10,8},{8,10},{14,12},{12,14},{18,16},{16,... | collective-permute-start | bytes 393224 | tf_op jit(solution)/shard_map/ppermute | solution.py:488
  95.0 2.5 %collective-permute-start.14 = (bf16[128,512]{1,0:T(8,128)(2,1)S(1)}, bf16[128,512]{1,0:T(8,128)(2,1)S(1)}, u32[]{:S(2)}, u32[]{:S(2)}) collective-permute-start(bf16[128,512]{1,0:T(8,128)(2,1)S(1)} %collective-permute-done.11.refs_4_), channel_id=1, source_target_pairs={{6,0},{4,2},{2,4},{0,6},{14,8},{12,10},{10,12},{8,14},{22,16},{20,... | collective-permute-start | bytes 393224 | tf_op jit(solution)/shard_map/ppermute | solution.py:488
  97.5 1.9 %collective-permute-done.9.refs_2_ = bf16[128,512]{1,0:T(8,128)(2,1)S(1)} collective-permute-done((bf16[128,512]{1,0:T(8,128)(2,1)S(1)}, bf16[128,512]{1,0:T(8,128)(2,1)S(1)}, u32[]{:S(2)}, u32[]{:S(2)}) %collective-permute-start.9) | collective-permute-done | bytes 131104 | tf_op jit(solution)/shard_map/ppermute | solution.py:488
  99.4 0.9 collective-permute-start.12
  100.3 0.1 dynamic-slice_bitcast_fusion.accum_ref
  100.4 1.9 %collective-permute-done.14.refs_7_ = bf16[128,512]{1,0:T(8,128)(2,1)S(1)} collective-permute-done((bf16[128,512]{1,0:T(8,128)(2,1)S(1)}, bf16[128,512]{1,0:T(8,128)(2,1)S(1)}, u32[]{:S(2)}, u32[]{:S(2)}) %collective-permute-start.14) | collective-permute-done | bytes 131104 | tf_op jit(solution)/shard_map/ppermute | solution.py:488
  102.2 2.1 %collective-permute-done.13.refs_6_ = bf16[128,512]{1,0:T(8,128)(2,1)S(1)} collective-permute-done((bf16[128,512]{1,0:T(8,128)(2,1)S(1)}, bf16[128,512]{1,0:T(8,128)(2,1)S(1)}, u32[]{:S(2)}, u32[]{:S(2)}) %collective-permute-start.13) | collective-permute-done | bytes 131104 | tf_op jit(solution)/shard_map/ppermute | solution.py:488
  104.3 0.3 collective-permute-done.12.refs_5_
  104.6 1.8 %collective-permute-done.7.far_ref = bf16[512,256]{1,0:T(8,128)(2,1)S(1)} collective-permute-done((bf16[512,256]{1,0:T(8,128)(2,1)S(1)}, bf16[512,256]{1,0:T(8,128)(2,1)S(1)}, u32[]{:S(2)}, u32[]{:S(2)}) %collective-permute-start.7) | collective-permute-done | bytes 262176 | tf_op jit(solution)/shard_map/ppermute | solution.py:631
  106.4 0.9 shard_map.134
  107.3 0.1 stack.47.spots_ref
  107.3 2.0 %shard_map.133 = (f32[1024,256]{1,0:T(8,128)}, f32[1024,256]{1,0:T(8,128)}) custom-call(s32[8]{0:T(128)S(1)} %stack.47.spots_ref, bf16[128,512]{1,0:T(8,128)(2,1)S(1)} %add_convert_fusion.2.refs_0_, bf16[128,512]{1,0:T(8,128)(2,1)S(1)} %collective-permute-done.8.refs_1_, bf16[128,512]{1,0:T(8,128)(2,1)S(1)} %collective-permute-done.9.refs_2_, ...), custom_call_target="tpu_custom_call" | custom-call | flops 524288 | bytes 3145728 | tf_op jit(solution)/shard_map/pallas_call | solution.py:361
  109.3 0.8 shard_map.135
  (31 shorter events, 0.2 us)
Async XLA Ops:
  0.6 99.7 %copy-start = (f32[1024]{0:T(1024)S(1)}, f32[1024]{0:T(1024)}, u32[]{:S(2)}) copy-start(f32[1024]{0:T(1024)} %param.10) | copy-start | bytes 12292
  1.7 18.1 %collective-permute-start = (bf16[512,256]{1,0:T(8,128)(2,1)S(1)}, bf16[512,256]{1,0:T(8,128)(2,1)S(1)}, u32[]{:S(2)}, u32[]{:S(2)}) collective-permute-start(bf16[512,256]{1,0:T(8,128)(2,1)S(1)} %get-tuple-element.74.first_ref.rows_ref), channel_id=1, source_target_pairs={{0,16},{2,18},{4,20},{6,22},{8,24},{10,26},{12,28},{14,30},{16,0},... | collective-permute-start | bytes 786440 | tf_op jit(solution)/shard_map/ppermute | solution.py:549
  19.8 2.3 %collective-permute-start.1 = (bf16[512,256]{1,0:T(8,128)(2,1)S(1)}, bf16[512,256]{1,0:T(8,128)(2,1)S(1)}, u32[]{:S(2)}, u32[]{:S(2)}) collective-permute-start(bf16[512,256]{1,0:T(8,128)(2,1)S(1)} %collective-permute-done.first_ref), channel_id=1, source_target_pairs={{1,0},{0,1},{3,2},{2,3},{5,4},{4,5},{7,6},{6,7},{9,8},{8,9},{11,10... | collective-permute-start | bytes 786440 | tf_op jit(solution)/shard_map/ppermute | solution.py:560
  22.0 5.9 %copy-start.4 = (bf16[1024,256]{1,0:T(8,128)(2,1)S(1)}, bf16[1024,256]{1,0:T(8,128)(2,1)}, u32[]{:S(2)}) copy-start(bf16[1024,256]{1,0:T(8,128)(2,1)} %param.11) | copy-start | bytes 1572868
  22.0 6.4 %copy-start.3 = (bf16[1024,256]{1,0:T(8,128)(2,1)S(1)}, bf16[1024,256]{1,0:T(8,128)(2,1)}, u32[]{:S(2)}) copy-start(bf16[1024,256]{1,0:T(8,128)(2,1)} %param.12) | copy-start | bytes 1572868
  22.1 6.5 %copy-start.6 = (bf16[2048]{0:T(1024)(128)(2,1)S(1)}, bf16[2048]{0:T(1024)(128)(2,1)}, u32[]{:S(2)}) copy-start(bf16[2048]{0:T(1024)(128)(2,1)} %param.14) | copy-start | bytes 12292
  22.1 6.5 %copy-start.5 = (s32[16,128]{1,0:T(8,128)S(1)}, s32[16,128]{1,0:T(8,128)}, u32[]{:S(2)}) copy-start(s32[16,128]{1,0:T(8,128)} %param.17) | copy-start | bytes 24580
  24.3 19.0 %all-to-all-start.1 = ((bf16[8,2,128,256]{3,2,1,0:T(8,128)(2,1)}), bf16[8,2,128,256]{3,2,1,0:T(8,128)(2,1)S(1)}, u32[]{:S(2)}, u32[]{:S(2)}) async-start(bf16[8,2,128,256]{3,2,1,0:T(8,128)(2,1)} %shard_map.129), calls=%async_computation.1 | async-start | bytes 2097152 | tf_op jit(solution)/shard_map/all_to_all | solution.py:572
  27.9 2.2 %collective-permute-start.2 = (bf16[1024,256]{1,0:T(8,128)(2,1)S(1)}, bf16[1024,256]{1,0:T(8,128)(2,1)}, u32[]{:S(2)}, u32[]{:S(2)}) collective-permute-start(bf16[1024,256]{1,0:T(8,128)(2,1)S(1)} %copy-done.4), channel_id=1, source_target_pairs={{1,0},{0,1},{3,2},{2,3},{5,4},{4,5},{7,6},{6,7},{9,8},{8,9},{11,10... | collective-permute-start | bytes 1572872 | tf_op jit(solution)/shard_map/ppermute | solution.py:538
  28.5 2.4 %collective-permute-start.3 = (bf16[1024,256]{1,0:T(8,128)(2,1)S(1)}, bf16[1024,256]{1,0:T(8,128)(2,1)}, u32[]{:S(2)}, u32[]{:S(2)}) collective-permute-start(bf16[1024,256]{1,0:T(8,128)(2,1)S(1)} %copy-done.3), channel_id=1, source_target_pairs={{1,0},{0,1},{3,2},{2,3},{5,4},{4,5},{7,6},{6,7},{9,8},{8,9},{11,10... | collective-permute-start | bytes 1572872 | tf_op jit(solution)/shard_map/ppermute | solution.py:538
  32.3 11.1 %copy-start.1 = (f32[2048]{0:T(1024)S(1)}, f32[2048]{0:T(1024)}, u32[]{:S(2)}) copy-start(f32[2048]{0:T(1024)} %param.13) | copy-start | bytes 24580
  32.3 11.1 %copy-start.2 = (f32[128]{0:T(128)S(1)}, f32[128]{0:T(128)}, u32[]{:S(2)}) copy-start(f32[128]{0:T(128)} %param.15) | copy-start | bytes 1540
  47.1 2.7 %collective-permute-start.4 = (bf16[1024,512]{1,0:T(8,128)(2,1)S(1)}, bf16[1024,512]{1,0:T(8,128)(2,1)S(1)}, u32[]{:S(2)}, u32[]{:S(2)}) collective-permute-start(bf16[1024,512]{1,0:T(8,128)(2,1)S(1)} %get-tuple-element.48), channel_id=1, source_target_pairs={{1,0},{0,1},{3,2},{2,3},{5,4},{4,5},{7,6},{6,7},{9,8},{8,9},{11,10... | collective-permute-start | bytes 3145736 | tf_op jit(solution)/shard_map/ppermute | solution.py:590
  81.2 7.6 %collective-permute-start.5 = (bf16[128,512]{1,0:T(8,128)(2,1)S(1)}, bf16[128,512]{1,0:T(8,128)(2,1)S(1)}, u32[]{:S(2)}, u32[]{:S(2)}) collective-permute-start(bf16[128,512]{1,0:T(8,128)(2,1)S(1)} %pad_maximum_fusion.3), channel_id=1, source_target_pairs={{0,16},{2,18},{4,20},{6,22},{8,24},{10,26},{12,28},{14,30},{16,0},... | collective-permute-start | bytes 393224 | tf_op jit(solution)/shard_map/ppermute | solution.py:612
  88.9 2.7 %collective-permute-start.6 = (bf16[512,512]{1,0:T(8,128)(2,1)S(1)}, bf16[512,512]{1,0:T(8,128)(2,1)S(1)}, u32[]{:S(2)}, u32[]{:S(2)}) collective-permute-start(bf16[512,512]{1,0:T(8,128)(2,1)S(1)} %get-tuple-element.52), channel_id=1, source_target_pairs={{1,0},{0,1},{3,2},{2,3},{5,4},{4,5},{7,6},{6,7},{9,8},{8,9},{11,10... | collective-permute-start | bytes 1572872 | tf_op jit(solution)/shard_map/ppermute | solution.py:617
  88.9 6.1 %collective-permute-start.11 = (bf16[128,512]{1,0:T(8,128)(2,1)S(1)}, bf16[128,512]{1,0:T(8,128)(2,1)S(1)}, u32[]{:S(2)}, u32[]{:S(2)}) collective-permute-start(bf16[128,512]{1,0:T(8,128)(2,1)S(1)} %add_convert_fusion.2.refs_0_), channel_id=1, source_target_pairs={{8,0},{10,2},{12,4},{14,6},{0,8},{2,10},{4,12},{6,14},{24,16},{26,... | collective-permute-start | bytes 393224 | tf_op jit(solution)/shard_map/ppermute | solution.py:488
  89.0 8.5 %collective-permute-start.10 = (bf16[128,512]{1,0:T(8,128)(2,1)S(1)}, bf16[128,512]{1,0:T(8,128)(2,1)S(1)}, u32[]{:S(2)}, u32[]{:S(2)}) collective-permute-start(bf16[128,512]{1,0:T(8,128)(2,1)S(1)} %add_convert_fusion.2.refs_0_), channel_id=1, source_target_pairs={{6,0},{4,2},{2,4},{0,6},{14,8},{12,10},{10,12},{8,14},{22,16},{20,... | collective-permute-start | bytes 393224 | tf_op jit(solution)/shard_map/ppermute | solution.py:488
  90.5 8.9 %collective-permute-start.9 = (bf16[128,512]{1,0:T(8,128)(2,1)S(1)}, bf16[128,512]{1,0:T(8,128)(2,1)S(1)}, u32[]{:S(2)}, u32[]{:S(2)}) collective-permute-start(bf16[128,512]{1,0:T(8,128)(2,1)S(1)} %add_convert_fusion.2.refs_0_), channel_id=1, source_target_pairs={{4,0},{6,2},{0,4},{2,6},{12,8},{14,10},{8,12},{10,14},{20,16},{22,... | collective-permute-start | bytes 393224 | tf_op jit(solution)/shard_map/ppermute | solution.py:488
  91.7 14.7 %collective-permute-start.7 = (bf16[512,256]{1,0:T(8,128)(2,1)S(1)}, bf16[512,256]{1,0:T(8,128)(2,1)S(1)}, u32[]{:S(2)}, u32[]{:S(2)}) collective-permute-start(bf16[512,256]{1,0:T(8,128)(2,1)S(1)} %add_convert_fusion.1), channel_id=1, source_target_pairs={{0,16},{2,18},{4,20},{6,22},{8,24},{10,26},{12,28},{14,30},{16,0},... | collective-permute-start | bytes 786440 | tf_op jit(solution)/shard_map/ppermute | solution.py:631
  93.5 6.9 %collective-permute-start.8 = (bf16[128,512]{1,0:T(8,128)(2,1)S(1)}, bf16[128,512]{1,0:T(8,128)(2,1)S(1)}, u32[]{:S(2)}, u32[]{:S(2)}) collective-permute-start(bf16[128,512]{1,0:T(8,128)(2,1)S(1)} %add_convert_fusion.2.refs_0_), channel_id=1, source_target_pairs={{2,0},{0,2},{6,4},{4,6},{10,8},{8,10},{14,12},{12,14},{18,16},{16,... | collective-permute-start | bytes 393224 | tf_op jit(solution)/shard_map/ppermute | solution.py:488
  95.0 7.2 %collective-permute-start.14 = (bf16[128,512]{1,0:T(8,128)(2,1)S(1)}, bf16[128,512]{1,0:T(8,128)(2,1)S(1)}, u32[]{:S(2)}, u32[]{:S(2)}) collective-permute-start(bf16[128,512]{1,0:T(8,128)(2,1)S(1)} %collective-permute-done.11.refs_4_), channel_id=1, source_target_pairs={{6,0},{4,2},{2,4},{0,6},{14,8},{12,10},{10,12},{8,14},{22,16},{20,... | collective-permute-start | bytes 393224 | tf_op jit(solution)/shard_map/ppermute | solution.py:488
  97.5 6.8 %collective-permute-start.13 = (bf16[128,512]{1,0:T(8,128)(2,1)S(1)}, bf16[128,512]{1,0:T(8,128)(2,1)S(1)}, u32[]{:S(2)}, u32[]{:S(2)}) collective-permute-start(bf16[128,512]{1,0:T(8,128)(2,1)S(1)} %collective-permute-done.11.refs_4_), channel_id=1, source_target_pairs={{4,0},{6,2},{0,4},{2,6},{12,8},{14,10},{8,12},{10,14},{20,16},{22,... | collective-permute-start | bytes 393224 | tf_op jit(solution)/shard_map/ppermute | solution.py:488
  99.4 5.2 %collective-permute-start.12 = (bf16[128,512]{1,0:T(8,128)(2,1)S(1)}, bf16[128,512]{1,0:T(8,128)(2,1)S(1)}, u32[]{:S(2)}, u32[]{:S(2)}) collective-permute-start(bf16[128,512]{1,0:T(8,128)(2,1)S(1)} %collective-permute-done.11.refs_4_), channel_id=1, source_target_pairs={{2,0},{0,2},{6,4},{4,6},{10,8},{8,10},{14,12},{12,14},{18,16},{16,... | collective-permute-start | bytes 393224 | tf_op jit(solution)/shard_map/ppermute | solution.py:488
  107.3 2.1 %collective-permute-start.15 = (bf16[512,256]{1,0:T(8,128)(2,1)S(1)}, bf16[512,256]{1,0:T(8,128)(2,1)S(1)}, u32[]{:S(2)}, u32[]{:S(2)}) collective-permute-start(bf16[512,256]{1,0:T(8,128)(2,1)S(1)} %get-tuple-element.65.mine_ref), channel_id=1, source_target_pairs={{1,0},{0,1},{3,2},{2,3},{5,4},{4,5},{7,6},{6,7},{9,8},{8,9},{11,10... | collective-permute-start | bytes 786440 | tf_op jit(solution)/shard_map/ppermute | solution.py:638

commit v12 on v11

--- a/solution.py
+++ b/solution.py
@@ -99,17 +99,21 @@
     half = first_ref.shape[0]
     position = lax.broadcasted_iota(jnp.int32, (SLOTS, 2 * half), 1) + swap_ref[0] * half
     position = jnp.where(position >= 2 * half, position - 2 * half, position).astype(jnp.int16)
-    for block in range(slots // SLOTS):
-        counts = None
-        for lookup in range(HOT):
-            column = columns[lookup * SLOTS : (lookup + 1) * SLOTS, block : block + 1]
-            found = ones_where(column == position)
-            counts = found if counts is None else counts + found
-        counts_ref[block * SLOTS : (block + 1) * SLOTS, :] = counts
-    sums = matmul(counts_ref[:, :half], first_ref[...])
-    sums = (sums + matmul(counts_ref[:, half:], second_ref[...])).astype(jnp.bfloat16)
-    for source in range(sources):
-        sums_ref[source] = sums[source * pools : (source + 1) * pools]
+    chunk = 2 * SLOTS
+    for start in range(0, slots, chunk):
+        for block in range(start // SLOTS, (start + chunk) // SLOTS):
+            counts = None
+            for lookup in range(HOT):
+                column = columns[lookup * SLOTS : (lookup + 1) * SLOTS, block : block + 1]
+                found = ones_where(column == position)
+                counts = found if counts is None else counts + found
+            counts_ref[block * SLOTS : (block + 1) * SLOTS, :] = counts
+        here = slice(start, start + chunk)
+        sums = matmul(counts_ref[here, :half], first_ref[...])
+        sums = (sums + matmul(counts_ref[here, half:], second_ref[...])).astype(jnp.bfloat16)
+        for source in range(start // pools, (start + chunk) // pools):
+            at = source * pools - start
+            sums_ref[source] = sums[at : at + pools]
     store = pltpu.make_async_copy(sums_ref, out_ref.at[:, part], sem)
     store.start()
     store.wait()
@@ -199,33 +203,44 @@
     return jnp.sum(jnp.where(diagonal(column.shape[0]), column, 0.0), axis=0, keepdims=True)
 
 
-def return_kernel(goals_ref, grads_ref, out_ref, pick_ref):
+def return_kernel(goals_ref, direct_ref, dhidden_ref, down_ref, out_ref, pick_ref, grads_ref):
     blocks = goals_ref.shape[0]
-    bags = grads_ref.shape[0]
+    bags, emb = grads_ref.shape
     samples = bags // FEAT
+    for f in range(FEAT):
+        part = slice(f * emb, (f + 1) * emb)
+        back_term = rows_dot(dhidden_ref[...], down_ref[part, :])
+        grads = direct_ref[:, part] + back_term
+        grads_ref[f * samples : (f + 1) * samples, :] = grads.astype(jnp.bfloat16)
     high, low = split_ids(goals_ref[...])
     unit = ones_where(diagonal(SLOTS))
     columns = joined((rows_dot(unit, high), rows_dot(unit, low))).astype(jnp.int16)
     place = lax.broadcasted_iota(jnp.int32, (SLOTS, bags), 1)
     order = ((place % samples) * FEAT + place // samples).astype(jnp.int16)
-    for block in range(blocks):
-        pick_ref[block * SLOTS : (block + 1) * SLOTS, :] = ones_where(
-            columns[:, block : block + 1] == order
-        )
-    out_ref[...] = matmul(pick_ref[...], grads_ref[...]).astype(jnp.bfloat16)
-
-
-def return_grads(goals, grads):
-    bags, emb = grads.shape
+    for block in range(0, blocks, 2):
+        for one in (block, block + 1):
+            pick_ref[one * SLOTS : (one + 1) * SLOTS, :] = ones_where(
+                columns[:, one : one + 1] == order
+            )
+        here = slice(block * SLOTS, (block + 2) * SLOTS)
+        out_ref[here, :] = matmul(pick_ref[here, :], grads_ref[...]).astype(jnp.bfloat16)
+
+
+def return_grads(goals, direct, dhidden, down_full):
+    samples, width = direct.shape
+    emb = width // FEAT
     slot_count = goals.size
     return kernel_call(
         return_kernel,
         jax.ShapeDtypeStruct((slot_count, emb), jnp.bfloat16),
-        (2 * slot_count * bags * emb, 2 * grads.size + 2 * slot_count * emb),
-        [pltpu.VMEM((slot_count, bags), jnp.bfloat16)],
-        operands=2,
-        room=12,
-    )(goals.reshape(slot_count // SLOTS, SLOTS), grads)
+        (2 * slot_count * samples * width, 4 * direct.size + 2 * slot_count * emb),
+        [
+            pltpu.VMEM((slot_count, samples * FEAT), jnp.bfloat16),
+            pltpu.VMEM((samples * FEAT, emb), jnp.bfloat16),
+        ],
+        operands=4,
+        room=16,
+    )(goals.reshape(slot_count // SLOTS, SLOTS), direct, dhidden, down_full)
 
 
 def dense_kernel(
@@ -238,7 +253,8 @@
     down_ref,
     up_ref,
     logits_ref,
-    grads_ref,
+    direct_ref,
+    dhidden_ref,
     kept_ref,
     sent_ref,
     place_ref,
@@ -277,12 +293,9 @@
         dmixed = dlogit * weight_ref[:, part].astype(jnp.float32)
         feats = wide_ref[:, part].astype(jnp.float32)
         dcross_ref[:, part] = (dmixed * feats).astype(jnp.bfloat16)
+        direct_ref[:, part] = dmixed * (shifted_ref[:, part] + 1.0)
     dhidden = matmul(dcross_ref[...], up_ref[...]).astype(jnp.bfloat16)
-    for f, part in enumerate(features):
-        dmixed = dlogit * weight_ref[:, part].astype(jnp.float32)
-        back_term = rows_dot(dhidden, down_ref[part, :])
-        grads = dmixed * (shifted_ref[:, part] + 1.0) + back_term
-        grads_ref[f * samples : (f + 1) * samples, :] = grads.astype(jnp.bfloat16)
+    dhidden_ref[...] = dhidden
     for step in range(FEAT):
         into_half = swap_ref[0] if step * emb < half else 1 - swap_ref[0]
         spot = (step * emb) % half
@@ -299,11 +312,12 @@
     slots, emb = arrived.shape
     width, rank = down_full.shape
     flops = 2 * slots * samples * width + 12 * samples * width * rank
-    logits, grads, kept, sent = kernel_call(
+    logits, direct, dhidden, kept, sent = kernel_call(
         dense_kernel,
         (
             jax.ShapeDtypeStruct((1, samples), jnp.float32),
-            jax.ShapeDtypeStruct((samples * FEAT, emb), jnp.bfloat16),
+            jax.ShapeDtypeStruct((samples, width), jnp.float32),
+            jax.ShapeDtypeStruct((samples, rank), jnp.bfloat16),
             jax.ShapeDtypeStruct((width // 2, 2 * rank), jnp.bfloat16),
             jax.ShapeDtypeStruct((width // 2, 2 * rank), jnp.bfloat16),
         ),
@@ -327,7 +341,7 @@
         down_full,
         up_full,
     )
-    return logits.reshape(samples), grads, kept, sent
+    return logits.reshape(samples), direct, dhidden, kept, sent
 
 
 def spread_kernel(count, scale, aliased, spots_ref, *refs):
@@ -576,7 +590,7 @@
     arrived, down_full, up_full, goals = lax.optimization_barrier(
         (arrived, down_full, up_full, goals)
     )
-    logits, bag_grads, kept, sent = dense_step(
+    logits, direct, dhidden, kept, sent = dense_step(
         swap,
         goals,
         arrived.reshape(slot_count, emb_width),
@@ -591,7 +605,7 @@
         narrow_sum = (kept.astype(jnp.float32) + came.astype(jnp.float32)).astype(jnp.bfloat16)
     else:
         narrow_sum = scatter_sum(jnp.concatenate([kept, sent], axis=0), "narrow", narrow_levels)
-    slot_grads = return_grads(goals, bag_grads)
+    slot_grads = return_grads(goals, direct, dhidden, down_full)
     groups = [group for _, group in half_levels]
     share_terms = narrow_sum.reshape(*groups, -1, narrow_sum.shape[1])
     order = list(range(len(groups)))[::-1] + [len(groups), len(groups) + 1]

time: 111 us -> 111 us (level)
  no operation moved by 1% of the time
where the time goes in v12:
time: 111 us; the launch traced here: 110 us
  blocking collectives  43.8 us (39%)
  waiting for transfers between devices  25.4 us (23%)
  starting transfers between devices  18.8 us (17%)
  Pallas kernels  16.5 us (15%)
  local copies, waits for them, and re-layouts  2.24 us (2%)
  other arithmetic  2.22 us (2%)
    all_to_all x1, blocking collectives, local(): lax.all_to_all(jnp.concatenate(outgoing, axis=1), 'table', split_axis=0,...  30.6 us
    all_to_all x1, blocking collectives, local(): lax.all_to_all(asked, 'table', split_axis=0, concat_axis=0, tiled=True, a...  13.2 us
    all_to_all x1, waiting for transfers between devices, local(): lax.all_to_all(sums, 'table', split_axis=0, concat_axis=0, tiled=True, ax...  10.9 us
    ppermute x7, starting transfers between devices, gathered_pieces(): came = lax.ppermute(block, axis, sent_from(axis, stride, group, step))  7.53 us
    ppermute x7, waiting for transfers between devices, gathered_pieces(): came = lax.ppermute(block, axis, sent_from(axis, stride, group, step))  6.1 us
    pallas_call x2, Pallas kernels, pool_lookups(): kernel_call(functools.partial(pool_kernel, part), jax.ShapeDtypeStruct((s...  4.37 us
    ppermute x1, starting transfers between devices, local(): far_share = lax.ppermute(own_share, 'table', across)  4.1 us
    all_to_all x1, starting transfers between devices, local(): lax.all_to_all(sums, 'table', split_axis=0, concat_axis=0, tiled=True, ax...  3.57 us
  transfers between devices with their start and end apart: 17, of which 10 were waited for; matrix products, arithmetic and copies ran while one was open for 2% of the time, Pallas kernels for 8%

profile of v12, /device:TPU:0, one launch (start us, length us, event | category | flops | bytes accessed | tf_op | source)
XLA Modules:
  0.0 110.1 jit_solution(15005841888617019456)
XLA Ops:
  0.6 0.0 copy-start
  0.7 1.1 constant_dynamic-slice_fusion.2
  1.7 4.1 %collective-permute-start = (bf16[512,256]{1,0:T(8,128)(2,1)S(1)}, bf16[512,256]{1,0:T(8,128)(2,1)S(1)}, u32[]{:S(2)}, u32[]{:S(2)}) collective-permute-start(bf16[512,256]{1,0:T(8,128)(2,1)S(1)} %get-tuple-element.76.first_ref.rows_ref), channel_id=1, source_target_pairs={{0,16},{2,18},{4,20},{6,22},{8,24},{10,26},{12,28},{14,30},{16,0},... | collective-permute-start | bytes 786440 | tf_op jit(solution)/shard_map/ppermute | solution.py:563
  5.8 0.7 constant_dynamic-slice_fusion.5
  6.6 13.2 %all_to_all.15.ids_ref = s32[8,1,1024]{2,1,0:T(1,128)S(1)} all-to-all(s32[8,1,1024]{2,1,0:T(1,128)S(1)} %broadcast_in_dim.3), channel_id=1, replica_groups={{0,2,4,6,8,10,12,14},{16,18,20,22,24,26,28,30},{1,3,5,7,9,11,13,15},{17..., dimensions={0} | all-to-all | bytes 65536 | tf_op jit(solution)/shard_map/all_to_all | solution.py:569
  19.8 2.2 %shard_map.128.refs_0_ = bf16[8,2,128,256]{3,2,1,0:T(8,128)(2,1)} custom-call(s32[1]{0:T(128)} %bitcast.swap_ref, s32[8,1,1024]{2,1,0:T(1,128)S(1)} %all_to_all.15.ids_ref, bf16[512,256]{1,0:T(8,128)(2,1)S(1)} %get-tuple-element.76.first_ref.rows_ref, bf16[512,256]{1,0:T(8,128)(2,1)S(1)} %get-tuple-element.75.second_ref), custom_call_target="tpu_custom_call" | custom-call | flops 536870912 | bytes 1048576 | tf_op jit(solution)/shard_map/pallas_call | solution.py:125
  22.0 0.0 copy-start.4
  22.1 2.2 %shard_map.129 = bf16[8,2,128,256]{3,2,1,0:T(8,128)(2,1)} custom-call(s32[1]{0:T(128)} %bitcast.swap_ref, s32[8,1,1024]{2,1,0:T(1,128)S(1)} %all_to_all.15.ids_ref, bf16[512,256]{1,0:T(8,128)(2,1)S(1)} %collective-permute-done.first_ref, bf16[512,256]{1,0:T(8,128)(2,1)S(1)} %collective-permute-done.1.second_ref, ...), custom_call_target="tpu_custom_call", output_to_operand_aliasing={{}: (4, {})} | custom-call | flops 536870912 | bytes 1048576 | tf_op jit(solution)/shard_map/pallas_call | solution.py:125
  24.3 3.6 %all-to-all-start.1 = ((bf16[8,2,128,256]{3,2,1,0:T(8,128)(2,1)}), bf16[8,2,128,256]{3,2,1,0:T(8,128)(2,1)S(1)}, u32[]{:S(2)}, u32[]{:S(2)}) async-start(bf16[8,2,128,256]{3,2,1,0:T(8,128)(2,1)} %shard_map.129), calls=%async_computation.1 | async-start | bytes 2097152 | tf_op jit(solution)/shard_map/all_to_all | solution.py:586
  27.9 0.6 collective-permute-start.2
  28.4 0.1 collective-permute-start.3
  28.6 1.5 %collective-permute-done.2 = bf16[1024,256]{1,0:T(8,128)(2,1)} collective-permute-done((bf16[1024,256]{1,0:T(8,128)(2,1)S(1)}, bf16[1024,256]{1,0:T(8,128)(2,1)}, u32[]{:S(2)}, u32[]{:S(2)}) %collective-permute-start.2) | collective-permute-done | bytes 524320 | tf_op jit(solution)/shard_map/ppermute | solution.py:552
  30.1 0.7 collective-permute-done.3
  30.8 1.4 %broadcast_select_fusion.1 = (bf16[1024,256]{1,0:T(8,128)(2,1)S(1)}, bf16[1024,256]{1,0:T(8,128)(2,1)S(1)}, bf16[1024,256]{1,0:T(8,128)(2,1)S(1)}, bf16[1024,256]{1,0:T(8,128)(2,1)S(1)}) fusion(bf16[1024,256]{1,0:T(8,128)(2,1)S(1)} %copy-done.3, bf16[1024,256]{1,0:T(8,128)(2,1)} %collective-permute-done.3, pred[]{:T(512)S(6)} %eq.24, ...), kind=kLoop, calls=%fused_computation.7 | loop fusion | flops 1048576 | bytes 4194305 | tf_op jit(solution)/shard_map/jit(_where)/select_n | solution.py:553
  32.2 0.1 pad_maximum_fusion.2.up_ref
  32.3 0.1 pad_maximum_fusion.1.down_ref
  32.4 10.9 %all-to-all-done.1 = bf16[8,2,128,256]{3,2,1,0:T(8,128)(2,1)S(1)} async-done(((bf16[8,2,128,256]{3,2,1,0:T(8,128)(2,1)}), bf16[8,2,128,256]{3,2,1,0:T(8,128)(2,1)S(1)}, u32[]{:S(2)}, u32[]{:S(2)}) %all-to-all-start.1) | async-done | bytes 1048608 | tf_op jit(solution)/shard_map/all_to_all | solution.py:586
  43.3 3.5 %shard_map.130 = (f32[1,128]{1,0:T(1,128)}, f32[128,2048]{1,0:T(8,128)S(1)}, bf16[128,256]{1,0:T(8,128)(2,1)S(1)}, bf16[1024,512]{1,0:T(8,128)(2,1)S(1)}, bf16[1024,512]{1,0:T(8,128)(2,1)S(1)}) custom-call(s32[1]{0:T(128)} %bitcast.swap_ref, s32[1,2048]{1,0:T(1,128)S(1)} %bitcast.27, f32[1,2048]{1,0:T(1,128)S(1)} %bitcast.29, ...), custom_call_target="tpu_custom_call" | custom-call | flops 1879048192 | bytes 5242880 | tf_op jit(solution)/shard_map/pallas_call | solution.py:315
  46.8 0.1 collective-permute-start.4
  46.9 1.8 %shard_map.131 = bf16[2048,256]{1,0:T(8,128)(2,1)S(1)} custom-call(s32[16,128]{1,0:T(8,128)S(1)} %bitcast.28, f32[128,2048]{1,0:T(8,128)S(1)} %get-tuple-element.47.direct_ref, bf16[128,256]{1,0:T(8,128)(2,1)S(1)} %get-tuple-element.48.dhidden_ref, bf16[2048,256]{1,0:T(8,128)(2,1)S(1)} %pad_maximum_fusion.1.down_ref), custom_call_target="tpu_custom_call" | custom-call | flops 1073741824 | bytes 2097152 | tf_op jit(solution)/shard_map/pallas_call | solution.py:233
  48.7 0.8 collective-permute-done.4
  49.6 0.3 add_convert_fusion
  49.9 0.1 copy.15
  49.9 0.1 fusion
  50.1 0.1 pad_maximum_fusion
  50.2 30.6 %all_to_all.16.grads_ref = bf16[8,512,256]{2,1,0:T(8,128)(2,1)S(1)} all-to-all(bf16[8,512,256]{2,1,0:T(8,128)(2,1)S(1)} %pad_maximum_fusion), channel_id=1, replica_groups={{0,2,4,6,8,10,12,14},{16,18,20,22,24,26,28,30},{1,3,5,7,9,11,13,15},{17..., dimensions={0} | all-to-all | bytes 4194304 | tf_op jit(solution)/shard_map/all_to_all | solution.py:616
  80.8 0.1 slice_reduce_fusion
  81.0 1.0 collective-permute-start.5
  82.0 3.2 %shard_map.132 = (bf16[512,512]{1,0:T(8,128)(2,1)S(1)}, bf16[512,512]{1,0:T(8,128)(2,1)S(1)}) custom-call(s32[1]{0:T(128)} %bitcast.swap_ref, s32[8,1,1024]{2,1,0:T(1,128)S(1)} %all_to_all.15.ids_ref, bf16[8,512,256]{2,1,0:T(8,128)(2,1)S(1)} %all_to_all.16.grads_ref), custom_call_target="tpu_custom_call" | custom-call | flops 1073741824 | bytes 3145728 | tf_op jit(solution)/shard_map/pallas_call | solution.py:179
  85.2 3.4 %collective-permute-done.5 = bf16[128,512]{1,0:T(8,128)(2,1)S(1)} collective-permute-done((bf16[128,512]{1,0:T(8,128)(2,1)S(1)}, bf16[128,512]{1,0:T(8,128)(2,1)S(1)}, u32[]{:S(2)}, u32[]{:S(2)}) %collective-permute-start.5) | collective-permute-done | bytes 131104 | tf_op jit(solution)/shard_map/ppermute | solution.py:626
  88.7 0.1 collective-permute-start.11
  88.7 1.5 %collective-permute-start.10 = (bf16[128,512]{1,0:T(8,128)(2,1)S(1)}, bf16[128,512]{1,0:T(8,128)(2,1)S(1)}, u32[]{:S(2)}, u32[]{:S(2)}) collective-permute-start(bf16[128,512]{1,0:T(8,128)(2,1)S(1)} %add_convert_fusion.2.refs_0_), channel_id=1, source_target_pairs={{6,0},{4,2},{2,4},{0,6},{14,8},{12,10},{10,12},{8,14},{22,16},{20,... | collective-permute-start | bytes 393224 | tf_op jit(solution)/shard_map/ppermute | solution.py:502
  90.2 1.1 collective-permute-start.9
  91.3 0.1 add_convert_fusion.1
  91.4 1.9 %collective-permute-start.7 = (bf16[512,256]{1,0:T(8,128)(2,1)S(1)}, bf16[512,256]{1,0:T(8,128)(2,1)S(1)}, u32[]{:S(2)}, u32[]{:S(2)}) collective-permute-start(bf16[512,256]{1,0:T(8,128)(2,1)S(1)} %add_convert_fusion.1), channel_id=1, source_target_pairs={{0,16},{2,18},{4,20},{6,22},{8,24},{10,26},{12,28},{14,30},{16,0},... | collective-permute-start | bytes 786440 | tf_op jit(solution)/shard_map/ppermute | solution.py:645
  93.3 1.5 %collective-permute-start.8 = (bf16[128,512]{1,0:T(8,128)(2,1)S(1)}, bf16[128,512]{1,0:T(8,128)(2,1)S(1)}, u32[]{:S(2)}, u32[]{:S(2)}) collective-permute-start(bf16[128,512]{1,0:T(8,128)(2,1)S(1)} %add_convert_fusion.2.refs_0_), channel_id=1, source_target_pairs={{2,0},{0,2},{6,4},{4,6},{10,8},{8,10},{14,12},{12,14},{18,16},{16,... | collective-permute-start | bytes 393224 | tf_op jit(solution)/shard_map/ppermute | solution.py:502
  94.8 2.5 %collective-permute-start.14 = (bf16[128,512]{1,0:T(8,128)(2,1)S(1)}, bf16[128,512]{1,0:T(8,128)(2,1)S(1)}, u32[]{:S(2)}, u32[]{:S(2)}) collective-permute-start(bf16[128,512]{1,0:T(8,128)(2,1)S(1)} %collective-permute-done.11.refs_4_), channel_id=1, source_target_pairs={{6,0},{4,2},{2,4},{0,6},{14,8},{12,10},{10,12},{8,14},{22,16},{20,... | collective-permute-start | bytes 393224 | tf_op jit(solution)/shard_map/ppermute | solution.py:502
  97.2 1.9 %collective-permute-done.9.refs_2_ = bf16[128,512]{1,0:T(8,128)(2,1)S(1)} collective-permute-done((bf16[128,512]{1,0:T(8,128)(2,1)S(1)}, bf16[128,512]{1,0:T(8,128)(2,1)S(1)}, u32[]{:S(2)}, u32[]{:S(2)}) %collective-permute-start.9) | collective-permute-done | bytes 131104 | tf_op jit(solution)/shard_map/ppermute | solution.py:502
  99.1 0.9 collective-permute-start.12
  100.1 0.1 dynamic-slice_bitcast_fusion.accum_ref
  100.1 2.0 %collective-permute-done.14.refs_7_ = bf16[128,512]{1,0:T(8,128)(2,1)S(1)} collective-permute-done((bf16[128,512]{1,0:T(8,128)(2,1)S(1)}, bf16[128,512]{1,0:T(8,128)(2,1)S(1)}, u32[]{:S(2)}, u32[]{:S(2)}) %collective-permute-start.14) | collective-permute-done | bytes 131104 | tf_op jit(solution)/shard_map/ppermute | solution.py:502
  102.1 2.0 %collective-permute-done.13.refs_6_ = bf16[128,512]{1,0:T(8,128)(2,1)S(1)} collective-permute-done((bf16[128,512]{1,0:T(8,128)(2,1)S(1)}, bf16[128,512]{1,0:T(8,128)(2,1)S(1)}, u32[]{:S(2)}, u32[]{:S(2)}) %collective-permute-start.13) | collective-permute-done | bytes 131104 | tf_op jit(solution)/shard_map/ppermute | solution.py:502
  104.0 0.3 collective-permute-done.12.refs_5_
  104.4 1.8 %collective-permute-done.7.far_ref = bf16[512,256]{1,0:T(8,128)(2,1)S(1)} collective-permute-done((bf16[512,256]{1,0:T(8,128)(2,1)S(1)}, bf16[512,256]{1,0:T(8,128)(2,1)S(1)}, u32[]{:S(2)}, u32[]{:S(2)}) %collective-permute-start.7) | collective-permute-done | bytes 262176 | tf_op jit(solution)/shard_map/ppermute | solution.py:645
  106.1 0.9 shard_map.134
  107.0 0.1 stack.47.spots_ref
  107.1 2.0 %shard_map.133 = (f32[1024,256]{1,0:T(8,128)}, f32[1024,256]{1,0:T(8,128)}) custom-call(s32[8]{0:T(128)S(1)} %stack.47.spots_ref, bf16[128,512]{1,0:T(8,128)(2,1)S(1)} %add_convert_fusion.2.refs_0_, bf16[128,512]{1,0:T(8,128)(2,1)S(1)} %collective-permute-done.8.refs_1_, bf16[128,512]{1,0:T(8,128)(2,1)S(1)} %collective-permute-done.9.refs_2_, ...), custom_call_target="tpu_custom_call" | custom-call | flops 524288 | bytes 3145728 | tf_op jit(solution)/shard_map/pallas_call | solution.py:375
  109.1 0.8 shard_map.135
  (31 shorter events, 0.2 us)
Async XLA Ops:
  0.6 99.4 %copy-start = (f32[1024]{0:T(1024)S(1)}, f32[1024]{0:T(1024)}, u32[]{:S(2)}) copy-start(f32[1024]{0:T(1024)} %param.10) | copy-start | bytes 12292
  1.7 18.1 %collective-permute-start = (bf16[512,256]{1,0:T(8,128)(2,1)S(1)}, bf16[512,256]{1,0:T(8,128)(2,1)S(1)}, u32[]{:S(2)}, u32[]{:S(2)}) collective-permute-start(bf16[512,256]{1,0:T(8,128)(2,1)S(1)} %get-tuple-element.76.first_ref.rows_ref), channel_id=1, source_target_pairs={{0,16},{2,18},{4,20},{6,22},{8,24},{10,26},{12,28},{14,30},{16,0},... | collective-permute-start | bytes 786440 | tf_op jit(solution)/shard_map/ppermute | solution.py:563
  19.8 2.2 %collective-permute-start.1 = (bf16[512,256]{1,0:T(8,128)(2,1)S(1)}, bf16[512,256]{1,0:T(8,128)(2,1)S(1)}, u32[]{:S(2)}, u32[]{:S(2)}) collective-permute-start(bf16[512,256]{1,0:T(8,128)(2,1)S(1)} %collective-permute-done.first_ref), channel_id=1, source_target_pairs={{1,0},{0,1},{3,2},{2,3},{5,4},{4,5},{7,6},{6,7},{9,8},{8,9},{11,10... | collective-permute-start | bytes 786440 | tf_op jit(solution)/shard_map/ppermute | solution.py:574
  22.0 5.8 %copy-start.4 = (bf16[1024,256]{1,0:T(8,128)(2,1)S(1)}, bf16[1024,256]{1,0:T(8,128)(2,1)}, u32[]{:S(2)}) copy-start(bf16[1024,256]{1,0:T(8,128)(2,1)} %param.11) | copy-start | bytes 1572868
  22.0 6.4 %copy-start.3 = (bf16[1024,256]{1,0:T(8,128)(2,1)S(1)}, bf16[1024,256]{1,0:T(8,128)(2,1)}, u32[]{:S(2)}) copy-start(bf16[1024,256]{1,0:T(8,128)(2,1)} %param.12) | copy-start | bytes 1572868
  22.0 6.5 %copy-start.6 = (bf16[2048]{0:T(1024)(128)(2,1)S(1)}, bf16[2048]{0:T(1024)(128)(2,1)}, u32[]{:S(2)}) copy-start(bf16[2048]{0:T(1024)(128)(2,1)} %param.14) | copy-start | bytes 12292
  22.0 6.5 %copy-start.5 = (s32[16,128]{1,0:T(8,128)S(1)}, s32[16,128]{1,0:T(8,128)}, u32[]{:S(2)}) copy-start(s32[16,128]{1,0:T(8,128)} %param.17) | copy-start | bytes 24580
  24.3 19.0 %all-to-all-start.1 = ((bf16[8,2,128,256]{3,2,1,0:T(8,128)(2,1)}), bf16[8,2,128,256]{3,2,1,0:T(8,128)(2,1)S(1)}, u32[]{:S(2)}, u32[]{:S(2)}) async-start(bf16[8,2,128,256]{3,2,1,0:T(8,128)(2,1)} %shard_map.129), calls=%async_computation.1 | async-start | bytes 2097152 | tf_op jit(solution)/shard_map/all_to_all | solution.py:586
  27.9 2.2 %collective-permute-start.2 = (bf16[1024,256]{1,0:T(8,128)(2,1)S(1)}, bf16[1024,256]{1,0:T(8,128)(2,1)}, u32[]{:S(2)}, u32[]{:S(2)}) collective-permute-start(bf16[1024,256]{1,0:T(8,128)(2,1)S(1)} %copy-done.4), channel_id=1, source_target_pairs={{1,0},{0,1},{3,2},{2,3},{5,4},{4,5},{7,6},{6,7},{9,8},{8,9},{11,10... | collective-permute-start | bytes 1572872 | tf_op jit(solution)/shard_map/ppermute | solution.py:552
  28.4 2.4 %collective-permute-start.3 = (bf16[1024,256]{1,0:T(8,128)(2,1)S(1)}, bf16[1024,256]{1,0:T(8,128)(2,1)}, u32[]{:S(2)}, u32[]{:S(2)}) collective-permute-start(bf16[1024,256]{1,0:T(8,128)(2,1)S(1)} %copy-done.3), channel_id=1, source_target_pairs={{1,0},{0,1},{3,2},{2,3},{5,4},{4,5},{7,6},{6,7},{9,8},{8,9},{11,10... | collective-permute-start | bytes 1572872 | tf_op jit(solution)/shard_map/ppermute | solution.py:552
  32.2 11.1 %copy-start.1 = (f32[2048]{0:T(1024)S(1)}, f32[2048]{0:T(1024)}, u32[]{:S(2)}) copy-start(f32[2048]{0:T(1024)} %param.13) | copy-start | bytes 24580
  32.2 11.1 %copy-start.2 = (f32[128]{0:T(128)S(1)}, f32[128]{0:T(128)}, u32[]{:S(2)}) copy-start(f32[128]{0:T(128)} %param.15) | copy-start | bytes 1540
  46.8 2.7 %collective-permute-start.4 = (bf16[1024,512]{1,0:T(8,128)(2,1)S(1)}, bf16[1024,512]{1,0:T(8,128)(2,1)S(1)}, u32[]{:S(2)}, u32[]{:S(2)}) collective-permute-start(bf16[1024,512]{1,0:T(8,128)(2,1)S(1)} %get-tuple-element.50), channel_id=1, source_target_pairs={{1,0},{0,1},{3,2},{2,3},{5,4},{4,5},{7,6},{6,7},{9,8},{8,9},{11,10... | collective-permute-start | bytes 3145736 | tf_op jit(solution)/shard_map/ppermute | solution.py:604
  81.0 7.6 %collective-permute-start.5 = (bf16[128,512]{1,0:T(8,128)(2,1)S(1)}, bf16[128,512]{1,0:T(8,128)(2,1)S(1)}, u32[]{:S(2)}, u32[]{:S(2)}) collective-permute-start(bf16[128,512]{1,0:T(8,128)(2,1)S(1)} %pad_maximum_fusion.3), channel_id=1, source_target_pairs={{0,16},{2,18},{4,20},{6,22},{8,24},{10,26},{12,28},{14,30},{16,0},... | collective-permute-start | bytes 393224 | tf_op jit(solution)/shard_map/ppermute | solution.py:626
  88.6 2.7 %collective-permute-start.6 = (bf16[512,512]{1,0:T(8,128)(2,1)S(1)}, bf16[512,512]{1,0:T(8,128)(2,1)S(1)}, u32[]{:S(2)}, u32[]{:S(2)}) collective-permute-start(bf16[512,512]{1,0:T(8,128)(2,1)S(1)} %get-tuple-element.54), channel_id=1, source_target_pairs={{1,0},{0,1},{3,2},{2,3},{5,4},{4,5},{7,6},{6,7},{9,8},{8,9},{11,10... | collective-permute-start | bytes 1572872 | tf_op jit(solution)/shard_map/ppermute | solution.py:631
  88.7 6.1 %collective-permute-start.11 = (bf16[128,512]{1,0:T(8,128)(2,1)S(1)}, bf16[128,512]{1,0:T(8,128)(2,1)S(1)}, u32[]{:S(2)}, u32[]{:S(2)}) collective-permute-start(bf16[128,512]{1,0:T(8,128)(2,1)S(1)} %add_convert_fusion.2.refs_0_), channel_id=1, source_target_pairs={{8,0},{10,2},{12,4},{14,6},{0,8},{2,10},{4,12},{6,14},{24,16},{26,... | collective-permute-start | bytes 393224 | tf_op jit(solution)/shard_map/ppermute | solution.py:502
  88.7 8.5 %collective-permute-start.10 = (bf16[128,512]{1,0:T(8,128)(2,1)S(1)}, bf16[128,512]{1,0:T(8,128)(2,1)S(1)}, u32[]{:S(2)}, u32[]{:S(2)}) collective-permute-start(bf16[128,512]{1,0:T(8,128)(2,1)S(1)} %add_convert_fusion.2.refs_0_), channel_id=1, source_target_pairs={{6,0},{4,2},{2,4},{0,6},{14,8},{12,10},{10,12},{8,14},{22,16},{20,... | collective-permute-start | bytes 393224 | tf_op jit(solution)/shard_map/ppermute | solution.py:502
  90.2 8.9 %collective-permute-start.9 = (bf16[128,512]{1,0:T(8,128)(2,1)S(1)}, bf16[128,512]{1,0:T(8,128)(2,1)S(1)}, u32[]{:S(2)}, u32[]{:S(2)}) collective-permute-start(bf16[128,512]{1,0:T(8,128)(2,1)S(1)} %add_convert_fusion.2.refs_0_), channel_id=1, source_target_pairs={{4,0},{6,2},{0,4},{2,6},{12,8},{14,10},{8,12},{10,14},{20,16},{22,... | collective-permute-start | bytes 393224 | tf_op jit(solution)/shard_map/ppermute | solution.py:502
  91.4 14.7 %collective-permute-start.7 = (bf16[512,256]{1,0:T(8,128)(2,1)S(1)}, bf16[512,256]{1,0:T(8,128)(2,1)S(1)}, u32[]{:S(2)}, u32[]{:S(2)}) collective-permute-start(bf16[512,256]{1,0:T(8,128)(2,1)S(1)} %add_convert_fusion.1), channel_id=1, source_target_pairs={{0,16},{2,18},{4,20},{6,22},{8,24},{10,26},{12,28},{14,30},{16,0},... | collective-permute-start | bytes 786440 | tf_op jit(solution)/shard_map/ppermute | solution.py:645
  93.3 6.8 %collective-permute-start.8 = (bf16[128,512]{1,0:T(8,128)(2,1)S(1)}, bf16[128,512]{1,0:T(8,128)(2,1)S(1)}, u32[]{:S(2)}, u32[]{:S(2)}) collective-permute-start(bf16[128,512]{1,0:T(8,128)(2,1)S(1)} %add_convert_fusion.2.refs_0_), channel_id=1, source_target_pairs={{2,0},{0,2},{6,4},{4,6},{10,8},{8,10},{14,12},{12,14},{18,16},{16,... | collective-permute-start | bytes 393224 | tf_op jit(solution)/shard_map/ppermute | solution.py:502
  94.8 7.3 %collective-permute-start.14 = (bf16[128,512]{1,0:T(8,128)(2,1)S(1)}, bf16[128,512]{1,0:T(8,128)(2,1)S(1)}, u32[]{:S(2)}, u32[]{:S(2)}) collective-permute-start(bf16[128,512]{1,0:T(8,128)(2,1)S(1)} %collective-permute-done.11.refs_4_), channel_id=1, source_target_pairs={{6,0},{4,2},{2,4},{0,6},{14,8},{12,10},{10,12},{8,14},{22,16},{20,... | collective-permute-start | bytes 393224 | tf_op jit(solution)/shard_map/ppermute | solution.py:502
  97.2 6.8 %collective-permute-start.13 = (bf16[128,512]{1,0:T(8,128)(2,1)S(1)}, bf16[128,512]{1,0:T(8,128)(2,1)S(1)}, u32[]{:S(2)}, u32[]{:S(2)}) collective-permute-start(bf16[128,512]{1,0:T(8,128)(2,1)S(1)} %collective-permute-done.11.refs_4_), channel_id=1, source_target_pairs={{4,0},{6,2},{0,4},{2,6},{12,8},{14,10},{8,12},{10,14},{20,16},{22,... | collective-permute-start | bytes 393224 | tf_op jit(solution)/shard_map/ppermute | solution.py:502
  99.1 5.2 %collective-permute-start.12 = (bf16[128,512]{1,0:T(8,128)(2,1)S(1)}, bf16[128,512]{1,0:T(8,128)(2,1)S(1)}, u32[]{:S(2)}, u32[]{:S(2)}) collective-permute-start(bf16[128,512]{1,0:T(8,128)(2,1)S(1)} %collective-permute-done.11.refs_4_), channel_id=1, source_target_pairs={{2,0},{0,2},{6,4},{4,6},{10,8},{8,10},{14,12},{12,14},{18,16},{16,... | collective-permute-start | bytes 393224 | tf_op jit(solution)/shard_map/ppermute | solution.py:502
  107.0 2.1 %collective-permute-start.15 = (bf16[512,256]{1,0:T(8,128)(2,1)S(1)}, bf16[512,256]{1,0:T(8,128)(2,1)S(1)}, u32[]{:S(2)}, u32[]{:S(2)}) collective-permute-start(bf16[512,256]{1,0:T(8,128)(2,1)S(1)} %get-tuple-element.67.mine_ref), channel_id=1, source_target_pairs={{1,0},{0,1},{3,2},{2,3},{5,4},{4,5},{7,6},{6,7},{9,8},{8,9},{11,10... | collective-permute-start | bytes 786440 | tf_op jit(solution)/shard_map/ppermute | solution.py:652

commit v13 on v12

--- a/solution.py
+++ b/solution.py
@@ -610,28 +610,27 @@
     share_terms = narrow_sum.reshape(*groups, -1, narrow_sum.shape[1])
     order = list(range(len(groups)))[::-1] + [len(groups), len(groups) + 1]
     share_terms = share_terms.transpose(order).reshape(near_count, -1, narrow_sum.shape[1])
-    rank = factor_down.shape[1]
-    outgoing = [slot_grads.reshape(near_count, 2 * pools_per, emb_width)]
-    outgoing += [share_terms[:, :, :rank], share_terms[:, :, rank:]]
-    returned = lax.all_to_all(
-        jnp.concatenate(outgoing, axis=1),
-        "table",
-        split_axis=0,
-        concat_axis=0,
-        tiled=True,
-        axis_index_groups=halves,
-    )
-    terms = jnp.sum(returned[:, 2 * pools_per :].astype(jnp.float32), axis=0)
-    half_sum = jnp.concatenate(jnp.split(terms, 2, axis=0), axis=1).astype(jnp.bfloat16)
-    other_sum = lax.ppermute(half_sum, "table", across)
+
+    def within_half(blocks):
+        return lax.all_to_all(
+            blocks, "table", split_axis=0, concat_axis=0, tiled=True, axis_index_groups=halves
+        )
+
+    returned = within_half(slot_grads.reshape(near_count, 2 * pools_per, emb_width))
+    returned, share_terms = lax.optimization_barrier((returned, share_terms))
+    terms = within_half(share_terms)
     mine, passed = row_grads(swap, asked, returned, pools_per, row_dev)
-    other_sum, mine, passed = lax.optimization_barrier((other_sum, mine, passed))
-    table_sum = summed([half_sum, other_sum])
     if paired:
         nears = [mine, lax.ppermute(passed, "narrow", sent_from("narrow", 1, 2, 1))]
     else:
         nears = [scatter_sum(jnp.concatenate([mine, passed], axis=0), "narrow", narrow_levels)]
     far_term = summed([term[:, emb_width:] for term in nears])
+    far_term = lax.ppermute(far_term, "table", across)
+    terms, mine = lax.optimization_barrier((terms, mine))
+    half_sum = jnp.sum(terms.astype(jnp.float32), axis=0).astype(jnp.bfloat16)
+    other_sum = lax.ppermute(half_sum, "table", across)
+    other_sum, far_term = lax.optimization_barrier((other_sum, far_term))
+    table_sum = summed([half_sum, other_sum])
     inner = gather_blocks(table_sum, "table", half_levels[2:])
     blocks, fan = [(0, inner)], 1
     if len(half_levels) > 1:
@@ -642,10 +641,6 @@
         pieces = [(spot * fan + place, piece) for spot, piece in pieces]
         early += pieces if i == 0 else pieces[:1]
         late += [] if i == 0 else pieces[1:]
-    far_term = lax.ppermute(far_term, "table", across)
-    spots, came = zip(*early, *late)
-    far_term, *came = lax.optimization_barrier((far_term, *came))
-    pieces = list(zip(spots, came))
     own_accum = lax.dynamic_slice_in_dim(accum, narrow_index * share_rows, share_rows, 0)
     new_share, new_accum = update_rows(own_share, far_term, own_accum, nears)
     if paired:
@@ -654,7 +649,15 @@
     else:
         new_rows = gather_blocks(new_share, "narrow", narrow_levels)
     scale = 1.0 / math.sqrt(samples * tables * narrows)
-    down_grad, up_grad = spread_pieces(pieces, scale, factor_down.shape[0])
+    down_grad, up_grad = spread_pieces(early, scale, factor_down.shape[0])
+    if late:
+        spots, last = zip(*late)
+        new_rows, down_grad, up_grad, *last = lax.optimization_barrier(
+            (new_rows, down_grad, up_grad, *last)
+        )
+        down_grad, up_grad = spread_pieces(
+            list(zip(spots, last)), scale, factor_down.shape[0], (down_grad, up_grad)
+        )
     return (logits, down_grad, up_grad, new_rows, new_accum)
 
 

time: 111 us -> 121 us (1.090)
  blocking collectives: 43.8 us -> 13.9 us
  waiting for transfers between devices: 25.4 us -> 54.3 us
  starting transfers between devices: 18.8 us -> 24.5 us
  Pallas kernels: 16.5 us -> 18.7 us
  other arithmetic: 2.22 us -> 4.39 us
  local copies, waits for them, and re-layouts: 2.24 us -> 3.61 us
    all_to_all x1 -> x0, blocking collectives: 30.6 us -> none  [local(): lax.all_to_all(jnp.concatenate(outgoing, axis=1), 'table', split_axis=0,...]
    all_to_all x0 -> x2, waiting for transfers between devices: none -> 22.8 us  [within_half(): lax.all_to_all(blocks, 'table', split_axis=0, concat_axis=0, tiled=True,...]
    all_to_all x0 -> x2, starting transfers between devices: none -> 8.75 us  [within_half(): lax.all_to_all(blocks, 'table', split_axis=0, concat_axis=0, tiled=True,...]
    ppermute x1, waiting for transfers between devices: 3.44 us -> 6.77 us  [local(): other_sum = lax.ppermute(half_sum, 'table', across)]
    ppermute x1, waiting for transfers between devices: 0.01 us -> 1.9 us  [local(): nears = [mine, lax.ppermute(passed, 'narrow', sent_from('narrow', 1, 2, 1))]]
    ppermute x7, waiting for transfers between devices: 6.1 us -> 7.96 us  [gathered_pieces(): came = lax.ppermute(block, axis, sent_from(axis, stride, group, step))]
    ppermute x1, waiting for transfers between devices: 0.85 us -> 2.65 us  [local(): came = lax.ppermute(sent, 'narrow', sent_from('narrow', 1, 2, 1))]
    ppermute x1, waiting for transfers between devices: 1.79 us -> 0.05 us  [local(): far_term = lax.ppermute(far_term, 'table', across)]
  transfers between devices with their start and end apart: 17 -> 19, of which waited for: 10 -> 12; matrix products, arithmetic and copies ran while one was open for 2% -> 5% of each run, Pallas kernels for 8% -> 7%
where the time goes in v13:
time: 121 us
  waiting for transfers between devices  54.3 us (45%)
  starting transfers between devices  24.5 us (20%)
  Pallas kernels  18.7 us (15%)
  blocking collectives  13.9 us (11%)
  other arithmetic  4.39 us (4%)
  local copies, waits for them, and re-layouts  3.61 us (3%)
    all_to_all x2, waiting for transfers between devices, within_half(): lax.all_to_all(blocks, 'table', split_axis=0, concat_axis=0, tiled=True,...  22.8 us
    all_to_all x1, blocking collectives, local(): lax.all_to_all(asked, 'table', split_axis=0, concat_axis=0, tiled=True, a...  13.9 us
    all_to_all x1, waiting for transfers between devices, local(): lax.all_to_all(sums, 'table', split_axis=0, concat_axis=0, tiled=True, ax...  9.91 us
    all_to_all x2, starting transfers between devices, within_half(): lax.all_to_all(blocks, 'table', split_axis=0, concat_axis=0, tiled=True,...  8.75 us
    ppermute x7, waiting for transfers between devices, gathered_pieces(): came = lax.ppermute(block, axis, sent_from(axis, stride, group, step))  7.96 us
    ppermute x1, waiting for transfers between devices, local(): other_sum = lax.ppermute(half_sum, 'table', across)  6.77 us
    ppermute x7, starting transfers between devices, gathered_pieces(): came = lax.ppermute(block, axis, sent_from(axis, stride, group, step))  6.08 us
    pallas_call x2, Pallas kernels, pool_lookups(): kernel_call(functools.partial(pool_kernel, part), jax.ShapeDtypeStruct((s...  4.39 us
  transfers between devices with their start and end apart: 19, of which 12 were waited for; matrix products, arithmetic and copies ran while one was open for 5% of the time, Pallas kernels for 7%

profile of v13, /device:TPU:0, one launch (start us, length us, event | category | flops | bytes accessed | tf_op | source)
XLA Modules:
  0.0 120.6 jit_solution(9129194780339146743)
XLA Ops:
  0.7 1.1 constant_dynamic-slice_fusion.2
  1.7 4.1 %collective-permute-start = (bf16[512,256]{1,0:T(8,128)(2,1)S(1)}, bf16[512,256]{1,0:T(8,128)(2,1)S(1)}, u32[]{:S(2)}, u32[]{:S(2)}) collective-permute-start(bf16[512,256]{1,0:T(8,128)(2,1)S(1)} %get-tuple-element.76.first_ref.rows_ref), channel_id=1, source_target_pairs={{0,16},{2,18},{4,20},{6,22},{8,24},{10,26},{12,28},{14,30},{16,0},... | collective-permute-start | bytes 786440 | tf_op jit(solution)/shard_map/ppermute | solution.py:563
  5.9 13.9 %all_to_all.20.ids_ref = s32[8,1,1024]{2,1,0:T(1,128)S(1)} all-to-all(s32[8,1,1024]{2,1,0:T(1,128)S(1)} %broadcast_in_dim.3), channel_id=1, replica_groups={{0,2,4,6,8,10,12,14},{16,18,20,22,24,26,28,30},{1,3,5,7,9,11,13,15},{17..., dimensions={0} | all-to-all | bytes 65536 | tf_op jit(solution)/shard_map/all_to_all | solution.py:569
  19.8 2.2 %shard_map.128.refs_0_ = bf16[8,2,128,256]{3,2,1,0:T(8,128)(2,1)} custom-call(s32[1]{0:T(128)} %bitcast.swap_ref, s32[8,1,1024]{2,1,0:T(1,128)S(1)} %all_to_all.20.ids_ref, bf16[512,256]{1,0:T(8,128)(2,1)S(1)} %get-tuple-element.76.first_ref.rows_ref, bf16[512,256]{1,0:T(8,128)(2,1)S(1)} %get-tuple-element.75.second_ref), custom_call_target="tpu_custom_call" | custom-call | flops 536870912 | bytes 1048576 | tf_op jit(solution)/shard_map/pallas_call | solution.py:125
  22.0 2.2 %shard_map.129 = bf16[8,2,128,256]{3,2,1,0:T(8,128)(2,1)} custom-call(s32[1]{0:T(128)} %bitcast.swap_ref, s32[8,1,1024]{2,1,0:T(1,128)S(1)} %all_to_all.20.ids_ref, bf16[512,256]{1,0:T(8,128)(2,1)S(1)} %collective-permute-done.first_ref, bf16[512,256]{1,0:T(8,128)(2,1)S(1)} %collective-permute-done.1.second_ref, ...), custom_call_target="tpu_custom_call", output_to_operand_aliasing={{}: (4, {})} | custom-call | flops 536870912 | bytes 1048576 | tf_op jit(solution)/shard_map/pallas_call | solution.py:125
  24.3 3.7 %all-to-all-start.1 = ((bf16[8,2,128,256]{3,2,1,0:T(8,128)(2,1)}), bf16[8,2,128,256]{3,2,1,0:T(8,128)(2,1)S(1)}, u32[]{:S(2)}, u32[]{:S(2)}) async-start(bf16[8,2,128,256]{3,2,1,0:T(8,128)(2,1)} %shard_map.129), calls=%async_computation.1 | async-start | bytes 2097152 | tf_op jit(solution)/shard_map/all_to_all | solution.py:586
  28.0 0.6 collective-permute-start.2
  28.6 0.1 collective-permute-start.3
  28.7 1.5 %collective-permute-done.2 = bf16[1024,256]{1,0:T(8,128)(2,1)} collective-permute-done((bf16[1024,256]{1,0:T(8,128)(2,1)S(1)}, bf16[1024,256]{1,0:T(8,128)(2,1)}, u32[]{:S(2)}, u32[]{:S(2)}) %collective-permute-start.2) | collective-permute-done | bytes 524320 | tf_op jit(solution)/shard_map/ppermute | solution.py:552
  30.2 0.7 collective-permute-done.3
  31.0 1.4 %broadcast_select_fusion.1 = (bf16[1024,256]{1,0:T(8,128)(2,1)S(1)}, bf16[1024,256]{1,0:T(8,128)(2,1)S(1)}, bf16[1024,256]{1,0:T(8,128)(2,1)S(1)}, bf16[1024,256]{1,0:T(8,128)(2,1)S(1)}) fusion(bf16[1024,256]{1,0:T(8,128)(2,1)S(1)} %copy-done.6, bf16[1024,256]{1,0:T(8,128)(2,1)} %collective-permute-done.3, pred[]{:T(512)S(6)} %eq.24, ...), kind=kLoop, calls=%fused_computation.5 | loop fusion | flops 1048576 | bytes 4194305 | tf_op jit(solution)/shard_map/jit(_where)/select_n | solution.py:553
  32.5 1.0 pad_maximum_fusion.1.up_ref
  33.5 9.9 %all-to-all-done.1 = bf16[8,2,128,256]{3,2,1,0:T(8,128)(2,1)S(1)} async-done(((bf16[8,2,128,256]{3,2,1,0:T(8,128)(2,1)}), bf16[8,2,128,256]{3,2,1,0:T(8,128)(2,1)S(1)}, u32[]{:S(2)}, u32[]{:S(2)}) %all-to-all-start.1) | async-done | bytes 1048608 | tf_op jit(solution)/shard_map/all_to_all | solution.py:586
  43.5 1.2 %copy-done.1 = bf16[2048,256]{1,0:T(8,128)(2,1)S(1)} copy-done((bf16[2048,256]{1,0:T(8,128)(2,1)S(1)}, bf16[2048,256]{1,0:T(8,128)(2,1)}, u32[]{:S(2)}) %copy-start.1) | copy-done | bytes 1048600
  44.7 3.5 %shard_map.130 = (f32[1,128]{1,0:T(1,128)}, f32[128,2048]{1,0:T(8,128)S(1)}, bf16[128,256]{1,0:T(8,128)(2,1)S(1)}, bf16[1024,512]{1,0:T(8,128)(2,1)S(1)}, bf16[1024,512]{1,0:T(8,128)(2,1)S(1)}) custom-call(s32[1]{0:T(128)} %bitcast.swap_ref, s32[1,2048]{1,0:T(1,128)S(1)} %bitcast.26, f32[1,2048]{1,0:T(1,128)S(1)} %bitcast.28, ...), custom_call_target="tpu_custom_call" | custom-call | flops 1879048192 | bytes 5242880 | tf_op jit(solution)/shard_map/pallas_call | solution.py:315
  48.2 2.8 %shard_map.131 = bf16[2048,256]{1,0:T(8,128)(2,1)} custom-call(s32[16,128]{1,0:T(8,128)S(1)} %bitcast.27, f32[128,2048]{1,0:T(8,128)S(1)} %get-tuple-element.48.direct_ref, bf16[128,256]{1,0:T(8,128)(2,1)S(1)} %get-tuple-element.49.dhidden_ref, bf16[2048,256]{1,0:T(8,128)(2,1)S(1)} %pad_maximum_fusion.down_ref), custom_call_target="tpu_custom_call" | custom-call | flops 1073741824 | bytes 2097152 | tf_op jit(solution)/shard_map/pallas_call | solution.py:233
  51.0 4.3 %all-to-all-start.2 = ((bf16[8,256,256]{2,1,0:T(8,128)(2,1)}), bf16[8,256,256]{2,1,0:T(8,128)(2,1)S(1)}, u32[]{:S(2)}, u32[]{:S(2)}) async-start(bf16[8,256,256]{2,1,0:T(8,128)(2,1)} %bitcast.12), calls=%async_computation.2 | async-start | bytes 2097152 | tf_op jit(solution)/shard_map/all_to_all | solution.py:615
  55.4 0.1 collective-permute-start.4
  55.4 2.6 %collective-permute-done.4 = bf16[1024,512]{1,0:T(8,128)(2,1)S(1)} collective-permute-done((bf16[1024,512]{1,0:T(8,128)(2,1)S(1)}, bf16[1024,512]{1,0:T(8,128)(2,1)S(1)}, u32[]{:S(2)}, u32[]{:S(2)}) %collective-permute-start.4) | collective-permute-done | bytes 1048608 | tf_op jit(solution)/shard_map/ppermute | solution.py:604
  58.1 0.3 add_convert_fusion
  58.4 1.0 copy.17
  59.4 10.5 %all-to-all-done.2.grads_ref = bf16[8,256,256]{2,1,0:T(8,128)(2,1)S(1)} async-done(((bf16[8,256,256]{2,1,0:T(8,128)(2,1)}), bf16[8,256,256]{2,1,0:T(8,128)(2,1)S(1)}, u32[]{:S(2)}, u32[]{:S(2)}) %all-to-all-start.2) | async-done | bytes 1048608 | tf_op jit(solution)/shard_map/all_to_all | solution.py:615
  69.9 4.4 %all-to-all-start.3 = ((bf16[8,128,512]{2,1,0:T(8,128)(2,1)}), bf16[8,128,512]{2,1,0:T(8,128)(2,1)}, u32[]{:S(2)}, u32[]{:S(2)}) async-start(bf16[8,128,512]{2,1,0:T(8,128)(2,1)} %bitcast.15), calls=%async_computation.3 | async-start | bytes 2097152 | tf_op jit(solution)/shard_map/all_to_all | solution.py:615
  74.3 3.2 %shard_map.132 = (bf16[512,512]{1,0:T(8,128)(2,1)S(1)}, bf16[512,512]{1,0:T(8,128)(2,1)S(1)}) custom-call(s32[1]{0:T(128)} %bitcast.swap_ref, s32[8,1,1024]{2,1,0:T(1,128)S(1)} %all_to_all.20.ids_ref, bf16[8,256,256]{2,1,0:T(8,128)(2,1)S(1)} %all-to-all-done.2.grads_ref), custom_call_target="tpu_custom_call" | custom-call | flops 1073741824 | bytes 2097152 | tf_op jit(solution)/shard_map/pallas_call | solution.py:179
  77.5 0.1 collective-permute-start.6
  77.6 1.9 %collective-permute-done.6.refs_1_ = bf16[512,512]{1,0:T(8,128)(2,1)S(1)} collective-permute-done((bf16[512,512]{1,0:T(8,128)(2,1)S(1)}, bf16[512,512]{1,0:T(8,128)(2,1)S(1)}, u32[]{:S(2)}, u32[]{:S(2)}) %collective-permute-start.6) | collective-permute-done | bytes 524320 | tf_op jit(solution)/shard_map/ppermute | solution.py:624
  79.5 0.1 add_convert_fusion.1
  79.6 1.0 collective-permute-start.7
  80.6 12.3 %all-to-all-done.3 = bf16[8,128,512]{2,1,0:T(8,128)(2,1)} async-done(((bf16[8,128,512]{2,1,0:T(8,128)(2,1)}), bf16[8,128,512]{2,1,0:T(8,128)(2,1)}, u32[]{:S(2)}, u32[]{:S(2)}) %all-to-all-start.3) | async-done | bytes 1048608 | tf_op jit(solution)/shard_map/all_to_all | solution.py:615
  92.9 1.4 %reduce_sum.12 = bf16[128,512]{1,0:T(8,128)(2,1)S(1)} reduce(bf16[8,128,512]{2,1,0:T(8,128)(2,1)} %all-to-all-done.3, bf16[]{:T(256)} %constant.160.clone.1), dimensions={0}, to_apply=%region_0.1 | reduce | flops 458752 | bytes 1179650 | tf_op jit(solution)/shard_map/reduce_sum | solution.py:630
  94.3 0.1 collective-permute-start.5
  94.4 0.1 dynamic-slice_bitcast_fusion.accum_ref
  94.5 6.8 %collective-permute-done.5 = bf16[128,512]{1,0:T(8,128)(2,1)S(1)} collective-permute-done((bf16[128,512]{1,0:T(8,128)(2,1)S(1)}, bf16[128,512]{1,0:T(8,128)(2,1)S(1)}, u32[]{:S(2)}, u32[]{:S(2)}) %collective-permute-start.5) | collective-permute-done | bytes 131104 | tf_op jit(solution)/shard_map/ppermute | solution.py:631
  101.4 0.9 shard_map.133
  102.3 0.6 collective-permute-start.10
  102.9 1.5 %collective-permute-start.11 = (bf16[128,512]{1,0:T(8,128)(2,1)S(1)}, bf16[128,512]{1,0:T(8,128)(2,1)S(1)}, u32[]{:S(2)}, u32[]{:S(2)}) collective-permute-start(bf16[128,512]{1,0:T(8,128)(2,1)S(1)} %add_convert_fusion.2.refs_0_), channel_id=1, source_target_pairs={{6,0},{4,2},{2,4},{0,6},{14,8},{12,10},{10,12},{8,14},{22,16},{20,... | collective-permute-start | bytes 393224 | tf_op jit(solution)/shard_map/ppermute | solution.py:502
  104.3 1.5 %collective-permute-start.9 = (bf16[128,512]{1,0:T(8,128)(2,1)S(1)}, bf16[128,512]{1,0:T(8,128)(2,1)S(1)}, u32[]{:S(2)}, u32[]{:S(2)}) collective-permute-start(bf16[128,512]{1,0:T(8,128)(2,1)S(1)} %add_convert_fusion.2.refs_0_), channel_id=1, source_target_pairs={{2,0},{0,2},{6,4},{4,6},{10,8},{8,10},{14,12},{12,14},{18,16},{16,... | collective-permute-start | bytes 393224 | tf_op jit(solution)/shard_map/ppermute | solution.py:502
  105.8 0.6 collective-permute-done.12.refs_4_
  106.4 0.6 collective-permute-start.13
  106.9 4.1 %collective-permute-done.10.refs_2_ = bf16[128,512]{1,0:T(8,128)(2,1)S(1)} collective-permute-done((bf16[128,512]{1,0:T(8,128)(2,1)S(1)}, bf16[128,512]{1,0:T(8,128)(2,1)S(1)}, u32[]{:S(2)}, u32[]{:S(2)}) %collective-permute-start.10) | collective-permute-done | bytes 131104 | tf_op jit(solution)/shard_map/ppermute | solution.py:502
  111.0 0.5 collective-permute-start.14
  111.5 1.4 %collective-permute-start.15 = (bf16[128,512]{1,0:T(8,128)(2,1)S(1)}, bf16[128,512]{1,0:T(8,128)(2,1)S(1)}, u32[]{:S(2)}, u32[]{:S(2)}) collective-permute-start(bf16[128,512]{1,0:T(8,128)(2,1)S(1)} %collective-permute-done.12.refs_4_), channel_id=1, source_target_pairs={{6,0},{4,2},{2,4},{0,6},{14,8},{12,10},{10,12},{8,14},{22,16},{20,... | collective-permute-start | bytes 393224 | tf_op jit(solution)/shard_map/ppermute | solution.py:502
  113.0 0.1 stack.51.spots_ref
  113.1 0.1 pad_add_fusion.2.spots_ref
  113.2 1.7 %shard_map.135 = (f32[1024,256]{1,0:T(8,128)}, f32[1024,256]{1,0:T(8,128)}) custom-call(s32[5]{0:T(128)S(1)} %stack.51.spots_ref, bf16[128,512]{1,0:T(8,128)(2,1)S(1)} %add_convert_fusion.2.refs_0_, bf16[128,512]{1,0:T(8,128)(2,1)S(1)} %collective-permute-done.9.refs_1_, bf16[128,512]{1,0:T(8,128)(2,1)S(1)} %collective-permute-done.10.refs_2_, ...), custom_call_target="tpu_custom_call" | custom-call | flops 327680 | bytes 1966080 | tf_op jit(solution)/shard_map/pallas_call | solution.py:375
  114.9 0.8 shard_map.134
  115.7 3.3 %collective-permute-done.14.refs_1_ = bf16[128,512]{1,0:T(8,128)(2,1)S(1)} collective-permute-done((bf16[128,512]{1,0:T(8,128)(2,1)S(1)}, bf16[128,512]{1,0:T(8,128)(2,1)S(1)}, u32[]{:S(2)}, u32[]{:S(2)}) %collective-permute-start.14) | collective-permute-done | bytes 131104 | tf_op jit(solution)/shard_map/ppermute | solution.py:502
  119.0 1.5 %shard_map.136 = (f32[1024,256]{1,0:T(8,128)}, f32[1024,256]{1,0:T(8,128)}) custom-call(s32[3]{0:T(128)S(1)} %pad_add_fusion.2.spots_ref, bf16[128,512]{1,0:T(8,128)(2,1)S(1)} %collective-permute-done.13.refs_0_, bf16[128,512]{1,0:T(8,128)(2,1)S(1)} %collective-permute-done.14.refs_1_, ...), custom_call_target="tpu_custom_call", output_to_operand_aliasing={{0}: (4, {}), {1}: (5, {})} | custom-call | flops 196608 | bytes 1179648 | tf_op jit(solution)/shard_map/pallas_call | solution.py:375
  (40 shorter events, 0.4 us)
Async XLA Ops:
  0.6 93.8 %copy-start = (f32[1024]{0:T(1024)S(1)}, f32[1024]{0:T(1024)}, u32[]{:S(2)}) copy-start(f32[1024]{0:T(1024)} %param.10) | copy-start | bytes 12292
  0.6 5.2 %copy-start.8 = (s32[16,512]{1,0:T(8,128)S(1)}, s32[16,512]{1,0:T(8,128)}, u32[]{:S(2)}) copy-start(s32[16,512]{1,0:T(8,128)} %param.16) | copy-start | bytes 98308
  1.7 18.1 %collective-permute-start = (bf16[512,256]{1,0:T(8,128)(2,1)S(1)}, bf16[512,256]{1,0:T(8,128)(2,1)S(1)}, u32[]{:S(2)}, u32[]{:S(2)}) collective-permute-start(bf16[512,256]{1,0:T(8,128)(2,1)S(1)} %get-tuple-element.76.first_ref.rows_ref), channel_id=1, source_target_pairs={{0,16},{2,18},{4,20},{6,22},{8,24},{10,26},{12,28},{14,30},{16,0},... | collective-permute-start | bytes 786440 | tf_op jit(solution)/shard_map/ppermute | solution.py:563
  19.8 2.2 %collective-permute-start.1 = (bf16[512,256]{1,0:T(8,128)(2,1)S(1)}, bf16[512,256]{1,0:T(8,128)(2,1)S(1)}, u32[]{:S(2)}, u32[]{:S(2)}) collective-permute-start(bf16[512,256]{1,0:T(8,128)(2,1)S(1)} %collective-permute-done.first_ref), channel_id=1, source_target_pairs={{1,0},{0,1},{3,2},{2,3},{5,4},{4,5},{7,6},{6,7},{9,8},{8,9},{11,10... | collective-permute-start | bytes 786440 | tf_op jit(solution)/shard_map/ppermute | solution.py:574
  24.2 3.8 %copy-start.7 = (bf16[1024,256]{1,0:T(8,128)(2,1)S(1)}, bf16[1024,256]{1,0:T(8,128)(2,1)}, u32[]{:S(2)}) copy-start(bf16[1024,256]{1,0:T(8,128)(2,1)} %param.11) | copy-start | bytes 1572868
  24.3 4.3 %copy-start.6 = (bf16[1024,256]{1,0:T(8,128)(2,1)S(1)}, bf16[1024,256]{1,0:T(8,128)(2,1)}, u32[]{:S(2)}) copy-start(bf16[1024,256]{1,0:T(8,128)(2,1)} %param.12) | copy-start | bytes 1572868
  24.3 4.4 %copy-start.10 = (bf16[2048]{0:T(1024)(128)(2,1)S(1)}, bf16[2048]{0:T(1024)(128)(2,1)}, u32[]{:S(2)}) copy-start(bf16[2048]{0:T(1024)(128)(2,1)} %param.14) | copy-start | bytes 12292
  24.3 4.4 %copy-start.9 = (s32[16,128]{1,0:T(8,128)S(1)}, s32[16,128]{1,0:T(8,128)}, u32[]{:S(2)}) copy-start(s32[16,128]{1,0:T(8,128)} %param.17) | copy-start | bytes 24580
  24.3 19.2 %all-to-all-start.1 = ((bf16[8,2,128,256]{3,2,1,0:T(8,128)(2,1)}), bf16[8,2,128,256]{3,2,1,0:T(8,128)(2,1)S(1)}, u32[]{:S(2)}, u32[]{:S(2)}) async-start(bf16[8,2,128,256]{3,2,1,0:T(8,128)(2,1)} %shard_map.129), calls=%async_computation.1 | async-start | bytes 2097152 | tf_op jit(solution)/shard_map/all_to_all | solution.py:586
  28.0 2.2 %collective-permute-start.2 = (bf16[1024,256]{1,0:T(8,128)(2,1)S(1)}, bf16[1024,256]{1,0:T(8,128)(2,1)}, u32[]{:S(2)}, u32[]{:S(2)}) collective-permute-start(bf16[1024,256]{1,0:T(8,128)(2,1)S(1)} %copy-done.7), channel_id=1, source_target_pairs={{1,0},{0,1},{3,2},{2,3},{5,4},{4,5},{7,6},{6,7},{9,8},{8,9},{11,10... | collective-permute-start | bytes 1572872 | tf_op jit(solution)/shard_map/ppermute | solution.py:552
  28.6 2.4 %collective-permute-start.3 = (bf16[1024,256]{1,0:T(8,128)(2,1)S(1)}, bf16[1024,256]{1,0:T(8,128)(2,1)}, u32[]{:S(2)}, u32[]{:S(2)}) collective-permute-start(bf16[1024,256]{1,0:T(8,128)(2,1)S(1)} %copy-done.6), channel_id=1, source_target_pairs={{1,0},{0,1},{3,2},{2,3},{5,4},{4,5},{7,6},{6,7},{9,8},{8,9},{11,10... | collective-permute-start | bytes 1572872 | tf_op jit(solution)/shard_map/ppermute | solution.py:552
  32.5 11.0 %copy-start.4 = (f32[2048]{0:T(1024)S(1)}, f32[2048]{0:T(1024)}, u32[]{:S(2)}) copy-start(f32[2048]{0:T(1024)} %param.13) | copy-start | bytes 24580
  32.5 11.0 %copy-start.5 = (f32[128]{0:T(128)S(1)}, f32[128]{0:T(128)}, u32[]{:S(2)}) copy-start(f32[128]{0:T(128)} %param.15) | copy-start | bytes 1540
  43.5 1.2 %copy-start.1 = (bf16[2048,256]{1,0:T(8,128)(2,1)S(1)}, bf16[2048,256]{1,0:T(8,128)(2,1)}, u32[]{:S(2)}) copy-start(bf16[2048,256]{1,0:T(8,128)(2,1)} %pad_maximum_fusion.1.up_ref) | copy-start | bytes 3145732
  48.2 2.8 %copy-start.2 = (bf16[1024,512]{1,0:T(8,128)(2,1)}, bf16[1024,512]{1,0:T(8,128)(2,1)S(1)}, u32[]{:S(2)}) copy-start(bf16[1024,512]{1,0:T(8,128)(2,1)S(1)} %get-tuple-element.51) | copy-start | bytes 3145732
  51.0 4.3 %copy-start.3 = (bf16[1024,512]{1,0:T(8,128)(2,1)S(1)}, bf16[1024,512]{1,0:T(8,128)(2,1)}, u32[]{:S(2)}) copy-start(bf16[1024,512]{1,0:T(8,128)(2,1)} %copy-done.2) | copy-start | bytes 3145732
  51.0 18.9 %all-to-all-start.2 = ((bf16[8,256,256]{2,1,0:T(8,128)(2,1)}), bf16[8,256,256]{2,1,0:T(8,128)(2,1)S(1)}, u32[]{:S(2)}, u32[]{:S(2)}) async-start(bf16[8,256,256]{2,1,0:T(8,128)(2,1)} %bitcast.12), calls=%async_computation.2 | async-start | bytes 2097152 | tf_op jit(solution)/shard_map/all_to_all | solution.py:615
  55.4 2.7 %collective-permute-start.4 = (bf16[1024,512]{1,0:T(8,128)(2,1)S(1)}, bf16[1024,512]{1,0:T(8,128)(2,1)S(1)}, u32[]{:S(2)}, u32[]{:S(2)}) collective-permute-start(bf16[1024,512]{1,0:T(8,128)(2,1)S(1)} %copy-done.3), channel_id=1, source_target_pairs={{1,0},{0,1},{3,2},{2,3},{5,4},{4,5},{7,6},{6,7},{9,8},{8,9},{11,10... | collective-permute-start | bytes 3145736 | tf_op jit(solution)/shard_map/ppermute | solution.py:604
  69.9 23.0 %all-to-all-start.3 = ((bf16[8,128,512]{2,1,0:T(8,128)(2,1)}), bf16[8,128,512]{2,1,0:T(8,128)(2,1)}, u32[]{:S(2)}, u32[]{:S(2)}) async-start(bf16[8,128,512]{2,1,0:T(8,128)(2,1)} %bitcast.15), calls=%async_computation.3 | async-start | bytes 2097152 | tf_op jit(solution)/shard_map/all_to_all | solution.py:615
  77.5 2.0 %collective-permute-start.6 = (bf16[512,512]{1,0:T(8,128)(2,1)S(1)}, bf16[512,512]{1,0:T(8,128)(2,1)S(1)}, u32[]{:S(2)}, u32[]{:S(2)}) collective-permute-start(bf16[512,512]{1,0:T(8,128)(2,1)S(1)} %get-tuple-element.56), channel_id=1, source_target_pairs={{1,0},{0,1},{3,2},{2,3},{5,4},{4,5},{7,6},{6,7},{9,8},{8,9},{11,10... | collective-permute-start | bytes 1572872 | tf_op jit(solution)/shard_map/ppermute | solution.py:624
  79.6 15.0 %collective-permute-start.7 = (bf16[512,256]{1,0:T(8,128)(2,1)S(1)}, bf16[512,256]{1,0:T(8,128)(2,1)S(1)}, u32[]{:S(2)}, u32[]{:S(2)}) collective-permute-start(bf16[512,256]{1,0:T(8,128)(2,1)S(1)} %add_convert_fusion.1), channel_id=1, source_target_pairs={{0,16},{2,18},{4,20},{6,22},{8,24},{10,26},{12,28},{14,30},{16,0},... | collective-permute-start | bytes 786440 | tf_op jit(solution)/shard_map/ppermute | solution.py:628
  94.3 7.0 %collective-permute-start.5 = (bf16[128,512]{1,0:T(8,128)(2,1)S(1)}, bf16[128,512]{1,0:T(8,128)(2,1)S(1)}, u32[]{:S(2)}, u32[]{:S(2)}) collective-permute-start(bf16[128,512]{1,0:T(8,128)(2,1)S(1)} %reduce_sum.12), channel_id=1, source_target_pairs={{0,16},{2,18},{4,20},{6,22},{8,24},{10,26},{12,28},{14,30},{16,0},... | collective-permute-start | bytes 393224 | tf_op jit(solution)/shard_map/ppermute | solution.py:631
  101.4 5.0 %collective-permute-start.12 = (bf16[128,512]{1,0:T(8,128)(2,1)S(1)}, bf16[128,512]{1,0:T(8,128)(2,1)S(1)}, u32[]{:S(2)}, u32[]{:S(2)}) collective-permute-start(bf16[128,512]{1,0:T(8,128)(2,1)S(1)} %add_convert_fusion.2.refs_0_), channel_id=1, source_target_pairs={{8,0},{10,2},{12,4},{14,6},{0,8},{2,10},{4,12},{6,14},{24,16},{26,... | collective-permute-start | bytes 393224 | tf_op jit(solution)/shard_map/ppermute | solution.py:502
  102.3 12.6 %collective-permute-start.8 = (bf16[512,256]{1,0:T(8,128)(2,1)S(1)}, bf16[512,256]{1,0:T(8,128)(2,1)S(1)}, u32[]{:S(2)}, u32[]{:S(2)}) collective-permute-start(bf16[512,256]{1,0:T(8,128)(2,1)S(1)} %get-tuple-element.58.mine_ref), channel_id=1, source_target_pairs={{1,0},{0,1},{3,2},{2,3},{5,4},{4,5},{7,6},{6,7},{9,8},{8,9},{11,10... | collective-permute-start | bytes 786440 | tf_op jit(solution)/shard_map/ppermute | solution.py:647
  102.3 8.7 %collective-permute-start.10 = (bf16[128,512]{1,0:T(8,128)(2,1)S(1)}, bf16[128,512]{1,0:T(8,128)(2,1)S(1)}, u32[]{:S(2)}, u32[]{:S(2)}) collective-permute-start(bf16[128,512]{1,0:T(8,128)(2,1)S(1)} %add_convert_fusion.2.refs_0_), channel_id=1, source_target_pairs={{4,0},{6,2},{0,4},{2,6},{12,8},{14,10},{8,12},{10,14},{20,16},{22,... | collective-permute-start | bytes 393224 | tf_op jit(solution)/shard_map/ppermute | solution.py:502
  102.9 8.7 %collective-permute-start.11 = (bf16[128,512]{1,0:T(8,128)(2,1)S(1)}, bf16[128,512]{1,0:T(8,128)(2,1)S(1)}, u32[]{:S(2)}, u32[]{:S(2)}) collective-permute-start(bf16[128,512]{1,0:T(8,128)(2,1)S(1)} %add_convert_fusion.2.refs_0_), channel_id=1, source_target_pairs={{6,0},{4,2},{2,4},{0,6},{14,8},{12,10},{10,12},{8,14},{22,16},{20,... | collective-permute-start | bytes 393224 | tf_op jit(solution)/shard_map/ppermute | solution.py:502
  104.3 8.8 %collective-permute-start.9 = (bf16[128,512]{1,0:T(8,128)(2,1)S(1)}, bf16[128,512]{1,0:T(8,128)(2,1)S(1)}, u32[]{:S(2)}, u32[]{:S(2)}) collective-permute-start(bf16[128,512]{1,0:T(8,128)(2,1)S(1)} %add_convert_fusion.2.refs_0_), channel_id=1, source_target_pairs={{2,0},{0,2},{6,4},{4,6},{10,8},{8,10},{14,12},{12,14},{18,16},{16,... | collective-permute-start | bytes 393224 | tf_op jit(solution)/shard_map/ppermute | solution.py:502
  106.4 9.3 %collective-permute-start.13 = (bf16[128,512]{1,0:T(8,128)(2,1)S(1)}, bf16[128,512]{1,0:T(8,128)(2,1)S(1)}, u32[]{:S(2)}, u32[]{:S(2)}) collective-permute-start(bf16[128,512]{1,0:T(8,128)(2,1)S(1)} %collective-permute-done.12.refs_4_), channel_id=1, source_target_pairs={{2,0},{0,2},{6,4},{4,6},{10,8},{8,10},{14,12},{12,14},{18,16},{16,... | collective-permute-start | bytes 393224 | tf_op jit(solution)/shard_map/ppermute | solution.py:502
  111.0 7.9 %collective-permute-start.14 = (bf16[128,512]{1,0:T(8,128)(2,1)S(1)}, bf16[128,512]{1,0:T(8,128)(2,1)S(1)}, u32[]{:S(2)}, u32[]{:S(2)}) collective-permute-start(bf16[128,512]{1,0:T(8,128)(2,1)S(1)} %collective-permute-done.12.refs_4_), channel_id=1, source_target_pairs={{4,0},{6,2},{0,4},{2,6},{12,8},{14,10},{8,12},{10,14},{20,16},{22,... | collective-permute-start | bytes 393224 | tf_op jit(solution)/shard_map/ppermute | solution.py:502
  111.5 7.4 %collective-permute-start.15 = (bf16[128,512]{1,0:T(8,128)(2,1)S(1)}, bf16[128,512]{1,0:T(8,128)(2,1)S(1)}, u32[]{:S(2)}, u32[]{:S(2)}) collective-permute-start(bf16[128,512]{1,0:T(8,128)(2,1)S(1)} %collective-permute-done.12.refs_4_), channel_id=1, source_target_pairs={{6,0},{4,2},{2,4},{0,6},{14,8},{12,10},{10,12},{8,14},{22,16},{20,... | collective-permute-start | bytes 393224 | tf_op jit(solution)/shard_map/ppermute | solution.py:502

commit v14 on v12

--- a/solution.py
+++ b/solution.py
@@ -505,7 +505,7 @@
 
 
 def gather_blocks(block, axis, levels):
-    for level in reversed(levels):
+    for level in levels:
         rows = block.shape[0]
         pieces = gathered_pieces(block, axis, level)
         block = jnp.zeros((len(pieces) * rows,) + block.shape[1:], block.dtype)
@@ -604,7 +604,7 @@
         came = lax.ppermute(sent, "narrow", sent_from("narrow", 1, 2, 1))
         narrow_sum = (kept.astype(jnp.float32) + came.astype(jnp.float32)).astype(jnp.bfloat16)
     else:
-        narrow_sum = scatter_sum(jnp.concatenate([kept, sent], axis=0), "narrow", narrow_levels)
+        narrow_sum = scatter_sum(jnp.concatenate([kept, sent], axis=0), "narrow", narrow_levels[::-1])
     slot_grads = return_grads(goals, direct, dhidden, down_full)
     groups = [group for _, group in half_levels]
     share_terms = narrow_sum.reshape(*groups, -1, narrow_sum.shape[1])
@@ -630,9 +630,9 @@
     if paired:
         nears = [mine, lax.ppermute(passed, "narrow", sent_from("narrow", 1, 2, 1))]
     else:
-        nears = [scatter_sum(jnp.concatenate([mine, passed], axis=0), "narrow", narrow_levels)]
+        nears = [scatter_sum(jnp.concatenate([mine, passed], axis=0), "narrow", narrow_levels[::-1])]
     far_term = summed([term[:, emb_width:] for term in nears])
-    inner = gather_blocks(table_sum, "table", half_levels[2:])
+    inner = gather_blocks(table_sum, "table", half_levels[2:][::-1])
     blocks, fan = [(0, inner)], 1
     if len(half_levels) > 1:
         blocks, fan = gathered_pieces(inner, "table", half_levels[1]), half_levels[1][1]

time: 111 us -> 111 us (level)
  no operation moved by 1% of the time
where the time goes in v14:
time: 111 us; the launch traced here: 110 us
  blocking collectives  43.8 us (39%)
  waiting for transfers between devices  25.4 us (23%)
  starting transfers between devices  18.8 us (17%)
  Pallas kernels  16.5 us (15%)
  local copies, waits for them, and re-layouts  2.24 us (2%)
  other arithmetic  2.22 us (2%)
    all_to_all x1, blocking collectives, local(): lax.all_to_all(jnp.concatenate(outgoing, axis=1), 'table', split_axis=0,...  30.6 us
    all_to_all x1, blocking collectives, local(): lax.all_to_all(asked, 'table', split_axis=0, concat_axis=0, tiled=True, a...  13.2 us
    all_to_all x1, waiting for transfers between devices, local(): lax.all_to_all(sums, 'table', split_axis=0, concat_axis=0, tiled=True, ax...  10.9 us
    ppermute x7, starting transfers between devices, gathered_pieces(): came = lax.ppermute(block, axis, sent_from(axis, stride, group, step))  7.53 us
    ppermute x7, waiting for transfers between devices, gathered_pieces(): came = lax.ppermute(block, axis, sent_from(axis, stride, group, step))  6.1 us
    pallas_call x2, Pallas kernels, pool_lookups(): kernel_call(functools.partial(pool_kernel, part), jax.ShapeDtypeStruct((s...  4.37 us
    ppermute x1, starting transfers between devices, local(): far_share = lax.ppermute(own_share, 'table', across)  4.1 us
    all_to_all x1, starting transfers between devices, local(): lax.all_to_all(sums, 'table', split_axis=0, concat_axis=0, tiled=True, ax...  3.57 us
  transfers between devices with their start and end apart: 17, of which 10 were waited for; matrix products, arithmetic and copies ran while one was open for 2% of the time, Pallas kernels for 8%

profile of v14, /device:TPU:0, one launch (start us, length us, event | category | flops | bytes accessed | tf_op | source)
XLA Modules:
  0.0 110.1 jit_solution(15005841888617019456)
XLA Ops:
  0.6 0.0 copy-start
  0.7 1.1 constant_dynamic-slice_fusion.2
  1.7 4.1 %collective-permute-start = (bf16[512,256]{1,0:T(8,128)(2,1)S(1)}, bf16[512,256]{1,0:T(8,128)(2,1)S(1)}, u32[]{:S(2)}, u32[]{:S(2)}) collective-permute-start(bf16[512,256]{1,0:T(8,128)(2,1)S(1)} %get-tuple-element.76.first_ref.rows_ref), channel_id=1, source_target_pairs={{0,16},{2,18},{4,20},{6,22},{8,24},{10,26},{12,28},{14,30},{16,0},... | collective-permute-start | bytes 786440 | tf_op jit(solution)/shard_map/ppermute | solution.py:563
  5.8 0.7 constant_dynamic-slice_fusion.5
  6.6 13.2 %all_to_all.15.ids_ref = s32[8,1,1024]{2,1,0:T(1,128)S(1)} all-to-all(s32[8,1,1024]{2,1,0:T(1,128)S(1)} %broadcast_in_dim.3), channel_id=1, replica_groups={{0,2,4,6,8,10,12,14},{16,18,20,22,24,26,28,30},{1,3,5,7,9,11,13,15},{17..., dimensions={0} | all-to-all | bytes 65536 | tf_op jit(solution)/shard_map/all_to_all | solution.py:569
  19.8 2.2 %shard_map.128.refs_0_ = bf16[8,2,128,256]{3,2,1,0:T(8,128)(2,1)} custom-call(s32[1]{0:T(128)} %bitcast.swap_ref, s32[8,1,1024]{2,1,0:T(1,128)S(1)} %all_to_all.15.ids_ref, bf16[512,256]{1,0:T(8,128)(2,1)S(1)} %get-tuple-element.76.first_ref.rows_ref, bf16[512,256]{1,0:T(8,128)(2,1)S(1)} %get-tuple-element.75.second_ref), custom_call_target="tpu_custom_call" | custom-call | flops 536870912 | bytes 1048576 | tf_op jit(solution)/shard_map/pallas_call | solution.py:125
  22.0 0.0 copy-start.4
  22.1 2.2 %shard_map.129 = bf16[8,2,128,256]{3,2,1,0:T(8,128)(2,1)} custom-call(s32[1]{0:T(128)} %bitcast.swap_ref, s32[8,1,1024]{2,1,0:T(1,128)S(1)} %all_to_all.15.ids_ref, bf16[512,256]{1,0:T(8,128)(2,1)S(1)} %collective-permute-done.first_ref, bf16[512,256]{1,0:T(8,128)(2,1)S(1)} %collective-permute-done.1.second_ref, ...), custom_call_target="tpu_custom_call", output_to_operand_aliasing={{}: (4, {})} | custom-call | flops 536870912 | bytes 1048576 | tf_op jit(solution)/shard_map/pallas_call | solution.py:125
  24.3 3.6 %all-to-all-start.1 = ((bf16[8,2,128,256]{3,2,1,0:T(8,128)(2,1)}), bf16[8,2,128,256]{3,2,1,0:T(8,128)(2,1)S(1)}, u32[]{:S(2)}, u32[]{:S(2)}) async-start(bf16[8,2,128,256]{3,2,1,0:T(8,128)(2,1)} %shard_map.129), calls=%async_computation.1 | async-start | bytes 2097152 | tf_op jit(solution)/shard_map/all_to_all | solution.py:586
  27.9 0.6 collective-permute-start.2
  28.4 0.1 collective-permute-start.3
  28.6 1.5 %collective-permute-done.2 = bf16[1024,256]{1,0:T(8,128)(2,1)} collective-permute-done((bf16[1024,256]{1,0:T(8,128)(2,1)S(1)}, bf16[1024,256]{1,0:T(8,128)(2,1)}, u32[]{:S(2)}, u32[]{:S(2)}) %collective-permute-start.2) | collective-permute-done | bytes 524320 | tf_op jit(solution)/shard_map/ppermute | solution.py:552
  30.1 0.7 collective-permute-done.3
  30.8 1.4 %broadcast_select_fusion.1 = (bf16[1024,256]{1,0:T(8,128)(2,1)S(1)}, bf16[1024,256]{1,0:T(8,128)(2,1)S(1)}, bf16[1024,256]{1,0:T(8,128)(2,1)S(1)}, bf16[1024,256]{1,0:T(8,128)(2,1)S(1)}) fusion(bf16[1024,256]{1,0:T(8,128)(2,1)S(1)} %copy-done.3, bf16[1024,256]{1,0:T(8,128)(2,1)} %collective-permute-done.3, pred[]{:T(512)S(6)} %eq.24, ...), kind=kLoop, calls=%fused_computation.7 | loop fusion | flops 1048576 | bytes 4194305 | tf_op jit(solution)/shard_map/jit(_where)/select_n | solution.py:553
  32.2 0.1 pad_maximum_fusion.2.up_ref
  32.3 0.1 pad_maximum_fusion.1.down_ref
  32.4 10.9 %all-to-all-done.1 = bf16[8,2,128,256]{3,2,1,0:T(8,128)(2,1)S(1)} async-done(((bf16[8,2,128,256]{3,2,1,0:T(8,128)(2,1)}), bf16[8,2,128,256]{3,2,1,0:T(8,128)(2,1)S(1)}, u32[]{:S(2)}, u32[]{:S(2)}) %all-to-all-start.1) | async-done | bytes 1048608 | tf_op jit(solution)/shard_map/all_to_all | solution.py:586
  43.3 3.5 %shard_map.130 = (f32[1,128]{1,0:T(1,128)}, f32[128,2048]{1,0:T(8,128)S(1)}, bf16[128,256]{1,0:T(8,128)(2,1)S(1)}, bf16[1024,512]{1,0:T(8,128)(2,1)S(1)}, bf16[1024,512]{1,0:T(8,128)(2,1)S(1)}) custom-call(s32[1]{0:T(128)} %bitcast.swap_ref, s32[1,2048]{1,0:T(1,128)S(1)} %bitcast.27, f32[1,2048]{1,0:T(1,128)S(1)} %bitcast.29, ...), custom_call_target="tpu_custom_call" | custom-call | flops 1879048192 | bytes 5242880 | tf_op jit(solution)/shard_map/pallas_call | solution.py:315
  46.8 0.1 collective-permute-start.4
  46.9 1.8 %shard_map.131 = bf16[2048,256]{1,0:T(8,128)(2,1)S(1)} custom-call(s32[16,128]{1,0:T(8,128)S(1)} %bitcast.28, f32[128,2048]{1,0:T(8,128)S(1)} %get-tuple-element.47.direct_ref, bf16[128,256]{1,0:T(8,128)(2,1)S(1)} %get-tuple-element.48.dhidden_ref, bf16[2048,256]{1,0:T(8,128)(2,1)S(1)} %pad_maximum_fusion.1.down_ref), custom_call_target="tpu_custom_call" | custom-call | flops 1073741824 | bytes 2097152 | tf_op jit(solution)/shard_map/pallas_call | solution.py:233
  48.7 0.8 collective-permute-done.4
  49.6 0.3 add_convert_fusion
  49.9 0.1 copy.15
  49.9 0.1 fusion
  50.1 0.1 pad_maximum_fusion
  50.2 30.6 %all_to_all.16.grads_ref = bf16[8,512,256]{2,1,0:T(8,128)(2,1)S(1)} all-to-all(bf16[8,512,256]{2,1,0:T(8,128)(2,1)S(1)} %pad_maximum_fusion), channel_id=1, replica_groups={{0,2,4,6,8,10,12,14},{16,18,20,22,24,26,28,30},{1,3,5,7,9,11,13,15},{17..., dimensions={0} | all-to-all | bytes 4194304 | tf_op jit(solution)/shard_map/all_to_all | solution.py:616
  80.8 0.1 slice_reduce_fusion
  81.0 1.0 collective-permute-start.5
  82.0 3.2 %shard_map.132 = (bf16[512,512]{1,0:T(8,128)(2,1)S(1)}, bf16[512,512]{1,0:T(8,128)(2,1)S(1)}) custom-call(s32[1]{0:T(128)} %bitcast.swap_ref, s32[8,1,1024]{2,1,0:T(1,128)S(1)} %all_to_all.15.ids_ref, bf16[8,512,256]{2,1,0:T(8,128)(2,1)S(1)} %all_to_all.16.grads_ref), custom_call_target="tpu_custom_call" | custom-call | flops 1073741824 | bytes 3145728 | tf_op jit(solution)/shard_map/pallas_call | solution.py:179
  85.2 3.4 %collective-permute-done.5 = bf16[128,512]{1,0:T(8,128)(2,1)S(1)} collective-permute-done((bf16[128,512]{1,0:T(8,128)(2,1)S(1)}, bf16[128,512]{1,0:T(8,128)(2,1)S(1)}, u32[]{:S(2)}, u32[]{:S(2)}) %collective-permute-start.5) | collective-permute-done | bytes 131104 | tf_op jit(solution)/shard_map/ppermute | solution.py:626
  88.7 0.1 collective-permute-start.11
  88.7 1.5 %collective-permute-start.10 = (bf16[128,512]{1,0:T(8,128)(2,1)S(1)}, bf16[128,512]{1,0:T(8,128)(2,1)S(1)}, u32[]{:S(2)}, u32[]{:S(2)}) collective-permute-start(bf16[128,512]{1,0:T(8,128)(2,1)S(1)} %add_convert_fusion.2.refs_0_), channel_id=1, source_target_pairs={{6,0},{4,2},{2,4},{0,6},{14,8},{12,10},{10,12},{8,14},{22,16},{20,... | collective-permute-start | bytes 393224 | tf_op jit(solution)/shard_map/ppermute | solution.py:502
  90.2 1.1 collective-permute-start.9
  91.3 0.1 add_convert_fusion.1
  91.4 1.9 %collective-permute-start.7 = (bf16[512,256]{1,0:T(8,128)(2,1)S(1)}, bf16[512,256]{1,0:T(8,128)(2,1)S(1)}, u32[]{:S(2)}, u32[]{:S(2)}) collective-permute-start(bf16[512,256]{1,0:T(8,128)(2,1)S(1)} %add_convert_fusion.1), channel_id=1, source_target_pairs={{0,16},{2,18},{4,20},{6,22},{8,24},{10,26},{12,28},{14,30},{16,0},... | collective-permute-start | bytes 786440 | tf_op jit(solution)/shard_map/ppermute | solution.py:645
  93.3 1.5 %collective-permute-start.8 = (bf16[128,512]{1,0:T(8,128)(2,1)S(1)}, bf16[128,512]{1,0:T(8,128)(2,1)S(1)}, u32[]{:S(2)}, u32[]{:S(2)}) collective-permute-start(bf16[128,512]{1,0:T(8,128)(2,1)S(1)} %add_convert_fusion.2.refs_0_), channel_id=1, source_target_pairs={{2,0},{0,2},{6,4},{4,6},{10,8},{8,10},{14,12},{12,14},{18,16},{16,... | collective-permute-start | bytes 393224 | tf_op jit(solution)/shard_map/ppermute | solution.py:502
  94.8 2.5 %collective-permute-start.14 = (bf16[128,512]{1,0:T(8,128)(2,1)S(1)}, bf16[128,512]{1,0:T(8,128)(2,1)S(1)}, u32[]{:S(2)}, u32[]{:S(2)}) collective-permute-start(bf16[128,512]{1,0:T(8,128)(2,1)S(1)} %collective-permute-done.11.refs_4_), channel_id=1, source_target_pairs={{6,0},{4,2},{2,4},{0,6},{14,8},{12,10},{10,12},{8,14},{22,16},{20,... | collective-permute-start | bytes 393224 | tf_op jit(solution)/shard_map/ppermute | solution.py:502
  97.2 1.9 %collective-permute-done.9.refs_2_ = bf16[128,512]{1,0:T(8,128)(2,1)S(1)} collective-permute-done((bf16[128,512]{1,0:T(8,128)(2,1)S(1)}, bf16[128,512]{1,0:T(8,128)(2,1)S(1)}, u32[]{:S(2)}, u32[]{:S(2)}) %collective-permute-start.9) | collective-permute-done | bytes 131104 | tf_op jit(solution)/shard_map/ppermute | solution.py:502
  99.1 0.9 collective-permute-start.12
  100.1 0.1 dynamic-slice_bitcast_fusion.accum_ref
  100.1 2.0 %collective-permute-done.14.refs_7_ = bf16[128,512]{1,0:T(8,128)(2,1)S(1)} collective-permute-done((bf16[128,512]{1,0:T(8,128)(2,1)S(1)}, bf16[128,512]{1,0:T(8,128)(2,1)S(1)}, u32[]{:S(2)}, u32[]{:S(2)}) %collective-permute-start.14) | collective-permute-done | bytes 131104 | tf_op jit(solution)/shard_map/ppermute | solution.py:502
  102.1 2.0 %collective-permute-done.13.refs_6_ = bf16[128,512]{1,0:T(8,128)(2,1)S(1)} collective-permute-done((bf16[128,512]{1,0:T(8,128)(2,1)S(1)}, bf16[128,512]{1,0:T(8,128)(2,1)S(1)}, u32[]{:S(2)}, u32[]{:S(2)}) %collective-permute-start.13) | collective-permute-done | bytes 131104 | tf_op jit(solution)/shard_map/ppermute | solution.py:502
  104.0 0.3 collective-permute-done.12.refs_5_
  104.4 1.8 %collective-permute-done.7.far_ref = bf16[512,256]{1,0:T(8,128)(2,1)S(1)} collective-permute-done((bf16[512,256]{1,0:T(8,128)(2,1)S(1)}, bf16[512,256]{1,0:T(8,128)(2,1)S(1)}, u32[]{:S(2)}, u32[]{:S(2)}) %collective-permute-start.7) | collective-permute-done | bytes 262176 | tf_op jit(solution)/shard_map/ppermute | solution.py:645
  106.1 0.9 shard_map.134
  107.0 0.1 stack.47.spots_ref
  107.1 2.0 %shard_map.133 = (f32[1024,256]{1,0:T(8,128)}, f32[1024,256]{1,0:T(8,128)}) custom-call(s32[8]{0:T(128)S(1)} %stack.47.spots_ref, bf16[128,512]{1,0:T(8,128)(2,1)S(1)} %add_convert_fusion.2.refs_0_, bf16[128,512]{1,0:T(8,128)(2,1)S(1)} %collective-permute-done.8.refs_1_, bf16[128,512]{1,0:T(8,128)(2,1)S(1)} %collective-permute-done.9.refs_2_, ...), custom_call_target="tpu_custom_call" | custom-call | flops 524288 | bytes 3145728 | tf_op jit(solution)/shard_map/pallas_call | solution.py:375
  109.1 0.8 shard_map.135
  (31 shorter events, 0.2 us)
Async XLA Ops:
  0.6 99.4 %copy-start = (f32[1024]{0:T(1024)S(1)}, f32[1024]{0:T(1024)}, u32[]{:S(2)}) copy-start(f32[1024]{0:T(1024)} %param.10) | copy-start | bytes 12292
  1.7 18.1 %collective-permute-start = (bf16[512,256]{1,0:T(8,128)(2,1)S(1)}, bf16[512,256]{1,0:T(8,128)(2,1)S(1)}, u32[]{:S(2)}, u32[]{:S(2)}) collective-permute-start(bf16[512,256]{1,0:T(8,128)(2,1)S(1)} %get-tuple-element.76.first_ref.rows_ref), channel_id=1, source_target_pairs={{0,16},{2,18},{4,20},{6,22},{8,24},{10,26},{12,28},{14,30},{16,0},... | collective-permute-start | bytes 786440 | tf_op jit(solution)/shard_map/ppermute | solution.py:563
  19.8 2.2 %collective-permute-start.1 = (bf16[512,256]{1,0:T(8,128)(2,1)S(1)}, bf16[512,256]{1,0:T(8,128)(2,1)S(1)}, u32[]{:S(2)}, u32[]{:S(2)}) collective-permute-start(bf16[512,256]{1,0:T(8,128)(2,1)S(1)} %collective-permute-done.first_ref), channel_id=1, source_target_pairs={{1,0},{0,1},{3,2},{2,3},{5,4},{4,5},{7,6},{6,7},{9,8},{8,9},{11,10... | collective-permute-start | bytes 786440 | tf_op jit(solution)/shard_map/ppermute | solution.py:574
  22.0 5.8 %copy-start.4 = (bf16[1024,256]{1,0:T(8,128)(2,1)S(1)}, bf16[1024,256]{1,0:T(8,128)(2,1)}, u32[]{:S(2)}) copy-start(bf16[1024,256]{1,0:T(8,128)(2,1)} %param.11) | copy-start | bytes 1572868
  22.0 6.4 %copy-start.3 = (bf16[1024,256]{1,0:T(8,128)(2,1)S(1)}, bf16[1024,256]{1,0:T(8,128)(2,1)}, u32[]{:S(2)}) copy-start(bf16[1024,256]{1,0:T(8,128)(2,1)} %param.12) | copy-start | bytes 1572868
  22.0 6.5 %copy-start.6 = (bf16[2048]{0:T(1024)(128)(2,1)S(1)}, bf16[2048]{0:T(1024)(128)(2,1)}, u32[]{:S(2)}) copy-start(bf16[2048]{0:T(1024)(128)(2,1)} %param.14) | copy-start | bytes 12292
  22.0 6.5 %copy-start.5 = (s32[16,128]{1,0:T(8,128)S(1)}, s32[16,128]{1,0:T(8,128)}, u32[]{:S(2)}) copy-start(s32[16,128]{1,0:T(8,128)} %param.17) | copy-start | bytes 24580
  24.3 19.0 %all-to-all-start.1 = ((bf16[8,2,128,256]{3,2,1,0:T(8,128)(2,1)}), bf16[8,2,128,256]{3,2,1,0:T(8,128)(2,1)S(1)}, u32[]{:S(2)}, u32[]{:S(2)}) async-start(bf16[8,2,128,256]{3,2,1,0:T(8,128)(2,1)} %shard_map.129), calls=%async_computation.1 | async-start | bytes 2097152 | tf_op jit(solution)/shard_map/all_to_all | solution.py:586
  27.9 2.2 %collective-permute-start.2 = (bf16[1024,256]{1,0:T(8,128)(2,1)S(1)}, bf16[1024,256]{1,0:T(8,128)(2,1)}, u32[]{:S(2)}, u32[]{:S(2)}) collective-permute-start(bf16[1024,256]{1,0:T(8,128)(2,1)S(1)} %copy-done.4), channel_id=1, source_target_pairs={{1,0},{0,1},{3,2},{2,3},{5,4},{4,5},{7,6},{6,7},{9,8},{8,9},{11,10... | collective-permute-start | bytes 1572872 | tf_op jit(solution)/shard_map/ppermute | solution.py:552
  28.4 2.4 %collective-permute-start.3 = (bf16[1024,256]{1,0:T(8,128)(2,1)S(1)}, bf16[1024,256]{1,0:T(8,128)(2,1)}, u32[]{:S(2)}, u32[]{:S(2)}) collective-permute-start(bf16[1024,256]{1,0:T(8,128)(2,1)S(1)} %copy-done.3), channel_id=1, source_target_pairs={{1,0},{0,1},{3,2},{2,3},{5,4},{4,5},{7,6},{6,7},{9,8},{8,9},{11,10... | collective-permute-start | bytes 1572872 | tf_op jit(solution)/shard_map/ppermute | solution.py:552
  32.2 11.1 %copy-start.1 = (f32[2048]{0:T(1024)S(1)}, f32[2048]{0:T(1024)}, u32[]{:S(2)}) copy-start(f32[2048]{0:T(1024)} %param.13) | copy-start | bytes 24580
  32.2 11.1 %copy-start.2 = (f32[128]{0:T(128)S(1)}, f32[128]{0:T(128)}, u32[]{:S(2)}) copy-start(f32[128]{0:T(128)} %param.15) | copy-start | bytes 1540
  46.8 2.7 %collective-permute-start.4 = (bf16[1024,512]{1,0:T(8,128)(2,1)S(1)}, bf16[1024,512]{1,0:T(8,128)(2,1)S(1)}, u32[]{:S(2)}, u32[]{:S(2)}) collective-permute-start(bf16[1024,512]{1,0:T(8,128)(2,1)S(1)} %get-tuple-element.50), channel_id=1, source_target_pairs={{1,0},{0,1},{3,2},{2,3},{5,4},{4,5},{7,6},{6,7},{9,8},{8,9},{11,10... | collective-permute-start | bytes 3145736 | tf_op jit(solution)/shard_map/ppermute | solution.py:604
  81.0 7.6 %collective-permute-start.5 = (bf16[128,512]{1,0:T(8,128)(2,1)S(1)}, bf16[128,512]{1,0:T(8,128)(2,1)S(1)}, u32[]{:S(2)}, u32[]{:S(2)}) collective-permute-start(bf16[128,512]{1,0:T(8,128)(2,1)S(1)} %pad_maximum_fusion.3), channel_id=1, source_target_pairs={{0,16},{2,18},{4,20},{6,22},{8,24},{10,26},{12,28},{14,30},{16,0},... | collective-permute-start | bytes 393224 | tf_op jit(solution)/shard_map/ppermute | solution.py:626
  88.6 2.7 %collective-permute-start.6 = (bf16[512,512]{1,0:T(8,128)(2,1)S(1)}, bf16[512,512]{1,0:T(8,128)(2,1)S(1)}, u32[]{:S(2)}, u32[]{:S(2)}) collective-permute-start(bf16[512,512]{1,0:T(8,128)(2,1)S(1)} %get-tuple-element.54), channel_id=1, source_target_pairs={{1,0},{0,1},{3,2},{2,3},{5,4},{4,5},{7,6},{6,7},{9,8},{8,9},{11,10... | collective-permute-start | bytes 1572872 | tf_op jit(solution)/shard_map/ppermute | solution.py:631
  88.7 6.1 %collective-permute-start.11 = (bf16[128,512]{1,0:T(8,128)(2,1)S(1)}, bf16[128,512]{1,0:T(8,128)(2,1)S(1)}, u32[]{:S(2)}, u32[]{:S(2)}) collective-permute-start(bf16[128,512]{1,0:T(8,128)(2,1)S(1)} %add_convert_fusion.2.refs_0_), channel_id=1, source_target_pairs={{8,0},{10,2},{12,4},{14,6},{0,8},{2,10},{4,12},{6,14},{24,16},{26,... | collective-permute-start | bytes 393224 | tf_op jit(solution)/shard_map/ppermute | solution.py:502
  88.7 8.5 %collective-permute-start.10 = (bf16[128,512]{1,0:T(8,128)(2,1)S(1)}, bf16[128,512]{1,0:T(8,128)(2,1)S(1)}, u32[]{:S(2)}, u32[]{:S(2)}) collective-permute-start(bf16[128,512]{1,0:T(8,128)(2,1)S(1)} %add_convert_fusion.2.refs_0_), channel_id=1, source_target_pairs={{6,0},{4,2},{2,4},{0,6},{14,8},{12,10},{10,12},{8,14},{22,16},{20,... | collective-permute-start | bytes 393224 | tf_op jit(solution)/shard_map/ppermute | solution.py:502
  90.2 8.9 %collective-permute-start.9 = (bf16[128,512]{1,0:T(8,128)(2,1)S(1)}, bf16[128,512]{1,0:T(8,128)(2,1)S(1)}, u32[]{:S(2)}, u32[]{:S(2)}) collective-permute-start(bf16[128,512]{1,0:T(8,128)(2,1)S(1)} %add_convert_fusion.2.refs_0_), channel_id=1, source_target_pairs={{4,0},{6,2},{0,4},{2,6},{12,8},{14,10},{8,12},{10,14},{20,16},{22,... | collective-permute-start | bytes 393224 | tf_op jit(solution)/shard_map/ppermute | solution.py:502
  91.4 14.7 %collective-permute-start.7 = (bf16[512,256]{1,0:T(8,128)(2,1)S(1)}, bf16[512,256]{1,0:T(8,128)(2,1)S(1)}, u32[]{:S(2)}, u32[]{:S(2)}) collective-permute-start(bf16[512,256]{1,0:T(8,128)(2,1)S(1)} %add_convert_fusion.1), channel_id=1, source_target_pairs={{0,16},{2,18},{4,20},{6,22},{8,24},{10,26},{12,28},{14,30},{16,0},... | collective-permute-start | bytes 786440 | tf_op jit(solution)/shard_map/ppermute | solution.py:645
  93.3 6.8 %collective-permute-start.8 = (bf16[128,512]{1,0:T(8,128)(2,1)S(1)}, bf16[128,512]{1,0:T(8,128)(2,1)S(1)}, u32[]{:S(2)}, u32[]{:S(2)}) collective-permute-start(bf16[128,512]{1,0:T(8,128)(2,1)S(1)} %add_convert_fusion.2.refs_0_), channel_id=1, source_target_pairs={{2,0},{0,2},{6,4},{4,6},{10,8},{8,10},{14,12},{12,14},{18,16},{16,... | collective-permute-start | bytes 393224 | tf_op jit(solution)/shard_map/ppermute | solution.py:502
  94.8 7.3 %collective-permute-start.14 = (bf16[128,512]{1,0:T(8,128)(2,1)S(1)}, bf16[128,512]{1,0:T(8,128)(2,1)S(1)}, u32[]{:S(2)}, u32[]{:S(2)}) collective-permute-start(bf16[128,512]{1,0:T(8,128)(2,1)S(1)} %collective-permute-done.11.refs_4_), channel_id=1, source_target_pairs={{6,0},{4,2},{2,4},{0,6},{14,8},{12,10},{10,12},{8,14},{22,16},{20,... | collective-permute-start | bytes 393224 | tf_op jit(solution)/shard_map/ppermute | solution.py:502
  97.2 6.8 %collective-permute-start.13 = (bf16[128,512]{1,0:T(8,128)(2,1)S(1)}, bf16[128,512]{1,0:T(8,128)(2,1)S(1)}, u32[]{:S(2)}, u32[]{:S(2)}) collective-permute-start(bf16[128,512]{1,0:T(8,128)(2,1)S(1)} %collective-permute-done.11.refs_4_), channel_id=1, source_target_pairs={{4,0},{6,2},{0,4},{2,6},{12,8},{14,10},{8,12},{10,14},{20,16},{22,... | collective-permute-start | bytes 393224 | tf_op jit(solution)/shard_map/ppermute | solution.py:502
  99.1 5.2 %collective-permute-start.12 = (bf16[128,512]{1,0:T(8,128)(2,1)S(1)}, bf16[128,512]{1,0:T(8,128)(2,1)S(1)}, u32[]{:S(2)}, u32[]{:S(2)}) collective-permute-start(bf16[128,512]{1,0:T(8,128)(2,1)S(1)} %collective-permute-done.11.refs_4_), channel_id=1, source_target_pairs={{2,0},{0,2},{6,4},{4,6},{10,8},{8,10},{14,12},{12,14},{18,16},{16,... | collective-permute-start | bytes 393224 | tf_op jit(solution)/shard_map/ppermute | solution.py:502
  107.0 2.1 %collective-permute-start.15 = (bf16[512,256]{1,0:T(8,128)(2,1)S(1)}, bf16[512,256]{1,0:T(8,128)(2,1)S(1)}, u32[]{:S(2)}, u32[]{:S(2)}) collective-permute-start(bf16[512,256]{1,0:T(8,128)(2,1)S(1)} %get-tuple-element.67.mine_ref), channel_id=1, source_target_pairs={{1,0},{0,1},{3,2},{2,3},{5,4},{4,5},{7,6},{6,7},{9,8},{8,9},{11,10... | collective-permute-start | bytes 786440 | tf_op jit(solution)/shard_map/ppermute | solution.py:652

commit v15 on v14

--- a/solution.py
+++ b/solution.py
@@ -643,9 +643,12 @@
         early += pieces if i == 0 else pieces[:1]
         late += [] if i == 0 else pieces[1:]
     far_term = lax.ppermute(far_term, "table", across)
-    spots, came = zip(*early, *late)
-    far_term, *came = lax.optimization_barrier((far_term, *came))
-    pieces = list(zip(spots, came))
+    scale = 1.0 / math.sqrt(samples * tables * narrows)
+    grads = spread_pieces(early, scale, factor_down.shape[0])
+    spots = [spot for spot, _ in late]
+    far_term, down_grad, up_grad, *came = lax.optimization_barrier(
+        (far_term, *grads, *(piece for _, piece in late))
+    )
     own_accum = lax.dynamic_slice_in_dim(accum, narrow_index * share_rows, share_rows, 0)
     new_share, new_accum = update_rows(own_share, far_term, own_accum, nears)
     if paired:
@@ -653,8 +656,10 @@
         new_rows = join_halves(swap, new_share, other_share)
     else:
         new_rows = gather_blocks(new_share, "narrow", narrow_levels)
-    scale = 1.0 / math.sqrt(samples * tables * narrows)
-    down_grad, up_grad = spread_pieces(pieces, scale, factor_down.shape[0])
+    if late:
+        down_grad, up_grad = spread_pieces(
+            list(zip(spots, came)), scale, factor_down.shape[0], (down_grad, up_grad)
+        )
     return (logits, down_grad, up_grad, new_rows, new_accum)
 
 

time: 111 us -> 109 us (0.982)
  waiting for transfers between devices: 25.4 us -> 23 us
  Pallas kernels: 16.5 us -> 17.7 us
    ppermute x1, waiting for transfers between devices: 1.79 us -> 0.22 us  [local(): far_term = lax.ppermute(far_term, 'table', across)]
    pallas_call x1 -> x2, Pallas kernels: 1.99 us -> 3.15 us  [spread_pieces(): kernel_call(functools.partial(spread_kernel, count, scale, len(given)), (...]
  transfers between devices with their start and end apart: 17 -> 17, of which waited for: 10 -> 10; matrix products, arithmetic and copies ran while one was open for 2% -> 2% of each run, Pallas kernels for 8% -> 9%
where the time goes in v15:
time: 109 us
  blocking collectives  43.8 us (40%)
  waiting for transfers between devices  23 us (21%)
  starting transfers between devices  18.9 us (17%)
  Pallas kernels  17.7 us (16%)
  other arithmetic  2.3 us (2%)
  local copies, waits for them, and re-layouts  2.24 us (2%)
    all_to_all x1, blocking collectives, local(): lax.all_to_all(jnp.concatenate(outgoing, axis=1), 'table', split_axis=0,...  30.6 us
    all_to_all x1, blocking collectives, local(): lax.all_to_all(asked, 'table', split_axis=0, concat_axis=0, tiled=True, a...  13.2 us
    all_to_all x1, waiting for transfers between devices, local(): lax.all_to_all(sums, 'table', split_axis=0, concat_axis=0, tiled=True, ax...  10.9 us
    ppermute x7, starting transfers between devices, gathered_pieces(): came = lax.ppermute(block, axis, sent_from(axis, stride, group, step))  7.05 us
    ppermute x7, waiting for transfers between devices, gathered_pieces(): came = lax.ppermute(block, axis, sent_from(axis, stride, group, step))  5.29 us
    pallas_call x2, Pallas kernels, pool_lookups(): kernel_call(functools.partial(pool_kernel, part), jax.ShapeDtypeStruct((s...  4.37 us
    ppermute x1, starting transfers between devices, local(): far_share = lax.ppermute(own_share, 'table', across)  4.1 us
    all_to_all x1, starting transfers between devices, local(): lax.all_to_all(sums, 'table', split_axis=0, concat_axis=0, tiled=True, ax...  3.57 us
  transfers between devices with their start and end apart: 17, of which 10 were waited for; matrix products, arithmetic and copies ran while one was open for 2% of the time, Pallas kernels for 9%

profile of v15, /device:TPU:0, one launch (start us, length us, event | category | flops | bytes accessed | tf_op | source)
XLA Modules:
  0.0 109.0 jit_solution(7653128311960694762)
XLA Ops:
  0.7 1.1 constant_dynamic-slice_fusion.2
  1.7 4.1 %collective-permute-start = (bf16[512,256]{1,0:T(8,128)(2,1)S(1)}, bf16[512,256]{1,0:T(8,128)(2,1)S(1)}, u32[]{:S(2)}, u32[]{:S(2)}) collective-permute-start(bf16[512,256]{1,0:T(8,128)(2,1)S(1)} %get-tuple-element.74.first_ref.rows_ref), channel_id=1, source_target_pairs={{0,16},{2,18},{4,20},{6,22},{8,24},{10,26},{12,28},{14,30},{16,0},... | collective-permute-start | bytes 786440 | tf_op jit(solution)/shard_map/ppermute | solution.py:563
  5.8 0.7 constant_dynamic-slice_fusion.5
  6.6 13.2 %all_to_all.15.ids_ref = s32[8,1,1024]{2,1,0:T(1,128)S(1)} all-to-all(s32[8,1,1024]{2,1,0:T(1,128)S(1)} %broadcast_in_dim.3), channel_id=1, replica_groups={{0,2,4,6,8,10,12,14},{16,18,20,22,24,26,28,30},{1,3,5,7,9,11,13,15},{17..., dimensions={0} | all-to-all | bytes 65536 | tf_op jit(solution)/shard_map/all_to_all | solution.py:569
  19.8 2.2 %shard_map.128.refs_0_ = bf16[8,2,128,256]{3,2,1,0:T(8,128)(2,1)} custom-call(s32[1]{0:T(128)} %bitcast.swap_ref, s32[8,1,1024]{2,1,0:T(1,128)S(1)} %all_to_all.15.ids_ref, bf16[512,256]{1,0:T(8,128)(2,1)S(1)} %get-tuple-element.74.first_ref.rows_ref, bf16[512,256]{1,0:T(8,128)(2,1)S(1)} %get-tuple-element.73.second_ref), custom_call_target="tpu_custom_call" | custom-call | flops 536870912 | bytes 1048576 | tf_op jit(solution)/shard_map/pallas_call | solution.py:125
  22.1 2.2 %shard_map.129 = bf16[8,2,128,256]{3,2,1,0:T(8,128)(2,1)} custom-call(s32[1]{0:T(128)} %bitcast.swap_ref, s32[8,1,1024]{2,1,0:T(1,128)S(1)} %all_to_all.15.ids_ref, bf16[512,256]{1,0:T(8,128)(2,1)S(1)} %collective-permute-done.first_ref, bf16[512,256]{1,0:T(8,128)(2,1)S(1)} %collective-permute-done.1.second_ref, ...), custom_call_target="tpu_custom_call", output_to_operand_aliasing={{}: (4, {})} | custom-call | flops 536870912 | bytes 1048576 | tf_op jit(solution)/shard_map/pallas_call | solution.py:125
  24.3 3.6 %all-to-all-start.1 = ((bf16[8,2,128,256]{3,2,1,0:T(8,128)(2,1)}), bf16[8,2,128,256]{3,2,1,0:T(8,128)(2,1)S(1)}, u32[]{:S(2)}, u32[]{:S(2)}) async-start(bf16[8,2,128,256]{3,2,1,0:T(8,128)(2,1)} %shard_map.129), calls=%async_computation.1 | async-start | bytes 2097152 | tf_op jit(solution)/shard_map/all_to_all | solution.py:586
  27.9 0.6 collective-permute-start.2
  28.4 0.1 collective-permute-start.3
  28.6 1.5 %collective-permute-done.2 = bf16[1024,256]{1,0:T(8,128)(2,1)} collective-permute-done((bf16[1024,256]{1,0:T(8,128)(2,1)S(1)}, bf16[1024,256]{1,0:T(8,128)(2,1)}, u32[]{:S(2)}, u32[]{:S(2)}) %collective-permute-start.2) | collective-permute-done | bytes 524320 | tf_op jit(solution)/shard_map/ppermute | solution.py:552
  30.1 0.7 collective-permute-done.3
  30.8 1.4 %broadcast_select_fusion.1 = (bf16[1024,256]{1,0:T(8,128)(2,1)S(1)}, bf16[1024,256]{1,0:T(8,128)(2,1)S(1)}, bf16[1024,256]{1,0:T(8,128)(2,1)S(1)}, bf16[1024,256]{1,0:T(8,128)(2,1)S(1)}) fusion(bf16[1024,256]{1,0:T(8,128)(2,1)S(1)} %copy-done.3, bf16[1024,256]{1,0:T(8,128)(2,1)} %collective-permute-done.3, pred[]{:T(512)S(6)} %eq.24, ...), kind=kLoop, calls=%fused_computation.7 | loop fusion | flops 1048576 | bytes 4194305 | tf_op jit(solution)/shard_map/jit(_where)/select_n | solution.py:553
  32.2 0.1 pad_maximum_fusion.1.down_ref
  32.3 0.1 pad_maximum_fusion.2.up_ref
  32.4 10.9 %all-to-all-done.1 = bf16[8,2,128,256]{3,2,1,0:T(8,128)(2,1)S(1)} async-done(((bf16[8,2,128,256]{3,2,1,0:T(8,128)(2,1)}), bf16[8,2,128,256]{3,2,1,0:T(8,128)(2,1)S(1)}, u32[]{:S(2)}, u32[]{:S(2)}) %all-to-all-start.1) | async-done | bytes 1048608 | tf_op jit(solution)/shard_map/all_to_all | solution.py:586
  43.3 3.5 %shard_map.130 = (f32[1,128]{1,0:T(1,128)}, f32[128,2048]{1,0:T(8,128)S(1)}, bf16[128,256]{1,0:T(8,128)(2,1)S(1)}, bf16[1024,512]{1,0:T(8,128)(2,1)S(1)}, bf16[1024,512]{1,0:T(8,128)(2,1)S(1)}) custom-call(s32[1]{0:T(128)} %bitcast.swap_ref, s32[1,2048]{1,0:T(1,128)S(1)} %bitcast.27, f32[1,2048]{1,0:T(1,128)S(1)} %bitcast.29, ...), custom_call_target="tpu_custom_call" | custom-call | flops 1879048192 | bytes 5242880 | tf_op jit(solution)/shard_map/pallas_call | solution.py:315
  46.8 0.1 collective-permute-start.4
  46.9 1.8 %shard_map.131 = bf16[2048,256]{1,0:T(8,128)(2,1)S(1)} custom-call(s32[16,128]{1,0:T(8,128)S(1)} %bitcast.28, f32[128,2048]{1,0:T(8,128)S(1)} %get-tuple-element.46.direct_ref, bf16[128,256]{1,0:T(8,128)(2,1)S(1)} %get-tuple-element.47.dhidden_ref, bf16[2048,256]{1,0:T(8,128)(2,1)S(1)} %pad_maximum_fusion.1.down_ref), custom_call_target="tpu_custom_call" | custom-call | flops 1073741824 | bytes 2097152 | tf_op jit(solution)/shard_map/pallas_call | solution.py:233
  48.7 0.8 collective-permute-done.4
  49.6 0.3 add_convert_fusion
  49.9 0.1 copy.17
  49.9 0.1 fusion
  50.1 0.1 pad_maximum_fusion
  50.2 30.6 %all_to_all.16.grads_ref = bf16[8,512,256]{2,1,0:T(8,128)(2,1)S(1)} all-to-all(bf16[8,512,256]{2,1,0:T(8,128)(2,1)S(1)} %pad_maximum_fusion), channel_id=1, replica_groups={{0,2,4,6,8,10,12,14},{16,18,20,22,24,26,28,30},{1,3,5,7,9,11,13,15},{17..., dimensions={0} | all-to-all | bytes 4194304 | tf_op jit(solution)/shard_map/all_to_all | solution.py:616
  80.8 0.1 slice_reduce_fusion
  81.0 1.0 collective-permute-start.5
  82.0 3.2 %shard_map.132 = (bf16[512,512]{1,0:T(8,128)(2,1)S(1)}, bf16[512,512]{1,0:T(8,128)(2,1)S(1)}) custom-call(s32[1]{0:T(128)} %bitcast.swap_ref, s32[8,1,1024]{2,1,0:T(1,128)S(1)} %all_to_all.15.ids_ref, bf16[8,512,256]{2,1,0:T(8,128)(2,1)S(1)} %all_to_all.16.grads_ref), custom_call_target="tpu_custom_call" | custom-call | flops 1073741824 | bytes 3145728 | tf_op jit(solution)/shard_map/pallas_call | solution.py:179
  85.2 3.4 %collective-permute-done.5 = bf16[128,512]{1,0:T(8,128)(2,1)S(1)} collective-permute-done((bf16[128,512]{1,0:T(8,128)(2,1)S(1)}, bf16[128,512]{1,0:T(8,128)(2,1)S(1)}, u32[]{:S(2)}, u32[]{:S(2)}) %collective-permute-start.5) | collective-permute-done | bytes 131104 | tf_op jit(solution)/shard_map/ppermute | solution.py:626
  88.7 1.5 %collective-permute-start.10 = (bf16[128,512]{1,0:T(8,128)(2,1)S(1)}, bf16[128,512]{1,0:T(8,128)(2,1)S(1)}, u32[]{:S(2)}, u32[]{:S(2)}) collective-permute-start(bf16[128,512]{1,0:T(8,128)(2,1)S(1)} %add_convert_fusion.2.refs_0_), channel_id=1, source_target_pairs={{6,0},{4,2},{2,4},{0,6},{14,8},{12,10},{10,12},{8,14},{22,16},{20,... | collective-permute-start | bytes 393224 | tf_op jit(solution)/shard_map/ppermute | solution.py:502
  90.2 0.6 collective-permute-start.8
  90.8 0.1 add_convert_fusion.1
  90.8 2.5 %collective-permute-start.7 = (bf16[512,256]{1,0:T(8,128)(2,1)S(1)}, bf16[512,256]{1,0:T(8,128)(2,1)S(1)}, u32[]{:S(2)}, u32[]{:S(2)}) collective-permute-start(bf16[512,256]{1,0:T(8,128)(2,1)S(1)} %add_convert_fusion.1), channel_id=1, source_target_pairs={{0,16},{2,18},{4,20},{6,22},{8,24},{10,26},{12,28},{14,30},{16,0},... | collective-permute-start | bytes 786440 | tf_op jit(solution)/shard_map/ppermute | solution.py:645
  93.3 1.5 %collective-permute-start.9 = (bf16[128,512]{1,0:T(8,128)(2,1)S(1)}, bf16[128,512]{1,0:T(8,128)(2,1)S(1)}, u32[]{:S(2)}, u32[]{:S(2)}) collective-permute-start(bf16[128,512]{1,0:T(8,128)(2,1)S(1)} %add_convert_fusion.2.refs_0_), channel_id=1, source_target_pairs={{4,0},{6,2},{0,4},{2,6},{12,8},{14,10},{8,12},{10,14},{20,16},{22,... | collective-permute-start | bytes 393224 | tf_op jit(solution)/shard_map/ppermute | solution.py:502
  94.8 2.5 %collective-permute-done.11.refs_4_ = bf16[128,512]{1,0:T(8,128)(2,1)S(1)} collective-permute-done((bf16[128,512]{1,0:T(8,128)(2,1)S(1)}, bf16[128,512]{1,0:T(8,128)(2,1)S(1)}, u32[]{:S(2)}, u32[]{:S(2)}) %collective-permute-start.11) | collective-permute-done | bytes 131104 | tf_op jit(solution)/shard_map/ppermute | solution.py:502
  97.2 0.4 collective-permute-start.12
  97.6 1.5 %collective-permute-start.13 = (bf16[128,512]{1,0:T(8,128)(2,1)S(1)}, bf16[128,512]{1,0:T(8,128)(2,1)S(1)}, u32[]{:S(2)}, u32[]{:S(2)}) collective-permute-start(bf16[128,512]{1,0:T(8,128)(2,1)S(1)} %collective-permute-done.11.refs_4_), channel_id=1, source_target_pairs={{4,0},{6,2},{0,4},{2,6},{12,8},{14,10},{8,12},{10,14},{20,16},{22,... | collective-permute-start | bytes 393224 | tf_op jit(solution)/shard_map/ppermute | solution.py:502
  99.1 1.7 %collective-permute-start.14 = (bf16[128,512]{1,0:T(8,128)(2,1)S(1)}, bf16[128,512]{1,0:T(8,128)(2,1)S(1)}, u32[]{:S(2)}, u32[]{:S(2)}) collective-permute-start(bf16[128,512]{1,0:T(8,128)(2,1)S(1)} %collective-permute-done.11.refs_4_), channel_id=1, source_target_pairs={{6,0},{4,2},{2,4},{0,6},{14,8},{12,10},{10,12},{8,14},{22,16},{20,... | collective-permute-start | bytes 393224 | tf_op jit(solution)/shard_map/ppermute | solution.py:502
  100.7 0.1 stack.51.spots_ref
  100.8 0.1 dynamic-slice_bitcast_fusion.accum_ref
  100.9 1.7 %shard_map.133 = (f32[1024,256]{1,0:T(8,128)}, f32[1024,256]{1,0:T(8,128)}) custom-call(s32[5]{0:T(128)S(1)} %stack.51.spots_ref, bf16[128,512]{1,0:T(8,128)(2,1)S(1)} %add_convert_fusion.2.refs_0_, bf16[128,512]{1,0:T(8,128)(2,1)S(1)} %collective-permute-done.8.refs_1_, bf16[128,512]{1,0:T(8,128)(2,1)S(1)} %collective-permute-done.9.refs_2_, ...), custom_call_target="tpu_custom_call" | custom-call | flops 327680 | bytes 1966080 | tf_op jit(solution)/shard_map/pallas_call | solution.py:375
  102.6 0.9 collective-permute-done.12.refs_0_
  103.5 0.2 collective-permute-done.13.refs_1_
  103.7 1.7 %collective-permute-done.14.refs_2_ = bf16[128,512]{1,0:T(8,128)(2,1)S(1)} collective-permute-done((bf16[128,512]{1,0:T(8,128)(2,1)S(1)}, bf16[128,512]{1,0:T(8,128)(2,1)S(1)}, u32[]{:S(2)}, u32[]{:S(2)}) %collective-permute-start.14) | collective-permute-done | bytes 131104 | tf_op jit(solution)/shard_map/ppermute | solution.py:502
  105.4 0.2 collective-permute-done.7.far_ref
  105.6 0.9 shard_map.135
  106.5 0.1 pad_add_fusion.2.spots_ref
  106.6 1.5 %shard_map.134 = (f32[1024,256]{1,0:T(8,128)}, f32[1024,256]{1,0:T(8,128)}) custom-call(s32[3]{0:T(128)S(1)} %pad_add_fusion.2.spots_ref, bf16[128,512]{1,0:T(8,128)(2,1)S(1)} %collective-permute-done.12.refs_0_, bf16[128,512]{1,0:T(8,128)(2,1)S(1)} %collective-permute-done.13.refs_1_, ...), custom_call_target="tpu_custom_call", output_to_operand_aliasing={{0}: (4, {}), {1}: (5, {})} | custom-call | flops 196608 | bytes 1179648 | tf_op jit(solution)/shard_map/pallas_call | solution.py:375
  108.0 0.8 shard_map.136
  (33 shorter events, 0.2 us)
Async XLA Ops:
  0.6 100.2 %copy-start = (f32[1024]{0:T(1024)S(1)}, f32[1024]{0:T(1024)}, u32[]{:S(2)}) copy-start(f32[1024]{0:T(1024)} %param.10) | copy-start | bytes 12292
  1.7 18.1 %collective-permute-start = (bf16[512,256]{1,0:T(8,128)(2,1)S(1)}, bf16[512,256]{1,0:T(8,128)(2,1)S(1)}, u32[]{:S(2)}, u32[]{:S(2)}) collective-permute-start(bf16[512,256]{1,0:T(8,128)(2,1)S(1)} %get-tuple-element.74.first_ref.rows_ref), channel_id=1, source_target_pairs={{0,16},{2,18},{4,20},{6,22},{8,24},{10,26},{12,28},{14,30},{16,0},... | collective-permute-start | bytes 786440 | tf_op jit(solution)/shard_map/ppermute | solution.py:563
  19.8 2.2 %collective-permute-start.1 = (bf16[512,256]{1,0:T(8,128)(2,1)S(1)}, bf16[512,256]{1,0:T(8,128)(2,1)S(1)}, u32[]{:S(2)}, u32[]{:S(2)}) collective-permute-start(bf16[512,256]{1,0:T(8,128)(2,1)S(1)} %collective-permute-done.first_ref), channel_id=1, source_target_pairs={{1,0},{0,1},{3,2},{2,3},{5,4},{4,5},{7,6},{6,7},{9,8},{8,9},{11,10... | collective-permute-start | bytes 786440 | tf_op jit(solution)/shard_map/ppermute | solution.py:574
  22.0 5.8 %copy-start.4 = (bf16[1024,256]{1,0:T(8,128)(2,1)S(1)}, bf16[1024,256]{1,0:T(8,128)(2,1)}, u32[]{:S(2)}) copy-start(bf16[1024,256]{1,0:T(8,128)(2,1)} %param.11) | copy-start | bytes 1572868
  22.0 6.4 %copy-start.3 = (bf16[1024,256]{1,0:T(8,128)(2,1)S(1)}, bf16[1024,256]{1,0:T(8,128)(2,1)}, u32[]{:S(2)}) copy-start(bf16[1024,256]{1,0:T(8,128)(2,1)} %param.12) | copy-start | bytes 1572868
  22.0 6.5 %copy-start.6 = (bf16[2048]{0:T(1024)(128)(2,1)S(1)}, bf16[2048]{0:T(1024)(128)(2,1)}, u32[]{:S(2)}) copy-start(bf16[2048]{0:T(1024)(128)(2,1)} %param.14) | copy-start | bytes 12292
  22.0 6.5 %copy-start.5 = (s32[16,128]{1,0:T(8,128)S(1)}, s32[16,128]{1,0:T(8,128)}, u32[]{:S(2)}) copy-start(s32[16,128]{1,0:T(8,128)} %param.17) | copy-start | bytes 24580
  24.3 19.0 %all-to-all-start.1 = ((bf16[8,2,128,256]{3,2,1,0:T(8,128)(2,1)}), bf16[8,2,128,256]{3,2,1,0:T(8,128)(2,1)S(1)}, u32[]{:S(2)}, u32[]{:S(2)}) async-start(bf16[8,2,128,256]{3,2,1,0:T(8,128)(2,1)} %shard_map.129), calls=%async_computation.1 | async-start | bytes 2097152 | tf_op jit(solution)/shard_map/all_to_all | solution.py:586
  27.9 2.2 %collective-permute-start.2 = (bf16[1024,256]{1,0:T(8,128)(2,1)S(1)}, bf16[1024,256]{1,0:T(8,128)(2,1)}, u32[]{:S(2)}, u32[]{:S(2)}) collective-permute-start(bf16[1024,256]{1,0:T(8,128)(2,1)S(1)} %copy-done.4), channel_id=1, source_target_pairs={{1,0},{0,1},{3,2},{2,3},{5,4},{4,5},{7,6},{6,7},{9,8},{8,9},{11,10... | collective-permute-start | bytes 1572872 | tf_op jit(solution)/shard_map/ppermute | solution.py:552
  28.4 2.4 %collective-permute-start.3 = (bf16[1024,256]{1,0:T(8,128)(2,1)S(1)}, bf16[1024,256]{1,0:T(8,128)(2,1)}, u32[]{:S(2)}, u32[]{:S(2)}) collective-permute-start(bf16[1024,256]{1,0:T(8,128)(2,1)S(1)} %copy-done.3), channel_id=1, source_target_pairs={{1,0},{0,1},{3,2},{2,3},{5,4},{4,5},{7,6},{6,7},{9,8},{8,9},{11,10... | collective-permute-start | bytes 1572872 | tf_op jit(solution)/shard_map/ppermute | solution.py:552
  32.2 11.1 %copy-start.1 = (f32[2048]{0:T(1024)S(1)}, f32[2048]{0:T(1024)}, u32[]{:S(2)}) copy-start(f32[2048]{0:T(1024)} %param.13) | copy-start | bytes 24580
  32.2 11.1 %copy-start.2 = (f32[128]{0:T(128)S(1)}, f32[128]{0:T(128)}, u32[]{:S(2)}) copy-start(f32[128]{0:T(128)} %param.15) | copy-start | bytes 1540
  46.8 2.7 %collective-permute-start.4 = (bf16[1024,512]{1,0:T(8,128)(2,1)S(1)}, bf16[1024,512]{1,0:T(8,128)(2,1)S(1)}, u32[]{:S(2)}, u32[]{:S(2)}) collective-permute-start(bf16[1024,512]{1,0:T(8,128)(2,1)S(1)} %get-tuple-element.49), channel_id=1, source_target_pairs={{1,0},{0,1},{3,2},{2,3},{5,4},{4,5},{7,6},{6,7},{9,8},{8,9},{11,10... | collective-permute-start | bytes 3145736 | tf_op jit(solution)/shard_map/ppermute | solution.py:604
  81.0 7.6 %collective-permute-start.5 = (bf16[128,512]{1,0:T(8,128)(2,1)S(1)}, bf16[128,512]{1,0:T(8,128)(2,1)S(1)}, u32[]{:S(2)}, u32[]{:S(2)}) collective-permute-start(bf16[128,512]{1,0:T(8,128)(2,1)S(1)} %pad_maximum_fusion.3), channel_id=1, source_target_pairs={{0,16},{2,18},{4,20},{6,22},{8,24},{10,26},{12,28},{14,30},{16,0},... | collective-permute-start | bytes 393224 | tf_op jit(solution)/shard_map/ppermute | solution.py:626
  88.6 2.1 %collective-permute-start.6 = (bf16[512,512]{1,0:T(8,128)(2,1)S(1)}, bf16[512,512]{1,0:T(8,128)(2,1)S(1)}, u32[]{:S(2)}, u32[]{:S(2)}) collective-permute-start(bf16[512,512]{1,0:T(8,128)(2,1)S(1)} %get-tuple-element.53), channel_id=1, source_target_pairs={{1,0},{0,1},{3,2},{2,3},{5,4},{4,5},{7,6},{6,7},{9,8},{8,9},{11,10... | collective-permute-start | bytes 1572872 | tf_op jit(solution)/shard_map/ppermute | solution.py:631
  88.7 9.0 %collective-permute-start.10 = (bf16[128,512]{1,0:T(8,128)(2,1)S(1)}, bf16[128,512]{1,0:T(8,128)(2,1)S(1)}, u32[]{:S(2)}, u32[]{:S(2)}) collective-permute-start(bf16[128,512]{1,0:T(8,128)(2,1)S(1)} %add_convert_fusion.2.refs_0_), channel_id=1, source_target_pairs={{6,0},{4,2},{2,4},{0,6},{14,8},{12,10},{10,12},{8,14},{22,16},{20,... | collective-permute-start | bytes 393224 | tf_op jit(solution)/shard_map/ppermute | solution.py:502
  90.2 7.1 %collective-permute-start.11 = (bf16[128,512]{1,0:T(8,128)(2,1)S(1)}, bf16[128,512]{1,0:T(8,128)(2,1)S(1)}, u32[]{:S(2)}, u32[]{:S(2)}) collective-permute-start(bf16[128,512]{1,0:T(8,128)(2,1)S(1)} %add_convert_fusion.2.refs_0_), channel_id=1, source_target_pairs={{8,0},{10,2},{12,4},{14,6},{0,8},{2,10},{4,12},{6,14},{24,16},{26,... | collective-permute-start | bytes 393224 | tf_op jit(solution)/shard_map/ppermute | solution.py:502
  90.2 8.9 %collective-permute-start.8 = (bf16[128,512]{1,0:T(8,128)(2,1)S(1)}, bf16[128,512]{1,0:T(8,128)(2,1)S(1)}, u32[]{:S(2)}, u32[]{:S(2)}) collective-permute-start(bf16[128,512]{1,0:T(8,128)(2,1)S(1)} %add_convert_fusion.2.refs_0_), channel_id=1, source_target_pairs={{2,0},{0,2},{6,4},{4,6},{10,8},{8,10},{14,12},{12,14},{18,16},{16,... | collective-permute-start | bytes 393224 | tf_op jit(solution)/shard_map/ppermute | solution.py:502
  90.8 14.8 %collective-permute-start.7 = (bf16[512,256]{1,0:T(8,128)(2,1)S(1)}, bf16[512,256]{1,0:T(8,128)(2,1)S(1)}, u32[]{:S(2)}, u32[]{:S(2)}) collective-permute-start(bf16[512,256]{1,0:T(8,128)(2,1)S(1)} %add_convert_fusion.1), channel_id=1, source_target_pairs={{0,16},{2,18},{4,20},{6,22},{8,24},{10,26},{12,28},{14,30},{16,0},... | collective-permute-start | bytes 786440 | tf_op jit(solution)/shard_map/ppermute | solution.py:645
  93.3 7.6 %collective-permute-start.9 = (bf16[128,512]{1,0:T(8,128)(2,1)S(1)}, bf16[128,512]{1,0:T(8,128)(2,1)S(1)}, u32[]{:S(2)}, u32[]{:S(2)}) collective-permute-start(bf16[128,512]{1,0:T(8,128)(2,1)S(1)} %add_convert_fusion.2.refs_0_), channel_id=1, source_target_pairs={{4,0},{6,2},{0,4},{2,6},{12,8},{14,10},{8,12},{10,14},{20,16},{22,... | collective-permute-start | bytes 393224 | tf_op jit(solution)/shard_map/ppermute | solution.py:502
  97.2 6.2 %collective-permute-start.12 = (bf16[128,512]{1,0:T(8,128)(2,1)S(1)}, bf16[128,512]{1,0:T(8,128)(2,1)S(1)}, u32[]{:S(2)}, u32[]{:S(2)}) collective-permute-start(bf16[128,512]{1,0:T(8,128)(2,1)S(1)} %collective-permute-done.11.refs_4_), channel_id=1, source_target_pairs={{2,0},{0,2},{6,4},{4,6},{10,8},{8,10},{14,12},{12,14},{18,16},{16,... | collective-permute-start | bytes 393224 | tf_op jit(solution)/shard_map/ppermute | solution.py:502
  97.6 6.1 %collective-permute-start.13 = (bf16[128,512]{1,0:T(8,128)(2,1)S(1)}, bf16[128,512]{1,0:T(8,128)(2,1)S(1)}, u32[]{:S(2)}, u32[]{:S(2)}) collective-permute-start(bf16[128,512]{1,0:T(8,128)(2,1)S(1)} %collective-permute-done.11.refs_4_), channel_id=1, source_target_pairs={{4,0},{6,2},{0,4},{2,6},{12,8},{14,10},{8,12},{10,14},{20,16},{22,... | collective-permute-start | bytes 393224 | tf_op jit(solution)/shard_map/ppermute | solution.py:502
  99.1 6.3 %collective-permute-start.14 = (bf16[128,512]{1,0:T(8,128)(2,1)S(1)}, bf16[128,512]{1,0:T(8,128)(2,1)S(1)}, u32[]{:S(2)}, u32[]{:S(2)}) collective-permute-start(bf16[128,512]{1,0:T(8,128)(2,1)S(1)} %collective-permute-done.11.refs_4_), channel_id=1, source_target_pairs={{6,0},{4,2},{2,4},{0,6},{14,8},{12,10},{10,12},{8,14},{22,16},{20,... | collective-permute-start | bytes 393224 | tf_op jit(solution)/shard_map/ppermute | solution.py:502
  106.5 1.6 %collective-permute-start.15 = (bf16[512,256]{1,0:T(8,128)(2,1)S(1)}, bf16[512,256]{1,0:T(8,128)(2,1)S(1)}, u32[]{:S(2)}, u32[]{:S(2)}) collective-permute-start(bf16[512,256]{1,0:T(8,128)(2,1)S(1)} %get-tuple-element.65.mine_ref), channel_id=1, source_target_pairs={{1,0},{0,1},{3,2},{2,3},{5,4},{4,5},{7,6},{6,7},{9,8},{8,9},{11,10... | collective-permute-start | bytes 786440 | tf_op jit(solution)/shard_map/ppermute | solution.py:655
